TPU v7x, 32 devices: a whole 2x2x4 slice. The times are simulated.
32 devices in a mesh: sph: 8 (over z, core), fit: 4 (over y, x).
Axes of the slice: x: 2, y: 2, z: 4, core: 2. Of those that a mesh axis runs over, the one named last changes fastest.
Arguments:
- tiles: bfloat16 [1024, 163840], P('fit', 'sph'), may hold values from -0.1875 to 0.1875
- coefs: bfloat16 [16, 1024], P(None, 'fit'), may hold values from -6 to 6
- centres: float32 [3, 512], P(None, ('sph', 'fit'))
- radii: float32 [512], P(('sph', 'fit')), may hold values from 1 to 1.6
- neighbours: int32 [512, 16], P(('sph', 'fit')), may hold values from 0 to 511, as said below
- counts: int32 [512], P(('sph', 'fit')), may hold values from 1 to 16
Outputs:
- moments: float32 [512, 16, 49], P(('sph', 'fit'))
- fock: float32 [16, 1024], P(None, 'fit')
Inputs may be any that keep to these rules, and one draw needn't show every extreme that they name: `neighbours`: every entry j of row i satisfies |j - i| <= 8; the first counts[i] entries of a row are distinct and differ from i, the rest equal i.
All inputs are finite; a program needn't handle non-finite values.
Results may differ from a plain program's by a relative error of at most 0.00086.
Values may be sent and summed in bfloat16 or wider, within the bound.
No kernel may reach another device: no remote copies, remote signals or barrier semaphores. Data moves between devices by JAX's collectives and lax.ppermute only.
A program may use at most 192 MiB of HBM per device.

v0:
```python
import math

import jax
import jax.numpy as jnp
from jax import lax
from jax.sharding import PartitionSpec as P

DEGREE = 6
NTH = 16
NPHI = 20
NG = 320
NDENS = 16


band = 0.1


def with_halo(array, sides, width):
    for axis, dim in sides:
        count, length = (lax.axis_size(axis), array.shape[dim])
        up = [(i, (i + 1) % count) for i in range(count - 1)]
        down = [(j, i) for i, j in up]
        last = lax.slice_in_dim(array, length - width, length, axis=dim)
        initial = lax.slice_in_dim(array, 0, width, axis=dim)
        before = lax.ppermute(last, axis, up)
        after = lax.ppermute(initial, axis, down)
        array = jnp.concatenate([before, array, after], axis=dim)
    return array


def solid(coord_x, coord_y, coord_z):
    radius_squared = coord_x * coord_x + coord_y * coord_y + coord_z * coord_z
    cos_part = [jnp.ones_like(coord_x)]
    sin_part = [jnp.zeros_like(coord_x)]
    for harmonic_order in range(1, DEGREE + 1):
        cprev = cos_part[-1]
        sprev = sin_part[-1]
        cos_part.append(cprev * coord_x - sprev * coord_y)
        sin_part.append(cprev * coord_y + sprev * coord_x)
    result = [None] * (DEGREE + 1) ** 2
    for harmonic_order in range(DEGREE + 1):
        dfact = 1.0
        for odd in range(1, 2 * harmonic_order, 2):
            dfact = dfact * odd
        lower_term = None
        current = dfact * jnp.ones_like(coord_x)
        for harmonic_degree in range(harmonic_order, DEGREE + 1):
            if harmonic_degree > harmonic_order:
                next_term = (2 * harmonic_degree - 1) * coord_z * current
                if lower_term is not None:
                    next_term = (
                        next_term
                        - (harmonic_degree + harmonic_order - 1) * radius_squared * lower_term
                    )
                lower_term = current
                current = next_term / (harmonic_degree - harmonic_order)
            scale = math.sqrt(
                (2 * harmonic_degree + 1)
                / (4 * math.pi)
                * math.factorial(harmonic_degree - harmonic_order)
                / math.factorial(harmonic_degree + harmonic_order)
            )
            if harmonic_order == 0:
                result[harmonic_degree * harmonic_degree + harmonic_degree] = scale * current
            else:
                result[harmonic_degree * harmonic_degree + harmonic_degree + harmonic_order] = (
                    math.sqrt(2.0) * scale * current * cos_part[harmonic_order]
                )
                result[harmonic_degree * harmonic_degree + harmonic_degree - harmonic_order] = (
                    math.sqrt(2.0) * scale * current * sin_part[harmonic_order]
                )
    return result


def grid_tables():
    polar_index = jnp.arange(NTH, dtype=jnp.float32)
    polar_nodes = -1.0 + (2.0 * polar_index + 1.0) / NTH
    angles = (jnp.arange(NPHI, dtype=jnp.float32) + 0.5) * (2.0 * math.pi / NPHI)
    cosines = jnp.repeat(polar_nodes, NPHI)
    sines = jnp.sqrt(1.0 - cosines * cosines)
    azimuth = jnp.tile(angles, NTH)
    dirs = jnp.stack([sines * jnp.cos(azimuth), sines * jnp.sin(azimuth), cosines])
    weights = jnp.full((NTH * NPHI,), 4.0 * math.pi / (NTH * NPHI), dtype=jnp.float32)
    ysurf = jnp.stack(solid(dirs[0], dirs[1], dirs[2]))
    levels = jnp.asarray(
        [
            float(harmonic_degree)
            for harmonic_degree in range(DEGREE + 1)
            for harmonic_order in range(2 * harmonic_degree + 1)
        ],
        dtype=jnp.float32,
    )
    couple = 4.0 * math.pi / (2.0 * levels + 1.0)
    invert = (2.0 * levels + 1.0) / (4.0 * math.pi)
    return (dirs, weights, ysurf, couple, invert)


def block_basis(own, near, valid, dirs, couple):
    centre = own[:3]
    radius = own[3]
    offset = centre[:, :, None] - near[:3]
    near_rad = jnp.where(valid > 0, near[3], 1.0)
    vec = (offset[:, :, :, None] + radius[None, :, None, None] * dirs[:, None, None, :]) / near_rad[
        None, :, :, None
    ]
    dist = jnp.sqrt(jnp.sum(vec * vec, axis=0))
    ramp = jnp.clip((1.0 - dist) / band, 0.0, 1.0)
    switch = ramp * ramp * (3.0 - 2.0 * ramp) * valid[:, :, None]
    harm = jnp.stack(solid(vec[0], vec[1], vec[2]), axis=2)
    basis = harm * couple[None, None, :, None] * switch[:, :, None, :]
    uncovered = jnp.maximum(0.0, 1.0 - jnp.sum(switch, axis=1))
    return (basis, uncovered)


def block_rhs(weighted, uncovered, potential):
    return -jnp.einsum(
        "lp,sdp->sdl", weighted, uncovered[:, None, :] * potential, precision=lax.Precision.HIGHEST
    )


def block_sweep(basis, weighted, invert, rhs, near_moments):
    field = jnp.einsum("sklp,skdl->sdp", basis, near_moments, precision=lax.Precision.HIGHEST)
    proj = jnp.einsum("lp,sdp->sdl", weighted, field, precision=lax.Precision.HIGHEST)
    return invert[None, None, :] * (rhs + proj)


def block_charges(ysurf, weights, uncovered, moments):
    surface = jnp.einsum("lp,sdl->sdp", ysurf, moments, precision=lax.Precision.HIGHEST)
    return (surface * (weights[None, None, :] * uncovered[:, None, :])).astype(jnp.bfloat16)


def body(tiles, coefs, centres, radii, neighbours, counts):
    spheres = neighbours.shape[0]
    slots = neighbours.shape[1]
    reach = slots // 2
    aux_local = tiles.shape[0]
    block = tiles.shape[1] // NG
    dirs, weights, ysurf, couple, invert = grid_tables()
    weighted = ysurf * weights[None, :]
    tile_three = tiles.reshape(aux_local, block, NG)
    fit_index = lax.axis_index("fit")
    first_sphere = (lax.axis_index("sph") * lax.axis_size("fit") + fit_index) * spheres
    whole = jnp.einsum("da,acn->cdn", coefs, tile_three, preferred_element_type=jnp.float32)
    whole = lax.psum(whole.reshape(block, NDENS * NG), "fit")
    potential = lax.dynamic_slice_in_dim(whole, fit_index * spheres, spheres, 0)
    potential = potential.reshape(spheres, NDENS, NG)
    geometry = jnp.concatenate([centres, radii[None, :]], axis=0)
    valid = (jnp.arange(slots)[None, :] < counts[:, None]).astype(jnp.float32)
    near_geo = with_halo(geometry, ((("sph", "fit"), 1),), reach)
    local = jnp.clip(neighbours - (first_sphere - reach), 0, spheres + 2 * reach - 1)
    basis, uncovered = block_basis(geometry, near_geo[:, local], valid, dirs, couple)
    rhs = block_rhs(weighted, uncovered, potential)
    moments = invert[None, None, :] * rhs
    for sweep in range(2):
        near_state = with_halo(moments, ((("sph", "fit"), 0),), reach)
        moments = block_sweep(basis, weighted, invert, rhs, near_state[local])
    charges = block_charges(ysurf, weights, uncovered, moments).reshape(spheres, NDENS * NG)
    piece = lax.all_gather(charges, "fit", axis=0, tiled=True)
    rows = piece.shape[0]
    shaped = piece.reshape(rows, NDENS, NG)
    partial_fock = lax.dot_general(
        shaped, tile_three, (((0, 2), (1, 2)), ((), ())), preferred_element_type=jnp.float32
    )
    fock = lax.psum(partial_fock, "sph")
    return (moments, fock)


def solution(mesh):
    placed = (
        P("fit", "sph"),
        P(None, "fit"),
        P(None, ("sph", "fit")),
        P(("sph", "fit")),
        P(("sph", "fit"), None),
        P(("sph", "fit")),
    )
    return jax.shard_map(
        body,
        mesh=mesh,
        in_specs=placed,
        out_specs=(P(("sph", "fit"), None, None), P(None, "fit")),
        check_vma=False,
    )
```

profile of v0, /device:TPU:0, one launch (start us, length us, event | category | flops | bytes accessed | tf_op | source)
XLA Modules:
  0.0 242.5 jit_solution(9293991548820046019)
XLA Ops:
  8.0 4.8 %collective-permute-start = (f32[4,8]{1,0:T(4,128)S(1)}, f32[4,8]{1,0:T(4,128)S(1)}, u32[]{:S(2)}, u32[]{:S(2)}) collective-permute-start(f32[4,8]{1,0:T(4,128)S(1)} %get-tuple-element.90), channel_id=1, source_target_pairs={{0,1},{1,2},{2,3},{3,4},{4,5},{5,6},{6,7},{7,8},{8,9},{9,10},{10,1... | collective-permute-start | bytes 392 | tf_op jit(solution)/shard_map/ppermute | solution.py:25
  12.9 1.4 collective-permute-start.1
  14.3 13.7 %copy.25 = bf16[256,20480]{0,1:T(8,128)(2,1)} copy(bf16[256,20480]{1,0:T(8,128)(2,1)} %param.7) | data formatting | bytes 20971520 | tf_op args[0]
  28.0 7.1 %convolution_bitcast_fusion = f32[64,16,320]{2,1,0:T(8,128)S(1)} fusion(bf16[256,64,320]{0,2,1:T(8,128)(2,1)} %bitcast.208, bf16[16,256]{1,0:T(8,128)(2,1)S(1)} %copy-done), kind=kOutput, calls=%fused_computation.8 | convolution fusion | flops 167772160 | bytes 11804672 | tf_op jit(solution)/shard_map/da,acn->cdn/dot_general | solution.py:143
  35.1 1.6 reshape.3985
  56.6 1.0 multiply_dynamic-update-slice_fusion.28
  57.6 1.0 multiply_dynamic-update-slice_fusion.27
  63.7 0.9 multiply_dynamic-update-slice_fusion.20
  64.6 1.0 multiply_dynamic-update-slice_fusion.19
  65.7 1.1 multiply_dynamic-update-slice_fusion.18
  66.7 1.1 multiply_dynamic-update-slice_fusion.17
  67.8 0.9 multiply_dynamic-update-slice_fusion.16
  74.8 1.0 multiply_dynamic-update-slice_fusion.8
  75.8 1.1 multiply_dynamic-update-slice_fusion.7
  76.9 1.1 multiply_dynamic-update-slice_fusion.6
  78.0 1.1 multiply_dynamic-update-slice_fusion.5
  79.4 1.0 multiply_dynamic-update-slice_fusion.4
  83.9 11.8 %all-reduce.2.cloned.1.call-done = f32[64,5120]{1,0:T(8,128)} async-done(((f32[64,5120]{1,0:T(8,128)}), f32[64,5120]{1,0:T(8,128)}) %all-reduce.2.cloned.1.call-update) | async-done | bytes 1310736 | tf_op jit(solution)/shard_map/psum | solution.py:144
  95.7 1.0 constant_dynamic-slice_fusion
  97.4 3.4 %collective-permute-start.2 = (f32[8,16,49]{2,1,0:T(8,128)S(1)}, f32[8,16,49]{2,1,0:T(8,128)S(1)}, u32[]{:S(2)}, u32[]{:S(2)}) collective-permute-start(f32[8,16,49]{2,1,0:T(8,128)S(1)} %get-tuple-element.58), channel_id=1, source_target_pairs={{0,1},{1,2},{2,3},{3,4},{4,5},{5,6},{6,7},{7,8},{8,9},{9,10},{10,1... | collective-permute-start | bytes 75272 | tf_op jit(solution)/shard_map/ppermute | solution.py:25
  100.7 1.5 collective-permute-start.3
  102.2 15.1 %multiply_multiply_fusion = f32[16,16,49,320]{3,1,2,0:T(8,128)} fusion(f32[16,16,49,320]{3,1,2,0:T(8,128)} %multiply_dynamic-update-slice_fusion, f32[16,16,320]{2,1,0:T(8,128)S(1)} %get-tuple-element.55, f32[49]{0:T(128)S(1)} %copy-done.8), kind=kLoop, calls=%fused_computation.7 | loop fusion | flops 8028160 | bytes 32440516 | tf_op jit(solution)/shard_map/mul | solution.py:110
  117.4 1.0 gather_fusion.1
  118.4 28.6 %fusion.4 = f32[16,16,320]{2,1,0:T(8,128)S(1)} fusion(f32[16,16,16,49]{3,2,1,0:T(8,128)S(1)} %bitcast.211, f32[16,16,49,320]{3,1,2,0:T(8,128)} %multiply_multiply_fusion), kind=kOutput, calls=%fused_computation.10 | convolution fusion | flops 770703360 | bytes 17186816 | tf_op jit(solution)/shard_map/sklp,skdl->sdp/dot_general | solution.py:122
  147.5 4.5 %collective-permute-start.4 = (f32[8,16,49]{2,1,0:T(8,128)S(1)}, f32[8,16,49]{2,1,0:T(8,128)S(1)}, u32[]{:S(2)}, u32[]{:S(2)}) collective-permute-start(f32[8,16,49]{2,1,0:T(8,128)S(1)} %get-tuple-element.56), channel_id=1, source_target_pairs={{0,1},{1,2},{2,3},{3,4},{4,5},{5,6},{6,7},{7,8},{8,9},{9,10},{10,1... | collective-permute-start | bytes 75272 | tf_op jit(solution)/shard_map/ppermute | solution.py:25
  152.1 1.5 collective-permute-start.5
  153.9 4.6 %collective-permute-done.5 = f32[8,16,49]{2,1,0:T(8,128)S(1)} collective-permute-done((f32[8,16,49]{2,1,0:T(8,128)S(1)}, f32[8,16,49]{2,1,0:T(8,128)S(1)}, u32[]{:S(2)}, u32[]{:S(2)}) %collective-permute-start.5) | collective-permute-done | bytes 25120 | tf_op jit(solution)/shard_map/ppermute | solution.py:26
  158.5 1.0 gather_fusion.2
  159.6 28.6 %fusion.7 = f32[16,16,320]{2,1,0:T(8,128)S(1)} fusion(f32[16,16,16,49]{3,2,1,0:T(8,128)S(1)} %bitcast.210, f32[16,16,49,320]{3,1,2,0:T(8,128)} %multiply_multiply_fusion), kind=kOutput, calls=%fused_computation.11 | convolution fusion | flops 770703360 | bytes 17186816 | tf_op jit(solution)/shard_map/sklp,skdl->sdp/dot_general | solution.py:122
  189.3 13.8 %all_gather.3 = bf16[64,5120]{1,0:T(8,128)(2,1)S(1)} all-gather(bf16[16,5120]{1,0:T(8,128)(2,1)S(1)} %reshape.3987), channel_id=1, replica_groups=mesh['sph'=8,'fit'=4] {'fit'}, dimensions={0}, use_global_device_ids=true | all-gather | bytes 819200 | tf_op jit(solution)/shard_map/all_gather | solution.py:158
  203.7 5.5 %convolution_bitcast_fusion.1 = f32[16,256]{1,0:T(8,128)S(1)} fusion(bf16[64,16,320]{2,1,0:T(8,128)(2,1)S(1)} %reshape.3988, bf16[256,64,320]{0,2,1:T(8,128)(2,1)} %bitcast.209), kind=kOutput, calls=%fused_computation.20 | convolution fusion | flops 167772160 | bytes 11157504 | tf_op jit(solution)/shard_map/dot_general | solution.py:161
  209.2 26.5 %psum.15 = f32[16,256]{1,0:T(8,128)} all-reduce(f32[16,256]{1,0:T(8,128)S(1)} %convolution_bitcast_fusion.1), channel_id=1, replica_groups=mesh['sph'=8,'fit'=4] {'sph'}, use_global_device_ids=true, to_apply=%region_3.4 | all-reduce | flops 4096 | bytes 32768 | tf_op jit(solution)/shard_map/psum | solution.py:164
  (109 shorter events, 38.9 us)
Async XLA Ops:
  7.2 20.8 %copy-start = (bf16[16,256]{1,0:T(8,128)(2,1)S(1)}, bf16[16,256]{1,0:T(8,128)(2,1)}, u32[]{:S(2)}) copy-start(bf16[16,256]{1,0:T(8,128)(2,1)} %param.8) | copy-start | bytes 24580
  7.2 88.5 %all-reduce.2.cloned.1.call-start = ((), (), s32[]{:S(2)}) async-start(), calls=%async_computation | async-start | bytes 2621440 | tf_op jit(solution)/shard_map/psum | solution.py:144
  8.0 30.6 %collective-permute-start = (f32[4,8]{1,0:T(4,128)S(1)}, f32[4,8]{1,0:T(4,128)S(1)}, u32[]{:S(2)}, u32[]{:S(2)}) collective-permute-start(f32[4,8]{1,0:T(4,128)S(1)} %get-tuple-element.90), channel_id=1, source_target_pairs={{0,1},{1,2},{2,3},{3,4},{4,5},{5,6},{6,7},{7,8},{8,9},{9,10},{10,1... | collective-permute-start | bytes 392 | tf_op jit(solution)/shard_map/ppermute | solution.py:25
  12.8 25.1 %copy-start.5 = (f32[16]{0:T(128)S(1)}, f32[16]{0:T(128)}, u32[]{:S(2)}) copy-start(f32[16]{0:T(128)} %param.10) | copy-start | bytes 196
  12.9 25.2 %copy-start.4 = (s32[16,16]{1,0:T(8,128)S(1)}, s32[16,16]{1,0:T(8,128)}, u32[]{:S(2)}) copy-start(s32[16,16]{1,0:T(8,128)} %param.11) | copy-start | bytes 3076
  12.9 25.3 %copy-start.7 = (s32[16]{0:T(128)S(1)}, s32[16]{0:T(128)}, u32[]{:S(2)}) copy-start(s32[16]{0:T(128)} %param.12) | copy-start | bytes 196
  12.9 25.8 %copy-start.3 = (f32[3,16]{1,0:T(4,128)S(1)}, f32[3,16]{1,0:T(4,128)}, u32[]{:S(2)}) copy-start(f32[3,16]{1,0:T(4,128)} %param.9) | copy-start | bytes 580
  12.9 25.7 %collective-permute-start.1 = (f32[4,8]{1,0:T(4,128)S(1)}, f32[4,8]{1,0:T(4,128)S(1)}, u32[]{:S(2)}, u32[]{:S(2)}) collective-permute-start(f32[4,8]{1,0:T(4,128)S(1)} %get-tuple-element.91), channel_id=1, source_target_pairs={{1,0},{2,1},{3,2},{4,3},{5,4},{6,5},{7,6},{8,7},{9,8},{10,9},{11,1... | collective-permute-start | bytes 392 | tf_op jit(solution)/shard_map/ppermute | solution.py:26
  62.0 34.9 %copy-start.6 = (f32[49]{0:T(128)S(1)}, f32[49]{0:T(128)}, u32[]{:S(2)}) copy-start(f32[49]{0:T(128)} %constant.272) | copy-start | bytes 592
  62.0 40.3 %copy-start.8 = (f32[49]{0:T(128)S(1)}, f32[49]{0:T(128)}, u32[]{:S(2)}) copy-start(f32[49]{0:T(128)} %constant.273) | copy-start | bytes 592
  97.4 20.0 %collective-permute-start.2 = (f32[8,16,49]{2,1,0:T(8,128)S(1)}, f32[8,16,49]{2,1,0:T(8,128)S(1)}, u32[]{:S(2)}, u32[]{:S(2)}) collective-permute-start(f32[8,16,49]{2,1,0:T(8,128)S(1)} %get-tuple-element.58), channel_id=1, source_target_pairs={{0,1},{1,2},{2,3},{3,4},{4,5},{5,6},{6,7},{7,8},{8,9},{9,10},{10,1... | collective-permute-start | bytes 75272 | tf_op jit(solution)/shard_map/ppermute | solution.py:25
  100.7 16.6 %collective-permute-start.3 = (f32[8,16,49]{2,1,0:T(8,128)S(1)}, f32[8,16,49]{2,1,0:T(8,128)S(1)}, u32[]{:S(2)}, u32[]{:S(2)}) collective-permute-start(f32[8,16,49]{2,1,0:T(8,128)S(1)} %get-tuple-element.59), channel_id=1, source_target_pairs={{1,0},{2,1},{3,2},{4,3},{5,4},{6,5},{7,6},{8,7},{9,8},{10,9},{11,1... | collective-permute-start | bytes 75272 | tf_op jit(solution)/shard_map/ppermute | solution.py:26
  147.5 6.4 %collective-permute-start.4 = (f32[8,16,49]{2,1,0:T(8,128)S(1)}, f32[8,16,49]{2,1,0:T(8,128)S(1)}, u32[]{:S(2)}, u32[]{:S(2)}) collective-permute-start(f32[8,16,49]{2,1,0:T(8,128)S(1)} %get-tuple-element.56), channel_id=1, source_target_pairs={{0,1},{1,2},{2,3},{3,4},{4,5},{5,6},{6,7},{7,8},{8,9},{9,10},{10,1... | collective-permute-start | bytes 75272 | tf_op jit(solution)/shard_map/ppermute | solution.py:25
  152.1 6.4 %collective-permute-start.5 = (f32[8,16,49]{2,1,0:T(8,128)S(1)}, f32[8,16,49]{2,1,0:T(8,128)S(1)}, u32[]{:S(2)}, u32[]{:S(2)}) collective-permute-start(f32[8,16,49]{2,1,0:T(8,128)S(1)} %get-tuple-element.57), channel_id=1, source_target_pairs={{1,0},{2,1},{3,2},{4,3},{5,4},{6,5},{7,6},{8,7},{9,8},{10,9},{11,1... | collective-permute-start | bytes 75272 | tf_op jit(solution)/shard_map/ppermute | solution.py:26
  159.5 76.1 %copy-start.1 = (bf16[16,256]{1,0:T(8,128)(2,1)S(1)}, bf16[16,256]{1,0:T(8,128)(2,1)}, u32[]{:S(2)}) copy-start(bf16[16,256]{1,0:T(8,128)(2,1)} %param.8) | copy-start | bytes 24580
  188.6 47.1 %copy-start.2 = (f32[16,16,49]{2,1,0:T(8,128)}, f32[16,16,49]{2,1,0:T(8,128)S(1)}, u32[]{:S(2)}) copy-start(f32[16,16,49]{2,1,0:T(8,128)S(1)} %fusion.11) | copy-start | bytes 150532
Sparse Core Ops, SparseCore 0:
  36.8 58.9 all-reduce.1
where the time goes:
time: 243 us
  matrix products  71.6 us (29%)
  other arithmetic  60.6 us (25%)
  blocking collectives  40.3 us (17%)
  local copies, waits for them, and re-layouts  21.7 us (9%)
  starting transfers between devices  17.2 us (7%)
  waiting for transfers between devices  16.7 us (7%)
  between operations  14.4 us (6%)
    dot_general x2, matrix products, block_sweep(): jnp.einsum('sklp,skdl->sdp', basis, near_moments, precision=lax.Precision...  57.2 us
    unnamed x47, other arithmetic  42.6 us
    psum x1, blocking collectives, body(): fock = lax.psum(partial_fock, 'sph')  26.5 us
    mul x1, other arithmetic, block_basis(): basis = harm * couple[None, None, :, None] * switch[:, :, None, :]  15.1 us
    unnamed x20, local copies, waits for them, and re-layouts  14.5 us
    all_gather x1, blocking collectives, body(): piece = lax.all_gather(charges, 'fit', axis=0, tiled=True)  13.8 us
    ppermute x3, starting transfers between devices, with_halo(): before = lax.ppermute(last, axis, up)  12.8 us
    psum x1, waiting for transfers between devices, body(): whole = lax.psum(whole.reshape(block, NDENS * NG), 'fit')  11.8 us
  transfers between devices with their start and end apart: 7, of which 3 were waited for; matrix products, arithmetic and copies ran while one was open for 35% of the time, Pallas kernels for 0%

commit v1 on v0

v1 whole, which is shorter than its diff:
```python
import functools
import math

import jax
import jax.numpy as jnp
import ml_dtypes
import numpy as np
from jax import lax
from jax.experimental import pallas as pl
from jax.experimental.pallas import tpu as pltpu
from jax.sharding import PartitionSpec as P

DEGREE = 6
LM = 49
NTH = 16
NPHI = 20
NG = 320
NDENS = 16
LP = 64
QUAD = 4
QN = QUAD * NG
BAND = 0.1
BF = jnp.bfloat16
F32 = jnp.float32


def gam(l, m):
    return (l + m - 1) * (l - 1 - m) / ((2 * l - 1) * (2 * l - 3))


def tables():
    c = -1.0 + (2.0 * np.arange(NTH) + 1.0) / NTH
    f = (np.arange(NPHI) + 0.5) * (2 * np.pi / NPHI)
    z = np.repeat(c, NPHI)
    s = np.sqrt(1 - z * z)
    az = np.tile(f, NTH)
    x, y = s * np.cos(az), s * np.sin(az)
    cos, sin = [np.ones_like(x)], [np.zeros_like(x)]
    for m in range(1, DEGREE + 1):
        cos.append(cos[m - 1] * x - sin[m - 1] * y)
        sin.append(cos[m - 1] * y + sin[m - 1] * x)
    ys, scale, invert = np.zeros((LM, NG)), np.zeros(LM), np.zeros(LM)
    for m in range(DEGREE + 1):
        q, lead = {m: np.ones_like(x)}, {m: 1.0}
        for odd in range(1, 2 * m, 2):
            lead[m] *= odd
        for l in range(m + 1, DEGREE + 1):
            q[l] = z * q[l - 1] - (gam(l, m) * q[l - 2] if l > m + 1 else 0.0)
            lead[l] = lead[l - 1] * (2 * l - 1) / (l - m)
        for l in range(m, DEGREE + 1):
            n = math.sqrt(
                (2 * l + 1) / (4 * math.pi) * math.factorial(l - m) / math.factorial(l + m)
            )
            n *= math.sqrt(2.0) if m else 1.0
            for sign, trig in ((1, cos[m]), (-1, sin[m])):
                if m == 0 and sign < 0:
                    continue
                i = l * l + l + sign * m
                ys[i] = n * lead[l] * q[l] * trig
                scale[i] = n * lead[l] * 4 * math.pi / (2 * l + 1)
                invert[i] = (2 * l + 1) / (4 * math.pi)
    return np.stack([x, y, z]), ys, scale, invert


def split(a):
    a = np.asarray(a, np.float32)
    hi = a.astype(ml_dtypes.bfloat16)
    return hi, (a - hi.astype(np.float32)).astype(ml_dtypes.bfloat16)


def halves(x):
    hi = x.astype(BF)
    return hi, (x - hi.astype(F32)).astype(BF)


def pair_weights():
    dirs, ys, _, _ = tables()
    w = np.zeros((2 * NG, 2 * LP))
    wy = ys.T * (4 * math.pi / NG)
    w[:NG, :LM] = wy
    w[NG:, LP : LP + LM] = wy
    d = np.zeros((8, 2 * NG), np.float32)
    d[:3, :NG] = dirs
    d[:3, NG:] = dirs
    return np.concatenate(split(w), 1), d


def quad_weights():
    _, ys, _, _ = tables()
    w = np.zeros((QN, QUAD * LP))
    for j in range(QUAD):
        w[j * NG : (j + 1) * NG, j * LP : j * LP + LM] = ys.T
    return split(w)


def lane_scales():
    _, _, scale, invert = tables()
    rows = np.zeros((8, 2 * LP), np.float32)
    for h in (0, LP):
        rows[0, h : h + LM] = scale * invert
        rows[1, h : h + LM] = invert
    return rows


def phi_kernel(chunk_ref, coef_ref, tile_ref, out_ref):
    out_ref[...] = jnp.dot(coef_ref[...], tile_ref[...], preferred_element_type=F32)


def phi_call(chunk, coefs, tiles, width):
    aux = tiles.shape[0]
    steps = 2
    wide = width // steps
    return pl.pallas_call(
        phi_kernel,
        grid_spec=pltpu.PrefetchScalarGridSpec(
            num_scalar_prefetch=1,
            grid=(steps,),
            in_specs=[
                pl.BlockSpec((NDENS, aux), lambda b, c: (0, 0)),
                pl.BlockSpec((aux, wide), lambda b, c: (0, c[0] * steps + b)),
            ],
            out_specs=pl.BlockSpec((NDENS, wide), lambda b, c: (0, b)),
        ),
        out_shape=jax.ShapeDtypeStruct((NDENS, width), F32),
        cost_estimate=pl.CostEstimate(
            flops=2 * NDENS * aux * width,
            bytes_accessed=2 * aux * width + 4 * NDENS * width,
            transcendentals=0,
        ),
        name="phi",
    )(chunk, coefs, tiles)


def pair_build(e, geo, mask, dir_ref, bh):
    lane = lax.broadcasted_iota(jnp.int32, (8, 128), 1)
    sub = lax.broadcasted_iota(jnp.int32, (8, 128), 0)
    own = jnp.broadcast_to(geo[pl.ds(e + 8, 1), :], (8, 128))
    mrow = jnp.broadcast_to(mask[pl.ds(e, 1), :], (8, 128))
    cols = []
    for g, start in ((0, e), (1, e + 9)):
        near = geo[pl.ds(start, 8), :]
        valid = jnp.sum(jnp.where(lane == sub + 8 * g, mrow, 0.0), axis=1, keepdims=True)
        on = valid > 0.0
        ir = 1.0 / jnp.where(on, near[:, 3:4], 1.0)
        off = jnp.where(on, own - near, 0.0)
        c = [off[:, 0:1] * ir, off[:, 1:2] * ir, off[:, 2:3] * ir, own[:, 3:4] * ir, valid]
        cols.append([jnp.broadcast_to(q, (8, 128)) for q in c])
    mid = [jnp.where(lane < 64, a, b) for a, b in zip(*cols)]
    sums = []
    for t in range(5):
        ox, oy, oz, q, valid = cols[0] if t < 2 else (mid if t == 2 else cols[1])
        ls = slice(128 * t, 128 * t + 128)
        x = ox + q * dir_ref[0:1, ls]
        y = oy + q * dir_ref[1:2, ls]
        z = oz + q * dir_ref[2:3, ls]
        r2 = x * x + y * y + z * z
        ramp = jnp.clip((1.0 - jnp.sqrt(r2)) * (1.0 / BAND), 0.0, 1.0)
        chi = ramp * ramp * (3.0 - 2.0 * ramp) * valid
        sums.append(jnp.sum(chi, axis=0, keepdims=True))
        cos, sin = [chi, chi * x], [None, chi * y]
        for m in range(2, DEGREE + 1):
            cos.append(cos[m - 1] * x - sin[m - 1] * y)
            sin.append(cos[m - 1] * y + sin[m - 1] * x)
        out = [None] * LM
        for m in range(DEGREE + 1):
            qm = {}
            for l in range(m, DEGREE + 1):
                if l == m + 1:
                    qm[l] = z
                elif l == m + 2:
                    qm[l] = z * z - gam(l, m) * r2
                elif l > m + 2:
                    qm[l] = z * qm[l - 1] - (gam(l, m) * r2) * qm[l - 2]
                for sign, trig in ((1, cos[m]), (-1, sin[m])):
                    if m == 0 and sign < 0:
                        continue
                    out[l * l + l + sign * m] = trig if l == m else trig * qm[l]
        out.append(jnp.zeros((8, 128), F32))
        for p in range(25):
            both = jnp.concatenate([out[2 * p], out[2 * p + 1]], axis=0)
            bh[16 * p : 16 * p + 16, ls] = both.astype(BF)
    return sums


def pair_finish(u, w_ref, t_ref, bh):
    r = jnp.dot(bh[...], w_ref[...], preferred_element_type=F32)
    tt = r[: LM * 8, : 2 * LP] + r[: LM * 8, 2 * LP :]
    a = jnp.swapaxes(tt.reshape(LM, 8, 2 * LP), 0, 1)
    a = jnp.concatenate([a, jnp.zeros((8, LP - LM, 2 * LP), F32)], 1).reshape(8 * LP, 2 * LP)
    hi, lo = halves(a)
    t_ref[u, :, : 2 * LP] = hi
    t_ref[u, :, 2 * LP :] = lo


def uncover(sums):
    low = lax.broadcasted_iota(jnp.int32, (1, 128), 1) < 64
    swap = lambda v: pltpu.roll(v, 64, 1)
    three = []
    for s in sums:
        r2, r3, r4 = swap(s[2]), swap(s[3]), swap(s[4])
        three.append([s[0] + jnp.where(low, r2, r3), s[1] + jnp.where(low, r3, r4), s[2] + r4])
    a, b = three
    b0, b1, b2 = swap(b[0]), swap(b[1]), swap(b[2])
    tiles = [a[0], a[1], jnp.where(low, a[2], b0), jnp.where(low, b0, b1), jnp.where(low, b1, b2)]
    return [jnp.maximum(0.0, 1.0 - t) for t in tiles]


def pair_kernel(
    first_ref, before_ref, own_ref, after_ref, nbr_ref, cnt_ref, dir_ref, w_ref,
    t_ref, unc_ref, geo, mask, *bhs
):
    spheres, slots = nbr_ref.shape
    reach = slots // 2
    step = pl.program_id(0)

    @pl.when(step == 0)
    def _():
        geo[...] = jnp.zeros_like(geo)
        geo[0:reach, 0:4] = before_ref[...]
        geo[reach : reach + spheres, 0:4] = own_ref[...]
        geo[reach + spheres :, 0:4] = after_ref[...]
        rel = nbr_ref[...] - first_ref[0]
        rel = rel - lax.broadcasted_iota(jnp.int32, (spheres, slots), 0)
        slot = lax.broadcasted_iota(jnp.int32, (spheres, slots), 1)
        listed = slot < jnp.broadcast_to(cnt_ref[...], (spheres, slots))
        lane = lax.broadcasted_iota(jnp.int32, (spheres, 128), 1)
        found = jnp.zeros((spheres, 128), F32)
        for c in range(slots):
            gap = c - reach if c < reach else c - reach + 1
            hit = jnp.where(listed & (rel == gap), 1.0, 0.0)
            hit = jnp.max(hit, axis=1, keepdims=True)
            found = jnp.where(lane == c, hit, found)
        mask[...] = found

    sums = []
    for u in range(QUAD):
        sums.append(pair_build(step * QUAD + u, geo, mask, dir_ref, bhs[u]))
        pair_finish(u, w_ref, t_ref, bhs[u])
    tiles = uncover(sums[:2]) + uncover(sums[2:])
    for t, v in enumerate(tiles):
        unc_ref[0, :, 128 * t : 128 * t + 128] = v


def pair_call(first, before, own, after, neighbours, counts):
    spheres, slots = neighbours.shape
    reach = slots // 2
    w, d = pair_weights()
    whole = lambda *shape: pl.BlockSpec(shape, lambda e, f: (0,) * len(shape))
    return pl.pallas_call(
        pair_kernel,
        grid_spec=pltpu.PrefetchScalarGridSpec(
            num_scalar_prefetch=1,
            grid=(spheres // QUAD,),
            in_specs=[
                whole(reach, 4),
                whole(spheres, 4),
                whole(reach, 4),
                whole(spheres, slots),
                whole(spheres, 1),
                whole(8, 2 * NG),
                whole(2 * NG, 4 * LP),
            ],
            out_specs=[
                pl.BlockSpec((QUAD, 8 * LP, 4 * LP), lambda e, f: (e, 0, 0)),
                pl.BlockSpec((1, 1, QN), lambda e, f: (e, 0, 0)),
            ],
            scratch_shapes=[
                pltpu.VMEM((spheres + 2 * reach, 128), F32),
                pltpu.VMEM((spheres, 128), F32),
            ]
            + [pltpu.VMEM((400, 2 * NG), BF)] * QUAD,
        ),
        out_shape=[
            jax.ShapeDtypeStruct((spheres, 8 * LP, 4 * LP), BF),
            jax.ShapeDtypeStruct((spheres // QUAD, 1, QN), F32),
        ],
        cost_estimate=pl.CostEstimate(
            flops=spheres * 2 * 400 * 640 * 256, bytes_accessed=spheres * 262144, transcendentals=0
        ),
        name="pairs",
    )(first, before, own, after, neighbours, counts, jnp.asarray(d), jnp.asarray(w))


def rhs_kernel(count, *refs):
    phis, (unc_ref, wh_ref, wl_ref, left_ref, right_ref) = refs[:count], refs[count:]
    quads = unc_ref.shape[0]
    rows = []
    for b in range(quads):
        ls = slice(b * QN, (b + 1) * QN)
        total = phis[0][:, ls]
        for p in phis[1:]:
            total = total + p[:, ls]
        rows.append(total * unc_ref[b])
    hi, lo = halves(jnp.concatenate(rows, 0))
    out = jnp.dot(hi, wh_ref[...], preferred_element_type=F32)
    out = out + jnp.dot(lo, wh_ref[...], preferred_element_type=F32)
    out = out + jnp.dot(hi, wl_ref[...], preferred_element_type=F32)
    out = out * (-4.0 * math.pi / NG)
    for b in range(quads):
        ref, at = (left_ref, b) if b < quads // 2 else (right_ref, b - quads // 2)
        ref[:, at * QUAD * LP : (at + 1) * QUAD * LP] = out[b * NDENS : (b + 1) * NDENS]


def rhs_call(phis, unc, wh, wl):
    half = unc.shape[0] // 2 * QUAD * LP
    return pl.pallas_call(
        functools.partial(rhs_kernel, len(phis)),
        out_shape=[jax.ShapeDtypeStruct((NDENS, half), F32)] * 2,
        cost_estimate=pl.CostEstimate(
            flops=6 * NDENS * unc.shape[0] * QN * 256, bytes_accessed=2700000, transcendentals=0
        ),
        name="rhs",
    )(*phis, unc, wh, wl)


def gather_field(t_ref, x, xs, e):
    low = lax.broadcasted_iota(jnp.int32, (NDENS, 128), 1) < LP
    parts = []
    for odd in (0, 1):
        i = e + odd
        below, above = (x, xs) if odd == 0 else (xs, x)
        lo_at = e * LP
        up_at = (e + 8) * LP if odd == 0 else (e + 10) * LP
        lhs = jnp.concatenate(
            [below[:, lo_at : lo_at + 8 * LP], above[:, up_at : up_at + 8 * LP]], 0
        )
        r = jnp.dot(lhs, t_ref[i], preferred_element_type=F32)
        n = NDENS
        a = r[0:n, : 2 * LP] + r[n : 2 * n, : 2 * LP] + r[0:n, 2 * LP :]
        b = r[2 * n : 3 * n, : 2 * LP] + r[3 * n :, : 2 * LP] + r[2 * n : 3 * n, 2 * LP :]
        parts.append((a, b))
    (a0, b0), (a1, b1) = parts
    return jnp.where(low, a0, b1) + pltpu.roll(jnp.where(low, a1, b0), LP, 1)


def sweep_kernel(
    spheres, before_ref, left_ref, right_ref, after_ref, t_ref, rl_ref, rr_ref, sc_ref,
    *rest
):
    x, xs = rest[-2:]
    half = left_ref.shape[1]
    at = 0
    for ref in (before_ref, left_ref, right_ref, after_ref):
        wide = ref.shape[1]
        for t in range(wide // 128):
            hi, lo = halves(ref[:, 128 * t : 128 * t + 128] * sc_ref[0:1, :])
            x[0:NDENS, at : at + 128] = hi
            x[NDENS:, at : at + 128] = lo
            at += 128
    total = at
    v = x[...].astype(F32)
    xs[...] = jnp.concatenate([v[:, LP:], v[:, :LP]], 1).astype(BF)
    for e in range(0, spheres, 2):
        got = gather_field(t_ref, x, xs, e)
        ls = slice(e * LP, e * LP + 128)
        if e * LP < half:
            src, ls_in = rl_ref, ls
        else:
            src, ls_in = rr_ref, slice(e * LP - half, e * LP - half + 128)
        new = src[:, ls_in] + got
        if len(rest) == 4:
            (rest[0] if e * LP < half else rest[1])[:, ls_in] = new
        else:
            rest[0][:, ls] = new * sc_ref[1:2, :]


def sweep_call(before, left, right, after, t, rl, rr, scales, last):
    spheres = t.shape[0]
    half = left.shape[1]
    if last:
        outs = [jax.ShapeDtypeStruct((NDENS, spheres * LP), F32)]
    else:
        outs = [jax.ShapeDtypeStruct((NDENS, half), F32)] * 2
    total = before.shape[1] + 2 * half + after.shape[1]
    return pl.pallas_call(
        functools.partial(sweep_kernel, spheres),
        out_shape=outs,
        scratch_shapes=[pltpu.VMEM((2 * NDENS, total), BF)] * 2,
        cost_estimate=pl.CostEstimate(
            flops=spheres * 2 * 64 * 512 * 256, bytes_accessed=spheres * 262144, transcendentals=0
        ),
        name="sweep",
    )(before, left, right, after, t, rl, rr, scales)


def charge_kernel(m_ref, unc_ref, yh_ref, yl_ref, out_ref):
    quads = unc_ref.shape[0]
    wide = QUAD * LP
    hi, lo = halves(jnp.concatenate([m_ref[:, b * wide : (b + 1) * wide] for b in range(quads)], 0))
    dims = (((1,), (1,)), ((), ()))
    out = lax.dot_general(hi, yh_ref[...], dims, preferred_element_type=F32)
    out = out + lax.dot_general(lo, yh_ref[...], dims, preferred_element_type=F32)
    out = out + lax.dot_general(hi, yl_ref[...], dims, preferred_element_type=F32)
    for b in range(quads):
        weight = unc_ref[b] * (4.0 * math.pi / NG)
        out_ref[:, b * QN : (b + 1) * QN] = (out[b * NDENS : (b + 1) * NDENS] * weight).astype(BF)


def charge_call(moments, unc, wh, wl):
    return pl.pallas_call(
        charge_kernel,
        out_shape=jax.ShapeDtypeStruct((NDENS, unc.shape[0] * QN), BF),
        cost_estimate=pl.CostEstimate(
            flops=6 * NDENS * unc.shape[0] * QN * 256, bytes_accessed=1500000, transcendentals=0
        ),
        name="charges",
    )(moments, unc, wh, wl)


def fock_kernel(count, steps, order_ref, tile_ref, *refs):
    charges, out_ref = refs[:count], refs[count]
    g = pl.program_id(0)

    @pl.when(g == 0)
    def _():
        out_ref[...] = jnp.zeros_like(out_ref)

    for k in range(count):

        @pl.when(g // steps == k)
        def _():
            out_ref[...] += lax.dot_general(
                charges[k][...], tile_ref[...], (((1,), (1,)), ((), ())),
                preferred_element_type=F32,
            )


def fock_call(order, tiles, charges):
    aux = tiles.shape[0]
    count = len(charges)
    width = charges[0].shape[1]
    steps = 2
    wide = width // steps

    def place(k):
        return pl.BlockSpec((NDENS, wide), lambda g, o: (0, jnp.clip(g - k * steps, 0, steps - 1)))

    return pl.pallas_call(
        functools.partial(fock_kernel, count, steps),
        grid_spec=pltpu.PrefetchScalarGridSpec(
            num_scalar_prefetch=1,
            grid=(count * steps,),
            in_specs=[
                pl.BlockSpec((aux, wide), lambda g, o: (0, o[g // steps] * steps + g % steps))
            ]
            + [place(k) for k in range(count)],
            out_specs=pl.BlockSpec((NDENS, aux), lambda g, o: (0, 0)),
        ),
        out_shape=jax.ShapeDtypeStruct((NDENS, aux), F32),
        cost_estimate=pl.CostEstimate(
            flops=2 * NDENS * aux * width * count,
            bytes_accessed=2 * aux * width * count,
            transcendentals=0,
        ),
        name="fock",
    )(order, tiles, *charges)


def trade(x, axis, k):
    count = lax.axis_size(axis)
    return lax.ppermute(x, axis, [(i, i ^ k) for i in range(count)])


def reach_out(last, initial):
    axes = ("sph", "fit")
    count = lax.axis_size("sph") * lax.axis_size("fit")
    up = [(i, i + 1) for i in range(count - 1)]
    down = [(i + 1, i) for i in range(count - 1)]
    return lax.ppermute(last, axes, up), lax.ppermute(initial, axes, down)


def body(tiles, coefs, centres, radii, neighbours, counts):
    spheres, slots = neighbours.shape
    reach = slots // 2
    fits = lax.axis_size("fit")
    sphs = lax.axis_size("sph")
    assert fits & (fits - 1) == 0 and sphs & (sphs - 1) == 0
    assert spheres % (2 * QUAD) == 0 and spheres // 2 == reach == 8
    fit = lax.axis_index("fit")
    first = (lax.axis_index("sph") * fits + fit) * spheres
    wh, wl = (jnp.asarray(a) for a in quad_weights())
    scales = jnp.asarray(lane_scales())

    own = jnp.concatenate([centres, radii[None, :]], axis=0).T
    before, after = reach_out(own[spheres - reach :], own[:reach])

    width = spheres * NG
    order = jnp.stack([fit ^ k for k in range(fits)]).astype(jnp.int32)
    partial = {}
    got = {}
    for k in list(range(fits - 1, 0, -1)) + [0]:
        partial[k] = phi_call(order[k : k + 1], coefs, tiles, width)
        if k:
            got[k] = trade(partial[k], "fit", k)

    t, unc = pair_call(
        first.reshape(1).astype(jnp.int32), before, own, after, neighbours, counts[:, None]
    )
    rl, rr = rhs_call([partial[0]] + [got[k] for k in range(1, fits)], unc, wh, wl)
    left, right = rl, rr
    for last in (False, True):
        below, above = reach_out(right, left)
        res = sweep_call(below, left, right, above, t, rl, rr, scales, last)
        if not last:
            left, right = res
    moments = res[0]
    charges = charge_call(moments, unc, wh, wl)
    all_charges = [charges] + [trade(charges, "fit", k) for k in range(1, fits)]
    fock = fock_call(order, tiles, all_charges)
    fock = fock + trade(fock, "sph", 1)
    bit = 2
    while bit < sphs:
        ks = [k for k in (bit, 2 * bit, 3 * bit) if k < sphs]
        fock = functools.reduce(jnp.add, [trade(fock, "sph", k) for k in ks], fock)
        bit *= 4
    shaped = moments.reshape(NDENS, spheres, LP)[:, :, :LM]
    return jnp.transpose(shaped, (1, 0, 2)), fock


def solution(mesh):
    placed = (
        P("fit", "sph"),
        P(None, "fit"),
        P(None, ("sph", "fit")),
        P(("sph", "fit")),
        P(("sph", "fit"), None),
        P(("sph", "fit")),
    )
    return jax.shard_map(
        body,
        mesh=mesh,
        in_specs=placed,
        out_specs=(P(("sph", "fit"), None, None), P(None, "fit")),
        check_vma=False,
    )
```

time: 243 us -> 99.4 us (0.41)
  matrix products: 71.6 us -> 0 us
  other arithmetic: 60.6 us -> 2 us
  Pallas kernels: 0 us -> 41.3 us
  blocking collectives: 40.3 us -> 0 us
  local copies, waits for them, and re-layouts: 21.7 us -> 5.65 us
  between operations: 14.4 us -> 0.78 us
  starting transfers between devices: 17.2 us -> 29.5 us
  waiting for transfers between devices: 16.7 us -> 19.5 us
    dot_general x8 -> x0, matrix products: 71.6 us -> none  [the longest x2 57.2 us: block_sweep(): jnp.einsum('sklp,skdl->sdp', basis, near_moments, precision=lax.Precision...]
    unnamed x47 -> x0, other arithmetic: 42.6 us -> none
    pallas_call x0 -> x10, Pallas kernels: none -> 41.3 us  [the longest x4 10.8 us: phi_call(): pl.pallas_call(phi_kernel, grid_spec=pltpu.PrefetchScalarGridSpec(num_sca...]
    psum x1 -> x0, blocking collectives: 26.5 us -> none  [body(): fock = lax.psum(partial_fock, 'sph')]
    mul x9 -> x0, other arithmetic: 15.3 us -> none  [the longest x1 15.1 us: block_basis(): basis = harm * couple[None, None, :, None] * switch[:, :, None, :]]
    ppermute x6 -> x16, waiting for transfers between devices: 4.93 us -> 19.5 us  [the longest x10 10 us: trade(): return lax.ppermute(x, axis, [(i, i ^ k) for i in range(count)])]
    all_gather x1 -> x0, blocking collectives: 13.8 us -> none  [body(): piece = lax.all_gather(charges, 'fit', axis=0, tiled=True)]
    ppermute x6 -> x16, starting transfers between devices: 17.2 us -> 29.5 us  [the longest x6 17 us: reach_out(): return (lax.ppermute(last, axes, up), lax.ppermute(initial, axes, down))]
  transfers between devices with their start and end apart: 7 -> 16, of which waited for: 3 -> 9; matrix products, arithmetic and copies ran while one was open for 35% -> 2% of each run, Pallas kernels for 0% -> 17%
where the time goes in v1:
time: 99.4 us; the launch traced here: 98.8 us
  Pallas kernels  41.3 us (42%)
  starting transfers between devices  29.5 us (30%)
  waiting for transfers between devices  19.5 us (20%)
  local copies, waits for them, and re-layouts  5.65 us (6%)
  other arithmetic  2 us (2%)
    ppermute x6, starting transfers between devices, reach_out(): return (lax.ppermute(last, axes, up), lax.ppermute(initial, axes, down))  17 us
    ppermute x10, starting transfers between devices, trade(): return lax.ppermute(x, axis, [(i, i ^ k) for i in range(count)])  12.5 us
    pallas_call x4, Pallas kernels, phi_call(): pl.pallas_call(phi_kernel, grid_spec=pltpu.PrefetchScalarGridSpec(num_sca...  10.8 us
    ppermute x10, waiting for transfers between devices, trade(): return lax.ppermute(x, axis, [(i, i ^ k) for i in range(count)])  10 us
    ppermute x6, waiting for transfers between devices, reach_out(): return (lax.ppermute(last, axes, up), lax.ppermute(initial, axes, down))  9.47 us
    pallas_call x1, Pallas kernels, fock_call(): pl.pallas_call(functools.partial(fock_kernel, count, steps), grid_spec=pl...  9.26 us
    pallas_call x1, Pallas kernels, pair_call(): pl.pallas_call(pair_kernel, grid_spec=pltpu.PrefetchScalarGridSpec(num_sc...  8.28 us
    pallas_call x2, Pallas kernels, sweep_call(): pl.pallas_call(functools.partial(sweep_kernel, spheres), out_shape=outs,...  7.44 us
  transfers between devices with their start and end apart: 16, of which 9 were waited for; matrix products, arithmetic and copies ran while one was open for 2% of the time, Pallas kernels for 17%

profile of v1, /device:TPU:0, one launch (start us, length us, event | category | flops | bytes accessed | tf_op | source)
XLA Modules:
  0.0 98.8 jit_solution(521633335718515127)
XLA Ops:
  0.6 2.7 %phi.7 = f32[16,5120]{1,0:T(8,128)} custom-call(s32[1]{0:T(128)} %bitcast.3.chunk_ref, bf16[16,256]{1,0:T(8,128)(2,1)} %coef_ref.7, bf16[256,20480]{1,0:T(8,128)(2,1)} %tile_ref.9), custom_call_target="tpu_custom_call" | custom-call | flops 41943040 | bytes 2949120 | tf_op jit(solution)/shard_map/phi/pallas_call | solution.py:113
  3.3 3.9 %collective-permute-start.2 = (f32[16,5120]{1,0:T(8,128)}, f32[16,5120]{1,0:T(8,128)S(1)}, u32[]{:S(2)}, u32[]{:S(2)}) collective-permute-start(f32[16,5120]{1,0:T(8,128)} %phi.7), channel_id=1, source_target_pairs={{0,3},{1,2},{2,1},{3,0},{4,7},{5,6},{6,5},{7,4},{8,11},{9,10},{10,... | collective-permute-start | bytes 983048 | tf_op jit(solution)/shard_map/ppermute | solution.py:461
  7.2 2.7 %phi.6 = f32[16,5120]{1,0:T(8,128)} custom-call(s32[1]{0:T(128)} %bitcast.2.chunk_ref, bf16[16,256]{1,0:T(8,128)(2,1)} %coef_ref.7, bf16[256,20480]{1,0:T(8,128)(2,1)} %tile_ref.9), custom_call_target="tpu_custom_call" | custom-call | flops 41943040 | bytes 2949120 | tf_op jit(solution)/shard_map/phi/pallas_call | solution.py:113
  10.5 2.7 %phi.5 = f32[16,5120]{1,0:T(8,128)} custom-call(s32[1]{0:T(128)} %bitcast.1.chunk_ref, bf16[16,256]{1,0:T(8,128)(2,1)} %coef_ref.7, bf16[256,20480]{1,0:T(8,128)(2,1)} %tile_ref.9), custom_call_target="tpu_custom_call" | custom-call | flops 41943040 | bytes 2949120 | tf_op jit(solution)/shard_map/phi/pallas_call | solution.py:113
  13.3 1.3 %collective-permute-start.4 = (f32[8,4]{1,0:T(8,128)S(1)}, f32[8,4]{1,0:T(8,128)S(1)}, u32[]{:S(2)}, u32[]{:S(2)}) collective-permute-start(f32[8,4]{1,0:T(8,128)S(1)} %get-tuple-element.14), channel_id=1, source_target_pairs={{1,0},{2,1},{3,2},{4,3},{5,4},{6,5},{7,6},{8,7},{9,8},{10,9},{11,1... | collective-permute-start | bytes 392 | tf_op jit(solution)/shard_map/ppermute | solution.py:469
  14.6 4.5 %collective-permute-start.3 = (f32[8,4]{1,0:T(8,128)S(1)}, f32[8,4]{1,0:T(8,128)S(1)}, u32[]{:S(2)}, u32[]{:S(2)}) collective-permute-start(f32[8,4]{1,0:T(8,128)S(1)} %get-tuple-element.15), channel_id=1, source_target_pairs={{0,1},{1,2},{2,3},{3,4},{4,5},{5,6},{6,7},{7,8},{8,9},{9,10},{10,1... | collective-permute-start | bytes 392 | tf_op jit(solution)/shard_map/ppermute | solution.py:469
  19.2 0.7 copy.18.cnt_ref
  19.9 2.7 %phi.4.refs_0_ = f32[16,5120]{1,0:T(8,128)} custom-call(s32[1]{0:T(128)} %bitcast.chunk_ref, bf16[16,256]{1,0:T(8,128)(2,1)} %coef_ref.7, bf16[256,20480]{1,0:T(8,128)(2,1)} %tile_ref.9), custom_call_target="tpu_custom_call" | custom-call | flops 41943040 | bytes 2949120 | tf_op jit(solution)/shard_map/phi/pallas_call | solution.py:113
  23.2 8.3 %pairs.1 = (bf16[16,512,256]{2,1,0:T(8,128)(2,1)}, f32[4,1,1280]{2,1,0:T(1,128)}) custom-call(s32[1]{0:T(128)} %bitcast.4.first_ref, f32[8,4]{1,0:T(8,128)} %copy-done.16, f32[16,4]{1,0:T(8,128)} %bitcast.15, f32[8,4]{1,0:T(8,128)} %copy-done.15, s32[16,16]{1,0:T(8,128)} %nbr_ref.1, s32[16,1]{1,0:T(8,128)} %copy.18.cnt_ref, ...), custom_call_target="tpu_custom_call" | custom-call | flops 2097152000 | bytes 4194304 | tf_op jit(solution)/shard_map/pairs/pallas_call | solution.py:249
  31.5 0.7 copy-done.1
  32.5 2.8 %rhs.1 = (f32[16,512]{1,0:T(8,128)}, f32[16,512]{1,0:T(8,128)}) custom-call(f32[16,5120]{1,0:T(8,128)} %phi.4.refs_0_, f32[16,5120]{1,0:T(8,128)} %copy-done.3, f32[16,5120]{1,0:T(8,128)} %copy-done.2, f32[16,5120]{1,0:T(8,128)} %copy-done.1, f32[4,1,1280]{2,1,0:T(1,128)} %get-tuple-element.8.refs_4_.unc_ref, ...), custom_call_target="tpu_custom_call" | custom-call | flops 125829120 | bytes 2700000 | tf_op jit(solution)/shard_map/rhs/pallas_call | solution.py:306
  35.2 4.7 %collective-permute-start.5 = (f32[16,512]{1,0:T(8,128)}, f32[16,512]{1,0:T(8,128)S(1)}, u32[]{:S(2)}, u32[]{:S(2)}) collective-permute-start(f32[16,512]{1,0:T(8,128)} %get-tuple-element.9.right_ref.rr_ref), channel_id=1, source_target_pairs={{0,1},{1,2},{2,3},{3,4},{4,5},{5,6},{6,7},{7,8},{8,9},{9,10},{10,1... | collective-permute-start | bytes 98312 | tf_op jit(solution)/shard_map/ppermute | solution.py:469
  40.0 1.3 %collective-permute-start.6 = (f32[16,512]{1,0:T(8,128)}, f32[16,512]{1,0:T(8,128)S(1)}, u32[]{:S(2)}, u32[]{:S(2)}) collective-permute-start(f32[16,512]{1,0:T(8,128)} %get-tuple-element.10.left_ref.rl_ref), channel_id=1, source_target_pairs={{1,0},{2,1},{3,2},{4,3},{5,4},{6,5},{7,6},{8,7},{9,8},{10,9},{11,1... | collective-permute-start | bytes 98312 | tf_op jit(solution)/shard_map/ppermute | solution.py:469
  41.9 4.1 %collective-permute-done.6.after_ref = f32[16,512]{1,0:T(8,128)S(1)} collective-permute-done((f32[16,512]{1,0:T(8,128)}, f32[16,512]{1,0:T(8,128)S(1)}, u32[]{:S(2)}, u32[]{:S(2)}) %collective-permute-start.6) | collective-permute-done | bytes 32800 | tf_op jit(solution)/shard_map/ppermute | solution.py:469
  46.6 3.7 %sweep.2 = (f32[16,512]{1,0:T(8,128)}, f32[16,512]{1,0:T(8,128)}) custom-call(f32[16,512]{1,0:T(8,128)} %copy-done.8, f32[16,512]{1,0:T(8,128)} %get-tuple-element.10.left_ref.rl_ref, f32[16,512]{1,0:T(8,128)} %get-tuple-element.9.right_ref.rr_ref, f32[16,512]{1,0:T(8,128)} %copy-done.10, bf16[16,512,256]{2,1,0:T(8,128)(2,1)} %get-tuple-element.11.t_ref, ...), custom_call_target="tpu_custom_call" | custom-call | flops 268435456 | bytes 4194304 | tf_op jit(solution)/shard_map/sweep/pallas_call | solution.py:375
  50.3 3.9 %collective-permute-start.7 = (f32[16,512]{1,0:T(8,128)}, f32[16,512]{1,0:T(8,128)S(1)}, u32[]{:S(2)}, u32[]{:S(2)}) collective-permute-start(f32[16,512]{1,0:T(8,128)} %get-tuple-element.12.right_ref), channel_id=1, source_target_pairs={{0,1},{1,2},{2,3},{3,4},{4,5},{5,6},{6,7},{7,8},{8,9},{9,10},{10,1... | collective-permute-start | bytes 98312 | tf_op jit(solution)/shard_map/ppermute | solution.py:469
  54.2 1.3 %collective-permute-start.8 = (f32[16,512]{1,0:T(8,128)}, f32[16,512]{1,0:T(8,128)S(1)}, u32[]{:S(2)}, u32[]{:S(2)}) collective-permute-start(f32[16,512]{1,0:T(8,128)} %get-tuple-element.13.left_ref), channel_id=1, source_target_pairs={{1,0},{2,1},{3,2},{4,3},{5,4},{6,5},{7,6},{8,7},{9,8},{10,9},{11,1... | collective-permute-start | bytes 98312 | tf_op jit(solution)/shard_map/ppermute | solution.py:469
  56.1 4.1 %collective-permute-done.8.after_ref = f32[16,512]{1,0:T(8,128)S(1)} collective-permute-done((f32[16,512]{1,0:T(8,128)}, f32[16,512]{1,0:T(8,128)S(1)}, u32[]{:S(2)}, u32[]{:S(2)}) %collective-permute-start.8) | collective-permute-done | bytes 32800 | tf_op jit(solution)/shard_map/ppermute | solution.py:469
  60.8 3.7 %sweep.3.m_ref = f32[16,1024]{1,0:T(8,128)} custom-call(f32[16,512]{1,0:T(8,128)} %copy-done.7, f32[16,512]{1,0:T(8,128)} %get-tuple-element.13.left_ref, f32[16,512]{1,0:T(8,128)} %get-tuple-element.12.right_ref, f32[16,512]{1,0:T(8,128)} %copy-done.9, bf16[16,512,256]{2,1,0:T(8,128)(2,1)} %get-tuple-element.11.t_ref, ...), custom_call_target="tpu_custom_call" | custom-call | flops 268435456 | bytes 4194304 | tf_op jit(solution)/shard_map/sweep/pallas_call | solution.py:375
  64.6 2.8 %charges.1.refs_0_ = bf16[16,5120]{1,0:T(8,128)(2,1)} custom-call(f32[16,1024]{1,0:T(8,128)} %sweep.3.m_ref, f32[4,1,1280]{2,1,0:T(1,128)} %get-tuple-element.8.refs_4_.unc_ref, bf16[1280,256]{1,0:T(8,128)(2,1)} %constant.29.clone.refs_5_.yh_ref, bf16[1280,256]{1,0:T(8,128)(2,1)} %constant.30.clone.refs_6_.yl_ref), custom_call_target="tpu_custom_call" | custom-call | flops 125829120 | bytes 1500000 | tf_op jit(solution)/shard_map/charges/pallas_call | solution.py:400
  67.4 3.1 %collective-permute-start.10 = (bf16[16,5120]{1,0:T(8,128)(2,1)}, bf16[16,5120]{1,0:T(8,128)(2,1)S(1)}, u32[]{:S(2)}, u32[]{:S(2)}) collective-permute-start(bf16[16,5120]{1,0:T(8,128)(2,1)} %charges.1.refs_0_), channel_id=1, source_target_pairs={{0,2},{1,3},{2,0},{3,1},{4,6},{5,7},{6,4},{7,5},{8,10},{9,11},{10,... | collective-permute-start | bytes 491528 | tf_op jit(solution)/shard_map/ppermute | solution.py:461
  71.5 4.1 %collective-permute-done.11.refs_3_ = bf16[16,5120]{1,0:T(8,128)(2,1)S(1)} collective-permute-done((bf16[16,5120]{1,0:T(8,128)(2,1)}, bf16[16,5120]{1,0:T(8,128)(2,1)S(1)}, u32[]{:S(2)}, u32[]{:S(2)}) %collective-permute-start.11) | collective-permute-done | bytes 163872 | tf_op jit(solution)/shard_map/ppermute | solution.py:461
  75.6 3.0 %collective-permute-done.10.refs_2_ = bf16[16,5120]{1,0:T(8,128)(2,1)S(1)} collective-permute-done((bf16[16,5120]{1,0:T(8,128)(2,1)}, bf16[16,5120]{1,0:T(8,128)(2,1)S(1)}, u32[]{:S(2)}, u32[]{:S(2)}) %collective-permute-start.10) | collective-permute-done | bytes 163872 | tf_op jit(solution)/shard_map/ppermute | solution.py:461
  78.6 0.7 copy-done.5
  79.3 0.7 copy-done.6
  80.0 9.3 %fock.1 = f32[16,256]{1,0:T(8,128)} custom-call(s32[4]{0:T(128)} %pad_add_fusion.order_ref, bf16[256,20480]{1,0:T(8,128)(2,1)} %tile_ref.9, bf16[16,5120]{1,0:T(8,128)(2,1)} %charges.1.refs_0_, bf16[16,5120]{1,0:T(8,128)(2,1)} %copy-done.6, bf16[16,5120]{1,0:T(8,128)(2,1)} %copy-done.5, bf16[16,5120]{1,0:T(8,128)(2,1)} %copy-done.4), custom_call_target="tpu_custom_call" | custom-call | flops 167772160 | bytes 10485760 | tf_op jit(solution)/shard_map/fock/pallas_call | solution.py:438
  89.4 1.3 %collective-permute-done.12 = f32[16,256]{1,0:T(8,128)S(1)} collective-permute-done((f32[16,256]{1,0:T(8,128)}, f32[16,256]{1,0:T(8,128)S(1)}, u32[]{:S(2)}, u32[]{:S(2)}) %collective-permute-start.12) | collective-permute-done | bytes 16416 | tf_op jit(solution)/shard_map/ppermute | solution.py:461
  90.6 0.7 add.16
  91.9 2.5 %collective-permute-start.14 = (f32[16,256]{1,0:T(8,128)S(1)}, f32[16,256]{1,0:T(8,128)S(1)}, u32[]{:S(2)}, u32[]{:S(2)}) collective-permute-start(f32[16,256]{1,0:T(8,128)S(1)} %add.16), channel_id=1, source_target_pairs={{0,16},{4,20},{8,24},{12,28},{16,0},{20,4},{24,8},{28,12},{1,17},{... | collective-permute-start | bytes 49160 | tf_op jit(solution)/shard_map/ppermute | solution.py:461
  94.4 1.3 %collective-permute-start.13 = (f32[16,256]{1,0:T(8,128)S(1)}, f32[16,256]{1,0:T(8,128)S(1)}, u32[]{:S(2)}, u32[]{:S(2)}) collective-permute-start(f32[16,256]{1,0:T(8,128)S(1)} %add.16), channel_id=1, source_target_pairs={{0,8},{4,12},{8,0},{12,4},{16,24},{20,28},{24,16},{28,20},{1,9},{5... | collective-permute-start | bytes 49160 | tf_op jit(solution)/shard_map/ppermute | solution.py:461
  95.8 0.7 copy.22
  97.0 1.2 %collective-permute-done.13 = f32[16,256]{1,0:T(8,128)S(1)} collective-permute-done((f32[16,256]{1,0:T(8,128)S(1)}, f32[16,256]{1,0:T(8,128)S(1)}, u32[]{:S(2)}, u32[]{:S(2)}) %collective-permute-start.13) | collective-permute-done | bytes 16416 | tf_op jit(solution)/shard_map/ppermute | solution.py:461
  (53 shorter events, 6.8 us)
Async XLA Ops:
  3.3 28.1 %collective-permute-start.2 = (f32[16,5120]{1,0:T(8,128)}, f32[16,5120]{1,0:T(8,128)S(1)}, u32[]{:S(2)}, u32[]{:S(2)}) collective-permute-start(f32[16,5120]{1,0:T(8,128)} %phi.7), channel_id=1, source_target_pairs={{0,3},{1,2},{2,1},{3,0},{4,7},{5,6},{6,5},{7,4},{8,11},{9,10},{10,... | collective-permute-start | bytes 983048 | tf_op jit(solution)/shard_map/ppermute | solution.py:461
  7.2 6.0 %copy-start.12 = (f32[3,16]{1,0:T(4,128)S(1)}, f32[3,16]{1,0:T(4,128)}, u32[]{:S(2)}) copy-start(f32[3,16]{1,0:T(4,128)} %param.13) | copy-start | bytes 580
  7.2 6.0 %copy-start.13 = (f32[16]{0:T(128)S(1)}, f32[16]{0:T(128)}, u32[]{:S(2)}) copy-start(f32[16]{0:T(128)} %param.14) | copy-start | bytes 196
  7.2 12.0 %copy-start.14 = (s32[16]{0:T(128)S(1)}, s32[16]{0:T(128)}, u32[]{:S(2)}) copy-start(s32[16]{0:T(128)} %param.16) | copy-start | bytes 196
  10.0 21.5 %collective-permute-start.1 = (f32[16,5120]{1,0:T(8,128)}, f32[16,5120]{1,0:T(8,128)S(1)}, u32[]{:S(2)}, u32[]{:S(2)}) collective-permute-start(f32[16,5120]{1,0:T(8,128)} %phi.6), channel_id=1, source_target_pairs={{0,2},{1,3},{2,0},{3,1},{4,6},{5,7},{6,4},{7,5},{8,10},{9,11},{10,... | collective-permute-start | bytes 983048 | tf_op jit(solution)/shard_map/ppermute | solution.py:461
  13.2 18.3 %collective-permute-start = (f32[16,5120]{1,0:T(8,128)}, f32[16,5120]{1,0:T(8,128)S(1)}, u32[]{:S(2)}, u32[]{:S(2)}) collective-permute-start(f32[16,5120]{1,0:T(8,128)} %phi.5), channel_id=1, source_target_pairs={{0,1},{1,0},{2,3},{3,2},{4,5},{5,4},{6,7},{7,6},{8,9},{9,8},{10,11... | collective-permute-start | bytes 983048 | tf_op jit(solution)/shard_map/ppermute | solution.py:461
  13.3 9.3 %copy-start.11 = (f32[4,16]{0,1:T(8,128)}, f32[4,16]{0,1:T(8,128)S(1)}, u32[]{:S(2)}) copy-start(f32[4,16]{0,1:T(8,128)S(1)} %copy.17) | copy-start | bytes 772
  13.3 9.3 %collective-permute-start.4 = (f32[8,4]{1,0:T(8,128)S(1)}, f32[8,4]{1,0:T(8,128)S(1)}, u32[]{:S(2)}, u32[]{:S(2)}) collective-permute-start(f32[8,4]{1,0:T(8,128)S(1)} %get-tuple-element.14), channel_id=1, source_target_pairs={{1,0},{2,1},{3,2},{4,3},{5,4},{6,5},{7,6},{8,7},{9,8},{10,9},{11,1... | collective-permute-start | bytes 392 | tf_op jit(solution)/shard_map/ppermute | solution.py:469
  14.6 8.0 %collective-permute-start.3 = (f32[8,4]{1,0:T(8,128)S(1)}, f32[8,4]{1,0:T(8,128)S(1)}, u32[]{:S(2)}, u32[]{:S(2)}) collective-permute-start(f32[8,4]{1,0:T(8,128)S(1)} %get-tuple-element.15), channel_id=1, source_target_pairs={{0,1},{1,2},{2,3},{3,4},{4,5},{5,6},{6,7},{7,8},{8,9},{9,10},{10,1... | collective-permute-start | bytes 392 | tf_op jit(solution)/shard_map/ppermute | solution.py:469
  22.6 0.6 copy-start.16
  31.5 0.7 copy-start.1
  31.5 0.9 copy-start.2
  31.5 0.9 copy-start.3
  35.2 6.6 %collective-permute-start.5 = (f32[16,512]{1,0:T(8,128)}, f32[16,512]{1,0:T(8,128)S(1)}, u32[]{:S(2)}, u32[]{:S(2)}) collective-permute-start(f32[16,512]{1,0:T(8,128)} %get-tuple-element.9.right_ref.rr_ref), channel_id=1, source_target_pairs={{0,1},{1,2},{2,3},{3,4},{4,5},{5,6},{6,7},{7,8},{8,9},{9,10},{10,1... | collective-permute-start | bytes 98312 | tf_op jit(solution)/shard_map/ppermute | solution.py:469
  40.0 6.0 %collective-permute-start.6 = (f32[16,512]{1,0:T(8,128)}, f32[16,512]{1,0:T(8,128)S(1)}, u32[]{:S(2)}, u32[]{:S(2)}) collective-permute-start(f32[16,512]{1,0:T(8,128)} %get-tuple-element.10.left_ref.rl_ref), channel_id=1, source_target_pairs={{1,0},{2,1},{3,2},{4,3},{5,4},{6,5},{7,6},{8,7},{9,8},{10,9},{11,1... | collective-permute-start | bytes 98312 | tf_op jit(solution)/shard_map/ppermute | solution.py:469
  41.9 4.1 %copy-start.8 = (f32[16,512]{1,0:T(8,128)}, f32[16,512]{1,0:T(8,128)S(1)}, u32[]{:S(2)}) copy-start(f32[16,512]{1,0:T(8,128)S(1)} %collective-permute-done.5.before_ref) | copy-start | bytes 98308
  46.0 0.6 copy-start.10
  50.3 5.8 %collective-permute-start.7 = (f32[16,512]{1,0:T(8,128)}, f32[16,512]{1,0:T(8,128)S(1)}, u32[]{:S(2)}, u32[]{:S(2)}) collective-permute-start(f32[16,512]{1,0:T(8,128)} %get-tuple-element.12.right_ref), channel_id=1, source_target_pairs={{0,1},{1,2},{2,3},{3,4},{4,5},{5,6},{6,7},{7,8},{8,9},{9,10},{10,1... | collective-permute-start | bytes 98312 | tf_op jit(solution)/shard_map/ppermute | solution.py:469
  54.2 6.0 %collective-permute-start.8 = (f32[16,512]{1,0:T(8,128)}, f32[16,512]{1,0:T(8,128)S(1)}, u32[]{:S(2)}, u32[]{:S(2)}) collective-permute-start(f32[16,512]{1,0:T(8,128)} %get-tuple-element.13.left_ref), channel_id=1, source_target_pairs={{1,0},{2,1},{3,2},{4,3},{5,4},{6,5},{7,6},{8,7},{9,8},{10,9},{11,1... | collective-permute-start | bytes 98312 | tf_op jit(solution)/shard_map/ppermute | solution.py:469
  56.1 4.1 %copy-start.7 = (f32[16,512]{1,0:T(8,128)}, f32[16,512]{1,0:T(8,128)S(1)}, u32[]{:S(2)}) copy-start(f32[16,512]{1,0:T(8,128)S(1)} %collective-permute-done.7.before_ref) | copy-start | bytes 98308
  60.2 0.6 copy-start.9
  64.6 31.2 %copy-start = (f32[16,1024]{1,0:T(8,128)S(1)}, f32[16,1024]{1,0:T(8,128)}, u32[]{:S(2)}) copy-start(f32[16,1024]{1,0:T(8,128)} %sweep.3.m_ref) | copy-start | bytes 196612
  67.4 8.2 %collective-permute-start.11 = (bf16[16,5120]{1,0:T(8,128)(2,1)}, bf16[16,5120]{1,0:T(8,128)(2,1)S(1)}, u32[]{:S(2)}, u32[]{:S(2)}) collective-permute-start(bf16[16,5120]{1,0:T(8,128)(2,1)} %charges.1.refs_0_), channel_id=1, source_target_pairs={{0,3},{1,2},{2,1},{3,0},{4,7},{5,6},{6,5},{7,4},{8,11},{9,10},{10,... | collective-permute-start | bytes 491528 | tf_op jit(solution)/shard_map/ppermute | solution.py:461
  67.4 11.3 %collective-permute-start.10 = (bf16[16,5120]{1,0:T(8,128)(2,1)}, bf16[16,5120]{1,0:T(8,128)(2,1)S(1)}, u32[]{:S(2)}, u32[]{:S(2)}) collective-permute-start(bf16[16,5120]{1,0:T(8,128)(2,1)} %charges.1.refs_0_), channel_id=1, source_target_pairs={{0,2},{1,3},{2,0},{3,1},{4,6},{5,7},{6,4},{7,5},{8,10},{9,11},{10,... | collective-permute-start | bytes 491528 | tf_op jit(solution)/shard_map/ppermute | solution.py:461
  70.4 8.2 %collective-permute-start.9 = (bf16[16,5120]{1,0:T(8,128)(2,1)}, bf16[16,5120]{1,0:T(8,128)(2,1)S(1)}, u32[]{:S(2)}, u32[]{:S(2)}) collective-permute-start(bf16[16,5120]{1,0:T(8,128)(2,1)} %charges.1.refs_0_), channel_id=1, source_target_pairs={{0,1},{1,0},{2,3},{3,2},{4,5},{5,4},{6,7},{7,6},{8,9},{9,8},{10,11... | collective-permute-start | bytes 491528 | tf_op jit(solution)/shard_map/ppermute | solution.py:461
  75.6 3.1 %copy-start.4 = (bf16[16,5120]{1,0:T(8,128)(2,1)}, bf16[16,5120]{1,0:T(8,128)(2,1)S(1)}, u32[]{:S(2)}) copy-start(bf16[16,5120]{1,0:T(8,128)(2,1)S(1)} %collective-permute-done.11.refs_3_) | copy-start | bytes 491524
  78.6 0.7 copy-start.5
  79.3 0.7 copy-start.6
  89.2 1.4 %collective-permute-start.12 = (f32[16,256]{1,0:T(8,128)}, f32[16,256]{1,0:T(8,128)S(1)}, u32[]{:S(2)}, u32[]{:S(2)}) collective-permute-start(f32[16,256]{1,0:T(8,128)} %fock.1), channel_id=1, source_target_pairs={{0,4},{4,0},{8,12},{12,8},{16,20},{20,16},{24,28},{28,24},{1,5},{5... | collective-permute-start | bytes 49160 | tf_op jit(solution)/shard_map/ppermute | solution.py:461
  91.4 5.6 %collective-permute-start.15 = (f32[16,256]{1,0:T(8,128)S(1)}, f32[16,256]{1,0:T(8,128)S(1)}, u32[]{:S(2)}, u32[]{:S(2)}) collective-permute-start(f32[16,256]{1,0:T(8,128)S(1)} %add.16), channel_id=1, source_target_pairs={{0,24},{4,28},{8,16},{12,20},{16,8},{20,12},{24,0},{28,4},{1,25},{... | collective-permute-start | bytes 49160 | tf_op jit(solution)/shard_map/ppermute | solution.py:461
  91.9 5.1 %collective-permute-start.14 = (f32[16,256]{1,0:T(8,128)S(1)}, f32[16,256]{1,0:T(8,128)S(1)}, u32[]{:S(2)}, u32[]{:S(2)}) collective-permute-start(f32[16,256]{1,0:T(8,128)S(1)} %add.16), channel_id=1, source_target_pairs={{0,16},{4,20},{8,24},{12,28},{16,0},{20,4},{24,8},{28,12},{1,17},{... | collective-permute-start | bytes 49160 | tf_op jit(solution)/shard_map/ppermute | solution.py:461
  94.4 3.7 %collective-permute-start.13 = (f32[16,256]{1,0:T(8,128)S(1)}, f32[16,256]{1,0:T(8,128)S(1)}, u32[]{:S(2)}, u32[]{:S(2)}) collective-permute-start(f32[16,256]{1,0:T(8,128)S(1)} %add.16), channel_id=1, source_target_pairs={{0,8},{4,12},{8,0},{12,4},{16,24},{20,28},{24,16},{28,20},{1,9},{5... | collective-permute-start | bytes 49160 | tf_op jit(solution)/shard_map/ppermute | solution.py:461
  (1 other events, 0.6 us)

commit v2 on v1

--- a/solution.py
+++ b/solution.py
@@ -19,6 +19,9 @@
 LP = 64
 QUAD = 4
 QN = QUAD * NG
+PN = 2 * NG
+PIECE = 1280
+VMEM_LIMIT = 60 << 20
 BAND = 0.1
 BF = jnp.bfloat16
 F32 = jnp.float32
@@ -85,12 +88,12 @@
     return np.concatenate(split(w), 1), d
 
 
-def quad_weights():
+def even_weights():
     _, ys, _, _ = tables()
-    w = np.zeros((QN, QUAD * LP))
-    for j in range(QUAD):
-        w[j * NG : (j + 1) * NG, j * LP : j * LP + LM] = ys.T
-    return split(w)
+    w = np.zeros((PN, 2 * LP))
+    w[:NG, :LM] = ys.T
+    w[NG:, LP : LP + LM] = ys.T
+    return np.concatenate(split(w), 1), np.concatenate(split(w.T), 1)
 
 
 def lane_scales():
@@ -102,33 +105,50 @@
     return rows
 
 
-def phi_kernel(chunk_ref, coef_ref, tile_ref, out_ref):
-    out_ref[...] = jnp.dot(coef_ref[...], tile_ref[...], preferred_element_type=F32)
-
-
-def phi_call(chunk, coefs, tiles, width):
+def pieces(tile_ref, buf, sem, starts):
+    copies = []
+    for p, start in enumerate(starts):
+        at = pl.ds(pl.multiple_of(start, 128), PIECE)
+        copies.append(pltpu.make_async_copy(tile_ref.at[:, at], buf.at[p], sem.at[p]))
+        copies[-1].start()
+    return copies
+
+
+def phi_kernel(count, width, chunk_ref, coef_ref, tile_ref, *rest):
+    outs, (buf, sem) = rest[:count], rest[count:]
+    per = width // PIECE
+    starts = [chunk_ref[k] * width + p * PIECE for k in range(count) for p in range(per)]
+    for i, copy in enumerate(pieces(tile_ref, buf, sem, starts)):
+        copy.wait()
+        ls = slice(i % per * PIECE, (i % per + 1) * PIECE)
+        outs[i // per][:, ls] = jnp.dot(coef_ref[...], buf[i], preferred_element_type=F32)
+
+
+def phi_call(chunks, coefs, tiles, width):
     aux = tiles.shape[0]
-    steps = 2
-    wide = width // steps
+    count = chunks.shape[0]
+    total = count * width // PIECE
     return pl.pallas_call(
-        phi_kernel,
-        grid_spec=pltpu.PrefetchScalarGridSpec(
-            num_scalar_prefetch=1,
-            grid=(steps,),
-            in_specs=[
-                pl.BlockSpec((NDENS, aux), lambda b, c: (0, 0)),
-                pl.BlockSpec((aux, wide), lambda b, c: (0, c[0] * steps + b)),
-            ],
-            out_specs=pl.BlockSpec((NDENS, wide), lambda b, c: (0, b)),
-        ),
-        out_shape=jax.ShapeDtypeStruct((NDENS, width), F32),
+        functools.partial(phi_kernel, count, width),
+        in_specs=[
+            pl.BlockSpec(memory_space=pltpu.SMEM),
+            pl.BlockSpec(memory_space=pltpu.VMEM),
+            pl.BlockSpec(memory_space=pl.ANY),
+        ],
+        out_specs=[pl.BlockSpec(memory_space=pltpu.VMEM)] * count,
+        out_shape=[jax.ShapeDtypeStruct((NDENS, width), F32)] * count,
+        scratch_shapes=[
+            pltpu.VMEM((total, aux, PIECE), BF),
+            pltpu.SemaphoreType.DMA((total,)),
+        ],
+        compiler_params=pltpu.CompilerParams(vmem_limit_bytes=VMEM_LIMIT),
         cost_estimate=pl.CostEstimate(
-            flops=2 * NDENS * aux * width,
-            bytes_accessed=2 * aux * width + 4 * NDENS * width,
+            flops=2 * NDENS * aux * width * count,
+            bytes_accessed=(2 * aux + 4 * NDENS) * width * count,
             transcendentals=0,
         ),
         name="phi",
-    )(chunk, coefs, tiles)
+    )(chunks, coefs, tiles)
 
 
 def pair_build(e, geo, mask, dir_ref, bh):
@@ -206,7 +226,7 @@
 
 
 def pair_kernel(
-    first_ref, before_ref, own_ref, after_ref, nbr_ref, cnt_ref, dir_ref, w_ref,
+    first_ref, cnt_ref, before_ref, own_ref, after_ref, nbr_ref, dir_ref, w_ref,
     t_ref, unc_ref, geo, mask, *bhs
 ):
     spheres, slots = nbr_ref.shape
@@ -222,7 +242,11 @@
         rel = nbr_ref[...] - first_ref[0]
         rel = rel - lax.broadcasted_iota(jnp.int32, (spheres, slots), 0)
         slot = lax.broadcasted_iota(jnp.int32, (spheres, slots), 1)
-        listed = slot < jnp.broadcast_to(cnt_ref[...], (spheres, slots))
+        row = lax.broadcasted_iota(jnp.int32, (spheres, slots), 0)
+        many = jnp.zeros((spheres, slots), jnp.int32)
+        for i in range(spheres):
+            many = jnp.where(row == i, cnt_ref[i], many)
+        listed = slot < many
         lane = lax.broadcasted_iota(jnp.int32, (spheres, 128), 1)
         found = jnp.zeros((spheres, 128), F32)
         for c in range(slots):
@@ -245,24 +269,23 @@
     spheres, slots = neighbours.shape
     reach = slots // 2
     w, d = pair_weights()
-    whole = lambda *shape: pl.BlockSpec(shape, lambda e, f: (0,) * len(shape))
+    whole = lambda *shape: pl.BlockSpec(shape, lambda e, f, c: (0,) * len(shape))
     return pl.pallas_call(
         pair_kernel,
         grid_spec=pltpu.PrefetchScalarGridSpec(
-            num_scalar_prefetch=1,
+            num_scalar_prefetch=2,
             grid=(spheres // QUAD,),
             in_specs=[
                 whole(reach, 4),
                 whole(spheres, 4),
                 whole(reach, 4),
                 whole(spheres, slots),
-                whole(spheres, 1),
                 whole(8, 2 * NG),
                 whole(2 * NG, 4 * LP),
             ],
             out_specs=[
-                pl.BlockSpec((QUAD, 8 * LP, 4 * LP), lambda e, f: (e, 0, 0)),
-                pl.BlockSpec((1, 1, QN), lambda e, f: (e, 0, 0)),
+                pl.BlockSpec((QUAD, 8 * LP, 4 * LP), lambda e, f, c: (e, 0, 0)),
+                pl.BlockSpec((1, 1, QN), lambda e, f, c: (e, 0, 0)),
             ],
             scratch_shapes=[
                 pltpu.VMEM((spheres + 2 * reach, 128), F32),
@@ -278,42 +301,42 @@
             flops=spheres * 2 * 400 * 640 * 256, bytes_accessed=spheres * 262144, transcendentals=0
         ),
         name="pairs",
-    )(first, before, own, after, neighbours, counts, jnp.asarray(d), jnp.asarray(w))
+    )(first, counts, before, own, after, neighbours, jnp.asarray(d), jnp.asarray(w))
 
 
 def rhs_kernel(count, *refs):
-    phis, (unc_ref, wh_ref, wl_ref, left_ref, right_ref) = refs[:count], refs[count:]
-    quads = unc_ref.shape[0]
+    phis, (unc_ref, w_ref, left_ref, right_ref) = refs[:count], refs[count:]
+    pairs = 2 * unc_ref.shape[0]
     rows = []
-    for b in range(quads):
-        ls = slice(b * QN, (b + 1) * QN)
+    for b in range(pairs):
+        ls = slice(b * PN, (b + 1) * PN)
         total = phis[0][:, ls]
         for p in phis[1:]:
             total = total + p[:, ls]
-        rows.append(total * unc_ref[b])
+        rows.append(total * unc_ref[b // 2, :, b % 2 * PN : (b % 2 + 1) * PN])
     hi, lo = halves(jnp.concatenate(rows, 0))
-    out = jnp.dot(hi, wh_ref[...], preferred_element_type=F32)
-    out = out + jnp.dot(lo, wh_ref[...], preferred_element_type=F32)
-    out = out + jnp.dot(hi, wl_ref[...], preferred_element_type=F32)
+    n = pairs * NDENS
+    r = jnp.dot(jnp.concatenate([hi, lo], 0), w_ref[...], preferred_element_type=F32)
+    out = r[:n, : 2 * LP] + r[:n, 2 * LP :] + r[n:, : 2 * LP]
     out = out * (-4.0 * math.pi / NG)
-    for b in range(quads):
-        ref, at = (left_ref, b) if b < quads // 2 else (right_ref, b - quads // 2)
-        ref[:, at * QUAD * LP : (at + 1) * QUAD * LP] = out[b * NDENS : (b + 1) * NDENS]
-
-
-def rhs_call(phis, unc, wh, wl):
+    for b in range(pairs):
+        ref, at = (left_ref, b) if b < pairs // 2 else (right_ref, b - pairs // 2)
+        ref[:, at * 2 * LP : (at + 1) * 2 * LP] = out[b * NDENS : (b + 1) * NDENS]
+
+
+def rhs_call(phis, unc, w):
     half = unc.shape[0] // 2 * QUAD * LP
     return pl.pallas_call(
         functools.partial(rhs_kernel, len(phis)),
         out_shape=[jax.ShapeDtypeStruct((NDENS, half), F32)] * 2,
         cost_estimate=pl.CostEstimate(
-            flops=6 * NDENS * unc.shape[0] * QN * 256, bytes_accessed=2700000, transcendentals=0
+            flops=6 * NDENS * unc.shape[0] * QN * 256, bytes_accessed=1700000, transcendentals=0
         ),
         name="rhs",
-    )(*phis, unc, wh, wl)
-
-
-def gather_field(t_ref, x, xs, e):
+    )(*phis, unc, w)
+
+
+def gather_field(ts, x, xs, e):
     low = lax.broadcasted_iota(jnp.int32, (NDENS, 128), 1) < LP
     parts = []
     for odd in (0, 1):
@@ -324,7 +347,7 @@
         lhs = jnp.concatenate(
             [below[:, lo_at : lo_at + 8 * LP], above[:, up_at : up_at + 8 * LP]], 0
         )
-        r = jnp.dot(lhs, t_ref[i], preferred_element_type=F32)
+        r = jnp.dot(lhs, ts[i], preferred_element_type=F32)
         n = NDENS
         a = r[0:n, : 2 * LP] + r[n : 2 * n, : 2 * LP] + r[0:n, 2 * LP :]
         b = r[2 * n : 3 * n, : 2 * LP] + r[3 * n :, : 2 * LP] + r[2 * n : 3 * n, 2 * LP :]
@@ -333,11 +356,12 @@
     return jnp.where(low, a0, b1) + pltpu.roll(jnp.where(low, a1, b0), LP, 1)
 
 
-def sweep_kernel(
-    spheres, before_ref, left_ref, right_ref, after_ref, t_ref, rl_ref, rr_ref, sc_ref,
-    *rest
-):
-    x, xs = rest[-2:]
+def sweep_kernel(spheres, last, before_ref, left_ref, right_ref, after_ref, t_ref, rl_ref,
+                 rr_ref, sc_ref, *rest):
+    x, xs, ts, sem = rest[-4:]
+    copies = [pltpu.make_async_copy(t_ref.at[i], ts.at[i], sem.at[i]) for i in range(spheres)]
+    for copy in copies:
+        copy.start()
     half = left_ref.shape[1]
     at = 0
     for ref in (before_ref, left_ref, right_ref, after_ref):
@@ -347,113 +371,99 @@
             x[0:NDENS, at : at + 128] = hi
             x[NDENS:, at : at + 128] = lo
             at += 128
-    total = at
     v = x[...].astype(F32)
     xs[...] = jnp.concatenate([v[:, LP:], v[:, :LP]], 1).astype(BF)
+    rows = []
     for e in range(0, spheres, 2):
-        got = gather_field(t_ref, x, xs, e)
-        ls = slice(e * LP, e * LP + 128)
-        if e * LP < half:
-            src, ls_in = rl_ref, ls
+        copies[e].wait()
+        copies[e + 1].wait()
+        got = gather_field(ts, x, xs, e)
+        at = e * LP
+        ref, at = (rl_ref, at) if at < half else (rr_ref, at - half)
+        new = ref[:, at : at + 128] + got
+        if last:
+            new = new * sc_ref[1:2, :]
+            rest[2][e] = new[:, :LM]
+            rest[2][e + 1] = pltpu.roll(new, LP, 1)[:, :LM]
+            rows.append(new)
         else:
-            src, ls_in = rr_ref, slice(e * LP - half, e * LP - half + 128)
-        new = src[:, ls_in] + got
-        if len(rest) == 4:
-            (rest[0] if e * LP < half else rest[1])[:, ls_in] = new
-        else:
-            rest[0][:, ls] = new * sc_ref[1:2, :]
-
-
-def sweep_call(before, left, right, after, t, rl, rr, scales, last):
+            rest[0 if e * LP < half else 1][:, at : at + 128] = new
+    if last:
+        unc_ref, y_ref, _, out_ref = rest[:4]
+        hi, lo = halves(jnp.concatenate(rows, 0))
+        n = len(rows) * NDENS
+        r = jnp.dot(jnp.concatenate([hi, lo], 0), y_ref[...], preferred_element_type=F32)
+        out = r[:n, :PN] + r[:n, PN:] + r[n:, :PN]
+        for b in range(len(rows)):
+            weight = unc_ref[b // 2, :, b % 2 * PN : (b % 2 + 1) * PN] * (4.0 * math.pi / NG)
+            out_ref[:, b * PN : (b + 1) * PN] = (out[b * NDENS : (b + 1) * NDENS] * weight).astype(BF)
+
+
+def sweep_call(before, left, right, after, t, rl, rr, scales, last=None):
     spheres = t.shape[0]
     half = left.shape[1]
-    if last:
-        outs = [jax.ShapeDtypeStruct((NDENS, spheres * LP), F32)]
+    if last is None:
+        outs = [jax.ShapeDtypeStruct((NDENS, half), F32)] * 2
+        more = ()
     else:
-        outs = [jax.ShapeDtypeStruct((NDENS, half), F32)] * 2
+        outs = [
+            jax.ShapeDtypeStruct((spheres, NDENS, LM), F32),
+            jax.ShapeDtypeStruct((NDENS, spheres * NG), BF),
+        ]
+        more = last
     total = before.shape[1] + 2 * half + after.shape[1]
+    vmem = pl.BlockSpec(memory_space=pltpu.VMEM)
     return pl.pallas_call(
-        functools.partial(sweep_kernel, spheres),
+        functools.partial(sweep_kernel, spheres, last is not None),
+        in_specs=[vmem] * 4 + [pl.BlockSpec(memory_space=pl.ANY)] + [vmem] * (3 + len(more)),
+        out_specs=[vmem] * 2,
         out_shape=outs,
-        scratch_shapes=[pltpu.VMEM((2 * NDENS, total), BF)] * 2,
+        scratch_shapes=[pltpu.VMEM((2 * NDENS, total), BF)] * 2
+        + [pltpu.VMEM(t.shape, BF), pltpu.SemaphoreType.DMA((spheres,))],
+        compiler_params=pltpu.CompilerParams(vmem_limit_bytes=VMEM_LIMIT),
         cost_estimate=pl.CostEstimate(
             flops=spheres * 2 * 64 * 512 * 256, bytes_accessed=spheres * 262144, transcendentals=0
         ),
         name="sweep",
-    )(before, left, right, after, t, rl, rr, scales)
-
-
-def charge_kernel(m_ref, unc_ref, yh_ref, yl_ref, out_ref):
-    quads = unc_ref.shape[0]
-    wide = QUAD * LP
-    hi, lo = halves(jnp.concatenate([m_ref[:, b * wide : (b + 1) * wide] for b in range(quads)], 0))
-    dims = (((1,), (1,)), ((), ()))
-    out = lax.dot_general(hi, yh_ref[...], dims, preferred_element_type=F32)
-    out = out + lax.dot_general(lo, yh_ref[...], dims, preferred_element_type=F32)
-    out = out + lax.dot_general(hi, yl_ref[...], dims, preferred_element_type=F32)
-    for b in range(quads):
-        weight = unc_ref[b] * (4.0 * math.pi / NG)
-        out_ref[:, b * QN : (b + 1) * QN] = (out[b * NDENS : (b + 1) * NDENS] * weight).astype(BF)
-
-
-def charge_call(moments, unc, wh, wl):
+    )(before, left, right, after, t, rl, rr, scales, *more)
+
+
+def fock_kernel(width, chunk_ref, charge_ref, tile_ref, *rest):
+    out_ref, buf, sem = rest[-3:]
+    total = rest[0][...] if len(rest) == 4 else None
+    starts = [chunk_ref[0] * width + p * PIECE for p in range(width // PIECE)]
+    for i, copy in enumerate(pieces(tile_ref, buf, sem, starts)):
+        copy.wait()
+        part = lax.dot_general(
+            charge_ref[:, i * PIECE : (i + 1) * PIECE], buf[i], (((1,), (1,)), ((), ())),
+            preferred_element_type=F32,
+        )
+        total = part if total is None else total + part
+    out_ref[...] = total
+
+
+def fock_call(chunk, charges, tiles, before=None):
+    aux = tiles.shape[0]
+    width = charges.shape[1]
+    total = width // PIECE
+    vmem = pl.BlockSpec(memory_space=pltpu.VMEM)
+    more = [] if before is None else [before]
     return pl.pallas_call(
-        charge_kernel,
-        out_shape=jax.ShapeDtypeStruct((NDENS, unc.shape[0] * QN), BF),
+        functools.partial(fock_kernel, width),
+        in_specs=[pl.BlockSpec(memory_space=pltpu.SMEM), vmem, pl.BlockSpec(memory_space=pl.ANY)]
+        + [vmem] * len(more),
+        out_specs=vmem,
+        out_shape=jax.ShapeDtypeStruct((NDENS, aux), F32),
+        scratch_shapes=[
+            pltpu.VMEM((total, aux, PIECE), BF),
+            pltpu.SemaphoreType.DMA((total,)),
+        ],
+        compiler_params=pltpu.CompilerParams(vmem_limit_bytes=VMEM_LIMIT),
         cost_estimate=pl.CostEstimate(
-            flops=6 * NDENS * unc.shape[0] * QN * 256, bytes_accessed=1500000, transcendentals=0
-        ),
-        name="charges",
-    )(moments, unc, wh, wl)
-
-
-def fock_kernel(count, steps, order_ref, tile_ref, *refs):
-    charges, out_ref = refs[:count], refs[count]
-    g = pl.program_id(0)
-
-    @pl.when(g == 0)
-    def _():
-        out_ref[...] = jnp.zeros_like(out_ref)
-
-    for k in range(count):
-
-        @pl.when(g // steps == k)
-        def _():
-            out_ref[...] += lax.dot_general(
-                charges[k][...], tile_ref[...], (((1,), (1,)), ((), ())),
-                preferred_element_type=F32,
-            )
-
-
-def fock_call(order, tiles, charges):
-    aux = tiles.shape[0]
-    count = len(charges)
-    width = charges[0].shape[1]
-    steps = 2
-    wide = width // steps
-
-    def place(k):
-        return pl.BlockSpec((NDENS, wide), lambda g, o: (0, jnp.clip(g - k * steps, 0, steps - 1)))
-
-    return pl.pallas_call(
-        functools.partial(fock_kernel, count, steps),
-        grid_spec=pltpu.PrefetchScalarGridSpec(
-            num_scalar_prefetch=1,
-            grid=(count * steps,),
-            in_specs=[
-                pl.BlockSpec((aux, wide), lambda g, o: (0, o[g // steps] * steps + g % steps))
-            ]
-            + [place(k) for k in range(count)],
-            out_specs=pl.BlockSpec((NDENS, aux), lambda g, o: (0, 0)),
-        ),
-        out_shape=jax.ShapeDtypeStruct((NDENS, aux), F32),
-        cost_estimate=pl.CostEstimate(
-            flops=2 * NDENS * aux * width * count,
-            bytes_accessed=2 * aux * width * count,
-            transcendentals=0,
+            flops=2 * NDENS * aux * width, bytes_accessed=2 * aux * width, transcendentals=0
         ),
         name="fock",
-    )(order, tiles, *charges)
+    )(chunk, charges, tiles, *more)
 
 
 def trade(x, axis, k):
@@ -464,8 +474,8 @@
 def reach_out(last, initial):
     axes = ("sph", "fit")
     count = lax.axis_size("sph") * lax.axis_size("fit")
-    up = [(i, i + 1) for i in range(count - 1)]
-    down = [(i + 1, i) for i in range(count - 1)]
+    up = [(i, (i + 1) % count) for i in range(count)]
+    down = [((i + 1) % count, i) for i in range(count)]
     return lax.ppermute(last, axes, up), lax.ppermute(initial, axes, down)
 
 
@@ -478,43 +488,37 @@
     assert spheres % (2 * QUAD) == 0 and spheres // 2 == reach == 8
     fit = lax.axis_index("fit")
     first = (lax.axis_index("sph") * fits + fit) * spheres
-    wh, wl = (jnp.asarray(a) for a in quad_weights())
+    w, wt = (jnp.asarray(a) for a in even_weights())
     scales = jnp.asarray(lane_scales())
+    width = spheres * NG
+    order = jnp.bitwise_xor(fit, jnp.arange(fits, dtype=jnp.int32))
 
     own = jnp.concatenate([centres, radii[None, :]], axis=0).T
     before, after = reach_out(own[spheres - reach :], own[:reach])
 
-    width = spheres * NG
-    order = jnp.stack([fit ^ k for k in range(fits)]).astype(jnp.int32)
-    partial = {}
-    got = {}
-    for k in list(range(fits - 1, 0, -1)) + [0]:
-        partial[k] = phi_call(order[k : k + 1], coefs, tiles, width)
-        if k:
-            got[k] = trade(partial[k], "fit", k)
+    sent = phi_call(order[1:], coefs, tiles, width)
+    got = [trade(sent[k - 1], "fit", k) for k in range(1, fits)]
+    mine = phi_call(order[:1], coefs, tiles, width)
 
     t, unc = pair_call(
-        first.reshape(1).astype(jnp.int32), before, own, after, neighbours, counts[:, None]
+        first.reshape(1).astype(jnp.int32), before, own, after, neighbours, counts
     )
-    rl, rr = rhs_call([partial[0]] + [got[k] for k in range(1, fits)], unc, wh, wl)
-    left, right = rl, rr
-    for last in (False, True):
-        below, above = reach_out(right, left)
-        res = sweep_call(below, left, right, above, t, rl, rr, scales, last)
-        if not last:
-            left, right = res
-    moments = res[0]
-    charges = charge_call(moments, unc, wh, wl)
-    all_charges = [charges] + [trade(charges, "fit", k) for k in range(1, fits)]
-    fock = fock_call(order, tiles, all_charges)
+    rl, rr = rhs_call([*mine, *got], unc, w)
+    below, above = reach_out(rr, rl)
+    left, right = sweep_call(below, rl, rr, above, t, rl, rr, scales)
+    below, above = reach_out(right, left)
+    moments, charges = sweep_call(below, left, right, above, t, rl, rr, scales, (unc, wt))
+    others = [trade(charges, "fit", k) for k in range(1, fits)]
+    fock = fock_call(order[:1], charges, tiles)
+    for k in range(1, fits):
+        fock = fock_call(order[k : k + 1], others[k - 1], tiles, fock)
     fock = fock + trade(fock, "sph", 1)
     bit = 2
     while bit < sphs:
         ks = [k for k in (bit, 2 * bit, 3 * bit) if k < sphs]
         fock = functools.reduce(jnp.add, [trade(fock, "sph", k) for k in ks], fock)
         bit *= 4
-    shaped = moments.reshape(NDENS, spheres, LP)[:, :, :LM]
-    return jnp.transpose(shaped, (1, 0, 2)), fock
+    return moments, fock
 
 
 def solution(mesh):

time: 99.4 us -> 99.8 us (level)
  Pallas kernels: 41.3 us -> 51 us
  waiting for transfers between devices: 19.5 us -> 11.6 us
  starting transfers between devices: 29.5 us -> 27.8 us
    pallas_call x8, Pallas kernels: 30.3 us -> 39.8 us  [the longest x4 19.6 us: fock_call(): pl.pallas_call(functools.partial(fock_kernel, width), in_specs=[pl.BlockS...]
    ppermute x10, waiting for transfers between devices: 10 us -> 3.53 us  [trade(): return lax.ppermute(x, axis, [(i, i ^ k) for i in range(count)])]
    ppermute x6, starting transfers between devices: 17 us -> 15.3 us  [reach_out(): return (lax.ppermute(last, axes, up), lax.ppermute(initial, axes, down))]
    ppermute x6, waiting for transfers between devices: 9.47 us -> 8.05 us  [reach_out(): return (lax.ppermute(last, axes, up), lax.ppermute(initial, axes, down))]
    slice x0 -> x2, local copies, waits for them, and re-layouts: none -> 1.23 us  [the longest x1 0.65 us: body(): fock = fock_call(order[k:k + 1], others[k - 1], tiles, fock)]
    unnamed x35 -> x30, local copies, waits for them, and re-layouts: 4.79 us -> 5.21 us
  transfers between devices with their start and end apart: 16 -> 16, of which waited for: 9 -> 8; matrix products, arithmetic and copies ran while one was open for 2% -> 1% of each run, Pallas kernels for 17% -> 28%
where the time goes in v2:
time: 99.8 us; the launch traced here: 99.1 us
  Pallas kernels  51 us (51%)
  starting transfers between devices  27.8 us (28%)
  waiting for transfers between devices  11.6 us (12%)
  local copies, waits for them, and re-layouts  6.53 us (7%)
  other arithmetic  1.35 us (1%)
    pallas_call x4, Pallas kernels, fock_call(): pl.pallas_call(functools.partial(fock_kernel, width), in_specs=[pl.BlockS...  19.6 us
    ppermute x6, starting transfers between devices, reach_out(): return (lax.ppermute(last, axes, up), lax.ppermute(initial, axes, down))  15.3 us
    ppermute x10, starting transfers between devices, trade(): return lax.ppermute(x, axis, [(i, i ^ k) for i in range(count)])  12.5 us
    pallas_call x2, Pallas kernels, sweep_call(): pl.pallas_call(functools.partial(sweep_kernel, spheres, last is not None)...  10.9 us
    pallas_call x2, Pallas kernels, phi_call(): pl.pallas_call(functools.partial(phi_kernel, count, width), in_specs=[pl....  9.35 us
    pallas_call x1, Pallas kernels, pair_call(): pl.pallas_call(pair_kernel, grid_spec=pltpu.PrefetchScalarGridSpec(num_sc...  8.88 us
    ppermute x6, waiting for transfers between devices, reach_out(): return (lax.ppermute(last, axes, up), lax.ppermute(initial, axes, down))  8.05 us
    unnamed x30, local copies, waits for them, and re-layouts  5.21 us
  transfers between devices with their start and end apart: 16, of which 8 were waited for; matrix products, arithmetic and copies ran while one was open for 1% of the time, Pallas kernels for 28%

profile of v2, /device:TPU:0, one launch (start us, length us, event | category | flops | bytes accessed | tf_op | source)
XLA Modules:
  0.0 99.1 jit_solution(13271920595918269247)
XLA Ops:
  1.2 5.3 %phi.3 = (f32[16,5120]{1,0:T(8,128)}, f32[16,5120]{1,0:T(8,128)}, f32[16,5120]{1,0:T(8,128)}) custom-call(s32[3]{0:T(128)} %slice.23.chunk_ref, bf16[16,256]{1,0:T(8,128)(2,1)} %coef_ref.3, bf16[256,20480]{1,0:T(8,128)(2,1)} %tile_ref.11), custom_call_target="tpu_custom_call" | custom-call | flops 125829120 | bytes 8847360 | tf_op jit(solution)/shard_map/phi/pallas_call | solution.py:131
  6.6 3.0 %collective-permute-start = (f32[16,5120]{1,0:T(8,128)}, f32[16,5120]{1,0:T(8,128)S(1)}, u32[]{:S(2)}, u32[]{:S(2)}) collective-permute-start(f32[16,5120]{1,0:T(8,128)} %get-tuple-element.13), channel_id=1, source_target_pairs={{0,1},{1,0},{2,3},{3,2},{4,5},{5,4},{6,7},{7,6},{8,9},{9,8},{10,11... | collective-permute-start | bytes 983048 | tf_op jit(solution)/shard_map/ppermute | solution.py:471
  9.6 1.5 %collective-permute-start.1 = (f32[16,5120]{1,0:T(8,128)}, f32[16,5120]{1,0:T(8,128)S(1)}, u32[]{:S(2)}, u32[]{:S(2)}) collective-permute-start(f32[16,5120]{1,0:T(8,128)} %get-tuple-element.14), channel_id=1, source_target_pairs={{0,2},{1,3},{2,0},{3,1},{4,6},{5,7},{6,4},{7,5},{8,10},{9,11},{10,... | collective-permute-start | bytes 983048 | tf_op jit(solution)/shard_map/ppermute | solution.py:471
  11.2 4.5 %collective-permute-start.4 = (f32[8,4]{1,0:T(8,128)S(1)}, f32[8,4]{1,0:T(8,128)S(1)}, u32[]{:S(2)}, u32[]{:S(2)}) collective-permute-start(f32[8,4]{1,0:T(8,128)S(1)} %get-tuple-element.24), channel_id=1, source_target_pairs={{1,0},{2,1},{3,2},{4,3},{5,4},{6,5},{7,6},{8,7},{9,8},{10,9},{11,1... | collective-permute-start | bytes 392 | tf_op jit(solution)/shard_map/ppermute | solution.py:479
  15.8 0.6 fusion.1
  16.4 4.0 %phi.2.refs_0_ = f32[16,5120]{1,0:T(8,128)} custom-call(s32[1]{0:T(128)} %get-tuple-element.29.chunk_ref, bf16[16,256]{1,0:T(8,128)(2,1)} %coef_ref.3, bf16[256,20480]{1,0:T(8,128)(2,1)} %tile_ref.11), custom_call_target="tpu_custom_call" | custom-call | flops 41943040 | bytes 2949120 | tf_op jit(solution)/shard_map/phi/pallas_call | solution.py:131
  20.5 4.2 %collective-permute-done.4.after_ref = f32[8,4]{1,0:T(8,128)S(1)} collective-permute-done((f32[8,4]{1,0:T(8,128)S(1)}, f32[8,4]{1,0:T(8,128)S(1)}, u32[]{:S(2)}, u32[]{:S(2)}) %collective-permute-start.4) | collective-permute-done | bytes 160 | tf_op jit(solution)/shard_map/ppermute | solution.py:479
  25.3 8.9 %pairs.1 = (bf16[16,512,256]{2,1,0:T(8,128)(2,1)}, f32[4,1,1280]{2,1,0:T(1,128)}) custom-call(s32[1]{0:T(128)} %bitcast.first_ref, s32[16]{0:T(128)} %cnt_ref.1, f32[8,4]{1,0:T(8,128)} %copy-done.14, f32[16,4]{1,0:T(8,128)} %bitcast.4, f32[8,4]{1,0:T(8,128)} %copy-done.13, s32[16,16]{1,0:T(8,128)} %nbr_ref.1, f32[8,640]{1,0:T(8,128)} %constant.26.clone.dir_ref, ...), custom_call_target="tpu_custom_call" | custom-call | flops 2097152000 | bytes 4194304 | tf_op jit(solution)/shard_map/pairs/pallas_call | solution.py:273
  34.2 0.7 copy-done
  35.2 2.3 %rhs.1 = (f32[16,512]{1,0:T(8,128)}, f32[16,512]{1,0:T(8,128)}) custom-call(f32[16,5120]{1,0:T(8,128)} %phi.2.refs_0_, f32[16,5120]{1,0:T(8,128)} %copy-done, f32[16,5120]{1,0:T(8,128)} %copy-done.1, f32[16,5120]{1,0:T(8,128)} %copy-done.2, f32[4,1,1280]{2,1,0:T(1,128)} %get-tuple-element.16.refs_4_.rest_0_, bf16[640,256]{1,0:T(8,128)(2,1)} %constant.23.clone.refs_5_), custom_call_target="tpu_custom_call" | custom-call | flops 125829120 | bytes 1700000 | tf_op jit(solution)/shard_map/rhs/pallas_call | solution.py:329
  37.5 2.7 %collective-permute-start.5 = (f32[16,512]{1,0:T(8,128)}, f32[16,512]{1,0:T(8,128)S(1)}, u32[]{:S(2)}, u32[]{:S(2)}) collective-permute-start(f32[16,512]{1,0:T(8,128)} %get-tuple-element.17.right_ref.rr_ref), channel_id=1, source_target_pairs={{0,1},{1,2},{2,3},{3,4},{4,5},{5,6},{6,7},{7,8},{8,9},{9,10},{10,1... | collective-permute-start | bytes 98312 | tf_op jit(solution)/shard_map/ppermute | solution.py:479
  40.1 2.7 %collective-permute-start.6 = (f32[16,512]{1,0:T(8,128)}, f32[16,512]{1,0:T(8,128)S(1)}, u32[]{:S(2)}, u32[]{:S(2)}) collective-permute-start(f32[16,512]{1,0:T(8,128)} %get-tuple-element.18.left_ref.rl_ref), channel_id=1, source_target_pairs={{1,0},{2,1},{3,2},{4,3},{5,4},{6,5},{7,6},{8,7},{9,8},{10,9},{11,1... | collective-permute-start | bytes 98312 | tf_op jit(solution)/shard_map/ppermute | solution.py:479
  42.8 1.8 %collective-permute-done.5.before_ref = f32[16,512]{1,0:T(8,128)S(1)} collective-permute-done((f32[16,512]{1,0:T(8,128)}, f32[16,512]{1,0:T(8,128)S(1)}, u32[]{:S(2)}, u32[]{:S(2)}) %collective-permute-start.5) | collective-permute-done | bytes 32800 | tf_op jit(solution)/shard_map/ppermute | solution.py:479
  45.3 4.9 %sweep.2 = (f32[16,512]{1,0:T(8,128)}, f32[16,512]{1,0:T(8,128)}) custom-call(f32[16,512]{1,0:T(8,128)} %copy-done.8, f32[16,512]{1,0:T(8,128)} %get-tuple-element.18.left_ref.rl_ref, f32[16,512]{1,0:T(8,128)} %get-tuple-element.17.right_ref.rr_ref, f32[16,512]{1,0:T(8,128)} %copy-done.9, bf16[16,512,256]{2,1,0:T(8,128)(2,1)} %get-tuple-element.19.t_ref, ...), custom_call_target="tpu_custom_call" | custom-call | flops 268435456 | bytes 4194304 | tf_op jit(solution)/shard_map/sweep/pallas_call | solution.py:416
  50.2 1.1 %collective-permute-start.7 = (f32[16,512]{1,0:T(8,128)}, f32[16,512]{1,0:T(8,128)S(1)}, u32[]{:S(2)}, u32[]{:S(2)}) collective-permute-start(f32[16,512]{1,0:T(8,128)} %get-tuple-element.20.right_ref), channel_id=1, source_target_pairs={{0,1},{1,2},{2,3},{3,4},{4,5},{5,6},{6,7},{7,8},{8,9},{9,10},{10,1... | collective-permute-start | bytes 98312 | tf_op jit(solution)/shard_map/ppermute | solution.py:479
  51.3 4.3 %collective-permute-start.8 = (f32[16,512]{1,0:T(8,128)}, f32[16,512]{1,0:T(8,128)S(1)}, u32[]{:S(2)}, u32[]{:S(2)}) collective-permute-start(f32[16,512]{1,0:T(8,128)} %get-tuple-element.21.left_ref), channel_id=1, source_target_pairs={{1,0},{2,1},{3,2},{4,3},{5,4},{6,5},{7,6},{8,7},{9,8},{10,9},{11,1... | collective-permute-start | bytes 98312 | tf_op jit(solution)/shard_map/ppermute | solution.py:479
  55.6 1.8 %collective-permute-done.7.before_ref = f32[16,512]{1,0:T(8,128)S(1)} collective-permute-done((f32[16,512]{1,0:T(8,128)}, f32[16,512]{1,0:T(8,128)S(1)}, u32[]{:S(2)}, u32[]{:S(2)}) %collective-permute-start.7) | collective-permute-done | bytes 32800 | tf_op jit(solution)/shard_map/ppermute | solution.py:479
  58.6 6.0 %sweep.3 = (f32[16,16,49]{2,1,0:T(8,128)}, bf16[16,5120]{1,0:T(8,128)(2,1)}) custom-call(f32[16,512]{1,0:T(8,128)} %copy-done.6, f32[16,512]{1,0:T(8,128)} %get-tuple-element.21.left_ref, f32[16,512]{1,0:T(8,128)} %get-tuple-element.20.right_ref, f32[16,512]{1,0:T(8,128)} %copy-done.7, bf16[16,512,256]{2,1,0:T(8,128)(2,1)} %get-tuple-element.19.t_ref, ...), custom_call_target="tpu_custom_call" | custom-call | flops 268435456 | bytes 4194304 | tf_op jit(solution)/shard_map/sweep/pallas_call | solution.py:416
  64.8 3.4 %collective-permute-start.9 = (bf16[16,5120]{1,0:T(8,128)(2,1)}, bf16[16,5120]{1,0:T(8,128)(2,1)S(1)}, u32[]{:S(2)}, u32[]{:S(2)}) collective-permute-start(bf16[16,5120]{1,0:T(8,128)(2,1)} %get-tuple-element.23.charge_ref), channel_id=1, source_target_pairs={{0,3},{1,2},{2,1},{3,0},{4,7},{5,6},{6,5},{7,4},{8,11},{9,10},{10,... | collective-permute-start | bytes 491528 | tf_op jit(solution)/shard_map/ppermute | solution.py:471
  68.2 5.0 %fock.4.rest_0_ = f32[16,256]{1,0:T(8,128)} custom-call(s32[1]{0:T(128)} %get-tuple-element.29.chunk_ref, bf16[16,5120]{1,0:T(8,128)(2,1)} %get-tuple-element.23.charge_ref, bf16[256,20480]{1,0:T(8,128)(2,1)} %tile_ref.11), custom_call_target="tpu_custom_call" | custom-call | flops 41943040 | bytes 2621440 | tf_op jit(solution)/shard_map/fock/pallas_call | solution.py:451
  73.3 0.6 copy-done.5
  73.9 4.9 %fock.5.rest_0_ = f32[16,256]{1,0:T(8,128)} custom-call(s32[1]{0:T(128)} %get-tuple-element.26.chunk_ref, bf16[16,5120]{1,0:T(8,128)(2,1)} %copy-done.5, bf16[256,20480]{1,0:T(8,128)(2,1)} %tile_ref.11, f32[16,256]{1,0:T(8,128)} %fock.4.rest_0_), custom_call_target="tpu_custom_call" | custom-call | flops 41943040 | bytes 2621440 | tf_op jit(solution)/shard_map/fock/pallas_call | solution.py:451
  78.8 0.6 copy-done.4
  79.4 4.9 %fock.6.rest_0_ = f32[16,256]{1,0:T(8,128)} custom-call(s32[1]{0:T(128)} %get-tuple-element.27.chunk_ref, bf16[16,5120]{1,0:T(8,128)(2,1)} %copy-done.4, bf16[256,20480]{1,0:T(8,128)(2,1)} %tile_ref.11, f32[16,256]{1,0:T(8,128)} %fock.5.rest_0_), custom_call_target="tpu_custom_call" | custom-call | flops 41943040 | bytes 2621440 | tf_op jit(solution)/shard_map/fock/pallas_call | solution.py:451
  84.3 0.6 copy-done.3
  85.0 4.9 %fock.7 = f32[16,256]{1,0:T(8,128)} custom-call(s32[1]{0:T(128)} %get-tuple-element.28.chunk_ref, bf16[16,5120]{1,0:T(8,128)(2,1)} %copy-done.3, bf16[256,20480]{1,0:T(8,128)(2,1)} %tile_ref.11, f32[16,256]{1,0:T(8,128)} %fock.6.rest_0_), custom_call_target="tpu_custom_call" | custom-call | flops 41943040 | bytes 2621440 | tf_op jit(solution)/shard_map/fock/pallas_call | solution.py:451
  89.9 1.4 %collective-permute-done.12 = f32[16,256]{1,0:T(8,128)S(1)} collective-permute-done((f32[16,256]{1,0:T(8,128)}, f32[16,256]{1,0:T(8,128)S(1)}, u32[]{:S(2)}, u32[]{:S(2)}) %collective-permute-start.12) | collective-permute-done | bytes 16416 | tf_op jit(solution)/shard_map/ppermute | solution.py:471
  91.3 0.7 add.16
  92.0 1.9 %collective-permute-start.15 = (f32[16,256]{1,0:T(8,128)S(1)}, f32[16,256]{1,0:T(8,128)S(1)}, u32[]{:S(2)}, u32[]{:S(2)}) collective-permute-start(f32[16,256]{1,0:T(8,128)S(1)} %add.16), channel_id=1, source_target_pairs={{0,24},{4,28},{8,16},{12,20},{16,8},{20,12},{24,0},{28,4},{1,25},{... | collective-permute-start | bytes 49160 | tf_op jit(solution)/shard_map/ppermute | solution.py:471
  93.9 2.5 %collective-permute-start.13 = (f32[16,256]{1,0:T(8,128)S(1)}, f32[16,256]{1,0:T(8,128)S(1)}, u32[]{:S(2)}, u32[]{:S(2)}) collective-permute-start(f32[16,256]{1,0:T(8,128)S(1)} %add.16), channel_id=1, source_target_pairs={{0,8},{4,12},{8,0},{12,4},{16,24},{20,28},{24,16},{28,20},{1,9},{5... | collective-permute-start | bytes 49160 | tf_op jit(solution)/shard_map/ppermute | solution.py:471
  96.4 1.2 %collective-permute-done.15 = f32[16,256]{1,0:T(8,128)S(1)} collective-permute-done((f32[16,256]{1,0:T(8,128)S(1)}, f32[16,256]{1,0:T(8,128)S(1)}, u32[]{:S(2)}, u32[]{:S(2)}) %collective-permute-start.15) | collective-permute-done | bytes 16416 | tf_op jit(solution)/shard_map/ppermute | solution.py:471
  97.6 1.0 collective-permute-done.14
  (48 shorter events, 4.4 us)
Async XLA Ops:
  0.6 10.5 %copy-start.12 = (f32[16]{0:T(128)S(1)}, f32[16]{0:T(128)}, u32[]{:S(2)}) copy-start(f32[16]{0:T(128)} %param.14) | copy-start | bytes 196
  0.6 10.5 %copy-start.11 = (f32[3,16]{1,0:T(4,128)S(1)}, f32[3,16]{1,0:T(4,128)}, u32[]{:S(2)}) copy-start(f32[3,16]{1,0:T(4,128)} %param.13) | copy-start | bytes 580
  6.6 27.6 %collective-permute-start = (f32[16,5120]{1,0:T(8,128)}, f32[16,5120]{1,0:T(8,128)S(1)}, u32[]{:S(2)}, u32[]{:S(2)}) collective-permute-start(f32[16,5120]{1,0:T(8,128)} %get-tuple-element.13), channel_id=1, source_target_pairs={{0,1},{1,0},{2,3},{3,2},{4,5},{5,4},{6,7},{7,6},{8,9},{9,8},{10,11... | collective-permute-start | bytes 983048 | tf_op jit(solution)/shard_map/ppermute | solution.py:471
  9.6 24.6 %collective-permute-start.1 = (f32[16,5120]{1,0:T(8,128)}, f32[16,5120]{1,0:T(8,128)S(1)}, u32[]{:S(2)}, u32[]{:S(2)}) collective-permute-start(f32[16,5120]{1,0:T(8,128)} %get-tuple-element.14), channel_id=1, source_target_pairs={{0,2},{1,3},{2,0},{3,1},{4,6},{5,7},{6,4},{7,5},{8,10},{9,11},{10,... | collective-permute-start | bytes 983048 | tf_op jit(solution)/shard_map/ppermute | solution.py:471
  11.1 23.1 %collective-permute-start.2 = (f32[16,5120]{1,0:T(8,128)}, f32[16,5120]{1,0:T(8,128)S(1)}, u32[]{:S(2)}, u32[]{:S(2)}) collective-permute-start(f32[16,5120]{1,0:T(8,128)} %get-tuple-element.15), channel_id=1, source_target_pairs={{0,3},{1,2},{2,1},{3,0},{4,7},{5,6},{6,5},{7,4},{8,11},{9,10},{10,... | collective-permute-start | bytes 983048 | tf_op jit(solution)/shard_map/ppermute | solution.py:471
  11.2 13.5 %copy-start.10 = (f32[4,16]{0,1:T(8,128)}, f32[4,16]{0,1:T(8,128)S(1)}, u32[]{:S(2)}) copy-start(f32[4,16]{0,1:T(8,128)S(1)} %copy.15) | copy-start | bytes 772
  11.2 13.5 %collective-permute-start.4 = (f32[8,4]{1,0:T(8,128)S(1)}, f32[8,4]{1,0:T(8,128)S(1)}, u32[]{:S(2)}, u32[]{:S(2)}) collective-permute-start(f32[8,4]{1,0:T(8,128)S(1)} %get-tuple-element.24), channel_id=1, source_target_pairs={{1,0},{2,1},{3,2},{4,3},{5,4},{6,5},{7,6},{8,7},{9,8},{10,9},{11,1... | collective-permute-start | bytes 392 | tf_op jit(solution)/shard_map/ppermute | solution.py:479
  15.8 8.9 %collective-permute-start.3 = (f32[8,4]{1,0:T(8,128)S(1)}, f32[8,4]{1,0:T(8,128)S(1)}, u32[]{:S(2)}, u32[]{:S(2)}) collective-permute-start(f32[8,4]{1,0:T(8,128)S(1)} %get-tuple-element.25), channel_id=1, source_target_pairs={{0,1},{1,2},{2,3},{3,4},{4,5},{5,6},{6,7},{7,8},{8,9},{9,10},{10,1... | collective-permute-start | bytes 392 | tf_op jit(solution)/shard_map/ppermute | solution.py:479
  24.7 0.6 copy-start.13
  24.7 0.6 copy-start.14
  34.2 0.7 copy-start
  34.2 0.9 copy-start.1
  34.2 1.0 copy-start.2
  37.5 7.2 %collective-permute-start.5 = (f32[16,512]{1,0:T(8,128)}, f32[16,512]{1,0:T(8,128)S(1)}, u32[]{:S(2)}, u32[]{:S(2)}) collective-permute-start(f32[16,512]{1,0:T(8,128)} %get-tuple-element.17.right_ref.rr_ref), channel_id=1, source_target_pairs={{0,1},{1,2},{2,3},{3,4},{4,5},{5,6},{6,7},{7,8},{8,9},{9,10},{10,1... | collective-permute-start | bytes 98312 | tf_op jit(solution)/shard_map/ppermute | solution.py:479
  40.1 4.6 %collective-permute-start.6 = (f32[16,512]{1,0:T(8,128)}, f32[16,512]{1,0:T(8,128)S(1)}, u32[]{:S(2)}, u32[]{:S(2)}) collective-permute-start(f32[16,512]{1,0:T(8,128)} %get-tuple-element.18.left_ref.rl_ref), channel_id=1, source_target_pairs={{1,0},{2,1},{3,2},{4,3},{5,4},{6,5},{7,6},{8,7},{9,8},{10,9},{11,1... | collective-permute-start | bytes 98312 | tf_op jit(solution)/shard_map/ppermute | solution.py:479
  44.6 0.6 copy-start.8
  44.7 0.6 copy-start.9
  50.2 7.2 %collective-permute-start.7 = (f32[16,512]{1,0:T(8,128)}, f32[16,512]{1,0:T(8,128)S(1)}, u32[]{:S(2)}, u32[]{:S(2)}) collective-permute-start(f32[16,512]{1,0:T(8,128)} %get-tuple-element.20.right_ref), channel_id=1, source_target_pairs={{0,1},{1,2},{2,3},{3,4},{4,5},{5,6},{6,7},{7,8},{8,9},{9,10},{10,1... | collective-permute-start | bytes 98312 | tf_op jit(solution)/shard_map/ppermute | solution.py:479
  51.3 6.3 %collective-permute-start.8 = (f32[16,512]{1,0:T(8,128)}, f32[16,512]{1,0:T(8,128)S(1)}, u32[]{:S(2)}, u32[]{:S(2)}) collective-permute-start(f32[16,512]{1,0:T(8,128)} %get-tuple-element.21.left_ref), channel_id=1, source_target_pairs={{1,0},{2,1},{3,2},{4,3},{5,4},{6,5},{7,6},{8,7},{9,8},{10,9},{11,1... | collective-permute-start | bytes 98312 | tf_op jit(solution)/shard_map/ppermute | solution.py:479
  57.4 0.6 copy-start.6
  58.0 0.6 copy-start.7
  64.6 8.6 %collective-permute-start.11 = (bf16[16,5120]{1,0:T(8,128)(2,1)}, bf16[16,5120]{1,0:T(8,128)(2,1)S(1)}, u32[]{:S(2)}, u32[]{:S(2)}) collective-permute-start(bf16[16,5120]{1,0:T(8,128)(2,1)} %get-tuple-element.23.charge_ref), channel_id=1, source_target_pairs={{0,1},{1,0},{2,3},{3,2},{4,5},{5,4},{6,7},{7,6},{8,9},{9,8},{10,11... | collective-permute-start | bytes 491528 | tf_op jit(solution)/shard_map/ppermute | solution.py:471
  64.7 14.1 %collective-permute-start.10 = (bf16[16,5120]{1,0:T(8,128)(2,1)}, bf16[16,5120]{1,0:T(8,128)(2,1)S(1)}, u32[]{:S(2)}, u32[]{:S(2)}) collective-permute-start(bf16[16,5120]{1,0:T(8,128)(2,1)} %get-tuple-element.23.charge_ref), channel_id=1, source_target_pairs={{0,2},{1,3},{2,0},{3,1},{4,6},{5,7},{6,4},{7,5},{8,10},{9,11},{10,... | collective-permute-start | bytes 491528 | tf_op jit(solution)/shard_map/ppermute | solution.py:471
  64.8 19.5 %collective-permute-start.9 = (bf16[16,5120]{1,0:T(8,128)(2,1)}, bf16[16,5120]{1,0:T(8,128)(2,1)S(1)}, u32[]{:S(2)}, u32[]{:S(2)}) collective-permute-start(bf16[16,5120]{1,0:T(8,128)(2,1)} %get-tuple-element.23.charge_ref), channel_id=1, source_target_pairs={{0,3},{1,2},{2,1},{3,0},{4,7},{5,6},{6,5},{7,4},{8,11},{9,10},{10,... | collective-permute-start | bytes 491528 | tf_op jit(solution)/shard_map/ppermute | solution.py:471
  73.3 0.7 copy-start.5
  78.8 0.7 copy-start.4
  84.3 0.7 copy-start.3
  89.8 1.5 %collective-permute-start.12 = (f32[16,256]{1,0:T(8,128)}, f32[16,256]{1,0:T(8,128)S(1)}, u32[]{:S(2)}, u32[]{:S(2)}) collective-permute-start(f32[16,256]{1,0:T(8,128)} %fock.7), channel_id=1, source_target_pairs={{0,4},{4,0},{8,12},{12,8},{16,20},{20,16},{24,28},{28,24},{1,5},{5... | collective-permute-start | bytes 49160 | tf_op jit(solution)/shard_map/ppermute | solution.py:471
  92.0 5.5 %collective-permute-start.15 = (f32[16,256]{1,0:T(8,128)S(1)}, f32[16,256]{1,0:T(8,128)S(1)}, u32[]{:S(2)}, u32[]{:S(2)}) collective-permute-start(f32[16,256]{1,0:T(8,128)S(1)} %add.16), channel_id=1, source_target_pairs={{0,24},{4,28},{8,16},{12,20},{16,8},{20,12},{24,0},{28,4},{1,25},{... | collective-permute-start | bytes 49160 | tf_op jit(solution)/shard_map/ppermute | solution.py:471
  93.9 4.6 %collective-permute-start.14 = (f32[16,256]{1,0:T(8,128)S(1)}, f32[16,256]{1,0:T(8,128)S(1)}, u32[]{:S(2)}, u32[]{:S(2)}) collective-permute-start(f32[16,256]{1,0:T(8,128)S(1)} %add.16), channel_id=1, source_target_pairs={{0,16},{4,20},{8,24},{12,28},{16,0},{20,4},{24,8},{28,12},{1,17},{... | collective-permute-start | bytes 49160 | tf_op jit(solution)/shard_map/ppermute | solution.py:471
  93.9 4.6 %collective-permute-start.13 = (f32[16,256]{1,0:T(8,128)S(1)}, f32[16,256]{1,0:T(8,128)S(1)}, u32[]{:S(2)}, u32[]{:S(2)}) collective-permute-start(f32[16,256]{1,0:T(8,128)S(1)} %add.16), channel_id=1, source_target_pairs={{0,8},{4,12},{8,0},{12,4},{16,24},{20,28},{24,16},{28,20},{1,9},{5... | collective-permute-start | bytes 49160 | tf_op jit(solution)/shard_map/ppermute | solution.py:471

commit v3 on v2

--- a/solution.py
+++ b/solution.py
@@ -20,8 +20,10 @@
 QUAD = 4
 QN = QUAD * NG
 PN = 2 * NG
-PIECE = 1280
-VMEM_LIMIT = 60 << 20
+PIECE = 2560
+PARAMS = pltpu.CompilerParams(vmem_limit_bytes=16 << 20)
+VMEM = pl.BlockSpec(memory_space=pltpu.VMEM)
+SMEM = pl.BlockSpec(memory_space=pltpu.SMEM)
 BAND = 0.1
 BF = jnp.bfloat16
 F32 = jnp.float32
@@ -105,50 +107,45 @@
     return rows
 
 
-def pieces(tile_ref, buf, sem, starts):
+def chunk_piece(k, width, p):
+    at = (lax.axis_index("fit") ^ k) * width + p * PIECE
+    return pl.ds(pl.multiple_of(at, 128), PIECE)
+
+
+def phi_kernel(width, coef_ref, far_ref, *rest):
+    outs, (tile_ref, sem) = rest[:-2], rest[-2:]
+    per = width // PIECE
+    todo = [(k, p) for k in [*range(1, len(outs)), 0] for p in range(per)]
     copies = []
-    for p, start in enumerate(starts):
-        at = pl.ds(pl.multiple_of(start, 128), PIECE)
-        copies.append(pltpu.make_async_copy(tile_ref.at[:, at], buf.at[p], sem.at[p]))
+    for i, (k, p) in enumerate(todo):
+        at = chunk_piece(k, width, p)
+        copies.append(pltpu.make_async_copy(far_ref.at[:, at], tile_ref.at[:, at], sem.at[i]))
         copies[-1].start()
-    return copies
-
-
-def phi_kernel(count, width, chunk_ref, coef_ref, tile_ref, *rest):
-    outs, (buf, sem) = rest[:count], rest[count:]
-    per = width // PIECE
-    starts = [chunk_ref[k] * width + p * PIECE for k in range(count) for p in range(per)]
-    for i, copy in enumerate(pieces(tile_ref, buf, sem, starts)):
+    for (k, p), copy in zip(todo, copies):
         copy.wait()
-        ls = slice(i % per * PIECE, (i % per + 1) * PIECE)
-        outs[i // per][:, ls] = jnp.dot(coef_ref[...], buf[i], preferred_element_type=F32)
-
-
-def phi_call(chunks, coefs, tiles, width):
-    aux = tiles.shape[0]
-    count = chunks.shape[0]
-    total = count * width // PIECE
+        outs[k][:, p * PIECE : (p + 1) * PIECE] = jnp.dot(
+            coef_ref[...], tile_ref[:, chunk_piece(k, width, p)], preferred_element_type=F32
+        )
+
+
+def phi_call(coefs, tiles, width):
+    aux, points = tiles.shape
+    count = points // width
     return pl.pallas_call(
-        functools.partial(phi_kernel, count, width),
-        in_specs=[
-            pl.BlockSpec(memory_space=pltpu.SMEM),
-            pl.BlockSpec(memory_space=pltpu.VMEM),
-            pl.BlockSpec(memory_space=pl.ANY),
-        ],
-        out_specs=[pl.BlockSpec(memory_space=pltpu.VMEM)] * count,
-        out_shape=[jax.ShapeDtypeStruct((NDENS, width), F32)] * count,
-        scratch_shapes=[
-            pltpu.VMEM((total, aux, PIECE), BF),
-            pltpu.SemaphoreType.DMA((total,)),
-        ],
-        compiler_params=pltpu.CompilerParams(vmem_limit_bytes=VMEM_LIMIT),
+        functools.partial(phi_kernel, width),
+        in_specs=[VMEM, pl.BlockSpec(memory_space=pltpu.HBM)],
+        out_specs=[VMEM] * (count + 1),
+        out_shape=[jax.ShapeDtypeStruct((NDENS, width), F32)] * count
+        + [jax.ShapeDtypeStruct(tiles.shape, tiles.dtype)],
+        scratch_shapes=[pltpu.SemaphoreType.DMA((points // PIECE,))],
+        compiler_params=PARAMS,
         cost_estimate=pl.CostEstimate(
-            flops=2 * NDENS * aux * width * count,
-            bytes_accessed=(2 * aux + 4 * NDENS) * width * count,
+            flops=2 * NDENS * aux * points,
+            bytes_accessed=(2 * aux + 4 * NDENS) * points,
             transcendentals=0,
         ),
         name="phi",
-    )(chunks, coefs, tiles)
+    )(coefs, pltpu.with_memory_space_constraint(tiles, pltpu.HBM))
 
 
 def pair_build(e, geo, mask, dir_ref, bh):
@@ -202,14 +199,14 @@
     return sums
 
 
-def pair_finish(u, w_ref, t_ref, bh):
+def pair_finish(e, w_ref, t_ref, bh):
     r = jnp.dot(bh[...], w_ref[...], preferred_element_type=F32)
     tt = r[: LM * 8, : 2 * LP] + r[: LM * 8, 2 * LP :]
     a = jnp.swapaxes(tt.reshape(LM, 8, 2 * LP), 0, 1)
     a = jnp.concatenate([a, jnp.zeros((8, LP - LM, 2 * LP), F32)], 1).reshape(8 * LP, 2 * LP)
     hi, lo = halves(a)
-    t_ref[u, :, : 2 * LP] = hi
-    t_ref[u, :, 2 * LP :] = lo
+    t_ref[e, :, : 2 * LP] = hi
+    t_ref[e, :, 2 * LP :] = lo
 
 
 def uncover(sums):
@@ -226,82 +223,69 @@
 
 
 def pair_kernel(
-    first_ref, cnt_ref, before_ref, own_ref, after_ref, nbr_ref, dir_ref, w_ref,
+    cnt_ref, before_ref, own_ref, after_ref, nbr_ref, dir_ref, w_ref,
     t_ref, unc_ref, geo, mask, *bhs
 ):
     spheres, slots = nbr_ref.shape
     reach = slots // 2
-    step = pl.program_id(0)
-
-    @pl.when(step == 0)
-    def _():
-        geo[...] = jnp.zeros_like(geo)
-        geo[0:reach, 0:4] = before_ref[...]
-        geo[reach : reach + spheres, 0:4] = own_ref[...]
-        geo[reach + spheres :, 0:4] = after_ref[...]
-        rel = nbr_ref[...] - first_ref[0]
-        rel = rel - lax.broadcasted_iota(jnp.int32, (spheres, slots), 0)
-        slot = lax.broadcasted_iota(jnp.int32, (spheres, slots), 1)
-        row = lax.broadcasted_iota(jnp.int32, (spheres, slots), 0)
-        many = jnp.zeros((spheres, slots), jnp.int32)
-        for i in range(spheres):
-            many = jnp.where(row == i, cnt_ref[i], many)
-        listed = slot < many
-        lane = lax.broadcasted_iota(jnp.int32, (spheres, 128), 1)
-        found = jnp.zeros((spheres, 128), F32)
-        for c in range(slots):
-            gap = c - reach if c < reach else c - reach + 1
-            hit = jnp.where(listed & (rel == gap), 1.0, 0.0)
-            hit = jnp.max(hit, axis=1, keepdims=True)
-            found = jnp.where(lane == c, hit, found)
-        mask[...] = found
-
-    sums = []
-    for u in range(QUAD):
-        sums.append(pair_build(step * QUAD + u, geo, mask, dir_ref, bhs[u]))
-        pair_finish(u, w_ref, t_ref, bhs[u])
-    tiles = uncover(sums[:2]) + uncover(sums[2:])
-    for t, v in enumerate(tiles):
-        unc_ref[0, :, 128 * t : 128 * t + 128] = v
-
-
-def pair_call(first, before, own, after, neighbours, counts):
+    first = (lax.axis_index("sph") * lax.axis_size("fit") + lax.axis_index("fit")) * spheres
+    rows = jnp.concatenate([before_ref[...], own_ref[...], after_ref[...]], axis=1)
+    wide = jnp.concatenate([rows, jnp.zeros((4, 128 - rows.shape[1]), F32)], axis=1)
+    wide = jnp.concatenate([wide, jnp.zeros((124, 128), F32)], axis=0)
+    geo[...] = wide.T[: rows.shape[1]]
+    row = lax.broadcasted_iota(jnp.int32, (spheres, slots), 0)
+    slot = lax.broadcasted_iota(jnp.int32, (spheres, slots), 1)
+    rel = nbr_ref[...] - first - row
+    many = jnp.zeros((spheres, slots), jnp.int32)
+    for i in range(spheres):
+        many = jnp.where(row == i, cnt_ref[i], many)
+    listed = slot < many
+    lane = lax.broadcasted_iota(jnp.int32, (spheres, 128), 1)
+    found = jnp.zeros((spheres, 128), F32)
+    for c in range(slots):
+        gap = c - reach if c < reach else c - reach + 1
+        hit = jnp.where(listed & (rel == gap), 1.0, 0.0)
+        hit = jnp.max(hit, axis=1, keepdims=True)
+        found = jnp.where(lane == c, hit, found)
+    mask[...] = found
+
+    def step(b, carry):
+        sums = []
+        for u in range(QUAD):
+            e = b * QUAD + u
+            sums.append(pair_build(e, geo, mask, dir_ref, bhs[u]))
+            pair_finish(e, w_ref, t_ref, bhs[u])
+        tiles = uncover(sums[:2]) + uncover(sums[2:])
+        for t, v in enumerate(tiles):
+            unc_ref[b, :, 128 * t : 128 * t + 128] = v
+        return carry
+
+    lax.fori_loop(0, spheres // QUAD, step, 0)
+
+
+def pair_call(before, own, after, neighbours, counts):
     spheres, slots = neighbours.shape
     reach = slots // 2
     w, d = pair_weights()
-    whole = lambda *shape: pl.BlockSpec(shape, lambda e, f, c: (0,) * len(shape))
     return pl.pallas_call(
         pair_kernel,
-        grid_spec=pltpu.PrefetchScalarGridSpec(
-            num_scalar_prefetch=2,
-            grid=(spheres // QUAD,),
-            in_specs=[
-                whole(reach, 4),
-                whole(spheres, 4),
-                whole(reach, 4),
-                whole(spheres, slots),
-                whole(8, 2 * NG),
-                whole(2 * NG, 4 * LP),
-            ],
-            out_specs=[
-                pl.BlockSpec((QUAD, 8 * LP, 4 * LP), lambda e, f, c: (e, 0, 0)),
-                pl.BlockSpec((1, 1, QN), lambda e, f, c: (e, 0, 0)),
-            ],
-            scratch_shapes=[
-                pltpu.VMEM((spheres + 2 * reach, 128), F32),
-                pltpu.VMEM((spheres, 128), F32),
-            ]
-            + [pltpu.VMEM((400, 2 * NG), BF)] * QUAD,
-        ),
+        in_specs=[SMEM] + [VMEM] * 6,
+        out_specs=[VMEM] * 2,
+        scratch_shapes=[
+            pltpu.VMEM((spheres + 2 * reach, 128), F32),
+            pltpu.VMEM((spheres, 128), F32),
+        ]
+        + [pltpu.VMEM((400, 2 * NG), BF)] * QUAD,
         out_shape=[
             jax.ShapeDtypeStruct((spheres, 8 * LP, 4 * LP), BF),
             jax.ShapeDtypeStruct((spheres // QUAD, 1, QN), F32),
         ],
+        compiler_params=PARAMS,
         cost_estimate=pl.CostEstimate(
             flops=spheres * 2 * 400 * 640 * 256, bytes_accessed=spheres * 262144, transcendentals=0
         ),
         name="pairs",
-    )(first, counts, before, own, after, neighbours, jnp.asarray(d), jnp.asarray(w))
+    )(counts, before, own, after, neighbours, jnp.asarray(d), jnp.asarray(w))
 
 
 def rhs_kernel(count, *refs):
@@ -328,6 +312,9 @@
     half = unc.shape[0] // 2 * QUAD * LP
     return pl.pallas_call(
         functools.partial(rhs_kernel, len(phis)),
+        in_specs=[VMEM] * (len(phis) + 2),
+        out_specs=[VMEM] * 2,
+        compiler_params=PARAMS,
         out_shape=[jax.ShapeDtypeStruct((NDENS, half), F32)] * 2,
         cost_estimate=pl.CostEstimate(
             flops=6 * NDENS * unc.shape[0] * QN * 256, bytes_accessed=1700000, transcendentals=0
@@ -336,7 +323,7 @@
     )(*phis, unc, w)
 
 
-def gather_field(ts, x, xs, e):
+def gather_field(t_ref, x, xs, e):
     low = lax.broadcasted_iota(jnp.int32, (NDENS, 128), 1) < LP
     parts = []
     for odd in (0, 1):
@@ -347,7 +334,7 @@
         lhs = jnp.concatenate(
             [below[:, lo_at : lo_at + 8 * LP], above[:, up_at : up_at + 8 * LP]], 0
         )
-        r = jnp.dot(lhs, ts[i], preferred_element_type=F32)
+        r = jnp.dot(lhs, t_ref[i], preferred_element_type=F32)
         n = NDENS
         a = r[0:n, : 2 * LP] + r[n : 2 * n, : 2 * LP] + r[0:n, 2 * LP :]
         b = r[2 * n : 3 * n, : 2 * LP] + r[3 * n :, : 2 * LP] + r[2 * n : 3 * n, 2 * LP :]
@@ -358,10 +345,7 @@
 
 def sweep_kernel(spheres, last, before_ref, left_ref, right_ref, after_ref, t_ref, rl_ref,
                  rr_ref, sc_ref, *rest):
-    x, xs, ts, sem = rest[-4:]
-    copies = [pltpu.make_async_copy(t_ref.at[i], ts.at[i], sem.at[i]) for i in range(spheres)]
-    for copy in copies:
-        copy.start()
+    x, xs = rest[-2:]
     half = left_ref.shape[1]
     at = 0
     for ref in (before_ref, left_ref, right_ref, after_ref):
@@ -375,9 +359,7 @@
     xs[...] = jnp.concatenate([v[:, LP:], v[:, :LP]], 1).astype(BF)
     rows = []
     for e in range(0, spheres, 2):
-        copies[e].wait()
-        copies[e + 1].wait()
-        got = gather_field(ts, x, xs, e)
+        got = gather_field(t_ref, x, xs, e)
         at = e * LP
         ref, at = (rl_ref, at) if at < half else (rr_ref, at - half)
         new = ref[:, at : at + 128] + got
@@ -412,15 +394,13 @@
         ]
         more = last
     total = before.shape[1] + 2 * half + after.shape[1]
-    vmem = pl.BlockSpec(memory_space=pltpu.VMEM)
     return pl.pallas_call(
         functools.partial(sweep_kernel, spheres, last is not None),
-        in_specs=[vmem] * 4 + [pl.BlockSpec(memory_space=pl.ANY)] + [vmem] * (3 + len(more)),
-        out_specs=[vmem] * 2,
+        in_specs=[VMEM] * (8 + len(more)),
+        out_specs=[VMEM] * 2,
         out_shape=outs,
-        scratch_shapes=[pltpu.VMEM((2 * NDENS, total), BF)] * 2
-        + [pltpu.VMEM(t.shape, BF), pltpu.SemaphoreType.DMA((spheres,))],
-        compiler_params=pltpu.CompilerParams(vmem_limit_bytes=VMEM_LIMIT),
+        scratch_shapes=[pltpu.VMEM((2 * NDENS, total), BF)] * 2,
+        compiler_params=PARAMS,
         cost_estimate=pl.CostEstimate(
             flops=spheres * 2 * 64 * 512 * 256, bytes_accessed=spheres * 262144, transcendentals=0
         ),
@@ -428,42 +408,34 @@
     )(before, left, right, after, t, rl, rr, scales, *more)
 
 
-def fock_kernel(width, chunk_ref, charge_ref, tile_ref, *rest):
-    out_ref, buf, sem = rest[-3:]
-    total = rest[0][...] if len(rest) == 4 else None
-    starts = [chunk_ref[0] * width + p * PIECE for p in range(width // PIECE)]
-    for i, copy in enumerate(pieces(tile_ref, buf, sem, starts)):
-        copy.wait()
+def fock_kernel(k, width, charge_ref, tile_ref, *rest):
+    total = rest[0][...] if len(rest) == 2 else None
+    for p in range(width // PIECE):
         part = lax.dot_general(
-            charge_ref[:, i * PIECE : (i + 1) * PIECE], buf[i], (((1,), (1,)), ((), ())),
+            charge_ref[:, p * PIECE : (p + 1) * PIECE],
+            tile_ref[:, chunk_piece(k, width, p)],
+            (((1,), (1,)), ((), ())),
             preferred_element_type=F32,
         )
         total = part if total is None else total + part
-    out_ref[...] = total
-
-
-def fock_call(chunk, charges, tiles, before=None):
+    rest[-1][...] = total
+
+
+def fock_call(k, charges, tiles, before=None):
     aux = tiles.shape[0]
     width = charges.shape[1]
-    total = width // PIECE
-    vmem = pl.BlockSpec(memory_space=pltpu.VMEM)
     more = [] if before is None else [before]
     return pl.pallas_call(
-        functools.partial(fock_kernel, width),
-        in_specs=[pl.BlockSpec(memory_space=pltpu.SMEM), vmem, pl.BlockSpec(memory_space=pl.ANY)]
-        + [vmem] * len(more),
-        out_specs=vmem,
+        functools.partial(fock_kernel, k, width),
+        in_specs=[VMEM] * (2 + len(more)),
+        out_specs=VMEM,
         out_shape=jax.ShapeDtypeStruct((NDENS, aux), F32),
-        scratch_shapes=[
-            pltpu.VMEM((total, aux, PIECE), BF),
-            pltpu.SemaphoreType.DMA((total,)),
-        ],
-        compiler_params=pltpu.CompilerParams(vmem_limit_bytes=VMEM_LIMIT),
+        compiler_params=PARAMS,
         cost_estimate=pl.CostEstimate(
             flops=2 * NDENS * aux * width, bytes_accessed=2 * aux * width, transcendentals=0
         ),
         name="fock",
-    )(chunk, charges, tiles, *more)
+    )(charges, tiles, *more)
 
 
 def trade(x, axis, k):
@@ -486,32 +458,25 @@
     sphs = lax.axis_size("sph")
     assert fits & (fits - 1) == 0 and sphs & (sphs - 1) == 0
     assert spheres % (2 * QUAD) == 0 and spheres // 2 == reach == 8
-    fit = lax.axis_index("fit")
-    first = (lax.axis_index("sph") * fits + fit) * spheres
     w, wt = (jnp.asarray(a) for a in even_weights())
     scales = jnp.asarray(lane_scales())
     width = spheres * NG
-    order = jnp.bitwise_xor(fit, jnp.arange(fits, dtype=jnp.int32))
-
-    own = jnp.concatenate([centres, radii[None, :]], axis=0).T
-    before, after = reach_out(own[spheres - reach :], own[:reach])
-
-    sent = phi_call(order[1:], coefs, tiles, width)
-    got = [trade(sent[k - 1], "fit", k) for k in range(1, fits)]
-    mine = phi_call(order[:1], coefs, tiles, width)
-
-    t, unc = pair_call(
-        first.reshape(1).astype(jnp.int32), before, own, after, neighbours, counts
-    )
-    rl, rr = rhs_call([*mine, *got], unc, w)
+
+    own = jnp.concatenate([centres, radii[None, :]], axis=0)
+    before, after = reach_out(own[:, spheres - reach :], own[:, :reach])
+    *phis, near_tiles = phi_call(coefs, tiles, width)
+    phis, before, after = lax.optimization_barrier((phis, before, after))
+    got = [trade(phis[k], "fit", k) for k in range(1, fits)]
+    t, unc = pair_call(before, own, after, neighbours, counts)
+    rl, rr = rhs_call([phis[0], *got], unc, w)
     below, above = reach_out(rr, rl)
     left, right = sweep_call(below, rl, rr, above, t, rl, rr, scales)
     below, above = reach_out(right, left)
     moments, charges = sweep_call(below, left, right, above, t, rl, rr, scales, (unc, wt))
     others = [trade(charges, "fit", k) for k in range(1, fits)]
-    fock = fock_call(order[:1], charges, tiles)
+    fock = fock_call(0, charges, near_tiles)
     for k in range(1, fits):
-        fock = fock_call(order[k : k + 1], others[k - 1], tiles, fock)
+        fock = fock_call(k, others[k - 1], near_tiles, fock)
     fock = fock + trade(fock, "sph", 1)
     bit = 2
     while bit < sphs:

time: 99.8 us -> 67.1 us (0.67)
  Pallas kernels: 51 us -> 17.1 us
  waiting for transfers between devices: 11.6 us -> 18.1 us
  local copies, waits for them, and re-layouts: 6.53 us -> 0.85 us
  starting transfers between devices: 27.8 us -> 28.8 us
    pallas_call x8 -> x7, Pallas kernels: 40.1 us -> 14.6 us  [the longest x1 6.71 us: pair_call(): pl.pallas_call(pair_kernel, in_specs=[SMEM] + [VMEM] * 6, out_specs=[VMEM...]
    ppermute x10, waiting for transfers between devices: 3.53 us -> 13.5 us  [trade(): return lax.ppermute(x, axis, [(i, i ^ k) for i in range(count)])]
    pallas_call x2, Pallas kernels: 10.9 us -> 2.47 us  [sweep_call(): pl.pallas_call(functools.partial(sweep_kernel, spheres, last is not None)...]
    unnamed x30 -> x16, local copies, waits for them, and re-layouts: 5.21 us -> 0.78 us
    ppermute x6, waiting for transfers between devices: 8.05 us -> 4.6 us  [reach_out(): return (lax.ppermute(last, axes, up), lax.ppermute(initial, axes, down))]
    ppermute x6, starting transfers between devices: 15.3 us -> 17.2 us  [reach_out(): return (lax.ppermute(last, axes, up), lax.ppermute(initial, axes, down))]
    slice x3 -> x1, local copies, waits for them, and re-layouts: 1.23 us -> 0.07 us  [body(): before, after = reach_out(own[:, spheres - reach:], own[:, :reach])]
  transfers between devices with their start and end apart: 16 -> 16, of which waited for: 8 -> 10; matrix products, arithmetic and copies ran while one was open for 1% -> 0% of each run, Pallas kernels for 28% -> 20%
where the time goes in v3:
time: 67.1 us; the launch traced here: 66.9 us
  starting transfers between devices  28.8 us (43%)
  waiting for transfers between devices  18.1 us (27%)
  Pallas kernels  17.1 us (25%)
  other arithmetic  1.37 us (2%)
  local copies, waits for them, and re-layouts  0.85 us (1%)
  between operations  0.72 us (1%)
    ppermute x6, starting transfers between devices, reach_out(): return (lax.ppermute(last, axes, up), lax.ppermute(initial, axes, down))  17.2 us
    ppermute x10, waiting for transfers between devices, trade(): return lax.ppermute(x, axis, [(i, i ^ k) for i in range(count)])  13.5 us
    ppermute x10, starting transfers between devices, trade(): return lax.ppermute(x, axis, [(i, i ^ k) for i in range(count)])  11.6 us
    pallas_call x1, Pallas kernels, pair_call(): pl.pallas_call(pair_kernel, in_specs=[SMEM] + [VMEM] * 6, out_specs=[VMEM...  6.71 us
    ppermute x6, waiting for transfers between devices, reach_out(): return (lax.ppermute(last, axes, up), lax.ppermute(initial, axes, down))  4.6 us
    pallas_call x1, Pallas kernels, phi_call(): pl.pallas_call(functools.partial(phi_kernel, width), in_specs=[VMEM, pl.B...  4.42 us
    pallas_call x4, Pallas kernels, fock_call(): pl.pallas_call(functools.partial(fock_kernel, k, width), in_specs=[VMEM]...  3.14 us
    pallas_call x2, Pallas kernels, sweep_call(): pl.pallas_call(functools.partial(sweep_kernel, spheres, last is not None)...  2.47 us
  transfers between devices with their start and end apart: 16, of which 10 were waited for; matrix products, arithmetic and copies ran while one was open for 0% of the time, Pallas kernels for 20%

profile of v3, /device:TPU:0, one launch (start us, length us, event | category | flops | bytes accessed | tf_op | source)
XLA Modules:
  0.0 66.9 jit_solution(9691223243610220273)
XLA Ops:
  0.7 0.8 %pad_maximum_fusion.own_ref = f32[4,16]{1,0:T(4,128)S(1)} fusion(f32[1,16]{1,0:T(1,128)} %bitcast.1, f32[3,16]{1,0:T(4,128)} %param.13), kind=kLoop, calls=%fused_computation.1 | loop fusion | flops 64 | bytes 512 | tf_op jit(solution)/shard_map/concatenate | solution.py:465
  1.4 0.1 fusion
  1.5 6.4 %collective-permute-start.1 = (f32[4,8]{1,0:T(4,128)S(1)}, f32[4,8]{1,0:T(4,128)S(1)}, u32[]{:S(2)}, u32[]{:S(2)}) collective-permute-start(f32[4,8]{1,0:T(4,128)S(1)} %get-tuple-element.40), channel_id=1, source_target_pairs={{1,0},{2,1},{3,2},{4,3},{5,4},{6,5},{7,6},{8,7},{9,8},{10,9},{11,1... | collective-permute-start | bytes 392 | tf_op jit(solution)/shard_map/ppermute | solution.py:451
  7.9 0.7 %copy-done.3 = bf16[16,256]{1,0:T(8,128)(2,1)S(1)} copy-done((bf16[16,256]{1,0:T(8,128)(2,1)S(1)}, bf16[16,256]{1,0:T(8,128)(2,1)}, u32[]{:S(2)}) %copy-start.3) | copy-done | bytes 8216
  8.6 4.4 %phi.1 = (f32[16,5120]{1,0:T(8,128)S(1)}, f32[16,5120]{1,0:T(8,128)S(1)}, f32[16,5120]{1,0:T(8,128)S(1)}, f32[16,5120]{1,0:T(8,128)S(1)}, bf16[256,20480]{1,0:T(8,128)(2,1)S(1)}) custom-call(bf16[16,256]{1,0:T(8,128)(2,1)S(1)} %copy-done.3, bf16[256,20480]{1,0:T(8,128)(2,1)} %far_ref.1), custom_call_target="tpu_custom_call" | custom-call | flops 167772160 | bytes 11796480 | tf_op jit(solution)/shard_map/phi/pallas_call | solution.py:134
  13.1 1.4 %collective-permute-done.before_ref = f32[4,8]{1,0:T(4,128)S(1)} collective-permute-done((f32[4,8]{1,0:T(4,128)S(1)}, f32[4,8]{1,0:T(4,128)S(1)}, u32[]{:S(2)}, u32[]{:S(2)}) %collective-permute-start) | collective-permute-done | bytes 160 | tf_op jit(solution)/shard_map/ppermute | solution.py:451
  14.5 3.5 %collective-permute-start.4 = (f32[16,5120]{1,0:T(8,128)S(1)}, f32[16,5120]{1,0:T(8,128)S(1)}, u32[]{:S(2)}, u32[]{:S(2)}) collective-permute-start(f32[16,5120]{1,0:T(8,128)S(1)} %get-tuple-element.28), channel_id=1, source_target_pairs={{0,3},{1,2},{2,1},{3,0},{4,7},{5,6},{6,5},{7,4},{8,11},{9,10},{10,... | collective-permute-start | bytes 983048 | tf_op jit(solution)/shard_map/ppermute | solution.py:443
  18.0 6.7 %pairs.1 = (bf16[16,512,256]{2,1,0:T(8,128)(2,1)S(1)}, f32[4,1,1280]{2,1,0:T(1,128)S(1)}) custom-call(s32[16]{0:T(128)S(1)} %copy-done.5, f32[4,8]{1,0:T(4,128)S(1)} %collective-permute-done.before_ref, f32[4,16]{1,0:T(4,128)S(1)} %pad_maximum_fusion.own_ref, f32[4,8]{1,0:T(4,128)S(1)} %collective-permute-done.1.after_ref, s32[16,16]{1,0:T(8,128)S(1)} %copy-done.4, ...), custom_call_target="tpu_custom_call" | custom-call | flops 2097152000 | bytes 4194304 | tf_op jit(solution)/shard_map/pairs/pallas_call | solution.py:270
  24.7 4.5 %collective-permute-done.3.refs_2_ = f32[16,5120]{1,0:T(8,128)S(1)} collective-permute-done((f32[16,5120]{1,0:T(8,128)S(1)}, f32[16,5120]{1,0:T(8,128)S(1)}, u32[]{:S(2)}, u32[]{:S(2)}) %collective-permute-start.3) | collective-permute-done | bytes 327712 | tf_op jit(solution)/shard_map/ppermute | solution.py:443
  29.2 0.3 rhs.1
  29.5 1.5 %collective-permute-start.5 = (f32[16,512]{1,0:T(8,128)S(1)}, f32[16,512]{1,0:T(8,128)S(1)}, u32[]{:S(2)}, u32[]{:S(2)}) collective-permute-start(f32[16,512]{1,0:T(8,128)S(1)} %get-tuple-element.32.right_ref.rr_ref), channel_id=1, source_target_pairs={{0,1},{1,2},{2,3},{3,4},{4,5},{5,6},{6,7},{7,8},{8,9},{9,10},{10,1... | collective-permute-start | bytes 98312 | tf_op jit(solution)/shard_map/ppermute | solution.py:451
  31.0 3.9 %collective-permute-start.6 = (f32[16,512]{1,0:T(8,128)S(1)}, f32[16,512]{1,0:T(8,128)S(1)}, u32[]{:S(2)}, u32[]{:S(2)}) collective-permute-start(f32[16,512]{1,0:T(8,128)S(1)} %get-tuple-element.33.left_ref.rl_ref), channel_id=1, source_target_pairs={{1,0},{2,1},{3,2},{4,3},{5,4},{6,5},{7,6},{8,7},{9,8},{10,9},{11,1... | collective-permute-start | bytes 98312 | tf_op jit(solution)/shard_map/ppermute | solution.py:451
  34.9 1.6 %collective-permute-done.5.before_ref = f32[16,512]{1,0:T(8,128)S(1)} collective-permute-done((f32[16,512]{1,0:T(8,128)S(1)}, f32[16,512]{1,0:T(8,128)S(1)}, u32[]{:S(2)}, u32[]{:S(2)}) %collective-permute-start.5) | collective-permute-done | bytes 32800 | tf_op jit(solution)/shard_map/ppermute | solution.py:451
  36.5 0.8 %sweep.2 = (f32[16,512]{1,0:T(8,128)S(1)}, f32[16,512]{1,0:T(8,128)S(1)}) custom-call(f32[16,512]{1,0:T(8,128)S(1)} %collective-permute-done.5.before_ref, f32[16,512]{1,0:T(8,128)S(1)} %get-tuple-element.33.left_ref.rl_ref, f32[16,512]{1,0:T(8,128)S(1)} %get-tuple-element.32.right_ref.rr_ref, f32[16,512]{1,0:T(8,128)S(1)} %collective-permute-done.6.after_ref, ...), custom_call_target="tpu_custom_call" | custom-call | flops 268435456 | bytes 4194304 | tf_op jit(solution)/shard_map/sweep/pallas_call | solution.py:397
  37.3 1.1 %collective-permute-start.7 = (f32[16,512]{1,0:T(8,128)S(1)}, f32[16,512]{1,0:T(8,128)S(1)}, u32[]{:S(2)}, u32[]{:S(2)}) collective-permute-start(f32[16,512]{1,0:T(8,128)S(1)} %get-tuple-element.35.right_ref), channel_id=1, source_target_pairs={{0,1},{1,2},{2,3},{3,4},{4,5},{5,6},{6,7},{7,8},{8,9},{9,10},{10,1... | collective-permute-start | bytes 98312 | tf_op jit(solution)/shard_map/ppermute | solution.py:451
  38.4 4.3 %collective-permute-start.8 = (f32[16,512]{1,0:T(8,128)S(1)}, f32[16,512]{1,0:T(8,128)S(1)}, u32[]{:S(2)}, u32[]{:S(2)}) collective-permute-start(f32[16,512]{1,0:T(8,128)S(1)} %get-tuple-element.36.left_ref), channel_id=1, source_target_pairs={{1,0},{2,1},{3,2},{4,3},{5,4},{6,5},{7,6},{8,7},{9,8},{10,9},{11,1... | collective-permute-start | bytes 98312 | tf_op jit(solution)/shard_map/ppermute | solution.py:451
  42.8 1.5 %collective-permute-done.7.before_ref = f32[16,512]{1,0:T(8,128)S(1)} collective-permute-done((f32[16,512]{1,0:T(8,128)S(1)}, f32[16,512]{1,0:T(8,128)S(1)}, u32[]{:S(2)}, u32[]{:S(2)}) %collective-permute-start.7) | collective-permute-done | bytes 32800 | tf_op jit(solution)/shard_map/ppermute | solution.py:451
  44.3 0.1 collective-permute-done.8.after_ref
  44.4 1.6 %sweep.3 = (f32[16,16,49]{2,1,0:T(8,128)}, bf16[16,5120]{1,0:T(8,128)(2,1)S(1)}) custom-call(f32[16,512]{1,0:T(8,128)S(1)} %collective-permute-done.7.before_ref, f32[16,512]{1,0:T(8,128)S(1)} %get-tuple-element.36.left_ref, f32[16,512]{1,0:T(8,128)S(1)} %get-tuple-element.35.right_ref, f32[16,512]{1,0:T(8,128)S(1)} %collective-permute-done.8.after_ref, ...), custom_call_target="tpu_custom_call" | custom-call | flops 268435456 | bytes 4194304 | tf_op jit(solution)/shard_map/sweep/pallas_call | solution.py:397
  46.0 3.5 %collective-permute-start.9 = (bf16[16,5120]{1,0:T(8,128)(2,1)S(1)}, bf16[16,5120]{1,0:T(8,128)(2,1)S(1)}, u32[]{:S(2)}, u32[]{:S(2)}) collective-permute-start(bf16[16,5120]{1,0:T(8,128)(2,1)S(1)} %get-tuple-element.38.charge_ref), channel_id=1, source_target_pairs={{0,3},{1,2},{2,1},{3,0},{4,7},{5,6},{6,5},{7,4},{8,11},{9,10},{10,... | collective-permute-start | bytes 491528 | tf_op jit(solution)/shard_map/ppermute | solution.py:443
  49.5 0.8 %fock.4.rest_0_ = f32[16,256]{1,0:T(8,128)S(1)} custom-call(bf16[16,5120]{1,0:T(8,128)(2,1)S(1)} %get-tuple-element.38.charge_ref, bf16[256,20480]{1,0:T(8,128)(2,1)S(1)} %get-tuple-element.39.tile_ref), custom_call_target="tpu_custom_call" | custom-call | flops 41943040 | bytes 2621440 | tf_op jit(solution)/shard_map/fock/pallas_call | solution.py:428
  50.3 2.2 %collective-permute-done.11.charge_ref = bf16[16,5120]{1,0:T(8,128)(2,1)S(1)} collective-permute-done((bf16[16,5120]{1,0:T(8,128)(2,1)S(1)}, bf16[16,5120]{1,0:T(8,128)(2,1)S(1)}, u32[]{:S(2)}, u32[]{:S(2)}) %collective-permute-start.11) | collective-permute-done | bytes 163872 | tf_op jit(solution)/shard_map/ppermute | solution.py:443
  52.5 0.8 %fock.5.rest_0_ = f32[16,256]{1,0:T(8,128)S(1)} custom-call(bf16[16,5120]{1,0:T(8,128)(2,1)S(1)} %collective-permute-done.11.charge_ref, bf16[256,20480]{1,0:T(8,128)(2,1)S(1)} %get-tuple-element.39.tile_ref, f32[16,256]{1,0:T(8,128)S(1)} %fock.4.rest_0_), custom_call_target="tpu_custom_call" | custom-call | flops 41943040 | bytes 2621440 | tf_op jit(solution)/shard_map/fock/pallas_call | solution.py:428
  53.3 1.5 %collective-permute-done.10.charge_ref = bf16[16,5120]{1,0:T(8,128)(2,1)S(1)} collective-permute-done((bf16[16,5120]{1,0:T(8,128)(2,1)S(1)}, bf16[16,5120]{1,0:T(8,128)(2,1)S(1)}, u32[]{:S(2)}, u32[]{:S(2)}) %collective-permute-start.10) | collective-permute-done | bytes 163872 | tf_op jit(solution)/shard_map/ppermute | solution.py:443
  54.8 0.8 %fock.6.rest_0_ = f32[16,256]{1,0:T(8,128)S(1)} custom-call(bf16[16,5120]{1,0:T(8,128)(2,1)S(1)} %collective-permute-done.10.charge_ref, bf16[256,20480]{1,0:T(8,128)(2,1)S(1)} %get-tuple-element.39.tile_ref, f32[16,256]{1,0:T(8,128)S(1)} %fock.5.rest_0_), custom_call_target="tpu_custom_call" | custom-call | flops 41943040 | bytes 2621440 | tf_op jit(solution)/shard_map/fock/pallas_call | solution.py:428
  55.6 0.8 %fock.7 = f32[16,256]{1,0:T(8,128)S(1)} custom-call(bf16[16,5120]{1,0:T(8,128)(2,1)S(1)} %collective-permute-done.9.charge_ref, bf16[256,20480]{1,0:T(8,128)(2,1)S(1)} %get-tuple-element.39.tile_ref, f32[16,256]{1,0:T(8,128)S(1)} %fock.6.rest_0_), custom_call_target="tpu_custom_call" | custom-call | flops 41943040 | bytes 2621440 | tf_op jit(solution)/shard_map/fock/pallas_call | solution.py:428
  56.4 1.2 %collective-permute-done.12 = f32[16,256]{1,0:T(8,128)S(1)} collective-permute-done((f32[16,256]{1,0:T(8,128)S(1)}, f32[16,256]{1,0:T(8,128)S(1)}, u32[]{:S(2)}, u32[]{:S(2)}) %collective-permute-start.12) | collective-permute-done | bytes 16416 | tf_op jit(solution)/shard_map/ppermute | solution.py:443
  57.6 4.0 %collective-permute-start.15 = (f32[16,256]{1,0:T(8,128)S(1)}, f32[16,256]{1,0:T(8,128)S(1)}, u32[]{:S(2)}, u32[]{:S(2)}) collective-permute-start(f32[16,256]{1,0:T(8,128)S(1)} %add.12), channel_id=1, source_target_pairs={{0,24},{4,28},{8,16},{12,20},{16,8},{20,12},{24,0},{28,4},{1,25},{... | collective-permute-start | bytes 49160 | tf_op jit(solution)/shard_map/ppermute | solution.py:443
  61.6 0.6 collective-permute-start.13
  62.3 1.1 %collective-permute-done.15 = f32[16,256]{1,0:T(8,128)S(1)} collective-permute-done((f32[16,256]{1,0:T(8,128)S(1)}, f32[16,256]{1,0:T(8,128)S(1)}, u32[]{:S(2)}, u32[]{:S(2)}) %collective-permute-start.15) | collective-permute-done | bytes 16416 | tf_op jit(solution)/shard_map/ppermute | solution.py:443
  63.4 2.9 %collective-permute-done.14 = f32[16,256]{1,0:T(8,128)S(1)} collective-permute-done((f32[16,256]{1,0:T(8,128)S(1)}, f32[16,256]{1,0:T(8,128)S(1)}, u32[]{:S(2)}, u32[]{:S(2)}) %collective-permute-start.14) | collective-permute-done | bytes 16416 | tf_op jit(solution)/shard_map/ppermute | solution.py:443
  66.3 0.6 add_add_fusion
  (29 shorter events, 0.1 us)
Async XLA Ops:
  0.6 28.5 %copy-start.1 = (bf16[640,256]{1,0:T(8,128)(2,1)S(1)}, bf16[640,256]{1,0:T(8,128)(2,1)}, u32[]{:S(2)}) copy-start(bf16[640,256]{1,0:T(8,128)(2,1)} %constant.10.clone.refs_5_) | copy-start | bytes 983044
  0.6 35.9 %copy-start.2 = (f32[8,128]{1,0:T(8,128)S(1)}, f32[8,128]{1,0:T(8,128)}, u32[]{:S(2)}) copy-start(f32[8,128]{1,0:T(8,128)} %constant.12.clone.sc_ref) | copy-start | bytes 12292
  1.5 11.6 %collective-permute-start.1 = (f32[4,8]{1,0:T(4,128)S(1)}, f32[4,8]{1,0:T(4,128)S(1)}, u32[]{:S(2)}, u32[]{:S(2)}) collective-permute-start(f32[4,8]{1,0:T(4,128)S(1)} %get-tuple-element.40), channel_id=1, source_target_pairs={{1,0},{2,1},{3,2},{4,3},{5,4},{6,5},{7,6},{8,7},{9,8},{10,9},{11,1... | collective-permute-start | bytes 392 | tf_op jit(solution)/shard_map/ppermute | solution.py:451
  7.9 36.5 %copy-start = (bf16[128,1280]{1,0:T(8,128)(2,1)S(1)}, bf16[128,1280]{1,0:T(8,128)(2,1)}, u32[]{:S(2)}) copy-start(bf16[128,1280]{1,0:T(8,128)(2,1)} %constant.11.clone.rest_1_) | copy-start | bytes 983044
  7.9 6.6 %collective-permute-start = (f32[4,8]{1,0:T(4,128)S(1)}, f32[4,8]{1,0:T(4,128)S(1)}, u32[]{:S(2)}, u32[]{:S(2)}) collective-permute-start(f32[4,8]{1,0:T(4,128)S(1)} %get-tuple-element.41), channel_id=1, source_target_pairs={{0,1},{1,2},{2,3},{3,4},{4,5},{5,6},{6,7},{7,8},{8,9},{9,10},{10,1... | collective-permute-start | bytes 392 | tf_op jit(solution)/shard_map/ppermute | solution.py:451
  7.9 0.7 %copy-start.3 = (bf16[16,256]{1,0:T(8,128)(2,1)S(1)}, bf16[16,256]{1,0:T(8,128)(2,1)}, u32[]{:S(2)}) copy-start(bf16[16,256]{1,0:T(8,128)(2,1)} %coef_ref.1) | copy-start | bytes 24580
  8.6 9.4 %copy-start.4 = (s32[16,16]{1,0:T(8,128)S(1)}, s32[16,16]{1,0:T(8,128)}, u32[]{:S(2)}) copy-start(s32[16,16]{1,0:T(8,128)} %nbr_ref.1) | copy-start | bytes 3076
  8.6 9.4 %copy-start.5 = (s32[16]{0:T(128)S(1)}, s32[16]{0:T(128)}, u32[]{:S(2)}) copy-start(s32[16]{0:T(128)} %cnt_ref.1) | copy-start | bytes 196
  8.6 9.4 %copy-start.6 = (bf16[640,256]{1,0:T(8,128)(2,1)S(1)}, bf16[640,256]{1,0:T(8,128)(2,1)}, u32[]{:S(2)}) copy-start(bf16[640,256]{1,0:T(8,128)(2,1)} %constant.14.clone.w_ref) | copy-start | bytes 983044
  8.6 9.4 %copy-start.7 = (f32[8,640]{1,0:T(8,128)S(1)}, f32[8,640]{1,0:T(8,128)}, u32[]{:S(2)}) copy-start(f32[8,640]{1,0:T(8,128)} %constant.13.clone.dir_ref) | copy-start | bytes 61444
  14.5 10.2 %collective-permute-start.2 = (f32[16,5120]{1,0:T(8,128)S(1)}, f32[16,5120]{1,0:T(8,128)S(1)}, u32[]{:S(2)}, u32[]{:S(2)}) collective-permute-start(f32[16,5120]{1,0:T(8,128)S(1)} %get-tuple-element.26), channel_id=1, source_target_pairs={{0,1},{1,0},{2,3},{3,2},{4,5},{5,4},{6,7},{7,6},{8,9},{9,8},{10,11... | collective-permute-start | bytes 983048 | tf_op jit(solution)/shard_map/ppermute | solution.py:443
  14.5 14.7 %collective-permute-start.3 = (f32[16,5120]{1,0:T(8,128)S(1)}, f32[16,5120]{1,0:T(8,128)S(1)}, u32[]{:S(2)}, u32[]{:S(2)}) collective-permute-start(f32[16,5120]{1,0:T(8,128)S(1)} %get-tuple-element.27), channel_id=1, source_target_pairs={{0,2},{1,3},{2,0},{3,1},{4,6},{5,7},{6,4},{7,5},{8,10},{9,11},{10,... | collective-permute-start | bytes 983048 | tf_op jit(solution)/shard_map/ppermute | solution.py:443
  14.5 14.7 %collective-permute-start.4 = (f32[16,5120]{1,0:T(8,128)S(1)}, f32[16,5120]{1,0:T(8,128)S(1)}, u32[]{:S(2)}, u32[]{:S(2)}) collective-permute-start(f32[16,5120]{1,0:T(8,128)S(1)} %get-tuple-element.28), channel_id=1, source_target_pairs={{0,3},{1,2},{2,1},{3,0},{4,7},{5,6},{6,5},{7,4},{8,11},{9,10},{10,... | collective-permute-start | bytes 983048 | tf_op jit(solution)/shard_map/ppermute | solution.py:443
  29.5 7.0 %collective-permute-start.5 = (f32[16,512]{1,0:T(8,128)S(1)}, f32[16,512]{1,0:T(8,128)S(1)}, u32[]{:S(2)}, u32[]{:S(2)}) collective-permute-start(f32[16,512]{1,0:T(8,128)S(1)} %get-tuple-element.32.right_ref.rr_ref), channel_id=1, source_target_pairs={{0,1},{1,2},{2,3},{3,4},{4,5},{5,6},{6,7},{7,8},{8,9},{9,10},{10,1... | collective-permute-start | bytes 98312 | tf_op jit(solution)/shard_map/ppermute | solution.py:451
  31.0 5.5 %collective-permute-start.6 = (f32[16,512]{1,0:T(8,128)S(1)}, f32[16,512]{1,0:T(8,128)S(1)}, u32[]{:S(2)}, u32[]{:S(2)}) collective-permute-start(f32[16,512]{1,0:T(8,128)S(1)} %get-tuple-element.33.left_ref.rl_ref), channel_id=1, source_target_pairs={{1,0},{2,1},{3,2},{4,3},{5,4},{6,5},{7,6},{8,7},{9,8},{10,9},{11,1... | collective-permute-start | bytes 98312 | tf_op jit(solution)/shard_map/ppermute | solution.py:451
  37.3 6.9 %collective-permute-start.7 = (f32[16,512]{1,0:T(8,128)S(1)}, f32[16,512]{1,0:T(8,128)S(1)}, u32[]{:S(2)}, u32[]{:S(2)}) collective-permute-start(f32[16,512]{1,0:T(8,128)S(1)} %get-tuple-element.35.right_ref), channel_id=1, source_target_pairs={{0,1},{1,2},{2,3},{3,4},{4,5},{5,6},{6,7},{7,8},{8,9},{9,10},{10,1... | collective-permute-start | bytes 98312 | tf_op jit(solution)/shard_map/ppermute | solution.py:451
  38.4 5.9 %collective-permute-start.8 = (f32[16,512]{1,0:T(8,128)S(1)}, f32[16,512]{1,0:T(8,128)S(1)}, u32[]{:S(2)}, u32[]{:S(2)}) collective-permute-start(f32[16,512]{1,0:T(8,128)S(1)} %get-tuple-element.36.left_ref), channel_id=1, source_target_pairs={{1,0},{2,1},{3,2},{4,3},{5,4},{6,5},{7,6},{8,7},{9,8},{10,9},{11,1... | collective-permute-start | bytes 98312 | tf_op jit(solution)/shard_map/ppermute | solution.py:451
  46.0 6.5 %collective-permute-start.11 = (bf16[16,5120]{1,0:T(8,128)(2,1)S(1)}, bf16[16,5120]{1,0:T(8,128)(2,1)S(1)}, u32[]{:S(2)}, u32[]{:S(2)}) collective-permute-start(bf16[16,5120]{1,0:T(8,128)(2,1)S(1)} %get-tuple-element.38.charge_ref), channel_id=1, source_target_pairs={{0,1},{1,0},{2,3},{3,2},{4,5},{5,4},{6,7},{7,6},{8,9},{9,8},{10,11... | collective-permute-start | bytes 491528 | tf_op jit(solution)/shard_map/ppermute | solution.py:443
  46.0 8.8 %collective-permute-start.10 = (bf16[16,5120]{1,0:T(8,128)(2,1)S(1)}, bf16[16,5120]{1,0:T(8,128)(2,1)S(1)}, u32[]{:S(2)}, u32[]{:S(2)}) collective-permute-start(bf16[16,5120]{1,0:T(8,128)(2,1)S(1)} %get-tuple-element.38.charge_ref), channel_id=1, source_target_pairs={{0,2},{1,3},{2,0},{3,1},{4,6},{5,7},{6,4},{7,5},{8,10},{9,11},{10,... | collective-permute-start | bytes 491528 | tf_op jit(solution)/shard_map/ppermute | solution.py:443
  46.0 9.6 %collective-permute-start.9 = (bf16[16,5120]{1,0:T(8,128)(2,1)S(1)}, bf16[16,5120]{1,0:T(8,128)(2,1)S(1)}, u32[]{:S(2)}, u32[]{:S(2)}) collective-permute-start(bf16[16,5120]{1,0:T(8,128)(2,1)S(1)} %get-tuple-element.38.charge_ref), channel_id=1, source_target_pairs={{0,3},{1,2},{2,1},{3,0},{4,7},{5,6},{6,5},{7,4},{8,11},{9,10},{10,... | collective-permute-start | bytes 491528 | tf_op jit(solution)/shard_map/ppermute | solution.py:443
  56.4 1.2 %collective-permute-start.12 = (f32[16,256]{1,0:T(8,128)S(1)}, f32[16,256]{1,0:T(8,128)S(1)}, u32[]{:S(2)}, u32[]{:S(2)}) collective-permute-start(f32[16,256]{1,0:T(8,128)S(1)} %fock.7), channel_id=1, source_target_pairs={{0,4},{4,0},{8,12},{12,8},{16,20},{20,16},{24,28},{28,24},{1,5},{5... | collective-permute-start | bytes 49160 | tf_op jit(solution)/shard_map/ppermute | solution.py:443
  57.6 5.7 %collective-permute-start.15 = (f32[16,256]{1,0:T(8,128)S(1)}, f32[16,256]{1,0:T(8,128)S(1)}, u32[]{:S(2)}, u32[]{:S(2)}) collective-permute-start(f32[16,256]{1,0:T(8,128)S(1)} %add.12), channel_id=1, source_target_pairs={{0,24},{4,28},{8,16},{12,20},{16,8},{20,12},{24,0},{28,4},{1,25},{... | collective-permute-start | bytes 49160 | tf_op jit(solution)/shard_map/ppermute | solution.py:443
  61.6 4.6 %collective-permute-start.14 = (f32[16,256]{1,0:T(8,128)S(1)}, f32[16,256]{1,0:T(8,128)S(1)}, u32[]{:S(2)}, u32[]{:S(2)}) collective-permute-start(f32[16,256]{1,0:T(8,128)S(1)} %add.12), channel_id=1, source_target_pairs={{0,16},{4,20},{8,24},{12,28},{16,0},{20,4},{24,8},{28,12},{1,17},{... | collective-permute-start | bytes 49160 | tf_op jit(solution)/shard_map/ppermute | solution.py:443
  61.6 4.6 %collective-permute-start.13 = (f32[16,256]{1,0:T(8,128)S(1)}, f32[16,256]{1,0:T(8,128)S(1)}, u32[]{:S(2)}, u32[]{:S(2)}) collective-permute-start(f32[16,256]{1,0:T(8,128)S(1)} %add.12), channel_id=1, source_target_pairs={{0,8},{4,12},{8,0},{12,4},{16,24},{20,28},{24,16},{28,20},{1,9},{5... | collective-permute-start | bytes 49160 | tf_op jit(solution)/shard_map/ppermute | solution.py:443

commit v4 on v3

--- a/solution.py
+++ b/solution.py
@@ -25,6 +25,7 @@
 VMEM = pl.BlockSpec(memory_space=pltpu.VMEM)
 SMEM = pl.BlockSpec(memory_space=pltpu.SMEM)
 BAND = 0.1
+REACH = 8
 BF = jnp.bfloat16
 F32 = jnp.float32
 
@@ -112,8 +113,10 @@
     return pl.ds(pl.multiple_of(at, 128), PIECE)
 
 
-def phi_kernel(width, coef_ref, far_ref, *rest):
-    outs, (tile_ref, sem) = rest[:-2], rest[-2:]
+def phi_kernel(width, far_coef_ref, far_ref, *rest):
+    outs, (tile_ref, coef_ref, sem, coef_sem) = rest[:-4], rest[-4:]
+    first = pltpu.make_async_copy(far_coef_ref, coef_ref, coef_sem)
+    first.start()
     per = width // PIECE
     todo = [(k, p) for k in [*range(1, len(outs)), 0] for p in range(per)]
     copies = []
@@ -121,6 +124,7 @@
         at = chunk_piece(k, width, p)
         copies.append(pltpu.make_async_copy(far_ref.at[:, at], tile_ref.at[:, at], sem.at[i]))
         copies[-1].start()
+    first.wait()
     for (k, p), copy in zip(todo, copies):
         copy.wait()
         outs[k][:, p * PIECE : (p + 1) * PIECE] = jnp.dot(
@@ -133,11 +137,15 @@
     count = points // width
     return pl.pallas_call(
         functools.partial(phi_kernel, width),
-        in_specs=[VMEM, pl.BlockSpec(memory_space=pltpu.HBM)],
+        in_specs=[pl.BlockSpec(memory_space=pltpu.HBM)] * 2,
         out_specs=[VMEM] * (count + 1),
         out_shape=[jax.ShapeDtypeStruct((NDENS, width), F32)] * count
         + [jax.ShapeDtypeStruct(tiles.shape, tiles.dtype)],
-        scratch_shapes=[pltpu.SemaphoreType.DMA((points // PIECE,))],
+        scratch_shapes=[
+            pltpu.VMEM(coefs.shape, coefs.dtype),
+            pltpu.SemaphoreType.DMA((points // PIECE,)),
+            pltpu.SemaphoreType.DMA,
+        ],
         compiler_params=PARAMS,
         cost_estimate=pl.CostEstimate(
             flops=2 * NDENS * aux * points,
@@ -145,7 +153,7 @@
             transcendentals=0,
         ),
         name="phi",
-    )(coefs, pltpu.with_memory_space_constraint(tiles, pltpu.HBM))
+    )(*(pltpu.with_memory_space_constraint(a, pltpu.HBM) for a in (coefs, tiles)))
 
 
 def pair_build(e, geo, mask, dir_ref, bh):
@@ -222,29 +230,25 @@
     return [jnp.maximum(0.0, 1.0 - t) for t in tiles]
 
 
-def pair_kernel(
-    cnt_ref, before_ref, own_ref, after_ref, nbr_ref, dir_ref, w_ref,
-    t_ref, unc_ref, geo, mask, *bhs
-):
-    spheres, slots = nbr_ref.shape
-    reach = slots // 2
+def pair_kernel(before_ref, own_ref, after_ref, dir_ref, w_ref, t_ref, unc_ref, geo, mask, *bhs):
+    spheres = own_ref.shape[1]
+    slots = 2 * REACH
+    wide = spheres + 2 * REACH
+    rows = jnp.concatenate([before_ref[...], own_ref[...], after_ref[...]], axis=1)
+    rows = jnp.concatenate([rows, jnp.zeros((rows.shape[0], 128 - rows.shape[1]), F32)], axis=1)
+    rows = jnp.concatenate([rows, jnp.zeros((128 - rows.shape[0], 128), F32)], axis=0)
+    geo[...] = rows.T[: geo.shape[0]]
     first = (lax.axis_index("sph") * lax.axis_size("fit") + lax.axis_index("fit")) * spheres
-    rows = jnp.concatenate([before_ref[...], own_ref[...], after_ref[...]], axis=1)
-    wide = jnp.concatenate([rows, jnp.zeros((4, 128 - rows.shape[1]), F32)], axis=1)
-    wide = jnp.concatenate([wide, jnp.zeros((124, 128), F32)], axis=0)
-    geo[...] = wide.T[: rows.shape[1]]
-    row = lax.broadcasted_iota(jnp.int32, (spheres, slots), 0)
-    slot = lax.broadcasted_iota(jnp.int32, (spheres, slots), 1)
-    rel = nbr_ref[...] - first - row
-    many = jnp.zeros((spheres, slots), jnp.int32)
-    for i in range(spheres):
-        many = jnp.where(row == i, cnt_ref[i], many)
-    listed = slot < many
-    lane = lax.broadcasted_iota(jnp.int32, (spheres, 128), 1)
-    found = jnp.zeros((spheres, 128), F32)
+    row = lax.broadcasted_iota(jnp.int32, (wide, slots), 0) + (first - REACH)
+    slot = lax.broadcasted_iota(jnp.int32, (wide, slots), 1)
+    about = geo[spheres - REACH : 2 * spheres + REACH, :]
+    rel = about[:, 4 : 4 + slots] - row.astype(F32)
+    listed = slot.astype(F32) < about[:, 4 + slots : 5 + slots]
+    lane = lax.broadcasted_iota(jnp.int32, (wide, 128), 1)
+    found = jnp.zeros((wide, 128), F32)
     for c in range(slots):
-        gap = c - reach if c < reach else c - reach + 1
-        hit = jnp.where(listed & (rel == gap), 1.0, 0.0)
+        gap = c - REACH if c < REACH else c - REACH + 1
+        hit = jnp.where(listed & (rel == float(gap)), 1.0, 0.0)
         hit = jnp.max(hit, axis=1, keepdims=True)
         found = jnp.where(lane == c, hit, found)
     mask[...] = found
@@ -260,81 +264,81 @@
             unc_ref[b, :, 128 * t : 128 * t + 128] = v
         return carry
 
-    lax.fori_loop(0, spheres // QUAD, step, 0)
-
-
-def pair_call(before, own, after, neighbours, counts):
-    spheres, slots = neighbours.shape
-    reach = slots // 2
+    lax.fori_loop(0, wide // QUAD, step, 0)
+
+
+def pair_call(before, own, after):
+    spheres = own.shape[1]
+    wide = spheres + 2 * REACH
     w, d = pair_weights()
     return pl.pallas_call(
         pair_kernel,
-        in_specs=[SMEM] + [VMEM] * 6,
+        in_specs=[VMEM] * 5,
         out_specs=[VMEM] * 2,
-        scratch_shapes=[
-            pltpu.VMEM((spheres + 2 * reach, 128), F32),
-            pltpu.VMEM((spheres, 128), F32),
-        ]
+        scratch_shapes=[pltpu.VMEM((3 * spheres, 128), F32), pltpu.VMEM((wide, 128), F32)]
         + [pltpu.VMEM((400, 2 * NG), BF)] * QUAD,
         out_shape=[
-            jax.ShapeDtypeStruct((spheres, 8 * LP, 4 * LP), BF),
-            jax.ShapeDtypeStruct((spheres // QUAD, 1, QN), F32),
+            jax.ShapeDtypeStruct((wide, 8 * LP, 4 * LP), BF),
+            jax.ShapeDtypeStruct((wide // QUAD, 1, QN), F32),
         ],
         compiler_params=PARAMS,
         cost_estimate=pl.CostEstimate(
-            flops=spheres * 2 * 400 * 640 * 256, bytes_accessed=spheres * 262144, transcendentals=0
+            flops=wide * 2 * 400 * 640 * 256, bytes_accessed=wide * 262144, transcendentals=0
         ),
         name="pairs",
-    )(counts, before, own, after, neighbours, jnp.asarray(d), jnp.asarray(w))
+    )(before, own, after, jnp.asarray(d), jnp.asarray(w))
+
+
+def own_uncovered(unc_ref, b):
+    b = b + REACH // 2
+    return unc_ref[b // 2, :, b % 2 * PN : (b % 2 + 1) * PN]
 
 
 def rhs_kernel(count, *refs):
-    phis, (unc_ref, w_ref, left_ref, right_ref) = refs[:count], refs[count:]
-    pairs = 2 * unc_ref.shape[0]
+    phis, (unc_ref, w_ref, out_ref) = refs[:count], refs[count:]
+    pairs = out_ref.shape[1] // (2 * LP)
     rows = []
     for b in range(pairs):
         ls = slice(b * PN, (b + 1) * PN)
         total = phis[0][:, ls]
         for p in phis[1:]:
             total = total + p[:, ls]
-        rows.append(total * unc_ref[b // 2, :, b % 2 * PN : (b % 2 + 1) * PN])
+        rows.append(total * own_uncovered(unc_ref, b))
     hi, lo = halves(jnp.concatenate(rows, 0))
     n = pairs * NDENS
     r = jnp.dot(jnp.concatenate([hi, lo], 0), w_ref[...], preferred_element_type=F32)
     out = r[:n, : 2 * LP] + r[:n, 2 * LP :] + r[n:, : 2 * LP]
     out = out * (-4.0 * math.pi / NG)
     for b in range(pairs):
-        ref, at = (left_ref, b) if b < pairs // 2 else (right_ref, b - pairs // 2)
-        ref[:, at * 2 * LP : (at + 1) * 2 * LP] = out[b * NDENS : (b + 1) * NDENS]
+        out_ref[:, b * 2 * LP : (b + 1) * 2 * LP] = out[b * NDENS : (b + 1) * NDENS]
 
 
 def rhs_call(phis, unc, w):
-    half = unc.shape[0] // 2 * QUAD * LP
+    spheres = phis[0].shape[1] // NG
     return pl.pallas_call(
         functools.partial(rhs_kernel, len(phis)),
         in_specs=[VMEM] * (len(phis) + 2),
-        out_specs=[VMEM] * 2,
+        out_specs=VMEM,
         compiler_params=PARAMS,
-        out_shape=[jax.ShapeDtypeStruct((NDENS, half), F32)] * 2,
+        out_shape=jax.ShapeDtypeStruct((NDENS, spheres * LP), F32),
         cost_estimate=pl.CostEstimate(
-            flops=6 * NDENS * unc.shape[0] * QN * 256, bytes_accessed=1700000, transcendentals=0
+            flops=6 * NDENS * spheres * NG * 256, bytes_accessed=1700000, transcendentals=0
         ),
         name="rhs",
     )(*phis, unc, w)
 
 
-def gather_field(t_ref, x, xs, e):
+def gather_field(t_ref, shift, x, xs, e):
     low = lax.broadcasted_iota(jnp.int32, (NDENS, 128), 1) < LP
     parts = []
     for odd in (0, 1):
-        i = e + odd
         below, above = (x, xs) if odd == 0 else (xs, x)
         lo_at = e * LP
         up_at = (e + 8) * LP if odd == 0 else (e + 10) * LP
         lhs = jnp.concatenate(
             [below[:, lo_at : lo_at + 8 * LP], above[:, up_at : up_at + 8 * LP]], 0
         )
-        r = jnp.dot(lhs, t_ref[i], preferred_element_type=F32)
+        r = jnp.dot(lhs, t_ref[e + odd + shift], preferred_element_type=F32)
         n = NDENS
         a = r[0:n, : 2 * LP] + r[n : 2 * n, : 2 * LP] + r[0:n, 2 * LP :]
         b = r[2 * n : 3 * n, : 2 * LP] + r[3 * n :, : 2 * LP] + r[2 * n : 3 * n, 2 * LP :]
@@ -343,69 +347,68 @@
     return jnp.where(low, a0, b1) + pltpu.roll(jnp.where(low, a1, b0), LP, 1)
 
 
-def sweep_kernel(spheres, last, before_ref, left_ref, right_ref, after_ref, t_ref, rl_ref,
-                 rr_ref, sc_ref, *rest):
-    x, xs = rest[-2:]
-    half = left_ref.shape[1]
-    at = 0
-    for ref in (before_ref, left_ref, right_ref, after_ref):
-        wide = ref.shape[1]
-        for t in range(wide // 128):
-            hi, lo = halves(ref[:, 128 * t : 128 * t + 128] * sc_ref[0:1, :])
-            x[0:NDENS, at : at + 128] = hi
-            x[NDENS:, at : at + 128] = lo
-            at += 128
+def put_scaled(x, at, value):
+    hi, lo = halves(value)
+    x[0:NDENS, at : at + 128] = hi
+    x[NDENS:, at : at + 128] = lo
+
+
+def put_shifted(xs, x):
     v = x[...].astype(F32)
     xs[...] = jnp.concatenate([v[:, LP:], v[:, :LP]], 1).astype(BF)
+
+
+def sweep_kernel(
+    before_ref, own_ref, after_ref, t_ref, sc_ref, unc_ref, y_ref,
+    m_ref, out_ref, x, xs, z, zs
+):
+    own = own_ref.shape[1]
+    spheres = own // LP
+    right = lambda at: (before_ref, own_ref, after_ref)[at // own][:, at % own : at % own + 128]
+    for at in range(0, 3 * own, 128):
+        put_scaled(x, at, right(at) * sc_ref[0:1, :])
+    put_shifted(xs, x)
+    for e in range(0, spheres + 2 * REACH, 2):
+        new = right((e + spheres - REACH) * LP) + gather_field(t_ref, 0, x, xs, e)
+        put_scaled(z, e * LP, new * sc_ref[0:1, :])
+    put_shifted(zs, z)
     rows = []
     for e in range(0, spheres, 2):
-        got = gather_field(t_ref, x, xs, e)
-        at = e * LP
-        ref, at = (rl_ref, at) if at < half else (rr_ref, at - half)
-        new = ref[:, at : at + 128] + got
-        if last:
-            new = new * sc_ref[1:2, :]
-            rest[2][e] = new[:, :LM]
-            rest[2][e + 1] = pltpu.roll(new, LP, 1)[:, :LM]
-            rows.append(new)
-        else:
-            rest[0 if e * LP < half else 1][:, at : at + 128] = new
-    if last:
-        unc_ref, y_ref, _, out_ref = rest[:4]
-        hi, lo = halves(jnp.concatenate(rows, 0))
-        n = len(rows) * NDENS
-        r = jnp.dot(jnp.concatenate([hi, lo], 0), y_ref[...], preferred_element_type=F32)
-        out = r[:n, :PN] + r[:n, PN:] + r[n:, :PN]
-        for b in range(len(rows)):
-            weight = unc_ref[b // 2, :, b % 2 * PN : (b % 2 + 1) * PN] * (4.0 * math.pi / NG)
-            out_ref[:, b * PN : (b + 1) * PN] = (out[b * NDENS : (b + 1) * NDENS] * weight).astype(BF)
-
-
-def sweep_call(before, left, right, after, t, rl, rr, scales, last=None):
-    spheres = t.shape[0]
-    half = left.shape[1]
-    if last is None:
-        outs = [jax.ShapeDtypeStruct((NDENS, half), F32)] * 2
-        more = ()
-    else:
-        outs = [
+        new = own_ref[:, e * LP : e * LP + 128] + gather_field(t_ref, REACH, z, zs, e)
+        new = new * sc_ref[1:2, :]
+        m_ref[e] = new[:, :LM]
+        m_ref[e + 1] = pltpu.roll(new, LP, 1)[:, :LM]
+        rows.append(new)
+    hi, lo = halves(jnp.concatenate(rows, 0))
+    n = len(rows) * NDENS
+    r = jnp.dot(jnp.concatenate([hi, lo], 0), y_ref[...], preferred_element_type=F32)
+    out = r[:n, :PN] + r[:n, PN:] + r[n:, :PN]
+    for b in range(len(rows)):
+        weight = own_uncovered(unc_ref, b) * (4.0 * math.pi / NG)
+        out_ref[:, b * PN : (b + 1) * PN] = (out[b * NDENS : (b + 1) * NDENS] * weight).astype(BF)
+
+
+def sweep_call(before, own, after, t, scales, unc, wt):
+    lanes = own.shape[1]
+    spheres = lanes // LP
+    return pl.pallas_call(
+        sweep_kernel,
+        in_specs=[VMEM] * 7,
+        out_specs=[VMEM] * 2,
+        out_shape=[
             jax.ShapeDtypeStruct((spheres, NDENS, LM), F32),
             jax.ShapeDtypeStruct((NDENS, spheres * NG), BF),
-        ]
-        more = last
-    total = before.shape[1] + 2 * half + after.shape[1]
-    return pl.pallas_call(
-        functools.partial(sweep_kernel, spheres, last is not None),
-        in_specs=[VMEM] * (8 + len(more)),
-        out_specs=[VMEM] * 2,
-        out_shape=outs,
-        scratch_shapes=[pltpu.VMEM((2 * NDENS, total), BF)] * 2,
+        ],
+        scratch_shapes=[pltpu.VMEM((2 * NDENS, 3 * lanes), BF)] * 2
+        + [pltpu.VMEM((2 * NDENS, lanes + 2 * REACH * LP), BF)] * 2,
         compiler_params=PARAMS,
         cost_estimate=pl.CostEstimate(
-            flops=spheres * 2 * 64 * 512 * 256, bytes_accessed=spheres * 262144, transcendentals=0
+            flops=3 * spheres * 2 * 64 * 512 * 256,
+            bytes_accessed=2 * spheres * 262144,
+            transcendentals=0,
         ),
-        name="sweep",
-    )(before, left, right, after, t, rl, rr, scales, *more)
+        name="sweeps",
+    )(before, own, after, t, scales, unc, wt)
 
 
 def fock_kernel(k, width, charge_ref, tile_ref, *rest):
@@ -443,36 +446,33 @@
     return lax.ppermute(x, axis, [(i, i ^ k) for i in range(count)])
 
 
-def reach_out(last, initial):
+def from_beside(x):
     axes = ("sph", "fit")
     count = lax.axis_size("sph") * lax.axis_size("fit")
     up = [(i, (i + 1) % count) for i in range(count)]
     down = [((i + 1) % count, i) for i in range(count)]
-    return lax.ppermute(last, axes, up), lax.ppermute(initial, axes, down)
+    return lax.ppermute(x, axes, up), lax.ppermute(x, axes, down)
 
 
 def body(tiles, coefs, centres, radii, neighbours, counts):
     spheres, slots = neighbours.shape
-    reach = slots // 2
     fits = lax.axis_size("fit")
     sphs = lax.axis_size("sph")
     assert fits & (fits - 1) == 0 and sphs & (sphs - 1) == 0
-    assert spheres % (2 * QUAD) == 0 and spheres // 2 == reach == 8
+    assert spheres % (2 * QUAD) == 0 and spheres == slots == 2 * REACH
     w, wt = (jnp.asarray(a) for a in even_weights())
     scales = jnp.asarray(lane_scales())
-    width = spheres * NG
-
-    own = jnp.concatenate([centres, radii[None, :]], axis=0)
-    before, after = reach_out(own[:, spheres - reach :], own[:, :reach])
-    *phis, near_tiles = phi_call(coefs, tiles, width)
+
+    own = [centres, radii[None, :], neighbours.T.astype(F32), counts[None, :].astype(F32)]
+    own = jnp.concatenate(own + [jnp.zeros((3, spheres), F32)], axis=0)
+    before, after = from_beside(own)
+    *phis, near_tiles = phi_call(coefs, tiles, spheres * NG)
     phis, before, after = lax.optimization_barrier((phis, before, after))
     got = [trade(phis[k], "fit", k) for k in range(1, fits)]
-    t, unc = pair_call(before, own, after, neighbours, counts)
-    rl, rr = rhs_call([phis[0], *got], unc, w)
-    below, above = reach_out(rr, rl)
-    left, right = sweep_call(below, rl, rr, above, t, rl, rr, scales)
-    below, above = reach_out(right, left)
-    moments, charges = sweep_call(below, left, right, above, t, rl, rr, scales, (unc, wt))
+    t, unc = pair_call(before, own, after)
+    rhs = rhs_call([phis[0], *got], unc, w)
+    below, above = from_beside(rhs)
+    moments, charges = sweep_call(below, rhs, above, t, scales, unc, wt)
     others = [trade(charges, "fit", k) for k in range(1, fits)]
     fock = fock_call(0, charges, near_tiles)
     for k in range(1, fits):

time: 67.1 us -> 62.1 us (0.925)
  starting transfers between devices: 28.8 us -> 20.1 us
  Pallas kernels: 17.1 us -> 23.4 us
  waiting for transfers between devices: 18.1 us -> 14.7 us
  local copies, waits for them, and re-layouts: 0.85 us -> 1.59 us
    ppermute x10, waiting for transfers between devices: 13.5 us -> 4.95 us  [trade(): return lax.ppermute(x, axis, [(i, i ^ k) for i in range(count)])]
    ppermute x6 -> x4, starting transfers between devices: 17.2 us -> 8.68 us  [from_beside(): return (lax.ppermute(x, axes, up), lax.ppermute(x, axes, down))]
    pallas_call x4 -> x3, Pallas kernels: 13.6 us -> 20 us  [the longest x1 12.9 us: pair_call(): pl.pallas_call(pair_kernel, in_specs=[VMEM] * 5, out_specs=[VMEM] * 2, sc...]
    ppermute x6 -> x4, waiting for transfers between devices: 4.6 us -> 9.79 us  [from_beside(): return (lax.ppermute(x, axes, up), lax.ppermute(x, axes, down))]
    concatenate x0 -> x1, local copies, waits for them, and re-layouts: none -> 0.79 us  [body(): own = jnp.concatenate(own + [jnp.zeros((3, spheres), F32)], axis=0)]
    concatenate x1 -> x0, other arithmetic: 0.75 us -> none  [body(): own = jnp.concatenate([centres, radii[None, :]], axis=0)]
    convert_element_type x0 -> x2, other arithmetic: none -> 0.71 us  [the longest x1 0.7 us: body(): counts[None, :].astype(F32)]
  transfers between devices with their start and end apart: 16 -> 14, of which waited for: 10 -> 8; matrix products, arithmetic and copies ran while one was open for 0% -> 0% of each run, Pallas kernels for 20% -> 32%
where the time goes in v4:
time: 62.1 us; the launch traced here: 61.9 us
  Pallas kernels  23.4 us (38%)
  starting transfers between devices  20.1 us (32%)
  waiting for transfers between devices  14.7 us (24%)
  local copies, waits for them, and re-layouts  1.59 us (3%)
  other arithmetic  1.32 us (2%)
  between operations  0.75 us (1%)
    pallas_call x1, Pallas kernels, pair_call(): pl.pallas_call(pair_kernel, in_specs=[VMEM] * 5, out_specs=[VMEM] * 2, sc...  12.9 us
    ppermute x10, starting transfers between devices, trade(): return lax.ppermute(x, axis, [(i, i ^ k) for i in range(count)])  11.4 us
    ppermute x4, waiting for transfers between devices, from_beside(): return (lax.ppermute(x, axes, up), lax.ppermute(x, axes, down))  9.79 us
    ppermute x4, starting transfers between devices, from_beside(): return (lax.ppermute(x, axes, up), lax.ppermute(x, axes, down))  8.68 us
    ppermute x10, waiting for transfers between devices, trade(): return lax.ppermute(x, axis, [(i, i ^ k) for i in range(count)])  4.95 us
    pallas_call x1, Pallas kernels, phi_call(): pl.pallas_call(functools.partial(phi_kernel, width), in_specs=[pl.BlockSp...  4.39 us
    pallas_call x4, Pallas kernels, fock_call(): pl.pallas_call(functools.partial(fock_kernel, k, width), in_specs=[VMEM]...  3.14 us
    pallas_call x1, Pallas kernels, sweep_call(): pl.pallas_call(sweep_kernel, in_specs=[VMEM] * 7, out_specs=[VMEM] * 2, o...  2.69 us
  transfers between devices with their start and end apart: 14, of which 8 were waited for; matrix products, arithmetic and copies ran while one was open for 0% of the time, Pallas kernels for 32%

profile of v4, /device:TPU:0, one launch (start us, length us, event | category | flops | bytes accessed | tf_op | source)
XLA Modules:
  0.0 61.9 jit_solution(7720665075227349803)
XLA Ops:
  0.6 0.0 copy-start.3
  0.6 0.0 copy-start.4
  0.7 0.7 %convert_bitcast_fusion.1 = f32[1,16]{1,0:T(1,128)S(1)} fusion(s32[16]{0:T(128)} %param.16), kind=kLoop, calls=%fused_computation.2 | loop fusion | flops 16 | bytes 128 | tf_op jit(solution)/shard_map/convert_element_type | solution.py:466
  1.4 0.8 %copy.13 = s32[16,16]{0,1:T(8,128)S(1)} copy(s32[16,16]{1,0:T(8,128)} %param.15) | data formatting | bytes 2048 | tf_op args[4]
  2.1 0.8 %concatenate.3.own_ref = f32[24,16]{1,0:T(8,128)S(1)} concatenate(f32[3,16]{1,0:T(4,128)} %param.13, f32[1,16]{1,0:T(1,128)} %bitcast.5, f32[16,16]{1,0:T(8,128)S(1)} %convert_bitcast_fusion, f32[1,16]{1,0:T(1,128)S(1)} %convert_bitcast_fusion.1, f32[3,16]{1,0:T(4,128)S(1)} %broadcast_in_dim.8), dimensions={0} | concatenate | bytes 3072 | tf_op jit(solution)/shard_map/concatenate | solution.py:467
  2.9 6.4 %collective-permute-start.1 = (f32[24,16]{1,0:T(8,128)S(1)}, f32[24,16]{1,0:T(8,128)S(1)}, u32[]{:S(2)}, u32[]{:S(2)}) collective-permute-start(f32[24,16]{1,0:T(8,128)S(1)} %concatenate.3.own_ref), channel_id=1, source_target_pairs={{1,0},{2,1},{3,2},{4,3},{5,4},{6,5},{7,6},{8,7},{9,8},{10,9},{11,1... | collective-permute-start | bytes 4616 | tf_op jit(solution)/shard_map/ppermute | solution.py:454
  9.4 0.0 collective-permute-start
  9.4 4.4 %phi.1 = (f32[16,5120]{1,0:T(8,128)S(1)}, f32[16,5120]{1,0:T(8,128)S(1)}, f32[16,5120]{1,0:T(8,128)S(1)}, f32[16,5120]{1,0:T(8,128)S(1)}, bf16[256,20480]{1,0:T(8,128)(2,1)S(1)}) custom-call(bf16[16,256]{1,0:T(8,128)(2,1)} %far_coef_ref.1, bf16[256,20480]{1,0:T(8,128)(2,1)} %far_ref.1), custom_call_target="tpu_custom_call" | custom-call | flops 167772160 | bytes 11796480 | tf_op jit(solution)/shard_map/phi/pallas_call | solution.py:138
  13.8 0.0 copy-start
  13.8 0.0 copy-start.2
  13.8 0.0 collective-permute-done.1.after_ref
  13.8 2.4 %collective-permute-done.before_ref = f32[24,16]{1,0:T(8,128)S(1)} collective-permute-done((f32[24,16]{1,0:T(8,128)S(1)}, f32[24,16]{1,0:T(8,128)S(1)}, u32[]{:S(2)}, u32[]{:S(2)}) %collective-permute-start) | collective-permute-done | bytes 1568 | tf_op jit(solution)/shard_map/ppermute | solution.py:454
  16.2 3.5 %collective-permute-start.4 = (f32[16,5120]{1,0:T(8,128)S(1)}, f32[16,5120]{1,0:T(8,128)S(1)}, u32[]{:S(2)}, u32[]{:S(2)}) collective-permute-start(f32[16,5120]{1,0:T(8,128)S(1)} %get-tuple-element.24), channel_id=1, source_target_pairs={{0,3},{1,2},{2,1},{3,0},{4,7},{5,6},{6,5},{7,4},{8,11},{9,10},{10,... | collective-permute-start | bytes 983048 | tf_op jit(solution)/shard_map/ppermute | solution.py:446
  19.7 12.9 %pairs.1 = (bf16[32,512,256]{2,1,0:T(8,128)(2,1)S(1)}, f32[8,1,1280]{2,1,0:T(1,128)S(1)}) custom-call(f32[24,16]{1,0:T(8,128)S(1)} %collective-permute-done.before_ref, f32[24,16]{1,0:T(8,128)S(1)} %concatenate.3.own_ref, f32[24,16]{1,0:T(8,128)S(1)} %collective-permute-done.1.after_ref, f32[8,640]{1,0:T(8,128)S(1)} %copy-done.4, bf16[640,256]{1,0:T(8,128)(2,1)S(1)} %copy-done.3), custom_call_target="tpu_custom_call" | custom-call | flops 4194304000 | bytes 8388608 | tf_op jit(solution)/shard_map/pairs/pallas_call | solution.py:274
  32.6 0.3 rhs.1.own_ref
  33.0 2.2 %collective-permute-start.6 = (f32[16,1024]{1,0:T(8,128)S(1)}, f32[16,1024]{1,0:T(8,128)S(1)}, u32[]{:S(2)}, u32[]{:S(2)}) collective-permute-start(f32[16,1024]{1,0:T(8,128)S(1)} %rhs.1.own_ref), channel_id=1, source_target_pairs={{1,0},{2,1},{3,2},{4,3},{5,4},{6,5},{7,6},{8,7},{9,8},{10,9},{11,1... | collective-permute-start | bytes 196616 | tf_op jit(solution)/shard_map/ppermute | solution.py:454
  35.2 2.1 %collective-permute-done.6.after_ref = f32[16,1024]{1,0:T(8,128)S(1)} collective-permute-done((f32[16,1024]{1,0:T(8,128)S(1)}, f32[16,1024]{1,0:T(8,128)S(1)}, u32[]{:S(2)}, u32[]{:S(2)}) %collective-permute-start.6) | collective-permute-done | bytes 65568 | tf_op jit(solution)/shard_map/ppermute | solution.py:454
  37.3 5.3 %collective-permute-done.5.before_ref = f32[16,1024]{1,0:T(8,128)S(1)} collective-permute-done((f32[16,1024]{1,0:T(8,128)S(1)}, f32[16,1024]{1,0:T(8,128)S(1)}, u32[]{:S(2)}, u32[]{:S(2)}) %collective-permute-start.5) | collective-permute-done | bytes 65568 | tf_op jit(solution)/shard_map/ppermute | solution.py:454
  42.6 2.7 %sweeps.1 = (f32[16,16,49]{2,1,0:T(8,128)}, bf16[16,5120]{1,0:T(8,128)(2,1)S(1)}) custom-call(f32[16,1024]{1,0:T(8,128)S(1)} %collective-permute-done.5.before_ref, f32[16,1024]{1,0:T(8,128)S(1)} %rhs.1.own_ref, f32[16,1024]{1,0:T(8,128)S(1)} %collective-permute-done.6.after_ref, bf16[32,512,256]{2,1,0:T(8,128)(2,1)S(1)} %get-tuple-element.28.t_ref, ...), custom_call_target="tpu_custom_call" | custom-call | flops 805306368 | bytes 8388608 | tf_op jit(solution)/shard_map/sweeps/pallas_call | solution.py:394
  45.3 3.5 %collective-permute-start.7 = (bf16[16,5120]{1,0:T(8,128)(2,1)S(1)}, bf16[16,5120]{1,0:T(8,128)(2,1)S(1)}, u32[]{:S(2)}, u32[]{:S(2)}) collective-permute-start(bf16[16,5120]{1,0:T(8,128)(2,1)S(1)} %get-tuple-element.30.charge_ref), channel_id=1, source_target_pairs={{0,3},{1,2},{2,1},{3,0},{4,7},{5,6},{6,5},{7,4},{8,11},{9,10},{10,... | collective-permute-start | bytes 491528 | tf_op jit(solution)/shard_map/ppermute | solution.py:446
  48.8 0.8 %fock.4.rest_0_ = f32[16,256]{1,0:T(8,128)S(1)} custom-call(bf16[16,5120]{1,0:T(8,128)(2,1)S(1)} %get-tuple-element.30.charge_ref, bf16[256,20480]{1,0:T(8,128)(2,1)S(1)} %get-tuple-element.31.tile_ref), custom_call_target="tpu_custom_call" | custom-call | flops 41943040 | bytes 2621440 | tf_op jit(solution)/shard_map/fock/pallas_call | solution.py:431
  49.6 1.1 %collective-permute-done.9.charge_ref = bf16[16,5120]{1,0:T(8,128)(2,1)S(1)} collective-permute-done((bf16[16,5120]{1,0:T(8,128)(2,1)S(1)}, bf16[16,5120]{1,0:T(8,128)(2,1)S(1)}, u32[]{:S(2)}, u32[]{:S(2)}) %collective-permute-start.9) | collective-permute-done | bytes 163872 | tf_op jit(solution)/shard_map/ppermute | solution.py:446
  50.6 0.8 %fock.5.rest_0_ = f32[16,256]{1,0:T(8,128)S(1)} custom-call(bf16[16,5120]{1,0:T(8,128)(2,1)S(1)} %collective-permute-done.9.charge_ref, bf16[256,20480]{1,0:T(8,128)(2,1)S(1)} %get-tuple-element.31.tile_ref, f32[16,256]{1,0:T(8,128)S(1)} %fock.4.rest_0_), custom_call_target="tpu_custom_call" | custom-call | flops 41943040 | bytes 2621440 | tf_op jit(solution)/shard_map/fock/pallas_call | solution.py:431
  51.4 1.0 %collective-permute-done.8.charge_ref = bf16[16,5120]{1,0:T(8,128)(2,1)S(1)} collective-permute-done((bf16[16,5120]{1,0:T(8,128)(2,1)S(1)}, bf16[16,5120]{1,0:T(8,128)(2,1)S(1)}, u32[]{:S(2)}, u32[]{:S(2)}) %collective-permute-start.8) | collective-permute-done | bytes 163872 | tf_op jit(solution)/shard_map/ppermute | solution.py:446
  52.4 0.8 %fock.6.rest_0_ = f32[16,256]{1,0:T(8,128)S(1)} custom-call(bf16[16,5120]{1,0:T(8,128)(2,1)S(1)} %collective-permute-done.8.charge_ref, bf16[256,20480]{1,0:T(8,128)(2,1)S(1)} %get-tuple-element.31.tile_ref, f32[16,256]{1,0:T(8,128)S(1)} %fock.5.rest_0_), custom_call_target="tpu_custom_call" | custom-call | flops 41943040 | bytes 2621440 | tf_op jit(solution)/shard_map/fock/pallas_call | solution.py:431
  53.2 0.8 %fock.7 = f32[16,256]{1,0:T(8,128)S(1)} custom-call(bf16[16,5120]{1,0:T(8,128)(2,1)S(1)} %collective-permute-done.7.charge_ref, bf16[256,20480]{1,0:T(8,128)(2,1)S(1)} %get-tuple-element.31.tile_ref, f32[16,256]{1,0:T(8,128)S(1)} %fock.6.rest_0_), custom_call_target="tpu_custom_call" | custom-call | flops 41943040 | bytes 2621440 | tf_op jit(solution)/shard_map/fock/pallas_call | solution.py:431
  54.0 1.2 %collective-permute-done.10 = f32[16,256]{1,0:T(8,128)S(1)} collective-permute-done((f32[16,256]{1,0:T(8,128)S(1)}, f32[16,256]{1,0:T(8,128)S(1)}, u32[]{:S(2)}, u32[]{:S(2)}) %collective-permute-start.10) | collective-permute-done | bytes 16416 | tf_op jit(solution)/shard_map/ppermute | solution.py:446
  55.2 0.8 %collective-permute-start.13 = (f32[16,256]{1,0:T(8,128)S(1)}, f32[16,256]{1,0:T(8,128)S(1)}, u32[]{:S(2)}, u32[]{:S(2)}) collective-permute-start(f32[16,256]{1,0:T(8,128)S(1)} %add.12), channel_id=1, source_target_pairs={{0,24},{4,28},{8,16},{12,20},{16,8},{20,12},{24,0},{28,4},{1,25},{... | collective-permute-start | bytes 49160 | tf_op jit(solution)/shard_map/ppermute | solution.py:446
  56.0 3.5 %collective-permute-start.11 = (f32[16,256]{1,0:T(8,128)S(1)}, f32[16,256]{1,0:T(8,128)S(1)}, u32[]{:S(2)}, u32[]{:S(2)}) collective-permute-start(f32[16,256]{1,0:T(8,128)S(1)} %add.12), channel_id=1, source_target_pairs={{0,8},{4,12},{8,0},{12,4},{16,24},{20,28},{24,16},{28,20},{1,9},{5... | collective-permute-start | bytes 49160 | tf_op jit(solution)/shard_map/ppermute | solution.py:446
  59.6 1.3 %collective-permute-done.13 = f32[16,256]{1,0:T(8,128)S(1)} collective-permute-done((f32[16,256]{1,0:T(8,128)S(1)}, f32[16,256]{1,0:T(8,128)S(1)}, u32[]{:S(2)}, u32[]{:S(2)}) %collective-permute-start.13) | collective-permute-done | bytes 16416 | tf_op jit(solution)/shard_map/ppermute | solution.py:446
  60.8 0.4 collective-permute-done.11
  61.3 0.6 add_add_fusion
  (21 shorter events, 0.1 us)
Async XLA Ops:
  0.6 19.1 %copy-start.3 = (bf16[640,256]{1,0:T(8,128)(2,1)S(1)}, bf16[640,256]{1,0:T(8,128)(2,1)}, u32[]{:S(2)}) copy-start(bf16[640,256]{1,0:T(8,128)(2,1)} %constant.16.clone.w_ref) | copy-start | bytes 983044
  0.6 19.0 %copy-start.4 = (f32[8,640]{1,0:T(8,128)S(1)}, f32[8,640]{1,0:T(8,128)}, u32[]{:S(2)}) copy-start(f32[8,640]{1,0:T(8,128)} %constant.15.clone.dir_ref) | copy-start | bytes 61444
  2.9 29.7 %copy-start.1 = (bf16[640,256]{1,0:T(8,128)(2,1)S(1)}, bf16[640,256]{1,0:T(8,128)(2,1)}, u32[]{:S(2)}) copy-start(bf16[640,256]{1,0:T(8,128)(2,1)} %constant.12.clone.refs_5_) | copy-start | bytes 983044
  2.9 10.9 %collective-permute-start.1 = (f32[24,16]{1,0:T(8,128)S(1)}, f32[24,16]{1,0:T(8,128)S(1)}, u32[]{:S(2)}, u32[]{:S(2)}) collective-permute-start(f32[24,16]{1,0:T(8,128)S(1)} %concatenate.3.own_ref), channel_id=1, source_target_pairs={{1,0},{2,1},{3,2},{4,3},{5,4},{6,5},{7,6},{8,7},{9,8},{10,9},{11,1... | collective-permute-start | bytes 4616 | tf_op jit(solution)/shard_map/ppermute | solution.py:454
  9.4 6.8 %collective-permute-start = (f32[24,16]{1,0:T(8,128)S(1)}, f32[24,16]{1,0:T(8,128)S(1)}, u32[]{:S(2)}, u32[]{:S(2)}) collective-permute-start(f32[24,16]{1,0:T(8,128)S(1)} %concatenate.3.own_ref), channel_id=1, source_target_pairs={{0,1},{1,2},{2,3},{3,4},{4,5},{5,6},{6,7},{7,8},{8,9},{9,10},{10,1... | collective-permute-start | bytes 4616 | tf_op jit(solution)/shard_map/ppermute | solution.py:454
  13.8 28.8 %copy-start = (bf16[128,1280]{1,0:T(8,128)(2,1)S(1)}, bf16[128,1280]{1,0:T(8,128)(2,1)}, u32[]{:S(2)}) copy-start(bf16[128,1280]{1,0:T(8,128)(2,1)} %constant.13.clone.y_ref) | copy-start | bytes 983044
  13.8 28.8 %copy-start.2 = (f32[8,128]{1,0:T(8,128)S(1)}, f32[8,128]{1,0:T(8,128)}, u32[]{:S(2)}) copy-start(f32[8,128]{1,0:T(8,128)} %constant.14.clone.sc_ref) | copy-start | bytes 12292
  16.2 16.4 %collective-permute-start.2 = (f32[16,5120]{1,0:T(8,128)S(1)}, f32[16,5120]{1,0:T(8,128)S(1)}, u32[]{:S(2)}, u32[]{:S(2)}) collective-permute-start(f32[16,5120]{1,0:T(8,128)S(1)} %get-tuple-element.22), channel_id=1, source_target_pairs={{0,1},{1,0},{2,3},{3,2},{4,5},{5,4},{6,7},{7,6},{8,9},{9,8},{10,11... | collective-permute-start | bytes 983048 | tf_op jit(solution)/shard_map/ppermute | solution.py:446
  16.2 16.4 %collective-permute-start.3 = (f32[16,5120]{1,0:T(8,128)S(1)}, f32[16,5120]{1,0:T(8,128)S(1)}, u32[]{:S(2)}, u32[]{:S(2)}) collective-permute-start(f32[16,5120]{1,0:T(8,128)S(1)} %get-tuple-element.23), channel_id=1, source_target_pairs={{0,2},{1,3},{2,0},{3,1},{4,6},{5,7},{6,4},{7,5},{8,10},{9,11},{10,... | collective-permute-start | bytes 983048 | tf_op jit(solution)/shard_map/ppermute | solution.py:446
  16.2 16.4 %collective-permute-start.4 = (f32[16,5120]{1,0:T(8,128)S(1)}, f32[16,5120]{1,0:T(8,128)S(1)}, u32[]{:S(2)}, u32[]{:S(2)}) collective-permute-start(f32[16,5120]{1,0:T(8,128)S(1)} %get-tuple-element.24), channel_id=1, source_target_pairs={{0,3},{1,2},{2,1},{3,0},{4,7},{5,6},{6,5},{7,4},{8,11},{9,10},{10,... | collective-permute-start | bytes 983048 | tf_op jit(solution)/shard_map/ppermute | solution.py:446
  33.0 4.3 %collective-permute-start.6 = (f32[16,1024]{1,0:T(8,128)S(1)}, f32[16,1024]{1,0:T(8,128)S(1)}, u32[]{:S(2)}, u32[]{:S(2)}) collective-permute-start(f32[16,1024]{1,0:T(8,128)S(1)} %rhs.1.own_ref), channel_id=1, source_target_pairs={{1,0},{2,1},{3,2},{4,3},{5,4},{6,5},{7,6},{8,7},{9,8},{10,9},{11,1... | collective-permute-start | bytes 196616 | tf_op jit(solution)/shard_map/ppermute | solution.py:454
  35.2 7.4 %collective-permute-start.5 = (f32[16,1024]{1,0:T(8,128)S(1)}, f32[16,1024]{1,0:T(8,128)S(1)}, u32[]{:S(2)}, u32[]{:S(2)}) collective-permute-start(f32[16,1024]{1,0:T(8,128)S(1)} %rhs.1.own_ref), channel_id=1, source_target_pairs={{0,1},{1,2},{2,3},{3,4},{4,5},{5,6},{6,7},{7,8},{8,9},{9,10},{10,1... | collective-permute-start | bytes 196616 | tf_op jit(solution)/shard_map/ppermute | solution.py:454
  45.3 5.3 %collective-permute-start.9 = (bf16[16,5120]{1,0:T(8,128)(2,1)S(1)}, bf16[16,5120]{1,0:T(8,128)(2,1)S(1)}, u32[]{:S(2)}, u32[]{:S(2)}) collective-permute-start(bf16[16,5120]{1,0:T(8,128)(2,1)S(1)} %get-tuple-element.30.charge_ref), channel_id=1, source_target_pairs={{0,1},{1,0},{2,3},{3,2},{4,5},{5,4},{6,7},{7,6},{8,9},{9,8},{10,11... | collective-permute-start | bytes 491528 | tf_op jit(solution)/shard_map/ppermute | solution.py:446
  45.3 7.1 %collective-permute-start.8 = (bf16[16,5120]{1,0:T(8,128)(2,1)S(1)}, bf16[16,5120]{1,0:T(8,128)(2,1)S(1)}, u32[]{:S(2)}, u32[]{:S(2)}) collective-permute-start(bf16[16,5120]{1,0:T(8,128)(2,1)S(1)} %get-tuple-element.30.charge_ref), channel_id=1, source_target_pairs={{0,2},{1,3},{2,0},{3,1},{4,6},{5,7},{6,4},{7,5},{8,10},{9,11},{10,... | collective-permute-start | bytes 491528 | tf_op jit(solution)/shard_map/ppermute | solution.py:446
  45.3 7.9 %collective-permute-start.7 = (bf16[16,5120]{1,0:T(8,128)(2,1)S(1)}, bf16[16,5120]{1,0:T(8,128)(2,1)S(1)}, u32[]{:S(2)}, u32[]{:S(2)}) collective-permute-start(bf16[16,5120]{1,0:T(8,128)(2,1)S(1)} %get-tuple-element.30.charge_ref), channel_id=1, source_target_pairs={{0,3},{1,2},{2,1},{3,0},{4,7},{5,6},{6,5},{7,4},{8,11},{9,10},{10,... | collective-permute-start | bytes 491528 | tf_op jit(solution)/shard_map/ppermute | solution.py:446
  54.0 1.2 %collective-permute-start.10 = (f32[16,256]{1,0:T(8,128)S(1)}, f32[16,256]{1,0:T(8,128)S(1)}, u32[]{:S(2)}, u32[]{:S(2)}) collective-permute-start(f32[16,256]{1,0:T(8,128)S(1)} %fock.7), channel_id=1, source_target_pairs={{0,4},{4,0},{8,12},{12,8},{16,20},{20,16},{24,28},{28,24},{1,5},{5... | collective-permute-start | bytes 49160 | tf_op jit(solution)/shard_map/ppermute | solution.py:446
  55.2 5.7 %collective-permute-start.13 = (f32[16,256]{1,0:T(8,128)S(1)}, f32[16,256]{1,0:T(8,128)S(1)}, u32[]{:S(2)}, u32[]{:S(2)}) collective-permute-start(f32[16,256]{1,0:T(8,128)S(1)} %add.12), channel_id=1, source_target_pairs={{0,24},{4,28},{8,16},{12,20},{16,8},{20,12},{24,0},{28,4},{1,25},{... | collective-permute-start | bytes 49160 | tf_op jit(solution)/shard_map/ppermute | solution.py:446
  56.0 4.8 %collective-permute-start.12 = (f32[16,256]{1,0:T(8,128)S(1)}, f32[16,256]{1,0:T(8,128)S(1)}, u32[]{:S(2)}, u32[]{:S(2)}) collective-permute-start(f32[16,256]{1,0:T(8,128)S(1)} %add.12), channel_id=1, source_target_pairs={{0,16},{4,20},{8,24},{12,28},{16,0},{20,4},{24,8},{28,12},{1,17},{... | collective-permute-start | bytes 49160 | tf_op jit(solution)/shard_map/ppermute | solution.py:446
  56.0 5.3 %collective-permute-start.11 = (f32[16,256]{1,0:T(8,128)S(1)}, f32[16,256]{1,0:T(8,128)S(1)}, u32[]{:S(2)}, u32[]{:S(2)}) collective-permute-start(f32[16,256]{1,0:T(8,128)S(1)} %add.12), channel_id=1, source_target_pairs={{0,8},{4,12},{8,0},{12,4},{16,24},{20,28},{24,16},{28,20},{1,9},{5... | collective-permute-start | bytes 49160 | tf_op jit(solution)/shard_map/ppermute | solution.py:446

commit v5 on v4

--- a/solution.py
+++ b/solution.py
@@ -113,8 +113,22 @@
     return pl.ds(pl.multiple_of(at, 128), PIECE)
 
 
+def code(x):
+    top = jnp.maximum(jnp.max(jnp.abs(x), axis=1, keepdims=True), 1e-30)
+    power = jnp.floor(jnp.log2(top)) - 13.0
+    q = jnp.floor(x * jnp.exp2(-power) + 0.5).astype(jnp.int32)
+    tail = jnp.broadcast_to(power, (x.shape[0], 128)).astype(jnp.int32)
+    return q.astype(jnp.int16), tail.astype(jnp.int16)
+
+
+def decode(ref, ls):
+    width = ref.shape[1] - 128
+    power = ref[:, width:].astype(jnp.int32).astype(F32)[:, 0:1]
+    return ref[:, ls].astype(jnp.int32).astype(F32) * jnp.exp2(power)
+
+
 def phi_kernel(width, far_coef_ref, far_ref, *rest):
-    outs, (tile_ref, coef_ref, sem, coef_sem) = rest[:-4], rest[-4:]
+    outs, (tile_ref, full, coef_ref, sem, coef_sem) = rest[:-5], rest[-5:]
     first = pltpu.make_async_copy(far_coef_ref, coef_ref, coef_sem)
     first.start()
     per = width // PIECE
@@ -127,9 +141,14 @@
     first.wait()
     for (k, p), copy in zip(todo, copies):
         copy.wait()
-        outs[k][:, p * PIECE : (p + 1) * PIECE] = jnp.dot(
+        out = full if k else outs[0]
+        out[:, p * PIECE : (p + 1) * PIECE] = jnp.dot(
             coef_ref[...], tile_ref[:, chunk_piece(k, width, p)], preferred_element_type=F32
         )
+        if k and p == per - 1:
+            q, tail = code(full[...])
+            outs[k][:, :width] = q
+            outs[k][:, width:] = tail
 
 
 def phi_call(coefs, tiles, width):
@@ -139,9 +158,11 @@
         functools.partial(phi_kernel, width),
         in_specs=[pl.BlockSpec(memory_space=pltpu.HBM)] * 2,
         out_specs=[VMEM] * (count + 1),
-        out_shape=[jax.ShapeDtypeStruct((NDENS, width), F32)] * count
+        out_shape=[jax.ShapeDtypeStruct((NDENS, width), F32)]
+        + [jax.ShapeDtypeStruct((NDENS, width + 128), jnp.int16)] * (count - 1)
         + [jax.ShapeDtypeStruct(tiles.shape, tiles.dtype)],
         scratch_shapes=[
+            pltpu.VMEM((NDENS, width), F32),
             pltpu.VMEM(coefs.shape, coefs.dtype),
             pltpu.SemaphoreType.DMA((points // PIECE,)),
             pltpu.SemaphoreType.DMA,
@@ -154,6 +175,38 @@
         ),
         name="phi",
     )(*(pltpu.with_memory_space_constraint(a, pltpu.HBM) for a in (coefs, tiles)))
+
+
+def pack_kernel(centre_ref, radius_ref, nbr_ref, cnt_ref, out_ref, c, r, n, k, sem):
+    copies = [
+        pltpu.make_async_copy(a, b, sem.at[i])
+        for i, (a, b) in enumerate(zip((centre_ref, radius_ref, nbr_ref, cnt_ref), (c, r, n, k)))
+    ]
+    for copy in copies:
+        copy.start()
+    for copy in copies:
+        copy.wait()
+    spheres, slots = n.shape
+    out_ref[...] = jnp.zeros_like(out_ref)
+    out_ref[0:3, :] = c[...]
+    out_ref[3:4, :] = r[...]
+    out_ref[4:5, :] = k[...].astype(F32)
+    out_ref[8:, :] = n[...].astype(F32)
+
+
+def pack_call(centres, radii, neighbours, counts):
+    spheres, slots = neighbours.shape
+    args = (centres, radii.reshape(1, spheres), neighbours, counts.reshape(1, spheres))
+    return pl.pallas_call(
+        pack_kernel,
+        in_specs=[pl.BlockSpec(memory_space=pltpu.HBM)] * 4,
+        out_specs=VMEM,
+        out_shape=jax.ShapeDtypeStruct((8 + spheres, spheres), F32),
+        scratch_shapes=[pltpu.VMEM(a.shape, a.dtype) for a in args]
+        + [pltpu.SemaphoreType.DMA((4,))],
+        compiler_params=PARAMS,
+        name="pack",
+    )(*(pltpu.with_memory_space_constraint(a, pltpu.HBM) for a in args))
 
 
 def pair_build(e, geo, mask, dir_ref, bh):
@@ -234,16 +287,17 @@
     spheres = own_ref.shape[1]
     slots = 2 * REACH
     wide = spheres + 2 * REACH
-    rows = jnp.concatenate([before_ref[...], own_ref[...], after_ref[...]], axis=1)
-    rows = jnp.concatenate([rows, jnp.zeros((rows.shape[0], 128 - rows.shape[1]), F32)], axis=1)
-    rows = jnp.concatenate([rows, jnp.zeros((128 - rows.shape[0], 128), F32)], axis=0)
+    packs = (before_ref, own_ref, after_ref)
+    rows = jnp.concatenate([p[0:8, :] for p in packs], axis=1)
+    rows = jnp.concatenate([rows, jnp.zeros((8, 128 - rows.shape[1]), F32)], axis=1)
+    rows = jnp.concatenate([rows, jnp.zeros((120, 128), F32)], axis=0)
     geo[...] = rows.T[: geo.shape[0]]
     first = (lax.axis_index("sph") * lax.axis_size("fit") + lax.axis_index("fit")) * spheres
     row = lax.broadcasted_iota(jnp.int32, (wide, slots), 0) + (first - REACH)
     slot = lax.broadcasted_iota(jnp.int32, (wide, slots), 1)
-    about = geo[spheres - REACH : 2 * spheres + REACH, :]
-    rel = about[:, 4 : 4 + slots] - row.astype(F32)
-    listed = slot.astype(F32) < about[:, 4 + slots : 5 + slots]
+    lists = [before_ref[8 + spheres - REACH :, :], own_ref[8:, :], after_ref[8 : 8 + REACH, :]]
+    rel = jnp.concatenate(lists, axis=0) - row.astype(F32)
+    listed = slot.astype(F32) < geo[spheres - REACH : 2 * spheres + REACH, 4:5]
     lane = lax.broadcasted_iota(jnp.int32, (wide, 128), 1)
     found = jnp.zeros((wide, 128), F32)
     for c in range(slots):
@@ -264,7 +318,7 @@
             unc_ref[b, :, 128 * t : 128 * t + 128] = v
         return carry
 
-    lax.fori_loop(0, wide // QUAD, step, 0)
+    lax.fori_loop(0, wide // QUAD, step, 0, unroll=8)
 
 
 def pair_call(before, own, after):
@@ -302,7 +356,7 @@
         ls = slice(b * PN, (b + 1) * PN)
         total = phis[0][:, ls]
         for p in phis[1:]:
-            total = total + p[:, ls]
+            total = total + decode(p, ls)
         rows.append(total * own_uncovered(unc_ref, b))
     hi, lo = halves(jnp.concatenate(rows, 0))
     n = pairs * NDENS
@@ -359,8 +413,7 @@
 
 
 def sweep_kernel(
-    before_ref, own_ref, after_ref, t_ref, sc_ref, unc_ref, y_ref,
-    m_ref, out_ref, x, xs, z, zs
+    before_ref, own_ref, after_ref, t_ref, sc_ref, unc_ref, m_ref, out_ref, x, xs, z, zs
 ):
     own = own_ref.shape[1]
     spheres = own // LP
@@ -372,32 +425,30 @@
         new = right((e + spheres - REACH) * LP) + gather_field(t_ref, 0, x, xs, e)
         put_scaled(z, e * LP, new * sc_ref[0:1, :])
     put_shifted(zs, z)
-    rows = []
     for e in range(0, spheres, 2):
         new = own_ref[:, e * LP : e * LP + 128] + gather_field(t_ref, REACH, z, zs, e)
         new = new * sc_ref[1:2, :]
         m_ref[e] = new[:, :LM]
         m_ref[e + 1] = pltpu.roll(new, LP, 1)[:, :LM]
-        rows.append(new)
-    hi, lo = halves(jnp.concatenate(rows, 0))
-    n = len(rows) * NDENS
-    r = jnp.dot(jnp.concatenate([hi, lo], 0), y_ref[...], preferred_element_type=F32)
-    out = r[:n, :PN] + r[:n, PN:] + r[n:, :PN]
-    for b in range(len(rows)):
-        weight = own_uncovered(unc_ref, b) * (4.0 * math.pi / NG)
-        out_ref[:, b * PN : (b + 1) * PN] = (out[b * NDENS : (b + 1) * NDENS] * weight).astype(BF)
-
-
-def sweep_call(before, own, after, t, scales, unc, wt):
+        out_ref[:, e * LP : e * LP + 128] = new
+    out_ref[:, own:] = jnp.zeros((NDENS, 384), F32)
+    pairs = spheres // 2
+    for b in range(pairs):
+        part = own_uncovered(unc_ref, b)
+        out_ref[b : b + 1, own:] = part[:, :384]
+        out_ref[pairs + b : pairs + b + 1, own : own + 256] = part[:, 384:]
+
+
+def sweep_call(before, own, after, t, scales, unc):
     lanes = own.shape[1]
     spheres = lanes // LP
     return pl.pallas_call(
         sweep_kernel,
-        in_specs=[VMEM] * 7,
+        in_specs=[VMEM] * 6,
         out_specs=[VMEM] * 2,
         out_shape=[
             jax.ShapeDtypeStruct((spheres, NDENS, LM), F32),
-            jax.ShapeDtypeStruct((NDENS, spheres * NG), BF),
+            jax.ShapeDtypeStruct((NDENS, lanes + 384), F32),
         ],
         scratch_shapes=[pltpu.VMEM((2 * NDENS, 3 * lanes), BF)] * 2
         + [pltpu.VMEM((2 * NDENS, lanes + 2 * REACH * LP), BF)] * 2,
@@ -408,37 +459,52 @@
             transcendentals=0,
         ),
         name="sweeps",
-    )(before, own, after, t, scales, unc, wt)
-
-
-def fock_kernel(k, width, charge_ref, tile_ref, *rest):
-    total = rest[0][...] if len(rest) == 2 else None
+    )(before, own, after, t, scales, unc)
+
+
+def fock_kernel(k, pay_ref, y_ref, tile_ref, *rest):
+    out_ref, charge = rest[-2:]
+    own = pay_ref.shape[1] - 384
+    pairs = own // (2 * LP)
+    width = pairs * PN
+    rows = [pay_ref[:, b * 2 * LP : (b + 1) * 2 * LP] for b in range(pairs)]
+    hi, lo = halves(jnp.concatenate(rows, 0))
+    n = pairs * NDENS
+    r = jnp.dot(jnp.concatenate([hi, lo], 0), y_ref[...], preferred_element_type=F32)
+    out = r[:n, :PN] + r[:n, PN:] + r[n:, :PN]
+    for b in range(pairs):
+        unc = jnp.concatenate(
+            [pay_ref[b : b + 1, own:], pay_ref[pairs + b : pairs + b + 1, own : own + 256]], 1
+        )
+        weight = unc * (4.0 * math.pi / NG)
+        charge[:, b * PN : (b + 1) * PN] = (out[b * NDENS : (b + 1) * NDENS] * weight).astype(BF)
+    total = rest[0][...] if len(rest) == 3 else None
     for p in range(width // PIECE):
         part = lax.dot_general(
-            charge_ref[:, p * PIECE : (p + 1) * PIECE],
+            charge[:, p * PIECE : (p + 1) * PIECE],
             tile_ref[:, chunk_piece(k, width, p)],
             (((1,), (1,)), ((), ())),
             preferred_element_type=F32,
         )
         total = part if total is None else total + part
-    rest[-1][...] = total
-
-
-def fock_call(k, charges, tiles, before=None):
+    out_ref[...] = total
+
+
+def fock_call(k, pay, wt, tiles, width, before=None):
     aux = tiles.shape[0]
-    width = charges.shape[1]
     more = [] if before is None else [before]
     return pl.pallas_call(
-        functools.partial(fock_kernel, k, width),
-        in_specs=[VMEM] * (2 + len(more)),
+        functools.partial(fock_kernel, k),
+        in_specs=[VMEM] * (3 + len(more)),
         out_specs=VMEM,
         out_shape=jax.ShapeDtypeStruct((NDENS, aux), F32),
+        scratch_shapes=[pltpu.VMEM((NDENS, width), BF)],
         compiler_params=PARAMS,
         cost_estimate=pl.CostEstimate(
             flops=2 * NDENS * aux * width, bytes_accessed=2 * aux * width, transcendentals=0
         ),
         name="fock",
-    )(charges, tiles, *more)
+    )(pay, wt, tiles, *more)
 
 
 def trade(x, axis, k):
@@ -463,20 +529,20 @@
     w, wt = (jnp.asarray(a) for a in even_weights())
     scales = jnp.asarray(lane_scales())
 
-    own = [centres, radii[None, :], neighbours.T.astype(F32), counts[None, :].astype(F32)]
-    own = jnp.concatenate(own + [jnp.zeros((3, spheres), F32)], axis=0)
+    width = spheres * NG
+    own = pack_call(centres, radii, neighbours, counts)
     before, after = from_beside(own)
-    *phis, near_tiles = phi_call(coefs, tiles, spheres * NG)
+    *phis, near_tiles = phi_call(coefs, tiles, width)
     phis, before, after = lax.optimization_barrier((phis, before, after))
     got = [trade(phis[k], "fit", k) for k in range(1, fits)]
     t, unc = pair_call(before, own, after)
     rhs = rhs_call([phis[0], *got], unc, w)
     below, above = from_beside(rhs)
-    moments, charges = sweep_call(below, rhs, above, t, scales, unc, wt)
-    others = [trade(charges, "fit", k) for k in range(1, fits)]
-    fock = fock_call(0, charges, near_tiles)
+    moments, pay = sweep_call(below, rhs, above, t, scales, unc)
+    others = [trade(pay, "fit", k) for k in range(1, fits)]
+    fock = fock_call(0, pay, wt, near_tiles, width)
     for k in range(1, fits):
-        fock = fock_call(k, others[k - 1], near_tiles, fock)
+        fock = fock_call(k, others[k - 1], wt, near_tiles, width, fock)
     fock = fock + trade(fock, "sph", 1)
     bit = 2
     while bit < sphs:

time: 62.1 us -> 58.7 us (0.945)
  waiting for transfers between devices: 14.7 us -> 12.6 us
  local copies, waits for them, and re-layouts: 1.59 us -> 0.03 us
  Pallas kernels: 23.4 us -> 24.5 us
  other arithmetic: 1.32 us -> 0.62 us
    pallas_call x5 -> x6, Pallas kernels: 5.83 us -> 8.66 us  [the longest x4 5.02 us: fock_call(): pl.pallas_call(functools.partial(fock_kernel, k), in_specs=[VMEM] * (3 +...]
    ppermute x10, waiting for transfers between devices: 4.95 us -> 2.95 us  [trade(): return lax.ppermute(x, axis, [(i, i ^ k) for i in range(count)])]
    pallas_call x1, Pallas kernels: 12.9 us -> 11 us  [pair_call(): pl.pallas_call(pair_kernel, in_specs=[VMEM] * 5, out_specs=[VMEM] * 2, sc...]
    concatenate x1 -> x0, local copies, waits for them, and re-layouts: 0.79 us -> none  [body(): own = jnp.concatenate(own + [jnp.zeros((3, spheres), F32)], axis=0)]
    unnamed x11 -> x10, local copies, waits for them, and re-layouts: 0.8 us -> 0.03 us
    convert_element_type x2 -> x0, other arithmetic: 0.71 us -> none  [the longest x1 0.7 us: body(): counts[None, :].astype(F32)]
  transfers between devices with their start and end apart: 14 -> 14, of which waited for: 8 -> 6; matrix products, arithmetic and copies ran while one was open for 0% -> 0% of each run, Pallas kernels for 32% -> 33%
where the time goes in v5:
time: 58.7 us; the launch traced here: 58.5 us
  Pallas kernels  24.5 us (42%)
  starting transfers between devices  20 us (34%)
  waiting for transfers between devices  12.6 us (21%)
  between operations  0.76 us (1%)
  other arithmetic  0.62 us (1%)
    ppermute x10, starting transfers between devices, trade(): return lax.ppermute(x, axis, [(i, i ^ k) for i in range(count)])  11.4 us
    pallas_call x1, Pallas kernels, pair_call(): pl.pallas_call(pair_kernel, in_specs=[VMEM] * 5, out_specs=[VMEM] * 2, sc...  11 us
    ppermute x4, waiting for transfers between devices, from_beside(): return (lax.ppermute(x, axes, up), lax.ppermute(x, axes, down))  9.69 us
    ppermute x4, starting transfers between devices, from_beside(): return (lax.ppermute(x, axes, up), lax.ppermute(x, axes, down))  8.69 us
    pallas_call x4, Pallas kernels, fock_call(): pl.pallas_call(functools.partial(fock_kernel, k), in_specs=[VMEM] * (3 +...  5.02 us
    pallas_call x1, Pallas kernels, phi_call(): pl.pallas_call(functools.partial(phi_kernel, width), in_specs=[pl.BlockSp...  4.39 us
    ppermute x10, waiting for transfers between devices, trade(): return lax.ppermute(x, axis, [(i, i ^ k) for i in range(count)])  2.95 us
    pallas_call x1, Pallas kernels, sweep_call(): pl.pallas_call(sweep_kernel, in_specs=[VMEM] * 6, out_specs=[VMEM] * 2, o...  2.83 us
  transfers between devices with their start and end apart: 14, of which 6 were waited for; matrix products, arithmetic and copies ran while one was open for 0% of the time, Pallas kernels for 33%

profile of v5, /device:TPU:0, one launch (start us, length us, event | category | flops | bytes accessed | tf_op | source)
XLA Modules:
  0.0 58.5 jit_solution(7739317202137754815)
XLA Ops:
  0.6 0.0 copy-start.3
  0.6 0.0 copy-start.4
  0.7 0.8 %pack.1.own_ref = f32[24,16]{1,0:T(8,128)S(1)} custom-call(f32[3,16]{1,0:T(4,128)} %centre_ref.1, f32[1,16]{1,0:T(1,128)} %bitcast.2, s32[16,16]{1,0:T(8,128)} %nbr_ref.1, s32[1,16]{1,0:T(1,128)} %bitcast.3), custom_call_target="tpu_custom_call" | custom-call | tf_op jit(solution)/shard_map/pack/pallas_call | solution.py:200
  1.5 0.0 copy-start.1
  1.5 6.4 %collective-permute-start.1 = (f32[24,16]{1,0:T(8,128)S(1)}, f32[24,16]{1,0:T(8,128)S(1)}, u32[]{:S(2)}, u32[]{:S(2)}) collective-permute-start(f32[24,16]{1,0:T(8,128)S(1)} %pack.1.own_ref), channel_id=1, source_target_pairs={{1,0},{2,1},{3,2},{4,3},{5,4},{6,5},{7,6},{8,7},{9,8},{10,9},{11,1... | collective-permute-start | bytes 4616 | tf_op jit(solution)/shard_map/ppermute | solution.py:520
  7.9 4.4 %phi.1 = (f32[16,5120]{1,0:T(8,128)S(1)}, s16[16,5248]{1,0:T(8,128)(2,1)S(1)}, s16[16,5248]{1,0:T(8,128)(2,1)S(1)}, s16[16,5248]{1,0:T(8,128)(2,1)S(1)}, bf16[256,20480]{1,0:T(8,128)(2,1)S(1)}) custom-call(bf16[16,256]{1,0:T(8,128)(2,1)} %far_coef_ref.1, bf16[256,20480]{1,0:T(8,128)(2,1)} %far_ref.1), custom_call_target="tpu_custom_call" | custom-call | flops 167772160 | bytes 11796480 | tf_op jit(solution)/shard_map/phi/pallas_call | solution.py:157
  12.3 0.0 copy-start.2
  12.3 0.0 collective-permute-done.1.after_ref
  12.3 2.4 %collective-permute-done.before_ref = f32[24,16]{1,0:T(8,128)S(1)} collective-permute-done((f32[24,16]{1,0:T(8,128)S(1)}, f32[24,16]{1,0:T(8,128)S(1)}, u32[]{:S(2)}, u32[]{:S(2)}) %collective-permute-start) | collective-permute-done | bytes 1568 | tf_op jit(solution)/shard_map/ppermute | solution.py:520
  14.8 0.0 collective-permute-start.2
  14.8 0.0 collective-permute-start.3
  14.8 3.5 %collective-permute-start.4 = (s16[16,5248]{1,0:T(8,128)(2,1)S(1)}, s16[16,5248]{1,0:T(8,128)(2,1)S(1)}, u32[]{:S(2)}, u32[]{:S(2)}) collective-permute-start(s16[16,5248]{1,0:T(8,128)(2,1)S(1)} %get-tuple-element.24), channel_id=1, source_target_pairs={{0,3},{1,2},{2,1},{3,0},{4,7},{5,6},{6,5},{7,4},{8,11},{9,10},{10,... | collective-permute-start | bytes 503816 | tf_op jit(solution)/shard_map/ppermute | solution.py:512
  18.2 11.0 %pairs.1 = (bf16[32,512,256]{2,1,0:T(8,128)(2,1)S(1)}, f32[8,1,1280]{2,1,0:T(1,128)S(1)}) custom-call(f32[24,16]{1,0:T(8,128)S(1)} %collective-permute-done.before_ref, f32[24,16]{1,0:T(8,128)S(1)} %pack.1.own_ref, f32[24,16]{1,0:T(8,128)S(1)} %collective-permute-done.1.after_ref, f32[8,640]{1,0:T(8,128)S(1)} %copy-done.4, bf16[640,256]{1,0:T(8,128)(2,1)S(1)} %copy-done.3), custom_call_target="tpu_custom_call" | custom-call | flops 4194304000 | bytes 8388608 | tf_op jit(solution)/shard_map/pairs/pallas_call | solution.py:328
  29.3 0.0 collective-permute-done.2.refs_1_
  29.3 0.0 collective-permute-done.3.refs_2_
  29.3 0.4 rhs.1.own_ref
  29.7 2.3 %collective-permute-start.6 = (f32[16,1024]{1,0:T(8,128)S(1)}, f32[16,1024]{1,0:T(8,128)S(1)}, u32[]{:S(2)}, u32[]{:S(2)}) collective-permute-start(f32[16,1024]{1,0:T(8,128)S(1)} %rhs.1.own_ref), channel_id=1, source_target_pairs={{1,0},{2,1},{3,2},{4,3},{5,4},{6,5},{7,6},{8,7},{9,8},{10,9},{11,1... | collective-permute-start | bytes 196616 | tf_op jit(solution)/shard_map/ppermute | solution.py:520
  32.0 0.0 collective-permute-start.5
  32.0 2.1 %collective-permute-done.6.after_ref = f32[16,1024]{1,0:T(8,128)S(1)} collective-permute-done((f32[16,1024]{1,0:T(8,128)S(1)}, f32[16,1024]{1,0:T(8,128)S(1)}, u32[]{:S(2)}, u32[]{:S(2)}) %collective-permute-start.6) | collective-permute-done | bytes 65568 | tf_op jit(solution)/shard_map/ppermute | solution.py:520
  34.0 5.2 %collective-permute-done.5.before_ref = f32[16,1024]{1,0:T(8,128)S(1)} collective-permute-done((f32[16,1024]{1,0:T(8,128)S(1)}, f32[16,1024]{1,0:T(8,128)S(1)}, u32[]{:S(2)}, u32[]{:S(2)}) %collective-permute-start.5) | collective-permute-done | bytes 65568 | tf_op jit(solution)/shard_map/ppermute | solution.py:520
  39.3 2.8 %sweeps.1 = (f32[16,16,49]{2,1,0:T(8,128)}, f32[16,1408]{1,0:T(8,128)S(1)}) custom-call(f32[16,1024]{1,0:T(8,128)S(1)} %collective-permute-done.5.before_ref, f32[16,1024]{1,0:T(8,128)S(1)} %rhs.1.own_ref, f32[16,1024]{1,0:T(8,128)S(1)} %collective-permute-done.6.after_ref, bf16[32,512,256]{2,1,0:T(8,128)(2,1)S(1)} %get-tuple-element.28.t_ref, ...), custom_call_target="tpu_custom_call" | custom-call | flops 805306368 | bytes 8388608 | tf_op jit(solution)/shard_map/sweeps/pallas_call | solution.py:445
  42.1 3.5 %collective-permute-start.7 = (f32[16,1408]{1,0:T(8,128)S(1)}, f32[16,1408]{1,0:T(8,128)S(1)}, u32[]{:S(2)}, u32[]{:S(2)}) collective-permute-start(f32[16,1408]{1,0:T(8,128)S(1)} %get-tuple-element.30.pay_ref), channel_id=1, source_target_pairs={{0,3},{1,2},{2,1},{3,0},{4,7},{5,6},{6,5},{7,4},{8,11},{9,10},{10,... | collective-permute-start | bytes 270344 | tf_op jit(solution)/shard_map/ppermute | solution.py:512
  45.6 1.2 %fock.4.rest_0_ = f32[16,256]{1,0:T(8,128)S(1)} custom-call(f32[16,1408]{1,0:T(8,128)S(1)} %get-tuple-element.30.pay_ref, bf16[128,1280]{1,0:T(8,128)(2,1)S(1)} %copy-done, bf16[256,20480]{1,0:T(8,128)(2,1)S(1)} %get-tuple-element.31.tile_ref), custom_call_target="tpu_custom_call" | custom-call | flops 41943040 | bytes 2621440 | tf_op jit(solution)/shard_map/fock/pallas_call | solution.py:496
  46.8 1.3 %fock.5.rest_0_ = f32[16,256]{1,0:T(8,128)S(1)} custom-call(f32[16,1408]{1,0:T(8,128)S(1)} %collective-permute-done.9.pay_ref, bf16[128,1280]{1,0:T(8,128)(2,1)S(1)} %copy-done, bf16[256,20480]{1,0:T(8,128)(2,1)S(1)} %get-tuple-element.31.tile_ref, f32[16,256]{1,0:T(8,128)S(1)} %fock.4.rest_0_), custom_call_target="tpu_custom_call" | custom-call | flops 41943040 | bytes 2621440 | tf_op jit(solution)/shard_map/fock/pallas_call | solution.py:496
  48.1 1.3 %fock.6.rest_0_ = f32[16,256]{1,0:T(8,128)S(1)} custom-call(f32[16,1408]{1,0:T(8,128)S(1)} %collective-permute-done.8.pay_ref, bf16[128,1280]{1,0:T(8,128)(2,1)S(1)} %copy-done, bf16[256,20480]{1,0:T(8,128)(2,1)S(1)} %get-tuple-element.31.tile_ref, f32[16,256]{1,0:T(8,128)S(1)} %fock.5.rest_0_), custom_call_target="tpu_custom_call" | custom-call | flops 41943040 | bytes 2621440 | tf_op jit(solution)/shard_map/fock/pallas_call | solution.py:496
  49.3 1.3 %fock.7 = f32[16,256]{1,0:T(8,128)S(1)} custom-call(f32[16,1408]{1,0:T(8,128)S(1)} %collective-permute-done.7.pay_ref, bf16[128,1280]{1,0:T(8,128)(2,1)S(1)} %copy-done, bf16[256,20480]{1,0:T(8,128)(2,1)S(1)} %get-tuple-element.31.tile_ref, f32[16,256]{1,0:T(8,128)S(1)} %fock.6.rest_0_), custom_call_target="tpu_custom_call" | custom-call | flops 41943040 | bytes 2621440 | tf_op jit(solution)/shard_map/fock/pallas_call | solution.py:496
  50.6 1.2 %collective-permute-done.10 = f32[16,256]{1,0:T(8,128)S(1)} collective-permute-done((f32[16,256]{1,0:T(8,128)S(1)}, f32[16,256]{1,0:T(8,128)S(1)}, u32[]{:S(2)}, u32[]{:S(2)}) %collective-permute-start.10) | collective-permute-done | bytes 16416 | tf_op jit(solution)/shard_map/ppermute | solution.py:512
  51.8 0.1 collective-permute-start.12
  51.9 4.3 %collective-permute-start.11 = (f32[16,256]{1,0:T(8,128)S(1)}, f32[16,256]{1,0:T(8,128)S(1)}, u32[]{:S(2)}, u32[]{:S(2)}) collective-permute-start(f32[16,256]{1,0:T(8,128)S(1)} %add.12), channel_id=1, source_target_pairs={{0,8},{4,12},{8,0},{12,4},{16,24},{20,28},{24,16},{28,20},{1,9},{5... | collective-permute-start | bytes 49160 | tf_op jit(solution)/shard_map/ppermute | solution.py:512
  56.2 1.1 %collective-permute-done.13 = f32[16,256]{1,0:T(8,128)S(1)} collective-permute-done((f32[16,256]{1,0:T(8,128)S(1)}, f32[16,256]{1,0:T(8,128)S(1)}, u32[]{:S(2)}, u32[]{:S(2)}) %collective-permute-start.13) | collective-permute-done | bytes 16416 | tf_op jit(solution)/shard_map/ppermute | solution.py:512
  57.4 0.6 collective-permute-done.11
  57.9 0.6 %add_add_fusion = f32[16,256]{1,0:T(8,128)} fusion(f32[16,256]{1,0:T(8,128)S(1)} %collective-permute-done.13, f32[16,256]{1,0:T(8,128)S(1)} %collective-permute-done.12, f32[16,256]{1,0:T(8,128)S(1)} %add.12, f32[16,256]{1,0:T(8,128)S(1)} %collective-permute-done.11), kind=kLoop, calls=%fused_computation | loop fusion | flops 12288 | bytes 81920 | tf_op jit(solution)/shard_map/add | solution.py:550
  (17 shorter events, 0.0 us)
Async XLA Ops:
  0.6 17.6 %copy-start.3 = (bf16[640,256]{1,0:T(8,128)(2,1)S(1)}, bf16[640,256]{1,0:T(8,128)(2,1)}, u32[]{:S(2)}) copy-start(bf16[640,256]{1,0:T(8,128)(2,1)} %constant.14.clone.w_ref) | copy-start | bytes 983044
  0.6 17.6 %copy-start.4 = (f32[8,640]{1,0:T(8,128)S(1)}, f32[8,640]{1,0:T(8,128)}, u32[]{:S(2)}) copy-start(f32[8,640]{1,0:T(8,128)} %constant.13.clone.dir_ref) | copy-start | bytes 61444
  1.5 27.9 %copy-start.1 = (bf16[640,256]{1,0:T(8,128)(2,1)S(1)}, bf16[640,256]{1,0:T(8,128)(2,1)}, u32[]{:S(2)}) copy-start(bf16[640,256]{1,0:T(8,128)(2,1)} %constant.10.clone.refs_5_) | copy-start | bytes 983044
  1.5 10.8 %collective-permute-start.1 = (f32[24,16]{1,0:T(8,128)S(1)}, f32[24,16]{1,0:T(8,128)S(1)}, u32[]{:S(2)}, u32[]{:S(2)}) collective-permute-start(f32[24,16]{1,0:T(8,128)S(1)} %pack.1.own_ref), channel_id=1, source_target_pairs={{1,0},{2,1},{3,2},{4,3},{5,4},{6,5},{7,6},{8,7},{9,8},{10,9},{11,1... | collective-permute-start | bytes 4616 | tf_op jit(solution)/shard_map/ppermute | solution.py:520
  7.9 6.8 %collective-permute-start = (f32[24,16]{1,0:T(8,128)S(1)}, f32[24,16]{1,0:T(8,128)S(1)}, u32[]{:S(2)}, u32[]{:S(2)}) collective-permute-start(f32[24,16]{1,0:T(8,128)S(1)} %pack.1.own_ref), channel_id=1, source_target_pairs={{0,1},{1,2},{2,3},{3,4},{4,5},{5,6},{6,7},{7,8},{8,9},{9,10},{10,1... | collective-permute-start | bytes 4616 | tf_op jit(solution)/shard_map/ppermute | solution.py:520
  12.3 26.9 %copy-start.2 = (f32[8,128]{1,0:T(8,128)S(1)}, f32[8,128]{1,0:T(8,128)}, u32[]{:S(2)}) copy-start(f32[8,128]{1,0:T(8,128)} %constant.12.clone.sc_ref) | copy-start | bytes 12292
  14.8 30.8 %copy-start = (bf16[128,1280]{1,0:T(8,128)(2,1)S(1)}, bf16[128,1280]{1,0:T(8,128)(2,1)}, u32[]{:S(2)}) copy-start(bf16[128,1280]{1,0:T(8,128)(2,1)} %constant.11.clone.y_ref) | copy-start | bytes 983044
  14.8 14.5 %collective-permute-start.2 = (s16[16,5248]{1,0:T(8,128)(2,1)S(1)}, s16[16,5248]{1,0:T(8,128)(2,1)S(1)}, u32[]{:S(2)}, u32[]{:S(2)}) collective-permute-start(s16[16,5248]{1,0:T(8,128)(2,1)S(1)} %get-tuple-element.22), channel_id=1, source_target_pairs={{0,1},{1,0},{2,3},{3,2},{4,5},{5,4},{6,7},{7,6},{8,9},{9,8},{10,11... | collective-permute-start | bytes 503816 | tf_op jit(solution)/shard_map/ppermute | solution.py:512
  14.8 14.6 %collective-permute-start.3 = (s16[16,5248]{1,0:T(8,128)(2,1)S(1)}, s16[16,5248]{1,0:T(8,128)(2,1)S(1)}, u32[]{:S(2)}, u32[]{:S(2)}) collective-permute-start(s16[16,5248]{1,0:T(8,128)(2,1)S(1)} %get-tuple-element.23), channel_id=1, source_target_pairs={{0,2},{1,3},{2,0},{3,1},{4,6},{5,7},{6,4},{7,5},{8,10},{9,11},{10,... | collective-permute-start | bytes 503816 | tf_op jit(solution)/shard_map/ppermute | solution.py:512
  14.8 14.6 %collective-permute-start.4 = (s16[16,5248]{1,0:T(8,128)(2,1)S(1)}, s16[16,5248]{1,0:T(8,128)(2,1)S(1)}, u32[]{:S(2)}, u32[]{:S(2)}) collective-permute-start(s16[16,5248]{1,0:T(8,128)(2,1)S(1)} %get-tuple-element.24), channel_id=1, source_target_pairs={{0,3},{1,2},{2,1},{3,0},{4,7},{5,6},{6,5},{7,4},{8,11},{9,10},{10,... | collective-permute-start | bytes 503816 | tf_op jit(solution)/shard_map/ppermute | solution.py:512
  29.7 4.3 %collective-permute-start.6 = (f32[16,1024]{1,0:T(8,128)S(1)}, f32[16,1024]{1,0:T(8,128)S(1)}, u32[]{:S(2)}, u32[]{:S(2)}) collective-permute-start(f32[16,1024]{1,0:T(8,128)S(1)} %rhs.1.own_ref), channel_id=1, source_target_pairs={{1,0},{2,1},{3,2},{4,3},{5,4},{6,5},{7,6},{8,7},{9,8},{10,9},{11,1... | collective-permute-start | bytes 196616 | tf_op jit(solution)/shard_map/ppermute | solution.py:520
  32.0 7.3 %collective-permute-start.5 = (f32[16,1024]{1,0:T(8,128)S(1)}, f32[16,1024]{1,0:T(8,128)S(1)}, u32[]{:S(2)}, u32[]{:S(2)}) collective-permute-start(f32[16,1024]{1,0:T(8,128)S(1)} %rhs.1.own_ref), channel_id=1, source_target_pairs={{0,1},{1,2},{2,3},{3,4},{4,5},{5,6},{6,7},{7,8},{8,9},{9,10},{10,1... | collective-permute-start | bytes 196616 | tf_op jit(solution)/shard_map/ppermute | solution.py:520
  42.1 4.7 %collective-permute-start.9 = (f32[16,1408]{1,0:T(8,128)S(1)}, f32[16,1408]{1,0:T(8,128)S(1)}, u32[]{:S(2)}, u32[]{:S(2)}) collective-permute-start(f32[16,1408]{1,0:T(8,128)S(1)} %get-tuple-element.30.pay_ref), channel_id=1, source_target_pairs={{0,1},{1,0},{2,3},{3,2},{4,5},{5,4},{6,7},{7,6},{8,9},{9,8},{10,11... | collective-permute-start | bytes 270344 | tf_op jit(solution)/shard_map/ppermute | solution.py:512
  42.1 6.0 %collective-permute-start.8 = (f32[16,1408]{1,0:T(8,128)S(1)}, f32[16,1408]{1,0:T(8,128)S(1)}, u32[]{:S(2)}, u32[]{:S(2)}) collective-permute-start(f32[16,1408]{1,0:T(8,128)S(1)} %get-tuple-element.30.pay_ref), channel_id=1, source_target_pairs={{0,2},{1,3},{2,0},{3,1},{4,6},{5,7},{6,4},{7,5},{8,10},{9,11},{10,... | collective-permute-start | bytes 270344 | tf_op jit(solution)/shard_map/ppermute | solution.py:512
  42.1 7.3 %collective-permute-start.7 = (f32[16,1408]{1,0:T(8,128)S(1)}, f32[16,1408]{1,0:T(8,128)S(1)}, u32[]{:S(2)}, u32[]{:S(2)}) collective-permute-start(f32[16,1408]{1,0:T(8,128)S(1)} %get-tuple-element.30.pay_ref), channel_id=1, source_target_pairs={{0,3},{1,2},{2,1},{3,0},{4,7},{5,6},{6,5},{7,4},{8,11},{9,10},{10,... | collective-permute-start | bytes 270344 | tf_op jit(solution)/shard_map/ppermute | solution.py:512
  50.6 1.2 %collective-permute-start.10 = (f32[16,256]{1,0:T(8,128)S(1)}, f32[16,256]{1,0:T(8,128)S(1)}, u32[]{:S(2)}, u32[]{:S(2)}) collective-permute-start(f32[16,256]{1,0:T(8,128)S(1)} %fock.7), channel_id=1, source_target_pairs={{0,4},{4,0},{8,12},{12,8},{16,20},{20,16},{24,28},{28,24},{1,5},{5... | collective-permute-start | bytes 49160 | tf_op jit(solution)/shard_map/ppermute | solution.py:512
  51.8 5.5 %collective-permute-start.13 = (f32[16,256]{1,0:T(8,128)S(1)}, f32[16,256]{1,0:T(8,128)S(1)}, u32[]{:S(2)}, u32[]{:S(2)}) collective-permute-start(f32[16,256]{1,0:T(8,128)S(1)} %add.12), channel_id=1, source_target_pairs={{0,24},{4,28},{8,16},{12,20},{16,8},{20,12},{24,0},{28,4},{1,25},{... | collective-permute-start | bytes 49160 | tf_op jit(solution)/shard_map/ppermute | solution.py:512
  51.8 5.5 %collective-permute-start.12 = (f32[16,256]{1,0:T(8,128)S(1)}, f32[16,256]{1,0:T(8,128)S(1)}, u32[]{:S(2)}, u32[]{:S(2)}) collective-permute-start(f32[16,256]{1,0:T(8,128)S(1)} %add.12), channel_id=1, source_target_pairs={{0,16},{4,20},{8,24},{12,28},{16,0},{20,4},{24,8},{28,12},{1,17},{... | collective-permute-start | bytes 49160 | tf_op jit(solution)/shard_map/ppermute | solution.py:512
  51.9 6.0 %collective-permute-start.11 = (f32[16,256]{1,0:T(8,128)S(1)}, f32[16,256]{1,0:T(8,128)S(1)}, u32[]{:S(2)}, u32[]{:S(2)}) collective-permute-start(f32[16,256]{1,0:T(8,128)S(1)} %add.12), channel_id=1, source_target_pairs={{0,8},{4,12},{8,0},{12,4},{16,24},{20,28},{24,16},{28,20},{1,9},{5... | collective-permute-start | bytes 49160 | tf_op jit(solution)/shard_map/ppermute | solution.py:512

commit v6 on v5

--- a/solution.py
+++ b/solution.py
@@ -283,7 +283,9 @@
     return [jnp.maximum(0.0, 1.0 - t) for t in tiles]
 
 
-def pair_kernel(before_ref, own_ref, after_ref, dir_ref, w_ref, t_ref, unc_ref, geo, mask, *bhs):
+def pair_kernel(
+    lo, hi, before_ref, own_ref, after_ref, dir_ref, w_ref, t_ref, unc_ref, geo, mask, *bhs
+):
     spheres = own_ref.shape[1]
     slots = 2 * REACH
     wide = spheres + 2 * REACH
@@ -310,34 +312,35 @@
     def step(b, carry):
         sums = []
         for u in range(QUAD):
-            e = b * QUAD + u
-            sums.append(pair_build(e, geo, mask, dir_ref, bhs[u]))
-            pair_finish(e, w_ref, t_ref, bhs[u])
+            at = b * QUAD + u
+            sums.append(pair_build(at + lo, geo, mask, dir_ref, bhs[u]))
+            pair_finish(at, w_ref, t_ref, bhs[u])
         tiles = uncover(sums[:2]) + uncover(sums[2:])
         for t, v in enumerate(tiles):
             unc_ref[b, :, 128 * t : 128 * t + 128] = v
         return carry
 
-    lax.fori_loop(0, wide // QUAD, step, 0, unroll=8)
-
-
-def pair_call(before, own, after):
+    lax.fori_loop(0, (hi - lo) // QUAD, step, 0, unroll=(hi - lo) // QUAD)
+
+
+def pair_call(before, own, after, lo, hi):
     spheres = own.shape[1]
     wide = spheres + 2 * REACH
+    count = hi - lo
     w, d = pair_weights()
     return pl.pallas_call(
-        pair_kernel,
+        functools.partial(pair_kernel, lo, hi),
         in_specs=[VMEM] * 5,
         out_specs=[VMEM] * 2,
         scratch_shapes=[pltpu.VMEM((3 * spheres, 128), F32), pltpu.VMEM((wide, 128), F32)]
         + [pltpu.VMEM((400, 2 * NG), BF)] * QUAD,
         out_shape=[
-            jax.ShapeDtypeStruct((wide, 8 * LP, 4 * LP), BF),
-            jax.ShapeDtypeStruct((wide // QUAD, 1, QN), F32),
+            jax.ShapeDtypeStruct((count, 8 * LP, 4 * LP), BF),
+            jax.ShapeDtypeStruct((count // QUAD, 1, QN), F32),
         ],
         compiler_params=PARAMS,
         cost_estimate=pl.CostEstimate(
-            flops=wide * 2 * 400 * 640 * 256, bytes_accessed=wide * 262144, transcendentals=0
+            flops=count * 2 * 400 * 640 * 256, bytes_accessed=count * 262144, transcendentals=0
         ),
         name="pairs",
     )(before, own, after, jnp.asarray(d), jnp.asarray(w))
@@ -382,7 +385,7 @@
     )(*phis, unc, w)
 
 
-def gather_field(t_ref, shift, x, xs, e):
+def gather_field(t_refs, shift, x, xs, e):
     low = lax.broadcasted_iota(jnp.int32, (NDENS, 128), 1) < LP
     parts = []
     for odd in (0, 1):
@@ -392,7 +395,10 @@
         lhs = jnp.concatenate(
             [below[:, lo_at : lo_at + 8 * LP], above[:, up_at : up_at + 8 * LP]], 0
         )
-        r = jnp.dot(lhs, t_ref[e + odd + shift], preferred_element_type=F32)
+        at = e + odd + shift
+        most = t_refs[0].shape[0]
+        t = t_refs[0][at] if at < most else t_refs[1][at - most]
+        r = jnp.dot(lhs, t, preferred_element_type=F32)
         n = NDENS
         a = r[0:n, : 2 * LP] + r[n : 2 * n, : 2 * LP] + r[0:n, 2 * LP :]
         b = r[2 * n : 3 * n, : 2 * LP] + r[3 * n :, : 2 * LP] + r[2 * n : 3 * n, 2 * LP :]
@@ -413,7 +419,8 @@
 
 
 def sweep_kernel(
-    before_ref, own_ref, after_ref, t_ref, sc_ref, unc_ref, m_ref, out_ref, x, xs, z, zs
+    before_ref, own_ref, after_ref, t_ref, rest_ref, sc_ref, unc_ref, m_ref, out_ref,
+    x, xs, z, zs
 ):
     own = own_ref.shape[1]
     spheres = own // LP
@@ -422,11 +429,11 @@
         put_scaled(x, at, right(at) * sc_ref[0:1, :])
     put_shifted(xs, x)
     for e in range(0, spheres + 2 * REACH, 2):
-        new = right((e + spheres - REACH) * LP) + gather_field(t_ref, 0, x, xs, e)
+        new = right((e + spheres - REACH) * LP) + gather_field((t_ref, rest_ref), 0, x, xs, e)
         put_scaled(z, e * LP, new * sc_ref[0:1, :])
     put_shifted(zs, z)
     for e in range(0, spheres, 2):
-        new = own_ref[:, e * LP : e * LP + 128] + gather_field(t_ref, REACH, z, zs, e)
+        new = own_ref[:, e * LP : e * LP + 128] + gather_field((t_ref, rest_ref), REACH, z, zs, e)
         new = new * sc_ref[1:2, :]
         m_ref[e] = new[:, :LM]
         m_ref[e + 1] = pltpu.roll(new, LP, 1)[:, :LM]
@@ -439,12 +446,12 @@
         out_ref[pairs + b : pairs + b + 1, own : own + 256] = part[:, 384:]
 
 
-def sweep_call(before, own, after, t, scales, unc):
+def sweep_call(before, own, after, t, rest, scales, unc):
     lanes = own.shape[1]
     spheres = lanes // LP
     return pl.pallas_call(
         sweep_kernel,
-        in_specs=[VMEM] * 6,
+        in_specs=[VMEM] * 7,
         out_specs=[VMEM] * 2,
         out_shape=[
             jax.ShapeDtypeStruct((spheres, NDENS, LM), F32),
@@ -459,7 +466,7 @@
             transcendentals=0,
         ),
         name="sweeps",
-    )(before, own, after, t, scales, unc)
+    )(before, own, after, t, rest, scales, unc)
 
 
 def fock_kernel(k, pay_ref, y_ref, tile_ref, *rest):
@@ -512,6 +519,11 @@
     return lax.ppermute(x, axis, [(i, i ^ k) for i in range(count)])
 
 
+def shift(x, axis, k):
+    count = lax.axis_size(axis)
+    return lax.ppermute(x, axis, [(i, (i + k) % count) for i in range(count)])
+
+
 def from_beside(x):
     axes = ("sph", "fit")
     count = lax.axis_size("sph") * lax.axis_size("fit")
@@ -535,10 +547,13 @@
     *phis, near_tiles = phi_call(coefs, tiles, width)
     phis, before, after = lax.optimization_barrier((phis, before, after))
     got = [trade(phis[k], "fit", k) for k in range(1, fits)]
-    t, unc = pair_call(before, own, after)
+    wide = spheres + 2 * REACH
+    t, unc = pair_call(before, own, after, 0, wide - REACH)
     rhs = rhs_call([phis[0], *got], unc, w)
     below, above = from_beside(rhs)
-    moments, pay = sweep_call(below, rhs, above, t, scales, unc)
+    late, _ = lax.optimization_barrier((own, rhs))
+    rest, _ = pair_call(before, late, after, wide - REACH, wide)
+    moments, pay = sweep_call(below, rhs, above, t, rest, scales, unc)
     others = [trade(pay, "fit", k) for k in range(1, fits)]
     fock = fock_call(0, pay, wt, near_tiles, width)
     for k in range(1, fits):
@@ -547,7 +562,11 @@
     bit = 2
     while bit < sphs:
         ks = [k for k in (bit, 2 * bit, 3 * bit) if k < sphs]
-        fock = functools.reduce(jnp.add, [trade(fock, "sph", k) for k in ks], fock)
+        if 4 * bit == sphs:
+            parts = [shift(fock, "sph", k) for k in ks]
+        else:
+            parts = [trade(fock, "sph", k) for k in ks]
+        fock = functools.reduce(jnp.add, parts, fock)
         bit *= 4
     return moments, fock
 

time: 58.7 us -> 56.3 us (0.959)
  starting transfers between devices: 20 us -> 17.7 us
  Pallas kernels: 24.5 us -> 25.2 us
  waiting for transfers between devices: 12.6 us -> 11.9 us
    ppermute x10 -> x7, starting transfers between devices: 11.4 us -> 6.98 us  [trade(): return lax.ppermute(x, axis, [(i, i ^ k) for i in range(count)])]
    ppermute x0 -> x3, waiting for transfers between devices: none -> 4.25 us  [shift(): return lax.ppermute(x, axis, [(i, (i + k) % count) for i in range(count)])]
    ppermute x4, waiting for transfers between devices: 9.69 us -> 6.38 us  [from_beside(): return (lax.ppermute(x, axes, up), lax.ppermute(x, axes, down))]
    ppermute x0 -> x3, starting transfers between devices: none -> 2.02 us  [shift(): return lax.ppermute(x, axis, [(i, (i + k) % count) for i in range(count)])]
    ppermute x10 -> x7, waiting for transfers between devices: 2.95 us -> 1.24 us  [trade(): return lax.ppermute(x, axis, [(i, i ^ k) for i in range(count)])]
    pallas_call x2 -> x3, Pallas kernels: 13.9 us -> 14.6 us  [the longest x2 11.8 us: pair_call(): pl.pallas_call(functools.partial(pair_kernel, lo, hi), in_specs=[VMEM] *...]
  transfers between devices with their start and end apart: 14 -> 14, of which waited for: 6 -> 6; matrix products, arithmetic and copies ran while one was open for 0% -> 0% of each run, Pallas kernels for 33% -> 36%
where the time goes in v6:
time: 56.3 us; the launch traced here: 56.2 us
  Pallas kernels  25.2 us (45%)
  starting transfers between devices  17.7 us (31%)
  waiting for transfers between devices  11.9 us (21%)
  between operations  0.75 us (1%)
  other arithmetic  0.62 us (1%)
    pallas_call x2, Pallas kernels, pair_call(): pl.pallas_call(functools.partial(pair_kernel, lo, hi), in_specs=[VMEM] *...  11.8 us
    ppermute x4, starting transfers between devices, from_beside(): return (lax.ppermute(x, axes, up), lax.ppermute(x, axes, down))  8.68 us
    ppermute x7, starting transfers between devices, trade(): return lax.ppermute(x, axis, [(i, i ^ k) for i in range(count)])  6.98 us
    ppermute x4, waiting for transfers between devices, from_beside(): return (lax.ppermute(x, axes, up), lax.ppermute(x, axes, down))  6.38 us
    pallas_call x4, Pallas kernels, fock_call(): pl.pallas_call(functools.partial(fock_kernel, k), in_specs=[VMEM] * (3 +...  5.02 us
    pallas_call x1, Pallas kernels, phi_call(): pl.pallas_call(functools.partial(phi_kernel, width), in_specs=[pl.BlockSp...  4.39 us
    ppermute x3, waiting for transfers between devices, shift(): return lax.ppermute(x, axis, [(i, (i + k) % count) for i in range(count)])  4.25 us
    pallas_call x1, Pallas kernels, sweep_call(): pl.pallas_call(sweep_kernel, in_specs=[VMEM] * 7, out_specs=[VMEM] * 2, o...  2.83 us
  transfers between devices with their start and end apart: 14, of which 6 were waited for; matrix products, arithmetic and copies ran while one was open for 0% of the time, Pallas kernels for 36%

profile of v6, /device:TPU:0, one launch (start us, length us, event | category | flops | bytes accessed | tf_op | source)
XLA Modules:
  0.0 56.2 jit_solution(16201813572037522184)
XLA Ops:
  0.6 0.0 copy-start.3
  0.6 0.0 copy-start.4
  0.7 0.8 %pack.1.own_ref = f32[24,16]{1,0:T(8,128)S(1)} custom-call(f32[3,16]{1,0:T(4,128)} %centre_ref.1, f32[1,16]{1,0:T(1,128)} %bitcast.2, s32[16,16]{1,0:T(8,128)} %nbr_ref.1, s32[1,16]{1,0:T(1,128)} %bitcast.3), custom_call_target="tpu_custom_call" | custom-call | tf_op jit(solution)/shard_map/pack/pallas_call | solution.py:200
  1.5 0.0 copy-start.1
  1.5 6.4 %collective-permute-start.1 = (f32[24,16]{1,0:T(8,128)S(1)}, f32[24,16]{1,0:T(8,128)S(1)}, u32[]{:S(2)}, u32[]{:S(2)}) collective-permute-start(f32[24,16]{1,0:T(8,128)S(1)} %pack.1.own_ref), channel_id=1, source_target_pairs={{1,0},{2,1},{3,2},{4,3},{5,4},{6,5},{7,6},{8,7},{9,8},{10,9},{11,1... | collective-permute-start | bytes 4616 | tf_op jit(solution)/shard_map/ppermute | solution.py:532
  7.9 0.0 collective-permute-start
  7.9 4.4 %phi.1 = (f32[16,5120]{1,0:T(8,128)S(1)}, s16[16,5248]{1,0:T(8,128)(2,1)S(1)}, s16[16,5248]{1,0:T(8,128)(2,1)S(1)}, s16[16,5248]{1,0:T(8,128)(2,1)S(1)}, bf16[256,20480]{1,0:T(8,128)(2,1)S(1)}) custom-call(bf16[16,256]{1,0:T(8,128)(2,1)} %far_coef_ref.1, bf16[256,20480]{1,0:T(8,128)(2,1)} %far_ref.1), custom_call_target="tpu_custom_call" | custom-call | flops 167772160 | bytes 11796480 | tf_op jit(solution)/shard_map/phi/pallas_call | solution.py:157
  12.3 0.0 copy-start.2
  12.3 2.4 %collective-permute-done.before_ref = f32[24,16]{1,0:T(8,128)S(1)} collective-permute-done((f32[24,16]{1,0:T(8,128)S(1)}, f32[24,16]{1,0:T(8,128)S(1)}, u32[]{:S(2)}, u32[]{:S(2)}) %collective-permute-start) | collective-permute-done | bytes 1568 | tf_op jit(solution)/shard_map/ppermute | solution.py:532
  14.8 0.0 collective-permute-start.2
  14.8 0.0 collective-permute-start.3
  14.8 3.5 %collective-permute-start.4 = (s16[16,5248]{1,0:T(8,128)(2,1)S(1)}, s16[16,5248]{1,0:T(8,128)(2,1)S(1)}, u32[]{:S(2)}, u32[]{:S(2)}) collective-permute-start(s16[16,5248]{1,0:T(8,128)(2,1)S(1)} %get-tuple-element.26), channel_id=1, source_target_pairs={{0,3},{1,2},{2,1},{3,0},{4,7},{5,6},{6,5},{7,4},{8,11},{9,10},{10,... | collective-permute-start | bytes 503816 | tf_op jit(solution)/shard_map/ppermute | solution.py:519
  18.2 8.4 %pairs.2 = (bf16[24,512,256]{2,1,0:T(8,128)(2,1)S(1)}, f32[6,1,1280]{2,1,0:T(1,128)S(1)}) custom-call(f32[24,16]{1,0:T(8,128)S(1)} %collective-permute-done.before_ref, f32[24,16]{1,0:T(8,128)S(1)} %pack.1.own_ref, f32[24,16]{1,0:T(8,128)S(1)} %collective-permute-done.1.after_ref, f32[8,640]{1,0:T(8,128)S(1)} %copy-done.4, bf16[640,256]{1,0:T(8,128)(2,1)S(1)} %copy-done.3), custom_call_target="tpu_custom_call" | custom-call | flops 3145728000 | bytes 6291456 | tf_op jit(solution)/shard_map/pairs/pallas_call | solution.py:331
  26.6 0.0 collective-permute-done.3.refs_2_
  26.7 0.4 rhs.1.own_ref
  27.1 2.2 %collective-permute-start.6 = (f32[16,1024]{1,0:T(8,128)S(1)}, f32[16,1024]{1,0:T(8,128)S(1)}, u32[]{:S(2)}, u32[]{:S(2)}) collective-permute-start(f32[16,1024]{1,0:T(8,128)S(1)} %rhs.1.own_ref), channel_id=1, source_target_pairs={{1,0},{2,1},{3,2},{4,3},{5,4},{6,5},{7,6},{8,7},{9,8},{10,9},{11,1... | collective-permute-start | bytes 196616 | tf_op jit(solution)/shard_map/ppermute | solution.py:532
  29.3 0.0 collective-permute-start.5
  29.3 3.4 %pairs.3 = (bf16[8,512,256]{2,1,0:T(8,128)(2,1)S(1)}, f32[2,1,1280]{2,1,0:T(1,128)}) custom-call(f32[24,16]{1,0:T(8,128)S(1)} %collective-permute-done.before_ref, f32[24,16]{1,0:T(8,128)S(1)} %pack.1.own_ref, f32[24,16]{1,0:T(8,128)S(1)} %collective-permute-done.1.after_ref, f32[8,640]{1,0:T(8,128)S(1)} %copy-done.4, bf16[640,256]{1,0:T(8,128)(2,1)S(1)} %copy-done.3), custom_call_target="tpu_custom_call" | custom-call | flops 1048576000 | bytes 2097152 | tf_op jit(solution)/shard_map/pairs/pallas_call | solution.py:331
  32.7 4.0 %collective-permute-done.5.before_ref = f32[16,1024]{1,0:T(8,128)S(1)} collective-permute-done((f32[16,1024]{1,0:T(8,128)S(1)}, f32[16,1024]{1,0:T(8,128)S(1)}, u32[]{:S(2)}, u32[]{:S(2)}) %collective-permute-start.5) | collective-permute-done | bytes 65568 | tf_op jit(solution)/shard_map/ppermute | solution.py:532
  36.7 2.8 %sweeps.1 = (f32[16,16,49]{2,1,0:T(8,128)}, f32[16,1408]{1,0:T(8,128)S(1)}) custom-call(f32[16,1024]{1,0:T(8,128)S(1)} %collective-permute-done.5.before_ref, f32[16,1024]{1,0:T(8,128)S(1)} %rhs.1.own_ref, f32[16,1024]{1,0:T(8,128)S(1)} %collective-permute-done.6.after_ref, bf16[24,512,256]{2,1,0:T(8,128)(2,1)S(1)} %get-tuple-element.30.t_ref, ...), custom_call_target="tpu_custom_call" | custom-call | flops 805306368 | bytes 8388608 | tf_op jit(solution)/shard_map/sweeps/pallas_call | solution.py:452
  39.5 3.5 %collective-permute-start.7 = (f32[16,1408]{1,0:T(8,128)S(1)}, f32[16,1408]{1,0:T(8,128)S(1)}, u32[]{:S(2)}, u32[]{:S(2)}) collective-permute-start(f32[16,1408]{1,0:T(8,128)S(1)} %get-tuple-element.34.pay_ref), channel_id=1, source_target_pairs={{0,3},{1,2},{2,1},{3,0},{4,7},{5,6},{6,5},{7,4},{8,11},{9,10},{10,... | collective-permute-start | bytes 270344 | tf_op jit(solution)/shard_map/ppermute | solution.py:519
  43.0 1.2 %fock.4.rest_0_ = f32[16,256]{1,0:T(8,128)S(1)} custom-call(f32[16,1408]{1,0:T(8,128)S(1)} %get-tuple-element.34.pay_ref, bf16[128,1280]{1,0:T(8,128)(2,1)S(1)} %copy-done, bf16[256,20480]{1,0:T(8,128)(2,1)S(1)} %get-tuple-element.35.tile_ref), custom_call_target="tpu_custom_call" | custom-call | flops 41943040 | bytes 2621440 | tf_op jit(solution)/shard_map/fock/pallas_call | solution.py:503
  44.3 1.3 %fock.5.rest_0_ = f32[16,256]{1,0:T(8,128)S(1)} custom-call(f32[16,1408]{1,0:T(8,128)S(1)} %collective-permute-done.9.pay_ref, bf16[128,1280]{1,0:T(8,128)(2,1)S(1)} %copy-done, bf16[256,20480]{1,0:T(8,128)(2,1)S(1)} %get-tuple-element.35.tile_ref, f32[16,256]{1,0:T(8,128)S(1)} %fock.4.rest_0_), custom_call_target="tpu_custom_call" | custom-call | flops 41943040 | bytes 2621440 | tf_op jit(solution)/shard_map/fock/pallas_call | solution.py:503
  45.5 1.3 %fock.6.rest_0_ = f32[16,256]{1,0:T(8,128)S(1)} custom-call(f32[16,1408]{1,0:T(8,128)S(1)} %collective-permute-done.8.pay_ref, bf16[128,1280]{1,0:T(8,128)(2,1)S(1)} %copy-done, bf16[256,20480]{1,0:T(8,128)(2,1)S(1)} %get-tuple-element.35.tile_ref, f32[16,256]{1,0:T(8,128)S(1)} %fock.5.rest_0_), custom_call_target="tpu_custom_call" | custom-call | flops 41943040 | bytes 2621440 | tf_op jit(solution)/shard_map/fock/pallas_call | solution.py:503
  46.8 1.3 %fock.7 = f32[16,256]{1,0:T(8,128)S(1)} custom-call(f32[16,1408]{1,0:T(8,128)S(1)} %collective-permute-done.7.pay_ref, bf16[128,1280]{1,0:T(8,128)(2,1)S(1)} %copy-done, bf16[256,20480]{1,0:T(8,128)(2,1)S(1)} %get-tuple-element.35.tile_ref, f32[16,256]{1,0:T(8,128)S(1)} %fock.6.rest_0_), custom_call_target="tpu_custom_call" | custom-call | flops 41943040 | bytes 2621440 | tf_op jit(solution)/shard_map/fock/pallas_call | solution.py:503
  48.0 1.2 %collective-permute-done.10 = f32[16,256]{1,0:T(8,128)S(1)} collective-permute-done((f32[16,256]{1,0:T(8,128)S(1)}, f32[16,256]{1,0:T(8,128)S(1)}, u32[]{:S(2)}, u32[]{:S(2)}) %collective-permute-start.10) | collective-permute-done | bytes 16416 | tf_op jit(solution)/shard_map/ppermute | solution.py:519
  49.3 0.1 collective-permute-start.12
  49.3 1.9 %collective-permute-start.11 = (f32[16,256]{1,0:T(8,128)S(1)}, f32[16,256]{1,0:T(8,128)S(1)}, u32[]{:S(2)}, u32[]{:S(2)}) collective-permute-start(f32[16,256]{1,0:T(8,128)S(1)} %add.12), channel_id=1, source_target_pairs={{0,8},{4,12},{8,16},{12,20},{16,24},{20,28},{24,0},{28,4},{1,9},{5... | collective-permute-start | bytes 49160 | tf_op jit(solution)/shard_map/ppermute | solution.py:524
  51.3 1.7 %collective-permute-done.13 = f32[16,256]{1,0:T(8,128)S(1)} collective-permute-done((f32[16,256]{1,0:T(8,128)S(1)}, f32[16,256]{1,0:T(8,128)S(1)}, u32[]{:S(2)}, u32[]{:S(2)}) %collective-permute-start.13) | collective-permute-done | bytes 16416 | tf_op jit(solution)/shard_map/ppermute | solution.py:524
  53.0 1.0 %collective-permute-done.12 = f32[16,256]{1,0:T(8,128)S(1)} collective-permute-done((f32[16,256]{1,0:T(8,128)S(1)}, f32[16,256]{1,0:T(8,128)S(1)}, u32[]{:S(2)}, u32[]{:S(2)}) %collective-permute-start.12) | collective-permute-done | bytes 16416 | tf_op jit(solution)/shard_map/ppermute | solution.py:524
  54.0 1.6 %collective-permute-done.11 = f32[16,256]{1,0:T(8,128)S(1)} collective-permute-done((f32[16,256]{1,0:T(8,128)S(1)}, f32[16,256]{1,0:T(8,128)S(1)}, u32[]{:S(2)}, u32[]{:S(2)}) %collective-permute-start.11) | collective-permute-done | bytes 16416 | tf_op jit(solution)/shard_map/ppermute | solution.py:524
  55.5 0.6 %add_add_fusion = f32[16,256]{1,0:T(8,128)} fusion(f32[16,256]{1,0:T(8,128)S(1)} %collective-permute-done.13, f32[16,256]{1,0:T(8,128)S(1)} %collective-permute-done.12, f32[16,256]{1,0:T(8,128)S(1)} %add.12, f32[16,256]{1,0:T(8,128)S(1)} %collective-permute-done.11), kind=kLoop, calls=%fused_computation | loop fusion | flops 12288 | bytes 81920 | tf_op jit(solution)/shard_map/add | solution.py:569
  (18 shorter events, 0.0 us)
Async XLA Ops:
  0.6 17.6 %copy-start.3 = (bf16[640,256]{1,0:T(8,128)(2,1)S(1)}, bf16[640,256]{1,0:T(8,128)(2,1)}, u32[]{:S(2)}) copy-start(bf16[640,256]{1,0:T(8,128)(2,1)} %constant.14.clone.w_ref) | copy-start | bytes 983044
  0.6 17.6 %copy-start.4 = (f32[8,640]{1,0:T(8,128)S(1)}, f32[8,640]{1,0:T(8,128)}, u32[]{:S(2)}) copy-start(f32[8,640]{1,0:T(8,128)} %constant.13.clone.dir_ref) | copy-start | bytes 61444
  1.5 25.2 %copy-start.1 = (bf16[640,256]{1,0:T(8,128)(2,1)S(1)}, bf16[640,256]{1,0:T(8,128)(2,1)}, u32[]{:S(2)}) copy-start(bf16[640,256]{1,0:T(8,128)(2,1)} %constant.10.clone.refs_5_) | copy-start | bytes 983044
  1.5 10.8 %collective-permute-start.1 = (f32[24,16]{1,0:T(8,128)S(1)}, f32[24,16]{1,0:T(8,128)S(1)}, u32[]{:S(2)}, u32[]{:S(2)}) collective-permute-start(f32[24,16]{1,0:T(8,128)S(1)} %pack.1.own_ref), channel_id=1, source_target_pairs={{1,0},{2,1},{3,2},{4,3},{5,4},{6,5},{7,6},{8,7},{9,8},{10,9},{11,1... | collective-permute-start | bytes 4616 | tf_op jit(solution)/shard_map/ppermute | solution.py:532
  7.9 6.8 %collective-permute-start = (f32[24,16]{1,0:T(8,128)S(1)}, f32[24,16]{1,0:T(8,128)S(1)}, u32[]{:S(2)}, u32[]{:S(2)}) collective-permute-start(f32[24,16]{1,0:T(8,128)S(1)} %pack.1.own_ref), channel_id=1, source_target_pairs={{0,1},{1,2},{2,3},{3,4},{4,5},{5,6},{6,7},{7,8},{8,9},{9,10},{10,1... | collective-permute-start | bytes 4616 | tf_op jit(solution)/shard_map/ppermute | solution.py:532
  12.3 24.4 %copy-start.2 = (f32[8,128]{1,0:T(8,128)S(1)}, f32[8,128]{1,0:T(8,128)}, u32[]{:S(2)}) copy-start(f32[8,128]{1,0:T(8,128)} %constant.12.clone.sc_ref) | copy-start | bytes 12292
  14.8 28.3 %copy-start = (bf16[128,1280]{1,0:T(8,128)(2,1)S(1)}, bf16[128,1280]{1,0:T(8,128)(2,1)}, u32[]{:S(2)}) copy-start(bf16[128,1280]{1,0:T(8,128)(2,1)} %constant.11.clone.y_ref) | copy-start | bytes 983044
  14.8 11.9 %collective-permute-start.2 = (s16[16,5248]{1,0:T(8,128)(2,1)S(1)}, s16[16,5248]{1,0:T(8,128)(2,1)S(1)}, u32[]{:S(2)}, u32[]{:S(2)}) collective-permute-start(s16[16,5248]{1,0:T(8,128)(2,1)S(1)} %get-tuple-element.24), channel_id=1, source_target_pairs={{0,1},{1,0},{2,3},{3,2},{4,5},{5,4},{6,7},{7,6},{8,9},{9,8},{10,11... | collective-permute-start | bytes 503816 | tf_op jit(solution)/shard_map/ppermute | solution.py:519
  14.8 11.9 %collective-permute-start.3 = (s16[16,5248]{1,0:T(8,128)(2,1)S(1)}, s16[16,5248]{1,0:T(8,128)(2,1)S(1)}, u32[]{:S(2)}, u32[]{:S(2)}) collective-permute-start(s16[16,5248]{1,0:T(8,128)(2,1)S(1)} %get-tuple-element.25), channel_id=1, source_target_pairs={{0,2},{1,3},{2,0},{3,1},{4,6},{5,7},{6,4},{7,5},{8,10},{9,11},{10,... | collective-permute-start | bytes 503816 | tf_op jit(solution)/shard_map/ppermute | solution.py:519
  14.8 11.9 %collective-permute-start.4 = (s16[16,5248]{1,0:T(8,128)(2,1)S(1)}, s16[16,5248]{1,0:T(8,128)(2,1)S(1)}, u32[]{:S(2)}, u32[]{:S(2)}) collective-permute-start(s16[16,5248]{1,0:T(8,128)(2,1)S(1)} %get-tuple-element.26), channel_id=1, source_target_pairs={{0,3},{1,2},{2,1},{3,0},{4,7},{5,6},{6,5},{7,4},{8,11},{9,10},{10,... | collective-permute-start | bytes 503816 | tf_op jit(solution)/shard_map/ppermute | solution.py:519
  27.1 5.7 %collective-permute-start.6 = (f32[16,1024]{1,0:T(8,128)S(1)}, f32[16,1024]{1,0:T(8,128)S(1)}, u32[]{:S(2)}, u32[]{:S(2)}) collective-permute-start(f32[16,1024]{1,0:T(8,128)S(1)} %rhs.1.own_ref), channel_id=1, source_target_pairs={{1,0},{2,1},{3,2},{4,3},{5,4},{6,5},{7,6},{8,7},{9,8},{10,9},{11,1... | collective-permute-start | bytes 196616 | tf_op jit(solution)/shard_map/ppermute | solution.py:532
  29.3 7.4 %collective-permute-start.5 = (f32[16,1024]{1,0:T(8,128)S(1)}, f32[16,1024]{1,0:T(8,128)S(1)}, u32[]{:S(2)}, u32[]{:S(2)}) collective-permute-start(f32[16,1024]{1,0:T(8,128)S(1)} %rhs.1.own_ref), channel_id=1, source_target_pairs={{0,1},{1,2},{2,3},{3,4},{4,5},{5,6},{6,7},{7,8},{8,9},{9,10},{10,1... | collective-permute-start | bytes 196616 | tf_op jit(solution)/shard_map/ppermute | solution.py:532
  39.5 4.7 %collective-permute-start.9 = (f32[16,1408]{1,0:T(8,128)S(1)}, f32[16,1408]{1,0:T(8,128)S(1)}, u32[]{:S(2)}, u32[]{:S(2)}) collective-permute-start(f32[16,1408]{1,0:T(8,128)S(1)} %get-tuple-element.34.pay_ref), channel_id=1, source_target_pairs={{0,1},{1,0},{2,3},{3,2},{4,5},{5,4},{6,7},{7,6},{8,9},{9,8},{10,11... | collective-permute-start | bytes 270344 | tf_op jit(solution)/shard_map/ppermute | solution.py:519
  39.5 6.0 %collective-permute-start.8 = (f32[16,1408]{1,0:T(8,128)S(1)}, f32[16,1408]{1,0:T(8,128)S(1)}, u32[]{:S(2)}, u32[]{:S(2)}) collective-permute-start(f32[16,1408]{1,0:T(8,128)S(1)} %get-tuple-element.34.pay_ref), channel_id=1, source_target_pairs={{0,2},{1,3},{2,0},{3,1},{4,6},{5,7},{6,4},{7,5},{8,10},{9,11},{10,... | collective-permute-start | bytes 270344 | tf_op jit(solution)/shard_map/ppermute | solution.py:519
  39.5 7.3 %collective-permute-start.7 = (f32[16,1408]{1,0:T(8,128)S(1)}, f32[16,1408]{1,0:T(8,128)S(1)}, u32[]{:S(2)}, u32[]{:S(2)}) collective-permute-start(f32[16,1408]{1,0:T(8,128)S(1)} %get-tuple-element.34.pay_ref), channel_id=1, source_target_pairs={{0,3},{1,2},{2,1},{3,0},{4,7},{5,6},{6,5},{7,4},{8,11},{9,10},{10,... | collective-permute-start | bytes 270344 | tf_op jit(solution)/shard_map/ppermute | solution.py:519
  48.0 1.2 %collective-permute-start.10 = (f32[16,256]{1,0:T(8,128)S(1)}, f32[16,256]{1,0:T(8,128)S(1)}, u32[]{:S(2)}, u32[]{:S(2)}) collective-permute-start(f32[16,256]{1,0:T(8,128)S(1)} %fock.7), channel_id=1, source_target_pairs={{0,4},{4,0},{8,12},{12,8},{16,20},{20,16},{24,28},{28,24},{1,5},{5... | collective-permute-start | bytes 49160 | tf_op jit(solution)/shard_map/ppermute | solution.py:519
  49.3 3.8 %collective-permute-start.13 = (f32[16,256]{1,0:T(8,128)S(1)}, f32[16,256]{1,0:T(8,128)S(1)}, u32[]{:S(2)}, u32[]{:S(2)}) collective-permute-start(f32[16,256]{1,0:T(8,128)S(1)} %add.12), channel_id=1, source_target_pairs={{0,24},{4,28},{8,0},{12,4},{16,8},{20,12},{24,16},{28,20},{1,25},{... | collective-permute-start | bytes 49160 | tf_op jit(solution)/shard_map/ppermute | solution.py:524
  49.3 4.7 %collective-permute-start.12 = (f32[16,256]{1,0:T(8,128)S(1)}, f32[16,256]{1,0:T(8,128)S(1)}, u32[]{:S(2)}, u32[]{:S(2)}) collective-permute-start(f32[16,256]{1,0:T(8,128)S(1)} %add.12), channel_id=1, source_target_pairs={{0,16},{4,20},{8,24},{12,28},{16,0},{20,4},{24,8},{28,12},{1,17},{... | collective-permute-start | bytes 49160 | tf_op jit(solution)/shard_map/ppermute | solution.py:524
  49.3 6.2 %collective-permute-start.11 = (f32[16,256]{1,0:T(8,128)S(1)}, f32[16,256]{1,0:T(8,128)S(1)}, u32[]{:S(2)}, u32[]{:S(2)}) collective-permute-start(f32[16,256]{1,0:T(8,128)S(1)} %add.12), channel_id=1, source_target_pairs={{0,8},{4,12},{8,16},{12,20},{16,24},{20,28},{24,0},{28,4},{1,9},{5... | collective-permute-start | bytes 49160 | tf_op jit(solution)/shard_map/ppermute | solution.py:524

commit v7 on v6

--- a/solution.py
+++ b/solution.py
@@ -26,6 +26,7 @@
 SMEM = pl.BlockSpec(memory_space=pltpu.SMEM)
 BAND = 0.1
 REACH = 8
+SOONER = 1
 BF = jnp.bfloat16
 F32 = jnp.float32
 
@@ -96,7 +97,9 @@
     w = np.zeros((PN, 2 * LP))
     w[:NG, :LM] = ys.T
     w[NG:, LP : LP + LM] = ys.T
-    return np.concatenate(split(w), 1), np.concatenate(split(w.T), 1)
+    hi, lo = split(w.T)
+    deep = np.block([[hi, lo], [hi, np.zeros_like(lo)]])
+    return np.concatenate(split(w), 1), deep
 
 
 def lane_scales():
@@ -127,50 +130,54 @@
     return ref[:, ls].astype(jnp.int32).astype(F32) * jnp.exp2(power)
 
 
-def phi_kernel(width, far_coef_ref, far_ref, *rest):
-    outs, (tile_ref, full, coef_ref, sem, coef_sem) = rest[:-5], rest[-5:]
+def fetch(far_ref, tile_ref, sem, k, width):
+    copies = []
+    for p in range(width // PIECE):
+        to = tile_ref.at[:, p * PIECE : (p + 1) * PIECE]
+        copies.append(pltpu.make_async_copy(far_ref.at[:, chunk_piece(k, width, p)], to, sem.at[p]))
+        copies[-1].start()
+    return copies
+
+
+def potentials(copies, coef_ref, tile_ref, out):
+    for p, copy in enumerate(copies):
+        copy.wait()
+        ls = slice(p * PIECE, (p + 1) * PIECE)
+        out[:, ls] = jnp.dot(coef_ref[...], tile_ref[:, ls], preferred_element_type=F32)
+
+
+def phi_kernel(peers, width, far_coef_ref, far_ref, *rest):
+    outs, tiles, (full, coef_ref, sem, coef_sem) = rest[:peers], rest[peers : 2 * peers], rest[-4:]
     first = pltpu.make_async_copy(far_coef_ref, coef_ref, coef_sem)
     first.start()
-    per = width // PIECE
-    todo = [(k, p) for k in [*range(1, len(outs)), 0] for p in range(per)]
-    copies = []
-    for i, (k, p) in enumerate(todo):
-        at = chunk_piece(k, width, p)
-        copies.append(pltpu.make_async_copy(far_ref.at[:, at], tile_ref.at[:, at], sem.at[i]))
-        copies[-1].start()
+    copies = [fetch(far_ref, t, sem.at[i], i + 1, width) for i, t in enumerate(tiles)]
     first.wait()
-    for (k, p), copy in zip(todo, copies):
-        copy.wait()
-        out = full if k else outs[0]
-        out[:, p * PIECE : (p + 1) * PIECE] = jnp.dot(
-            coef_ref[...], tile_ref[:, chunk_piece(k, width, p)], preferred_element_type=F32
-        )
-        if k and p == per - 1:
-            q, tail = code(full[...])
-            outs[k][:, :width] = q
-            outs[k][:, width:] = tail
+    for i in range(peers):
+        potentials(copies[i], coef_ref, tiles[i], full)
+        q, tail = code(full[...])
+        outs[i][:, :width] = q
+        outs[i][:, width:] = tail
 
 
 def phi_call(coefs, tiles, width):
     aux, points = tiles.shape
-    count = points // width
+    peers = points // width - 1
     return pl.pallas_call(
-        functools.partial(phi_kernel, width),
+        functools.partial(phi_kernel, peers, width),
         in_specs=[pl.BlockSpec(memory_space=pltpu.HBM)] * 2,
-        out_specs=[VMEM] * (count + 1),
-        out_shape=[jax.ShapeDtypeStruct((NDENS, width), F32)]
-        + [jax.ShapeDtypeStruct((NDENS, width + 128), jnp.int16)] * (count - 1)
-        + [jax.ShapeDtypeStruct(tiles.shape, tiles.dtype)],
+        out_specs=[VMEM] * (2 * peers),
+        out_shape=[jax.ShapeDtypeStruct((NDENS, width + 128), jnp.int16)] * peers
+        + [jax.ShapeDtypeStruct((aux, width), tiles.dtype)] * peers,
         scratch_shapes=[
             pltpu.VMEM((NDENS, width), F32),
             pltpu.VMEM(coefs.shape, coefs.dtype),
-            pltpu.SemaphoreType.DMA((points // PIECE,)),
+            pltpu.SemaphoreType.DMA((peers, width // PIECE)),
             pltpu.SemaphoreType.DMA,
         ],
         compiler_params=PARAMS,
         cost_estimate=pl.CostEstimate(
-            flops=2 * NDENS * aux * points,
-            bytes_accessed=(2 * aux + 4 * NDENS) * points,
+            flops=2 * NDENS * aux * width * peers,
+            bytes_accessed=(2 * aux + 4 * NDENS) * width * peers,
             transcendentals=0,
         ),
         name="phi",
@@ -283,9 +290,12 @@
     return [jnp.maximum(0.0, 1.0 - t) for t in tiles]
 
 
-def pair_kernel(
-    lo, hi, before_ref, own_ref, after_ref, dir_ref, w_ref, t_ref, unc_ref, geo, mask, *bhs
-):
+def pair_kernel(quads, extra, before_ref, own_ref, after_ref, dir_ref, w_ref, *rest):
+    if extra:
+        coef_ref, far_ref, t_ref, unc_ref, phi_ref, tile_ref, geo, mask, sem, *bhs = rest
+        copies = fetch(far_ref, tile_ref, sem, 0, tile_ref.shape[1])
+    else:
+        t_ref, unc_ref, geo, mask, *bhs = rest
     spheres = own_ref.shape[1]
     slots = 2 * REACH
     wide = spheres + 2 * REACH
@@ -309,45 +319,58 @@
         found = jnp.where(lane == c, hit, found)
     mask[...] = found
 
-    def step(b, carry):
+    for b, quad in enumerate(quads):
         sums = []
         for u in range(QUAD):
-            at = b * QUAD + u
-            sums.append(pair_build(at + lo, geo, mask, dir_ref, bhs[u]))
-            pair_finish(at, w_ref, t_ref, bhs[u])
+            sums.append(pair_build(quad * QUAD + u, geo, mask, dir_ref, bhs[u]))
+            pair_finish(b * QUAD + u, w_ref, t_ref, bhs[u])
         tiles = uncover(sums[:2]) + uncover(sums[2:])
         for t, v in enumerate(tiles):
             unc_ref[b, :, 128 * t : 128 * t + 128] = v
-        return carry
-
-    lax.fori_loop(0, (hi - lo) // QUAD, step, 0, unroll=(hi - lo) // QUAD)
-
-
-def pair_call(before, own, after, lo, hi):
+    if extra:
+        potentials(copies, coef_ref, tile_ref, phi_ref)
+
+
+def pair_call(before, own, after, quads, coefs=None, tiles=None):
     spheres = own.shape[1]
     wide = spheres + 2 * REACH
-    count = hi - lo
+    count = len(quads)
+    width = spheres * NG
     w, d = pair_weights()
+    extra = tiles is not None
+    in_specs = [VMEM] * 5
+    out_shape = [
+        jax.ShapeDtypeStruct((count * QUAD, 8 * LP, 4 * LP), BF),
+        jax.ShapeDtypeStruct((count, 1, QN), F32),
+    ]
+    scratch = [pltpu.VMEM((3 * spheres, 128), F32), pltpu.VMEM((wide, 128), F32)]
+    more = ()
+    if extra:
+        in_specs = in_specs + [VMEM, pl.BlockSpec(memory_space=pltpu.HBM)]
+        out_shape = out_shape + [
+            jax.ShapeDtypeStruct((NDENS, width), F32),
+            jax.ShapeDtypeStruct((tiles.shape[0], width), tiles.dtype),
+        ]
+        scratch = scratch + [pltpu.SemaphoreType.DMA((width // PIECE,))]
+        more = (coefs, pltpu.with_memory_space_constraint(tiles, pltpu.HBM))
     return pl.pallas_call(
-        functools.partial(pair_kernel, lo, hi),
-        in_specs=[VMEM] * 5,
-        out_specs=[VMEM] * 2,
-        scratch_shapes=[pltpu.VMEM((3 * spheres, 128), F32), pltpu.VMEM((wide, 128), F32)]
-        + [pltpu.VMEM((400, 2 * NG), BF)] * QUAD,
-        out_shape=[
-            jax.ShapeDtypeStruct((count, 8 * LP, 4 * LP), BF),
-            jax.ShapeDtypeStruct((count // QUAD, 1, QN), F32),
-        ],
+        functools.partial(pair_kernel, quads, extra),
+        in_specs=in_specs,
+        out_specs=[VMEM] * len(out_shape),
+        scratch_shapes=scratch + [pltpu.VMEM((400, 2 * NG), BF)] * QUAD,
+        out_shape=out_shape,
         compiler_params=PARAMS,
         cost_estimate=pl.CostEstimate(
-            flops=count * 2 * 400 * 640 * 256, bytes_accessed=count * 262144, transcendentals=0
+            flops=count * QUAD * 2 * 400 * 640 * 256,
+            bytes_accessed=count * QUAD * 262144,
+            transcendentals=0,
         ),
         name="pairs",
-    )(before, own, after, jnp.asarray(d), jnp.asarray(w))
+    )(before, own, after, jnp.asarray(d), jnp.asarray(w), *more)
 
 
 def own_uncovered(unc_ref, b):
-    b = b + REACH // 2
+    b = b + SOONER * QUAD // 2
     return unc_ref[b // 2, :, b % 2 * PN : (b % 2 + 1) * PN]
 
 
@@ -395,9 +418,13 @@
         lhs = jnp.concatenate(
             [below[:, lo_at : lo_at + 8 * LP], above[:, up_at : up_at + 8 * LP]], 0
         )
-        at = e + odd + shift
+        at = e + odd + shift - (REACH - SOONER * QUAD)
         most = t_refs[0].shape[0]
-        t = t_refs[0][at] if at < most else t_refs[1][at - most]
+        if 0 <= at < most:
+            t = t_refs[0][at]
+        else:
+            lowest = REACH - SOONER * QUAD
+            t = t_refs[1][at - most + lowest if at > 0 else at + lowest]
         r = jnp.dot(lhs, t, preferred_element_type=F32)
         n = NDENS
         a = r[0:n, : 2 * LP] + r[n : 2 * n, : 2 * LP] + r[0:n, 2 * LP :]
@@ -469,16 +496,15 @@
     )(before, own, after, t, rest, scales, unc)
 
 
-def fock_kernel(k, pay_ref, y_ref, tile_ref, *rest):
+def fock_kernel(pay_ref, y_ref, tile_ref, *rest):
     out_ref, charge = rest[-2:]
     own = pay_ref.shape[1] - 384
     pairs = own // (2 * LP)
     width = pairs * PN
     rows = [pay_ref[:, b * 2 * LP : (b + 1) * 2 * LP] for b in range(pairs)]
     hi, lo = halves(jnp.concatenate(rows, 0))
-    n = pairs * NDENS
-    r = jnp.dot(jnp.concatenate([hi, lo], 0), y_ref[...], preferred_element_type=F32)
-    out = r[:n, :PN] + r[:n, PN:] + r[n:, :PN]
+    r = jnp.dot(jnp.concatenate([hi, lo], 1), y_ref[...], preferred_element_type=F32)
+    out = r[:, :PN] + r[:, PN:]
     for b in range(pairs):
         unc = jnp.concatenate(
             [pay_ref[b : b + 1, own:], pay_ref[pairs + b : pairs + b + 1, own : own + 256]], 1
@@ -489,7 +515,7 @@
     for p in range(width // PIECE):
         part = lax.dot_general(
             charge[:, p * PIECE : (p + 1) * PIECE],
-            tile_ref[:, chunk_piece(k, width, p)],
+            tile_ref[:, p * PIECE : (p + 1) * PIECE],
             (((1,), (1,)), ((), ())),
             preferred_element_type=F32,
         )
@@ -497,11 +523,11 @@
     out_ref[...] = total
 
 
-def fock_call(k, pay, wt, tiles, width, before=None):
-    aux = tiles.shape[0]
+def fock_call(pay, wt, tiles, before=None):
+    aux, width = tiles.shape
     more = [] if before is None else [before]
     return pl.pallas_call(
-        functools.partial(fock_kernel, k),
+        fock_kernel,
         in_specs=[VMEM] * (3 + len(more)),
         out_specs=VMEM,
         out_shape=jax.ShapeDtypeStruct((NDENS, aux), F32),
@@ -544,20 +570,23 @@
     width = spheres * NG
     own = pack_call(centres, radii, neighbours, counts)
     before, after = from_beside(own)
-    *phis, near_tiles = phi_call(coefs, tiles, width)
-    phis, before, after = lax.optimization_barrier((phis, before, after))
-    got = [trade(phis[k], "fit", k) for k in range(1, fits)]
-    wide = spheres + 2 * REACH
-    t, unc = pair_call(before, own, after, 0, wide - REACH)
-    rhs = rhs_call([phis[0], *got], unc, w)
+    sent = phi_call(coefs, tiles, width)
+    sent, near_tiles = sent[: fits - 1], sent[fits - 1 :]
+    sent, before, after = lax.optimization_barrier((sent, before, after))
+    got = [trade(sent[k - 1], "fit", k) for k in range(1, fits)]
+    below_own, last_own = REACH // QUAD, (REACH + spheres) // QUAD
+    soon = range(below_own - SOONER, last_own)
+    later = [*range(below_own - SOONER), *range(last_own, last_own + below_own)]
+    t, unc, mine, tile = pair_call(before, own, after, list(soon), coefs, tiles)
+    rhs = rhs_call([mine, *got], unc, w)
     below, above = from_beside(rhs)
     late, _ = lax.optimization_barrier((own, rhs))
-    rest, _ = pair_call(before, late, after, wide - REACH, wide)
+    rest, _ = pair_call(before, late, after, later)
     moments, pay = sweep_call(below, rhs, above, t, rest, scales, unc)
     others = [trade(pay, "fit", k) for k in range(1, fits)]
-    fock = fock_call(0, pay, wt, near_tiles, width)
-    for k in range(1, fits):
-        fock = fock_call(k, others[k - 1], wt, near_tiles, width, fock)
+    fock = fock_call(pay, wt, tile)
+    for other, near in zip(others, near_tiles):
+        fock = fock_call(other, wt, near, fock)
     fock = fock + trade(fock, "sph", 1)
     bit = 2
     while bit < sphs:

time: 56.3 us -> 57 us (1.012)
  Pallas kernels: 25.2 us -> 27.2 us
  waiting for transfers between devices: 11.9 us -> 9.97 us
  starting transfers between devices: 17.7 us -> 18.3 us
    ppermute x4, waiting for transfers between devices: 6.38 us -> 4.02 us  [from_beside(): return (lax.ppermute(x, axes, up), lax.ppermute(x, axes, down))]
    pallas_call x7, Pallas kernels: 21.2 us -> 23.2 us  [the longest x2 13.9 us: pair_call(): pl.pallas_call(functools.partial(pair_kernel, quads, extra), in_specs=in_...]
    ppermute x4, starting transfers between devices: 8.68 us -> 9.29 us  [from_beside(): return (lax.ppermute(x, axes, up), lax.ppermute(x, axes, down))]
  transfers between devices with their start and end apart: 14 -> 14, of which waited for: 6 -> 6; matrix products, arithmetic and copies ran while one was open for 0% -> 0% of each run, Pallas kernels for 36% -> 39%
where the time goes in v7:
time: 57 us; the launch traced here: 56.8 us
  Pallas kernels  27.2 us (48%)
  starting transfers between devices  18.3 us (32%)
  waiting for transfers between devices  9.97 us (17%)
  between operations  0.75 us (1%)
  other arithmetic  0.62 us (1%)
    pallas_call x2, Pallas kernels, pair_call(): pl.pallas_call(functools.partial(pair_kernel, quads, extra), in_specs=in_...  13.9 us
    ppermute x4, starting transfers between devices, from_beside(): return (lax.ppermute(x, axes, up), lax.ppermute(x, axes, down))  9.29 us
    ppermute x7, starting transfers between devices, trade(): return lax.ppermute(x, axis, [(i, i ^ k) for i in range(count)])  6.98 us
    pallas_call x1, Pallas kernels, phi_call(): pl.pallas_call(functools.partial(phi_kernel, peers, width), in_specs=[pl....  4.9 us
    ppermute x3, waiting for transfers between devices, shift(): return lax.ppermute(x, axis, [(i, (i + k) % count) for i in range(count)])  4.72 us
    pallas_call x4, Pallas kernels, fock_call(): pl.pallas_call(fock_kernel, in_specs=[VMEM] * (3 + len(more)), out_specs=...  4.39 us
    ppermute x4, waiting for transfers between devices, from_beside(): return (lax.ppermute(x, axes, up), lax.ppermute(x, axes, down))  4.02 us
    pallas_call x1, Pallas kernels, sweep_call(): pl.pallas_call(sweep_kernel, in_specs=[VMEM] * 7, out_specs=[VMEM] * 2, o...  2.83 us
  transfers between devices with their start and end apart: 14, of which 6 were waited for; matrix products, arithmetic and copies ran while one was open for 0% of the time, Pallas kernels for 39%

profile of v7, /device:TPU:0, one launch (start us, length us, event | category | flops | bytes accessed | tf_op | source)
XLA Modules:
  0.0 56.8 jit_solution(3220389527736761156)
XLA Ops:
  0.6 0.8 %pack.1.own_ref = f32[24,16]{1,0:T(8,128)S(1)} custom-call(f32[3,16]{1,0:T(4,128)} %centre_ref.1, f32[1,16]{1,0:T(1,128)} %bitcast.2, s32[16,16]{1,0:T(8,128)} %nbr_ref.1, s32[1,16]{1,0:T(1,128)} %bitcast.3), custom_call_target="tpu_custom_call" | custom-call | tf_op jit(solution)/shard_map/pack/pallas_call | solution.py:207
  1.4 0.0 copy-start.2
  1.4 0.0 copy-start.3
  1.4 0.0 copy-start.4
  1.4 6.4 %collective-permute-start.1 = (f32[24,16]{1,0:T(8,128)S(1)}, f32[24,16]{1,0:T(8,128)S(1)}, u32[]{:S(2)}, u32[]{:S(2)}) collective-permute-start(f32[24,16]{1,0:T(8,128)S(1)} %pack.1.own_ref), channel_id=1, source_target_pairs={{1,0},{2,1},{3,2},{4,3},{5,4},{6,5},{7,6},{8,7},{9,8},{10,9},{11,1... | collective-permute-start | bytes 4616 | tf_op jit(solution)/shard_map/ppermute | solution.py:558
  7.9 4.9 %phi.1 = (s16[16,5248]{1,0:T(8,128)(2,1)S(1)}, s16[16,5248]{1,0:T(8,128)(2,1)S(1)}, s16[16,5248]{1,0:T(8,128)(2,1)S(1)}, bf16[256,5120]{1,0:T(8,128)(2,1)S(1)}, ...) custom-call(bf16[16,256]{1,0:T(8,128)(2,1)} %rest_0_.1, bf16[256,20480]{1,0:T(8,128)(2,1)} %rest_1_.1), custom_call_target="tpu_custom_call" | custom-call | flops 125829120 | bytes 8847360 | tf_op jit(solution)/shard_map/phi/pallas_call | solution.py:165
  12.8 0.0 collective-permute-done.1.after_ref
  12.8 1.8 %collective-permute-done.before_ref = f32[24,16]{1,0:T(8,128)S(1)} collective-permute-done((f32[24,16]{1,0:T(8,128)S(1)}, f32[24,16]{1,0:T(8,128)S(1)}, u32[]{:S(2)}, u32[]{:S(2)}) %collective-permute-start) | collective-permute-done | bytes 1568 | tf_op jit(solution)/shard_map/ppermute | solution.py:558
  14.6 0.0 collective-permute-start.2
  14.6 0.0 collective-permute-start.3
  14.6 3.5 %collective-permute-start.4 = (s16[16,5248]{1,0:T(8,128)(2,1)S(1)}, s16[16,5248]{1,0:T(8,128)(2,1)S(1)}, u32[]{:S(2)}, u32[]{:S(2)}) collective-permute-start(s16[16,5248]{1,0:T(8,128)(2,1)S(1)} %get-tuple-element.29), channel_id=1, source_target_pairs={{0,3},{1,2},{2,1},{3,0},{4,7},{5,6},{6,5},{7,4},{8,11},{9,10},{10,... | collective-permute-start | bytes 503816 | tf_op jit(solution)/shard_map/ppermute | solution.py:545
  18.1 8.8 %pairs.2 = (bf16[20,512,256]{2,1,0:T(8,128)(2,1)S(1)}, f32[5,1,1280]{2,1,0:T(1,128)S(1)}, f32[16,5120]{1,0:T(8,128)S(1)}, bf16[256,5120]{1,0:T(8,128)(2,1)S(1)}) custom-call(f32[24,16]{1,0:T(8,128)S(1)} %collective-permute-done.before_ref, f32[24,16]{1,0:T(8,128)S(1)} %pack.1.own_ref, f32[24,16]{1,0:T(8,128)S(1)} %collective-permute-done.1.after_ref, ...), custom_call_target="tpu_custom_call" | custom-call | flops 2621440000 | bytes 5242880 | tf_op jit(solution)/shard_map/pairs/pallas_call | solution.py:356
  26.9 0.0 collective-permute-done.3.refs_2_
  27.0 0.4 rhs.1.own_ref
  27.4 0.0 copy-start.5
  27.4 2.9 %collective-permute-start.6 = (f32[16,1024]{1,0:T(8,128)S(1)}, f32[16,1024]{1,0:T(8,128)S(1)}, u32[]{:S(2)}, u32[]{:S(2)}) collective-permute-start(f32[16,1024]{1,0:T(8,128)S(1)} %rhs.1.own_ref), channel_id=1, source_target_pairs={{1,0},{2,1},{3,2},{4,3},{5,4},{6,5},{7,6},{8,7},{9,8},{10,9},{11,1... | collective-permute-start | bytes 196616 | tf_op jit(solution)/shard_map/ppermute | solution.py:558
  30.2 0.0 collective-permute-start.5
  30.2 5.1 %pairs.3 = (bf16[12,512,256]{2,1,0:T(8,128)(2,1)S(1)}, f32[3,1,1280]{2,1,0:T(1,128)}) custom-call(f32[24,16]{1,0:T(8,128)S(1)} %collective-permute-done.before_ref, f32[24,16]{1,0:T(8,128)S(1)} %pack.1.own_ref, f32[24,16]{1,0:T(8,128)S(1)} %collective-permute-done.1.after_ref, f32[8,640]{1,0:T(8,128)S(1)} %copy-done.4, bf16[640,256]{1,0:T(8,128)(2,1)S(1)} %copy-done.2), custom_call_target="tpu_custom_call" | custom-call | flops 1572864000 | bytes 3145728 | tf_op jit(solution)/shard_map/pairs/pallas_call | solution.py:356
  35.3 2.2 %collective-permute-done.5.before_ref = f32[16,1024]{1,0:T(8,128)S(1)} collective-permute-done((f32[16,1024]{1,0:T(8,128)S(1)}, f32[16,1024]{1,0:T(8,128)S(1)}, u32[]{:S(2)}, u32[]{:S(2)}) %collective-permute-start.5) | collective-permute-done | bytes 65568 | tf_op jit(solution)/shard_map/ppermute | solution.py:558
  37.5 2.8 %sweeps.1 = (f32[16,16,49]{2,1,0:T(8,128)}, f32[16,1408]{1,0:T(8,128)S(1)}) custom-call(f32[16,1024]{1,0:T(8,128)S(1)} %collective-permute-done.5.before_ref, f32[16,1024]{1,0:T(8,128)S(1)} %rhs.1.own_ref, f32[16,1024]{1,0:T(8,128)S(1)} %collective-permute-done.6.after_ref, bf16[20,512,256]{2,1,0:T(8,128)(2,1)S(1)} %get-tuple-element.31.t_ref, ...), custom_call_target="tpu_custom_call" | custom-call | flops 805306368 | bytes 8388608 | tf_op jit(solution)/shard_map/sweeps/pallas_call | solution.py:479
  40.4 3.5 %collective-permute-start.7 = (f32[16,1408]{1,0:T(8,128)S(1)}, f32[16,1408]{1,0:T(8,128)S(1)}, u32[]{:S(2)}, u32[]{:S(2)}) collective-permute-start(f32[16,1408]{1,0:T(8,128)S(1)} %get-tuple-element.35.pay_ref), channel_id=1, source_target_pairs={{0,3},{1,2},{2,1},{3,0},{4,7},{5,6},{6,5},{7,4},{8,11},{9,10},{10,... | collective-permute-start | bytes 270344 | tf_op jit(solution)/shard_map/ppermute | solution.py:545
  43.8 1.1 %fock.4.rest_0_ = f32[16,256]{1,0:T(8,128)S(1)} custom-call(f32[16,1408]{1,0:T(8,128)S(1)} %get-tuple-element.35.pay_ref, bf16[256,1280]{1,0:T(8,128)(2,1)S(1)} %copy-done, bf16[256,5120]{1,0:T(8,128)(2,1)S(1)} %get-tuple-element.39.tile_ref), custom_call_target="tpu_custom_call" | custom-call | flops 41943040 | bytes 2621440 | tf_op jit(solution)/shard_map/fock/pallas_call | solution.py:529
  44.9 1.1 %fock.5.rest_0_ = f32[16,256]{1,0:T(8,128)S(1)} custom-call(f32[16,1408]{1,0:T(8,128)S(1)} %collective-permute-done.9.pay_ref, bf16[256,1280]{1,0:T(8,128)(2,1)S(1)} %copy-done, bf16[256,5120]{1,0:T(8,128)(2,1)S(1)} %get-tuple-element.38.tile_ref, f32[16,256]{1,0:T(8,128)S(1)} %fock.4.rest_0_), custom_call_target="tpu_custom_call" | custom-call | flops 41943040 | bytes 2621440 | tf_op jit(solution)/shard_map/fock/pallas_call | solution.py:529
  46.0 1.1 %fock.6.rest_0_ = f32[16,256]{1,0:T(8,128)S(1)} custom-call(f32[16,1408]{1,0:T(8,128)S(1)} %collective-permute-done.8.pay_ref, bf16[256,1280]{1,0:T(8,128)(2,1)S(1)} %copy-done, bf16[256,5120]{1,0:T(8,128)(2,1)S(1)} %get-tuple-element.37.tile_ref, f32[16,256]{1,0:T(8,128)S(1)} %fock.5.rest_0_), custom_call_target="tpu_custom_call" | custom-call | flops 41943040 | bytes 2621440 | tf_op jit(solution)/shard_map/fock/pallas_call | solution.py:529
  47.1 1.1 %fock.7 = f32[16,256]{1,0:T(8,128)S(1)} custom-call(f32[16,1408]{1,0:T(8,128)S(1)} %collective-permute-done.7.pay_ref, bf16[256,1280]{1,0:T(8,128)(2,1)S(1)} %copy-done, bf16[256,5120]{1,0:T(8,128)(2,1)S(1)} %get-tuple-element.36.tile_ref, f32[16,256]{1,0:T(8,128)S(1)} %fock.6.rest_0_), custom_call_target="tpu_custom_call" | custom-call | flops 41943040 | bytes 2621440 | tf_op jit(solution)/shard_map/fock/pallas_call | solution.py:529
  48.2 1.2 %collective-permute-done.10 = f32[16,256]{1,0:T(8,128)S(1)} collective-permute-done((f32[16,256]{1,0:T(8,128)S(1)}, f32[16,256]{1,0:T(8,128)S(1)}, u32[]{:S(2)}, u32[]{:S(2)}) %collective-permute-start.10) | collective-permute-done | bytes 16416 | tf_op jit(solution)/shard_map/ppermute | solution.py:545
  49.5 1.2 %collective-permute-start.13 = (f32[16,256]{1,0:T(8,128)S(1)}, f32[16,256]{1,0:T(8,128)S(1)}, u32[]{:S(2)}, u32[]{:S(2)}) collective-permute-start(f32[16,256]{1,0:T(8,128)S(1)} %add.12), channel_id=1, source_target_pairs={{0,24},{4,28},{8,0},{12,4},{16,8},{20,12},{24,16},{28,20},{1,25},{... | collective-permute-start | bytes 49160 | tf_op jit(solution)/shard_map/ppermute | solution.py:550
  50.7 0.8 %collective-permute-start.11 = (f32[16,256]{1,0:T(8,128)S(1)}, f32[16,256]{1,0:T(8,128)S(1)}, u32[]{:S(2)}, u32[]{:S(2)}) collective-permute-start(f32[16,256]{1,0:T(8,128)S(1)} %add.12), channel_id=1, source_target_pairs={{0,8},{4,12},{8,16},{12,20},{16,24},{20,28},{24,0},{28,4},{1,9},{5... | collective-permute-start | bytes 49160 | tf_op jit(solution)/shard_map/ppermute | solution.py:550
  51.5 1.7 %collective-permute-done.13 = f32[16,256]{1,0:T(8,128)S(1)} collective-permute-done((f32[16,256]{1,0:T(8,128)S(1)}, f32[16,256]{1,0:T(8,128)S(1)}, u32[]{:S(2)}, u32[]{:S(2)}) %collective-permute-start.13) | collective-permute-done | bytes 16416 | tf_op jit(solution)/shard_map/ppermute | solution.py:550
  53.2 2.5 %collective-permute-done.12 = f32[16,256]{1,0:T(8,128)S(1)} collective-permute-done((f32[16,256]{1,0:T(8,128)S(1)}, f32[16,256]{1,0:T(8,128)S(1)}, u32[]{:S(2)}, u32[]{:S(2)}) %collective-permute-start.12) | collective-permute-done | bytes 16416 | tf_op jit(solution)/shard_map/ppermute | solution.py:550
  55.7 0.6 collective-permute-done.11
  56.2 0.6 %add_add_fusion = f32[16,256]{1,0:T(8,128)} fusion(f32[16,256]{1,0:T(8,128)S(1)} %collective-permute-done.13, f32[16,256]{1,0:T(8,128)S(1)} %collective-permute-done.12, f32[16,256]{1,0:T(8,128)S(1)} %add.12, f32[16,256]{1,0:T(8,128)S(1)} %collective-permute-done.11), kind=kLoop, calls=%fused_computation | loop fusion | flops 12288 | bytes 81920 | tf_op jit(solution)/shard_map/add | solution.py:598
  (20 shorter events, 0.0 us)
Async XLA Ops:
  1.4 16.7 %copy-start.2 = (bf16[640,256]{1,0:T(8,128)(2,1)S(1)}, bf16[640,256]{1,0:T(8,128)(2,1)}, u32[]{:S(2)}) copy-start(bf16[640,256]{1,0:T(8,128)(2,1)} %constant.14.clone.w_ref) | copy-start | bytes 983044
  1.4 16.7 %copy-start.3 = (bf16[16,256]{1,0:T(8,128)(2,1)S(1)}, bf16[16,256]{1,0:T(8,128)(2,1)}, u32[]{:S(2)}) copy-start(bf16[16,256]{1,0:T(8,128)(2,1)} %rest_0_.1) | copy-start | bytes 24580
  1.4 16.7 %copy-start.4 = (f32[8,640]{1,0:T(8,128)S(1)}, f32[8,640]{1,0:T(8,128)}, u32[]{:S(2)}) copy-start(f32[8,640]{1,0:T(8,128)} %constant.13.clone.dir_ref) | copy-start | bytes 61444
  1.4 11.3 %collective-permute-start.1 = (f32[24,16]{1,0:T(8,128)S(1)}, f32[24,16]{1,0:T(8,128)S(1)}, u32[]{:S(2)}, u32[]{:S(2)}) collective-permute-start(f32[24,16]{1,0:T(8,128)S(1)} %pack.1.own_ref), channel_id=1, source_target_pairs={{1,0},{2,1},{3,2},{4,3},{5,4},{6,5},{7,6},{8,7},{9,8},{10,9},{11,1... | collective-permute-start | bytes 4616 | tf_op jit(solution)/shard_map/ppermute | solution.py:558
  7.9 6.7 %collective-permute-start = (f32[24,16]{1,0:T(8,128)S(1)}, f32[24,16]{1,0:T(8,128)S(1)}, u32[]{:S(2)}, u32[]{:S(2)}) collective-permute-start(f32[24,16]{1,0:T(8,128)S(1)} %pack.1.own_ref), channel_id=1, source_target_pairs={{0,1},{1,2},{2,3},{3,4},{4,5},{5,6},{6,7},{7,8},{8,9},{9,10},{10,1... | collective-permute-start | bytes 4616 | tf_op jit(solution)/shard_map/ppermute | solution.py:558
  14.6 12.4 %copy-start.1 = (bf16[640,256]{1,0:T(8,128)(2,1)S(1)}, bf16[640,256]{1,0:T(8,128)(2,1)}, u32[]{:S(2)}) copy-start(bf16[640,256]{1,0:T(8,128)(2,1)} %constant.10.clone.refs_5_) | copy-start | bytes 983044
  14.6 12.3 %collective-permute-start.2 = (s16[16,5248]{1,0:T(8,128)(2,1)S(1)}, s16[16,5248]{1,0:T(8,128)(2,1)S(1)}, u32[]{:S(2)}, u32[]{:S(2)}) collective-permute-start(s16[16,5248]{1,0:T(8,128)(2,1)S(1)} %get-tuple-element.27), channel_id=1, source_target_pairs={{0,1},{1,0},{2,3},{3,2},{4,5},{5,4},{6,7},{7,6},{8,9},{9,8},{10,11... | collective-permute-start | bytes 503816 | tf_op jit(solution)/shard_map/ppermute | solution.py:545
  14.6 12.4 %collective-permute-start.3 = (s16[16,5248]{1,0:T(8,128)(2,1)S(1)}, s16[16,5248]{1,0:T(8,128)(2,1)S(1)}, u32[]{:S(2)}, u32[]{:S(2)}) collective-permute-start(s16[16,5248]{1,0:T(8,128)(2,1)S(1)} %get-tuple-element.28), channel_id=1, source_target_pairs={{0,2},{1,3},{2,0},{3,1},{4,6},{5,7},{6,4},{7,5},{8,10},{9,11},{10,... | collective-permute-start | bytes 503816 | tf_op jit(solution)/shard_map/ppermute | solution.py:545
  14.6 12.4 %collective-permute-start.4 = (s16[16,5248]{1,0:T(8,128)(2,1)S(1)}, s16[16,5248]{1,0:T(8,128)(2,1)S(1)}, u32[]{:S(2)}, u32[]{:S(2)}) collective-permute-start(s16[16,5248]{1,0:T(8,128)(2,1)S(1)} %get-tuple-element.29), channel_id=1, source_target_pairs={{0,3},{1,2},{2,1},{3,0},{4,7},{5,6},{6,5},{7,4},{8,11},{9,10},{10,... | collective-permute-start | bytes 503816 | tf_op jit(solution)/shard_map/ppermute | solution.py:545
  27.4 10.2 %copy-start.5 = (f32[8,128]{1,0:T(8,128)S(1)}, f32[8,128]{1,0:T(8,128)}, u32[]{:S(2)}) copy-start(f32[8,128]{1,0:T(8,128)} %constant.12.clone.sc_ref) | copy-start | bytes 12292
  27.4 7.9 %collective-permute-start.6 = (f32[16,1024]{1,0:T(8,128)S(1)}, f32[16,1024]{1,0:T(8,128)S(1)}, u32[]{:S(2)}, u32[]{:S(2)}) collective-permute-start(f32[16,1024]{1,0:T(8,128)S(1)} %rhs.1.own_ref), channel_id=1, source_target_pairs={{1,0},{2,1},{3,2},{4,3},{5,4},{6,5},{7,6},{8,7},{9,8},{10,9},{11,1... | collective-permute-start | bytes 196616 | tf_op jit(solution)/shard_map/ppermute | solution.py:558
  30.2 7.3 %collective-permute-start.5 = (f32[16,1024]{1,0:T(8,128)S(1)}, f32[16,1024]{1,0:T(8,128)S(1)}, u32[]{:S(2)}, u32[]{:S(2)}) collective-permute-start(f32[16,1024]{1,0:T(8,128)S(1)} %rhs.1.own_ref), channel_id=1, source_target_pairs={{0,1},{1,2},{2,3},{3,4},{4,5},{5,6},{6,7},{7,8},{8,9},{9,10},{10,1... | collective-permute-start | bytes 196616 | tf_op jit(solution)/shard_map/ppermute | solution.py:558
  37.5 6.3 %copy-start = (bf16[256,1280]{1,0:T(8,128)(2,1)S(1)}, bf16[256,1280]{1,0:T(8,128)(2,1)}, u32[]{:S(2)}) copy-start(bf16[256,1280]{1,0:T(8,128)(2,1)} %constant.11.clone.y_ref) | copy-start | bytes 1966084
  40.3 4.6 %collective-permute-start.9 = (f32[16,1408]{1,0:T(8,128)S(1)}, f32[16,1408]{1,0:T(8,128)S(1)}, u32[]{:S(2)}, u32[]{:S(2)}) collective-permute-start(f32[16,1408]{1,0:T(8,128)S(1)} %get-tuple-element.35.pay_ref), channel_id=1, source_target_pairs={{0,1},{1,0},{2,3},{3,2},{4,5},{5,4},{6,7},{7,6},{8,9},{9,8},{10,11... | collective-permute-start | bytes 270344 | tf_op jit(solution)/shard_map/ppermute | solution.py:545
  40.4 5.7 %collective-permute-start.8 = (f32[16,1408]{1,0:T(8,128)S(1)}, f32[16,1408]{1,0:T(8,128)S(1)}, u32[]{:S(2)}, u32[]{:S(2)}) collective-permute-start(f32[16,1408]{1,0:T(8,128)S(1)} %get-tuple-element.35.pay_ref), channel_id=1, source_target_pairs={{0,2},{1,3},{2,0},{3,1},{4,6},{5,7},{6,4},{7,5},{8,10},{9,11},{10,... | collective-permute-start | bytes 270344 | tf_op jit(solution)/shard_map/ppermute | solution.py:545
  40.4 6.8 %collective-permute-start.7 = (f32[16,1408]{1,0:T(8,128)S(1)}, f32[16,1408]{1,0:T(8,128)S(1)}, u32[]{:S(2)}, u32[]{:S(2)}) collective-permute-start(f32[16,1408]{1,0:T(8,128)S(1)} %get-tuple-element.35.pay_ref), channel_id=1, source_target_pairs={{0,3},{1,2},{2,1},{3,0},{4,7},{5,6},{6,5},{7,4},{8,11},{9,10},{10,... | collective-permute-start | bytes 270344 | tf_op jit(solution)/shard_map/ppermute | solution.py:545
  48.2 1.2 %collective-permute-start.10 = (f32[16,256]{1,0:T(8,128)S(1)}, f32[16,256]{1,0:T(8,128)S(1)}, u32[]{:S(2)}, u32[]{:S(2)}) collective-permute-start(f32[16,256]{1,0:T(8,128)S(1)} %fock.7), channel_id=1, source_target_pairs={{0,4},{4,0},{8,12},{12,8},{16,20},{20,16},{24,28},{28,24},{1,5},{5... | collective-permute-start | bytes 49160 | tf_op jit(solution)/shard_map/ppermute | solution.py:545
  49.5 3.7 %collective-permute-start.13 = (f32[16,256]{1,0:T(8,128)S(1)}, f32[16,256]{1,0:T(8,128)S(1)}, u32[]{:S(2)}, u32[]{:S(2)}) collective-permute-start(f32[16,256]{1,0:T(8,128)S(1)} %add.12), channel_id=1, source_target_pairs={{0,24},{4,28},{8,0},{12,4},{16,8},{20,12},{24,16},{28,20},{1,25},{... | collective-permute-start | bytes 49160 | tf_op jit(solution)/shard_map/ppermute | solution.py:550
  50.7 5.0 %collective-permute-start.12 = (f32[16,256]{1,0:T(8,128)S(1)}, f32[16,256]{1,0:T(8,128)S(1)}, u32[]{:S(2)}, u32[]{:S(2)}) collective-permute-start(f32[16,256]{1,0:T(8,128)S(1)} %add.12), channel_id=1, source_target_pairs={{0,16},{4,20},{8,24},{12,28},{16,0},{20,4},{24,8},{28,12},{1,17},{... | collective-permute-start | bytes 49160 | tf_op jit(solution)/shard_map/ppermute | solution.py:550
  50.7 5.5 %collective-permute-start.11 = (f32[16,256]{1,0:T(8,128)S(1)}, f32[16,256]{1,0:T(8,128)S(1)}, u32[]{:S(2)}, u32[]{:S(2)}) collective-permute-start(f32[16,256]{1,0:T(8,128)S(1)} %add.12), channel_id=1, source_target_pairs={{0,8},{4,12},{8,16},{12,20},{16,24},{20,28},{24,0},{28,4},{1,9},{5... | collective-permute-start | bytes 49160 | tf_op jit(solution)/shard_map/ppermute | solution.py:550

commit v8 on v6

--- a/solution.py
+++ b/solution.py
@@ -26,6 +26,7 @@
 SMEM = pl.BlockSpec(memory_space=pltpu.SMEM)
 BAND = 0.1
 REACH = 8
+SOONER = 1
 BF = jnp.bfloat16
 F32 = jnp.float32
 
@@ -96,7 +97,9 @@
     w = np.zeros((PN, 2 * LP))
     w[:NG, :LM] = ys.T
     w[NG:, LP : LP + LM] = ys.T
-    return np.concatenate(split(w), 1), np.concatenate(split(w.T), 1)
+    hi, lo = split(w.T)
+    deep = np.block([[hi, lo], [hi, np.zeros_like(lo)]])
+    return np.concatenate(split(w), 1), deep
 
 
 def lane_scales():
@@ -283,9 +286,7 @@
     return [jnp.maximum(0.0, 1.0 - t) for t in tiles]
 
 
-def pair_kernel(
-    lo, hi, before_ref, own_ref, after_ref, dir_ref, w_ref, t_ref, unc_ref, geo, mask, *bhs
-):
+def pair_setup(before_ref, own_ref, after_ref, geo, mask):
     spheres = own_ref.shape[1]
     slots = 2 * REACH
     wide = spheres + 2 * REACH
@@ -309,45 +310,61 @@
         found = jnp.where(lane == c, hit, found)
     mask[...] = found
 
-    def step(b, carry):
+
+def pair_work(quads, geo, mask, dir_ref, w_ref, t_ref, unc_ref, bhs):
+    for b, quad in enumerate(quads):
         sums = []
         for u in range(QUAD):
-            at = b * QUAD + u
-            sums.append(pair_build(at + lo, geo, mask, dir_ref, bhs[u]))
-            pair_finish(at, w_ref, t_ref, bhs[u])
-        tiles = uncover(sums[:2]) + uncover(sums[2:])
-        for t, v in enumerate(tiles):
-            unc_ref[b, :, 128 * t : 128 * t + 128] = v
-        return carry
-
-    lax.fori_loop(0, (hi - lo) // QUAD, step, 0, unroll=(hi - lo) // QUAD)
-
-
-def pair_call(before, own, after, lo, hi):
-    spheres = own.shape[1]
-    wide = spheres + 2 * REACH
-    count = hi - lo
-    w, d = pair_weights()
+            sums.append(pair_build(quad * QUAD + u, geo, mask, dir_ref, bhs[u]))
+            pair_finish(b * QUAD + u, w_ref, t_ref, bhs[u])
+        if unc_ref is not None:
+            tiles = uncover(sums[:2]) + uncover(sums[2:])
+            for t, v in enumerate(tiles):
+                unc_ref[b, :, 128 * t : 128 * t + 128] = v
+
+
+def first_pair_kernel(
+    quads, before_ref, own_ref, after_ref, dir_ref, w_ref, t_ref, unc_ref, geo, mask, *bhs
+):
+    pair_setup(before_ref, own_ref, after_ref, geo, mask)
+    pair_work(quads, geo, mask, dir_ref, w_ref, t_ref, unc_ref, bhs)
+
+
+def next_pair_kernel(quads, geo, mask, dir_ref, w_ref, t_ref, *bhs):
+    pair_work(quads, geo, mask, dir_ref, w_ref, t_ref, None, bhs)
+
+
+def pair_call(quads, consts, packs=None, known=None):
+    count = len(quads)
+    out_shape = [jax.ShapeDtypeStruct((count * QUAD, 8 * LP, 4 * LP), BF)]
+    if known is None:
+        kernel, args = first_pair_kernel, packs
+        spheres = packs[1].shape[1]
+        out_shape += [
+            jax.ShapeDtypeStruct((count, 1, QN), F32),
+            jax.ShapeDtypeStruct((3 * spheres, 128), F32),
+            jax.ShapeDtypeStruct((spheres + 2 * REACH, 128), F32),
+        ]
+    else:
+        kernel, args = next_pair_kernel, known
     return pl.pallas_call(
-        functools.partial(pair_kernel, lo, hi),
-        in_specs=[VMEM] * 5,
-        out_specs=[VMEM] * 2,
-        scratch_shapes=[pltpu.VMEM((3 * spheres, 128), F32), pltpu.VMEM((wide, 128), F32)]
-        + [pltpu.VMEM((400, 2 * NG), BF)] * QUAD,
-        out_shape=[
-            jax.ShapeDtypeStruct((count, 8 * LP, 4 * LP), BF),
-            jax.ShapeDtypeStruct((count // QUAD, 1, QN), F32),
-        ],
+        functools.partial(kernel, quads),
+        in_specs=[VMEM] * (len(args) + 2),
+        out_specs=[VMEM] * len(out_shape),
+        scratch_shapes=[pltpu.VMEM((400, 2 * NG), BF)] * QUAD,
+        out_shape=out_shape,
         compiler_params=PARAMS,
         cost_estimate=pl.CostEstimate(
-            flops=count * 2 * 400 * 640 * 256, bytes_accessed=count * 262144, transcendentals=0
+            flops=count * QUAD * 2 * 400 * 640 * 256,
+            bytes_accessed=count * QUAD * 262144,
+            transcendentals=0,
         ),
         name="pairs",
-    )(before, own, after, jnp.asarray(d), jnp.asarray(w))
+    )(*args, *consts)
 
 
 def own_uncovered(unc_ref, b):
-    b = b + REACH // 2
+    b = b + SOONER * QUAD // 2
     return unc_ref[b // 2, :, b % 2 * PN : (b % 2 + 1) * PN]
 
 
@@ -395,9 +412,12 @@
         lhs = jnp.concatenate(
             [below[:, lo_at : lo_at + 8 * LP], above[:, up_at : up_at + 8 * LP]], 0
         )
-        at = e + odd + shift
-        most = t_refs[0].shape[0]
-        t = t_refs[0][at] if at < most else t_refs[1][at - most]
+        lowest, most = REACH - SOONER * QUAD, t_refs[0].shape[0]
+        at = e + odd + shift - lowest
+        if 0 <= at < most:
+            t = t_refs[0][at]
+        else:
+            t = t_refs[1][at + lowest - (most if at > 0 else 0)]
         r = jnp.dot(lhs, t, preferred_element_type=F32)
         n = NDENS
         a = r[0:n, : 2 * LP] + r[n : 2 * n, : 2 * LP] + r[0:n, 2 * LP :]
@@ -476,9 +496,8 @@
     width = pairs * PN
     rows = [pay_ref[:, b * 2 * LP : (b + 1) * 2 * LP] for b in range(pairs)]
     hi, lo = halves(jnp.concatenate(rows, 0))
-    n = pairs * NDENS
-    r = jnp.dot(jnp.concatenate([hi, lo], 0), y_ref[...], preferred_element_type=F32)
-    out = r[:n, :PN] + r[:n, PN:] + r[n:, :PN]
+    r = jnp.dot(jnp.concatenate([hi, lo], 1), y_ref[...], preferred_element_type=F32)
+    out = r[:, :PN] + r[:, PN:]
     for b in range(pairs):
         unc = jnp.concatenate(
             [pay_ref[b : b + 1, own:], pay_ref[pairs + b : pairs + b + 1, own : own + 256]], 1
@@ -547,12 +566,16 @@
     *phis, near_tiles = phi_call(coefs, tiles, width)
     phis, before, after = lax.optimization_barrier((phis, before, after))
     got = [trade(phis[k], "fit", k) for k in range(1, fits)]
-    wide = spheres + 2 * REACH
-    t, unc = pair_call(before, own, after, 0, wide - REACH)
+    below_own, last_own = REACH // QUAD, (REACH + spheres) // QUAD
+    soon = [*range(below_own - SOONER, last_own)]
+    later = [*range(below_own - SOONER), *range(last_own, last_own + below_own)]
+    pw, dirs = pair_weights()
+    consts = (jnp.asarray(dirs), jnp.asarray(pw))
+    t, unc, geo, mask = pair_call(soon, consts, packs=(before, own, after))
     rhs = rhs_call([phis[0], *got], unc, w)
     below, above = from_beside(rhs)
-    late, _ = lax.optimization_barrier((own, rhs))
-    rest, _ = pair_call(before, late, after, wide - REACH, wide)
+    mask, _ = lax.optimization_barrier((mask, rhs))
+    (rest,) = pair_call(later, consts, known=(geo, mask))
     moments, pay = sweep_call(below, rhs, above, t, rest, scales, unc)
     others = [trade(pay, "fit", k) for k in range(1, fits)]
     fock = fock_call(0, pay, wt, near_tiles, width)

time: 56.3 us -> 54.5 us (0.968)
  Pallas kernels: 25.2 us -> 23.7 us
    pallas_call x2, Pallas kernels: 11.8 us -> 10.9 us  [pair_call(): pl.pallas_call(functools.partial(kernel, quads), in_specs=[VMEM] * (len(a...]
    pallas_call x4, Pallas kernels: 5.02 us -> 4.4 us  [fock_call(): pl.pallas_call(functools.partial(fock_kernel, k), in_specs=[VMEM] * (3 +...]
  transfers between devices with their start and end apart: 14 -> 14, of which waited for: 6 -> 6; matrix products, arithmetic and copies ran while one was open for 0% -> 0% of each run, Pallas kernels for 36% -> 34%
where the time goes in v8:
time: 54.5 us; the launch traced here: 54.2 us
  Pallas kernels  23.7 us (43%)
  starting transfers between devices  17.7 us (32%)
  waiting for transfers between devices  11.5 us (21%)
  between operations  0.76 us (1%)
  other arithmetic  0.62 us (1%)
    pallas_call x2, Pallas kernels, pair_call(): pl.pallas_call(functools.partial(kernel, quads), in_specs=[VMEM] * (len(a...  10.9 us
    ppermute x4, starting transfers between devices, from_beside(): return (lax.ppermute(x, axes, up), lax.ppermute(x, axes, down))  8.68 us
    ppermute x7, starting transfers between devices, trade(): return lax.ppermute(x, axis, [(i, i ^ k) for i in range(count)])  6.98 us
    ppermute x4, waiting for transfers between devices, from_beside(): return (lax.ppermute(x, axes, up), lax.ppermute(x, axes, down))  5.99 us
    pallas_call x4, Pallas kernels, fock_call(): pl.pallas_call(functools.partial(fock_kernel, k), in_specs=[VMEM] * (3 +...  4.4 us
    pallas_call x1, Pallas kernels, phi_call(): pl.pallas_call(functools.partial(phi_kernel, width), in_specs=[pl.BlockSp...  4.39 us
    ppermute x3, waiting for transfers between devices, shift(): return lax.ppermute(x, axis, [(i, (i + k) % count) for i in range(count)])  4.25 us
    pallas_call x1, Pallas kernels, sweep_call(): pl.pallas_call(sweep_kernel, in_specs=[VMEM] * 7, out_specs=[VMEM] * 2, o...  2.81 us
  transfers between devices with their start and end apart: 14, of which 6 were waited for; matrix products, arithmetic and copies ran while one was open for 0% of the time, Pallas kernels for 34%

profile of v8, /device:TPU:0, one launch (start us, length us, event | category | flops | bytes accessed | tf_op | source)
XLA Modules:
  0.0 54.2 jit_solution(17372455217942431893)
XLA Ops:
  0.6 0.0 copy-start.3
  0.6 0.0 copy-start.4
  0.7 0.0 copy-start.1
  0.7 0.8 %pack.1.own_ref = f32[24,16]{1,0:T(8,128)S(1)} custom-call(f32[3,16]{1,0:T(4,128)} %centre_ref.1, f32[1,16]{1,0:T(1,128)} %bitcast.2, s32[16,16]{1,0:T(8,128)} %nbr_ref.1, s32[1,16]{1,0:T(1,128)} %bitcast.3), custom_call_target="tpu_custom_call" | custom-call | tf_op jit(solution)/shard_map/pack/pallas_call | solution.py:203
  1.5 6.4 %collective-permute-start.1 = (f32[24,16]{1,0:T(8,128)S(1)}, f32[24,16]{1,0:T(8,128)S(1)}, u32[]{:S(2)}, u32[]{:S(2)}) collective-permute-start(f32[24,16]{1,0:T(8,128)S(1)} %pack.1.own_ref), channel_id=1, source_target_pairs={{1,0},{2,1},{3,2},{4,3},{5,4},{6,5},{7,6},{8,7},{9,8},{10,9},{11,1... | collective-permute-start | bytes 4616 | tf_op jit(solution)/shard_map/ppermute | solution.py:551
  7.9 4.4 %phi.1 = (f32[16,5120]{1,0:T(8,128)S(1)}, s16[16,5248]{1,0:T(8,128)(2,1)S(1)}, s16[16,5248]{1,0:T(8,128)(2,1)S(1)}, s16[16,5248]{1,0:T(8,128)(2,1)S(1)}, bf16[256,20480]{1,0:T(8,128)(2,1)S(1)}) custom-call(bf16[16,256]{1,0:T(8,128)(2,1)} %far_coef_ref.1, bf16[256,20480]{1,0:T(8,128)(2,1)} %far_ref.1), custom_call_target="tpu_custom_call" | custom-call | flops 167772160 | bytes 11796480 | tf_op jit(solution)/shard_map/phi/pallas_call | solution.py:160
  12.3 0.0 copy-start.2
  12.4 0.0 collective-permute-done.1.after_ref
  12.4 2.4 %collective-permute-done.before_ref = f32[24,16]{1,0:T(8,128)S(1)} collective-permute-done((f32[24,16]{1,0:T(8,128)S(1)}, f32[24,16]{1,0:T(8,128)S(1)}, u32[]{:S(2)}, u32[]{:S(2)}) %collective-permute-start) | collective-permute-done | bytes 1568 | tf_op jit(solution)/shard_map/ppermute | solution.py:551
  14.8 0.0 collective-permute-start.3
  14.8 3.5 %collective-permute-start.4 = (s16[16,5248]{1,0:T(8,128)(2,1)S(1)}, s16[16,5248]{1,0:T(8,128)(2,1)S(1)}, u32[]{:S(2)}, u32[]{:S(2)}) collective-permute-start(s16[16,5248]{1,0:T(8,128)(2,1)S(1)} %get-tuple-element.27), channel_id=1, source_target_pairs={{0,3},{1,2},{2,1},{3,0},{4,7},{5,6},{6,5},{7,4},{8,11},{9,10},{10,... | collective-permute-start | bytes 503816 | tf_op jit(solution)/shard_map/ppermute | solution.py:538
  18.3 7.1 %pairs.2 = (bf16[20,512,256]{2,1,0:T(8,128)(2,1)S(1)}, f32[5,1,1280]{2,1,0:T(1,128)S(1)}, f32[48,128]{1,0:T(8,128)S(1)}, f32[32,128]{1,0:T(8,128)S(1)}) custom-call(f32[24,16]{1,0:T(8,128)S(1)} %collective-permute-done.before_ref, f32[24,16]{1,0:T(8,128)S(1)} %pack.1.own_ref, f32[24,16]{1,0:T(8,128)S(1)} %collective-permute-done.1.after_ref, ...), custom_call_target="tpu_custom_call" | custom-call | flops 2621440000 | bytes 5242880 | tf_op jit(solution)/shard_map/pairs/pallas_call | solution.py:350
  25.4 0.0 collective-permute-done.2.refs_1_
  25.4 0.0 collective-permute-done.3.refs_2_
  25.4 0.4 rhs.1.own_ref
  25.8 2.2 %collective-permute-start.6 = (f32[16,1024]{1,0:T(8,128)S(1)}, f32[16,1024]{1,0:T(8,128)S(1)}, u32[]{:S(2)}, u32[]{:S(2)}) collective-permute-start(f32[16,1024]{1,0:T(8,128)S(1)} %rhs.1.own_ref), channel_id=1, source_target_pairs={{1,0},{2,1},{3,2},{4,3},{5,4},{6,5},{7,6},{8,7},{9,8},{10,9},{11,1... | collective-permute-start | bytes 196616 | tf_op jit(solution)/shard_map/ppermute | solution.py:551
  28.0 0.0 collective-permute-start.5
  28.0 3.8 %pairs.3.rest_ref = bf16[12,512,256]{2,1,0:T(8,128)(2,1)S(1)} custom-call(f32[48,128]{1,0:T(8,128)S(1)} %get-tuple-element.32.geo, f32[32,128]{1,0:T(8,128)S(1)} %get-tuple-element.34.mask, f32[8,640]{1,0:T(8,128)S(1)} %copy-done.4, bf16[640,256]{1,0:T(8,128)(2,1)S(1)} %copy-done.3), custom_call_target="tpu_custom_call" | custom-call | flops 1572864000 | bytes 3145728 | tf_op jit(solution)/shard_map/pairs/pallas_call | solution.py:350
  31.8 3.6 %collective-permute-done.5.before_ref = f32[16,1024]{1,0:T(8,128)S(1)} collective-permute-done((f32[16,1024]{1,0:T(8,128)S(1)}, f32[16,1024]{1,0:T(8,128)S(1)}, u32[]{:S(2)}, u32[]{:S(2)}) %collective-permute-start.5) | collective-permute-done | bytes 65568 | tf_op jit(solution)/shard_map/ppermute | solution.py:551
  35.4 2.8 %sweeps.1 = (f32[16,16,49]{2,1,0:T(8,128)}, f32[16,1408]{1,0:T(8,128)S(1)}) custom-call(f32[16,1024]{1,0:T(8,128)S(1)} %collective-permute-done.5.before_ref, f32[16,1024]{1,0:T(8,128)S(1)} %rhs.1.own_ref, f32[16,1024]{1,0:T(8,128)S(1)} %collective-permute-done.6.after_ref, bf16[20,512,256]{2,1,0:T(8,128)(2,1)S(1)} %get-tuple-element.31.t_ref, ...), custom_call_target="tpu_custom_call" | custom-call | flops 805306368 | bytes 8388608 | tf_op jit(solution)/shard_map/sweeps/pallas_call | solution.py:472
  38.2 3.5 %collective-permute-start.7 = (f32[16,1408]{1,0:T(8,128)S(1)}, f32[16,1408]{1,0:T(8,128)S(1)}, u32[]{:S(2)}, u32[]{:S(2)}) collective-permute-start(f32[16,1408]{1,0:T(8,128)S(1)} %get-tuple-element.36.pay_ref), channel_id=1, source_target_pairs={{0,3},{1,2},{2,1},{3,0},{4,7},{5,6},{6,5},{7,4},{8,11},{9,10},{10,... | collective-permute-start | bytes 270344 | tf_op jit(solution)/shard_map/ppermute | solution.py:538
  41.7 1.1 %fock.4.rest_0_ = f32[16,256]{1,0:T(8,128)S(1)} custom-call(f32[16,1408]{1,0:T(8,128)S(1)} %get-tuple-element.36.pay_ref, bf16[256,1280]{1,0:T(8,128)(2,1)S(1)} %copy-done, bf16[256,20480]{1,0:T(8,128)(2,1)S(1)} %get-tuple-element.37.tile_ref), custom_call_target="tpu_custom_call" | custom-call | flops 41943040 | bytes 2621440 | tf_op jit(solution)/shard_map/fock/pallas_call | solution.py:522
  42.8 1.1 %fock.5.rest_0_ = f32[16,256]{1,0:T(8,128)S(1)} custom-call(f32[16,1408]{1,0:T(8,128)S(1)} %collective-permute-done.9.pay_ref, bf16[256,1280]{1,0:T(8,128)(2,1)S(1)} %copy-done, bf16[256,20480]{1,0:T(8,128)(2,1)S(1)} %get-tuple-element.37.tile_ref, f32[16,256]{1,0:T(8,128)S(1)} %fock.4.rest_0_), custom_call_target="tpu_custom_call" | custom-call | flops 41943040 | bytes 2621440 | tf_op jit(solution)/shard_map/fock/pallas_call | solution.py:522
  43.9 1.1 %fock.6.rest_0_ = f32[16,256]{1,0:T(8,128)S(1)} custom-call(f32[16,1408]{1,0:T(8,128)S(1)} %collective-permute-done.8.pay_ref, bf16[256,1280]{1,0:T(8,128)(2,1)S(1)} %copy-done, bf16[256,20480]{1,0:T(8,128)(2,1)S(1)} %get-tuple-element.37.tile_ref, f32[16,256]{1,0:T(8,128)S(1)} %fock.5.rest_0_), custom_call_target="tpu_custom_call" | custom-call | flops 41943040 | bytes 2621440 | tf_op jit(solution)/shard_map/fock/pallas_call | solution.py:522
  45.0 1.1 %fock.7 = f32[16,256]{1,0:T(8,128)S(1)} custom-call(f32[16,1408]{1,0:T(8,128)S(1)} %collective-permute-done.7.pay_ref, bf16[256,1280]{1,0:T(8,128)(2,1)S(1)} %copy-done, bf16[256,20480]{1,0:T(8,128)(2,1)S(1)} %get-tuple-element.37.tile_ref, f32[16,256]{1,0:T(8,128)S(1)} %fock.6.rest_0_), custom_call_target="tpu_custom_call" | custom-call | flops 41943040 | bytes 2621440 | tf_op jit(solution)/shard_map/fock/pallas_call | solution.py:522
  46.1 1.2 %collective-permute-done.10 = f32[16,256]{1,0:T(8,128)S(1)} collective-permute-done((f32[16,256]{1,0:T(8,128)S(1)}, f32[16,256]{1,0:T(8,128)S(1)}, u32[]{:S(2)}, u32[]{:S(2)}) %collective-permute-start.10) | collective-permute-done | bytes 16416 | tf_op jit(solution)/shard_map/ppermute | solution.py:538
  47.4 0.1 collective-permute-start.12
  47.4 1.9 %collective-permute-start.11 = (f32[16,256]{1,0:T(8,128)S(1)}, f32[16,256]{1,0:T(8,128)S(1)}, u32[]{:S(2)}, u32[]{:S(2)}) collective-permute-start(f32[16,256]{1,0:T(8,128)S(1)} %add.12), channel_id=1, source_target_pairs={{0,8},{4,12},{8,16},{12,20},{16,24},{20,28},{24,0},{28,4},{1,9},{5... | collective-permute-start | bytes 49160 | tf_op jit(solution)/shard_map/ppermute | solution.py:543
  49.4 1.7 %collective-permute-done.13 = f32[16,256]{1,0:T(8,128)S(1)} collective-permute-done((f32[16,256]{1,0:T(8,128)S(1)}, f32[16,256]{1,0:T(8,128)S(1)}, u32[]{:S(2)}, u32[]{:S(2)}) %collective-permute-start.13) | collective-permute-done | bytes 16416 | tf_op jit(solution)/shard_map/ppermute | solution.py:543
  51.1 1.0 %collective-permute-done.12 = f32[16,256]{1,0:T(8,128)S(1)} collective-permute-done((f32[16,256]{1,0:T(8,128)S(1)}, f32[16,256]{1,0:T(8,128)S(1)}, u32[]{:S(2)}, u32[]{:S(2)}) %collective-permute-start.12) | collective-permute-done | bytes 16416 | tf_op jit(solution)/shard_map/ppermute | solution.py:543
  52.1 1.6 %collective-permute-done.11 = f32[16,256]{1,0:T(8,128)S(1)} collective-permute-done((f32[16,256]{1,0:T(8,128)S(1)}, f32[16,256]{1,0:T(8,128)S(1)}, u32[]{:S(2)}, u32[]{:S(2)}) %collective-permute-start.11) | collective-permute-done | bytes 16416 | tf_op jit(solution)/shard_map/ppermute | solution.py:543
  53.6 0.6 %add_add_fusion = f32[16,256]{1,0:T(8,128)} fusion(f32[16,256]{1,0:T(8,128)S(1)} %collective-permute-done.13, f32[16,256]{1,0:T(8,128)S(1)} %collective-permute-done.12, f32[16,256]{1,0:T(8,128)S(1)} %add.12, f32[16,256]{1,0:T(8,128)S(1)} %collective-permute-done.11), kind=kLoop, calls=%fused_computation | loop fusion | flops 12288 | bytes 81920 | tf_op jit(solution)/shard_map/add | solution.py:592
  (18 shorter events, 0.0 us)
Async XLA Ops:
  0.6 17.6 %copy-start.3 = (bf16[640,256]{1,0:T(8,128)(2,1)S(1)}, bf16[640,256]{1,0:T(8,128)(2,1)}, u32[]{:S(2)}) copy-start(bf16[640,256]{1,0:T(8,128)(2,1)} %constant.14.clone.w_ref) | copy-start | bytes 983044
  0.6 17.6 %copy-start.4 = (f32[8,640]{1,0:T(8,128)S(1)}, f32[8,640]{1,0:T(8,128)}, u32[]{:S(2)}) copy-start(f32[8,640]{1,0:T(8,128)} %constant.13.clone.dir_ref) | copy-start | bytes 61444
  0.7 24.7 %copy-start.1 = (bf16[640,256]{1,0:T(8,128)(2,1)S(1)}, bf16[640,256]{1,0:T(8,128)(2,1)}, u32[]{:S(2)}) copy-start(bf16[640,256]{1,0:T(8,128)(2,1)} %constant.10.clone.refs_5_) | copy-start | bytes 983044
  1.5 10.8 %collective-permute-start.1 = (f32[24,16]{1,0:T(8,128)S(1)}, f32[24,16]{1,0:T(8,128)S(1)}, u32[]{:S(2)}, u32[]{:S(2)}) collective-permute-start(f32[24,16]{1,0:T(8,128)S(1)} %pack.1.own_ref), channel_id=1, source_target_pairs={{1,0},{2,1},{3,2},{4,3},{5,4},{6,5},{7,6},{8,7},{9,8},{10,9},{11,1... | collective-permute-start | bytes 4616 | tf_op jit(solution)/shard_map/ppermute | solution.py:551
  7.9 6.8 %collective-permute-start = (f32[24,16]{1,0:T(8,128)S(1)}, f32[24,16]{1,0:T(8,128)S(1)}, u32[]{:S(2)}, u32[]{:S(2)}) collective-permute-start(f32[24,16]{1,0:T(8,128)S(1)} %pack.1.own_ref), channel_id=1, source_target_pairs={{0,1},{1,2},{2,3},{3,4},{4,5},{5,6},{6,7},{7,8},{8,9},{9,10},{10,1... | collective-permute-start | bytes 4616 | tf_op jit(solution)/shard_map/ppermute | solution.py:551
  12.3 23.1 %copy-start.2 = (f32[8,128]{1,0:T(8,128)S(1)}, f32[8,128]{1,0:T(8,128)}, u32[]{:S(2)}) copy-start(f32[8,128]{1,0:T(8,128)} %constant.12.clone.sc_ref) | copy-start | bytes 12292
  14.8 26.9 %copy-start = (bf16[256,1280]{1,0:T(8,128)(2,1)S(1)}, bf16[256,1280]{1,0:T(8,128)(2,1)}, u32[]{:S(2)}) copy-start(bf16[256,1280]{1,0:T(8,128)(2,1)} %constant.11.clone.y_ref) | copy-start | bytes 1966084
  14.8 10.6 %collective-permute-start.2 = (s16[16,5248]{1,0:T(8,128)(2,1)S(1)}, s16[16,5248]{1,0:T(8,128)(2,1)S(1)}, u32[]{:S(2)}, u32[]{:S(2)}) collective-permute-start(s16[16,5248]{1,0:T(8,128)(2,1)S(1)} %get-tuple-element.25), channel_id=1, source_target_pairs={{0,1},{1,0},{2,3},{3,2},{4,5},{5,4},{6,7},{7,6},{8,9},{9,8},{10,11... | collective-permute-start | bytes 503816 | tf_op jit(solution)/shard_map/ppermute | solution.py:538
  14.8 10.6 %collective-permute-start.3 = (s16[16,5248]{1,0:T(8,128)(2,1)S(1)}, s16[16,5248]{1,0:T(8,128)(2,1)S(1)}, u32[]{:S(2)}, u32[]{:S(2)}) collective-permute-start(s16[16,5248]{1,0:T(8,128)(2,1)S(1)} %get-tuple-element.26), channel_id=1, source_target_pairs={{0,2},{1,3},{2,0},{3,1},{4,6},{5,7},{6,4},{7,5},{8,10},{9,11},{10,... | collective-permute-start | bytes 503816 | tf_op jit(solution)/shard_map/ppermute | solution.py:538
  14.8 10.6 %collective-permute-start.4 = (s16[16,5248]{1,0:T(8,128)(2,1)S(1)}, s16[16,5248]{1,0:T(8,128)(2,1)S(1)}, u32[]{:S(2)}, u32[]{:S(2)}) collective-permute-start(s16[16,5248]{1,0:T(8,128)(2,1)S(1)} %get-tuple-element.27), channel_id=1, source_target_pairs={{0,3},{1,2},{2,1},{3,0},{4,7},{5,6},{6,5},{7,4},{8,11},{9,10},{10,... | collective-permute-start | bytes 503816 | tf_op jit(solution)/shard_map/ppermute | solution.py:538
  25.8 6.1 %collective-permute-start.6 = (f32[16,1024]{1,0:T(8,128)S(1)}, f32[16,1024]{1,0:T(8,128)S(1)}, u32[]{:S(2)}, u32[]{:S(2)}) collective-permute-start(f32[16,1024]{1,0:T(8,128)S(1)} %rhs.1.own_ref), channel_id=1, source_target_pairs={{1,0},{2,1},{3,2},{4,3},{5,4},{6,5},{7,6},{8,7},{9,8},{10,9},{11,1... | collective-permute-start | bytes 196616 | tf_op jit(solution)/shard_map/ppermute | solution.py:551
  28.0 7.4 %collective-permute-start.5 = (f32[16,1024]{1,0:T(8,128)S(1)}, f32[16,1024]{1,0:T(8,128)S(1)}, u32[]{:S(2)}, u32[]{:S(2)}) collective-permute-start(f32[16,1024]{1,0:T(8,128)S(1)} %rhs.1.own_ref), channel_id=1, source_target_pairs={{0,1},{1,2},{2,3},{3,4},{4,5},{5,6},{6,7},{7,8},{8,9},{9,10},{10,1... | collective-permute-start | bytes 196616 | tf_op jit(solution)/shard_map/ppermute | solution.py:551
  38.2 4.6 %collective-permute-start.9 = (f32[16,1408]{1,0:T(8,128)S(1)}, f32[16,1408]{1,0:T(8,128)S(1)}, u32[]{:S(2)}, u32[]{:S(2)}) collective-permute-start(f32[16,1408]{1,0:T(8,128)S(1)} %get-tuple-element.36.pay_ref), channel_id=1, source_target_pairs={{0,1},{1,0},{2,3},{3,2},{4,5},{5,4},{6,7},{7,6},{8,9},{9,8},{10,11... | collective-permute-start | bytes 270344 | tf_op jit(solution)/shard_map/ppermute | solution.py:538
  38.2 5.7 %collective-permute-start.8 = (f32[16,1408]{1,0:T(8,128)S(1)}, f32[16,1408]{1,0:T(8,128)S(1)}, u32[]{:S(2)}, u32[]{:S(2)}) collective-permute-start(f32[16,1408]{1,0:T(8,128)S(1)} %get-tuple-element.36.pay_ref), channel_id=1, source_target_pairs={{0,2},{1,3},{2,0},{3,1},{4,6},{5,7},{6,4},{7,5},{8,10},{9,11},{10,... | collective-permute-start | bytes 270344 | tf_op jit(solution)/shard_map/ppermute | solution.py:538
  38.2 6.8 %collective-permute-start.7 = (f32[16,1408]{1,0:T(8,128)S(1)}, f32[16,1408]{1,0:T(8,128)S(1)}, u32[]{:S(2)}, u32[]{:S(2)}) collective-permute-start(f32[16,1408]{1,0:T(8,128)S(1)} %get-tuple-element.36.pay_ref), channel_id=1, source_target_pairs={{0,3},{1,2},{2,1},{3,0},{4,7},{5,6},{6,5},{7,4},{8,11},{9,10},{10,... | collective-permute-start | bytes 270344 | tf_op jit(solution)/shard_map/ppermute | solution.py:538
  46.1 1.2 %collective-permute-start.10 = (f32[16,256]{1,0:T(8,128)S(1)}, f32[16,256]{1,0:T(8,128)S(1)}, u32[]{:S(2)}, u32[]{:S(2)}) collective-permute-start(f32[16,256]{1,0:T(8,128)S(1)} %fock.7), channel_id=1, source_target_pairs={{0,4},{4,0},{8,12},{12,8},{16,20},{20,16},{24,28},{28,24},{1,5},{5... | collective-permute-start | bytes 49160 | tf_op jit(solution)/shard_map/ppermute | solution.py:538
  47.4 3.8 %collective-permute-start.13 = (f32[16,256]{1,0:T(8,128)S(1)}, f32[16,256]{1,0:T(8,128)S(1)}, u32[]{:S(2)}, u32[]{:S(2)}) collective-permute-start(f32[16,256]{1,0:T(8,128)S(1)} %add.12), channel_id=1, source_target_pairs={{0,24},{4,28},{8,0},{12,4},{16,8},{20,12},{24,16},{28,20},{1,25},{... | collective-permute-start | bytes 49160 | tf_op jit(solution)/shard_map/ppermute | solution.py:543
  47.4 4.7 %collective-permute-start.12 = (f32[16,256]{1,0:T(8,128)S(1)}, f32[16,256]{1,0:T(8,128)S(1)}, u32[]{:S(2)}, u32[]{:S(2)}) collective-permute-start(f32[16,256]{1,0:T(8,128)S(1)} %add.12), channel_id=1, source_target_pairs={{0,16},{4,20},{8,24},{12,28},{16,0},{20,4},{24,8},{28,12},{1,17},{... | collective-permute-start | bytes 49160 | tf_op jit(solution)/shard_map/ppermute | solution.py:543
  47.4 6.2 %collective-permute-start.11 = (f32[16,256]{1,0:T(8,128)S(1)}, f32[16,256]{1,0:T(8,128)S(1)}, u32[]{:S(2)}, u32[]{:S(2)}) collective-permute-start(f32[16,256]{1,0:T(8,128)S(1)} %add.12), channel_id=1, source_target_pairs={{0,8},{4,12},{8,16},{12,20},{16,24},{20,28},{24,0},{28,4},{1,9},{5... | collective-permute-start | bytes 49160 | tf_op jit(solution)/shard_map/ppermute | solution.py:543

commit v9 on v8

--- a/solution.py
+++ b/solution.py
@@ -439,8 +439,7 @@
 
 
 def sweep_kernel(
-    before_ref, own_ref, after_ref, t_ref, rest_ref, sc_ref, unc_ref, m_ref, out_ref,
-    x, xs, z, zs
+    before_ref, own_ref, after_ref, t_ref, rest_ref, sc_ref, unc_ref, out_ref, x, xs, z, zs
 ):
     own = own_ref.shape[1]
     spheres = own // LP
@@ -455,8 +454,6 @@
     for e in range(0, spheres, 2):
         new = own_ref[:, e * LP : e * LP + 128] + gather_field((t_ref, rest_ref), REACH, z, zs, e)
         new = new * sc_ref[1:2, :]
-        m_ref[e] = new[:, :LM]
-        m_ref[e + 1] = pltpu.roll(new, LP, 1)[:, :LM]
         out_ref[:, e * LP : e * LP + 128] = new
     out_ref[:, own:] = jnp.zeros((NDENS, 384), F32)
     pairs = spheres // 2
@@ -472,11 +469,8 @@
     return pl.pallas_call(
         sweep_kernel,
         in_specs=[VMEM] * 7,
-        out_specs=[VMEM] * 2,
-        out_shape=[
-            jax.ShapeDtypeStruct((spheres, NDENS, LM), F32),
-            jax.ShapeDtypeStruct((NDENS, lanes + 384), F32),
-        ],
+        out_specs=VMEM,
+        out_shape=jax.ShapeDtypeStruct((NDENS, lanes + 384), F32),
         scratch_shapes=[pltpu.VMEM((2 * NDENS, 3 * lanes), BF)] * 2
         + [pltpu.VMEM((2 * NDENS, lanes + 2 * REACH * LP), BF)] * 2,
         compiler_params=PARAMS,
@@ -487,6 +481,25 @@
         ),
         name="sweeps",
     )(before, own, after, t, rest, scales, unc)
+
+
+def moment_kernel(pay_ref, m_ref):
+    for e in range(0, m_ref.shape[0], 2):
+        both = pay_ref[:, e * LP : e * LP + 128]
+        m_ref[e] = both[:, :LM]
+        m_ref[e + 1] = pltpu.roll(both, LP, 1)[:, :LM]
+
+
+def moment_call(pay, spheres):
+    return pl.pallas_call(
+        moment_kernel,
+        in_specs=[VMEM],
+        out_specs=VMEM,
+        out_shape=jax.ShapeDtypeStruct((spheres, NDENS, LM), F32),
+        compiler_params=PARAMS,
+        cost_estimate=pl.CostEstimate(flops=0, bytes_accessed=200000, transcendentals=0),
+        name="moments",
+    )(pay)
 
 
 def fock_kernel(k, pay_ref, y_ref, tile_ref, *rest):
@@ -576,12 +589,14 @@
     below, above = from_beside(rhs)
     mask, _ = lax.optimization_barrier((mask, rhs))
     (rest,) = pair_call(later, consts, known=(geo, mask))
-    moments, pay = sweep_call(below, rhs, above, t, rest, scales, unc)
+    pay = sweep_call(below, rhs, above, t, rest, scales, unc)
     others = [trade(pay, "fit", k) for k in range(1, fits)]
     fock = fock_call(0, pay, wt, near_tiles, width)
     for k in range(1, fits):
         fock = fock_call(k, others[k - 1], wt, near_tiles, width, fock)
     fock = fock + trade(fock, "sph", 1)
+    held, _ = lax.optimization_barrier((pay, fock))
+    moments = moment_call(held, spheres)
     bit = 2
     while bit < sphs:
         ks = [k for k in (bit, 2 * bit, 3 * bit) if k < sphs]

time: 54.5 us -> 53.7 us (0.985)
  waiting for transfers between devices: 11.5 us -> 10.7 us
    ppermute x3, waiting for transfers between devices: 4.25 us -> 3.51 us  [shift(): return lax.ppermute(x, axis, [(i, (i + k) % count) for i in range(count)])]
    pallas_call x1 -> x2, Pallas kernels: 2.81 us -> 2.81 us  [the longest x1 2.08 us: sweep_call(): pl.pallas_call(sweep_kernel, in_specs=[VMEM] * 7, out_specs=VMEM, out_sha...]
  transfers between devices with their start and end apart: 14 -> 14, of which waited for: 6 -> 6; matrix products, arithmetic and copies ran while one was open for 0% -> 0% of each run, Pallas kernels for 34% -> 36%
where the time goes in v9:
time: 53.7 us; the launch traced here: 53.5 us
  Pallas kernels  23.7 us (44%)
  starting transfers between devices  17.7 us (33%)
  waiting for transfers between devices  10.7 us (20%)
  between operations  0.78 us (1%)
  other arithmetic  0.62 us (1%)
    pallas_call x2, Pallas kernels, pair_call(): pl.pallas_call(functools.partial(kernel, quads), in_specs=[VMEM] * (len(a...  10.9 us
    ppermute x4, starting transfers between devices, from_beside(): return (lax.ppermute(x, axes, up), lax.ppermute(x, axes, down))  8.68 us
    ppermute x7, starting transfers between devices, trade(): return lax.ppermute(x, axis, [(i, i ^ k) for i in range(count)])  6.98 us
    ppermute x4, waiting for transfers between devices, from_beside(): return (lax.ppermute(x, axes, up), lax.ppermute(x, axes, down))  5.98 us
    pallas_call x4, Pallas kernels, fock_call(): pl.pallas_call(functools.partial(fock_kernel, k), in_specs=[VMEM] * (3 +...  4.4 us
    pallas_call x1, Pallas kernels, phi_call(): pl.pallas_call(functools.partial(phi_kernel, width), in_specs=[pl.BlockSp...  4.39 us
    ppermute x3, waiting for transfers between devices, shift(): return lax.ppermute(x, axis, [(i, (i + k) % count) for i in range(count)])  3.51 us
    pallas_call x1, Pallas kernels, sweep_call(): pl.pallas_call(sweep_kernel, in_specs=[VMEM] * 7, out_specs=VMEM, out_sha...  2.08 us
  transfers between devices with their start and end apart: 14, of which 6 were waited for; matrix products, arithmetic and copies ran while one was open for 0% of the time, Pallas kernels for 36%

profile of v9, /device:TPU:0, one launch (start us, length us, event | category | flops | bytes accessed | tf_op | source)
XLA Modules:
  0.0 53.5 jit_solution(18317082730168839818)
XLA Ops:
  0.6 0.0 copy-start.3
  0.6 0.0 copy-start.4
  0.7 0.0 copy-start.1
  0.7 0.8 %pack.1.own_ref = f32[24,16]{1,0:T(8,128)S(1)} custom-call(f32[3,16]{1,0:T(4,128)} %centre_ref.1, f32[1,16]{1,0:T(1,128)} %bitcast.2, s32[16,16]{1,0:T(8,128)} %nbr_ref.1, s32[1,16]{1,0:T(1,128)} %bitcast.3), custom_call_target="tpu_custom_call" | custom-call | tf_op jit(solution)/shard_map/pack/pallas_call | solution.py:203
  1.5 6.4 %collective-permute-start.1 = (f32[24,16]{1,0:T(8,128)S(1)}, f32[24,16]{1,0:T(8,128)S(1)}, u32[]{:S(2)}, u32[]{:S(2)}) collective-permute-start(f32[24,16]{1,0:T(8,128)S(1)} %pack.1.own_ref), channel_id=1, source_target_pairs={{1,0},{2,1},{3,2},{4,3},{5,4},{6,5},{7,6},{8,7},{9,8},{10,9},{11,1... | collective-permute-start | bytes 4616 | tf_op jit(solution)/shard_map/ppermute | solution.py:564
  7.9 4.4 %phi.1 = (f32[16,5120]{1,0:T(8,128)S(1)}, s16[16,5248]{1,0:T(8,128)(2,1)S(1)}, s16[16,5248]{1,0:T(8,128)(2,1)S(1)}, s16[16,5248]{1,0:T(8,128)(2,1)S(1)}, bf16[256,20480]{1,0:T(8,128)(2,1)S(1)}) custom-call(bf16[16,256]{1,0:T(8,128)(2,1)} %far_coef_ref.1, bf16[256,20480]{1,0:T(8,128)(2,1)} %far_ref.1), custom_call_target="tpu_custom_call" | custom-call | flops 167772160 | bytes 11796480 | tf_op jit(solution)/shard_map/phi/pallas_call | solution.py:160
  12.3 0.0 copy-start.2
  12.4 2.4 %collective-permute-done.before_ref = f32[24,16]{1,0:T(8,128)S(1)} collective-permute-done((f32[24,16]{1,0:T(8,128)S(1)}, f32[24,16]{1,0:T(8,128)S(1)}, u32[]{:S(2)}, u32[]{:S(2)}) %collective-permute-start) | collective-permute-done | bytes 1568 | tf_op jit(solution)/shard_map/ppermute | solution.py:564
  14.8 3.5 %collective-permute-start.4 = (s16[16,5248]{1,0:T(8,128)(2,1)S(1)}, s16[16,5248]{1,0:T(8,128)(2,1)S(1)}, u32[]{:S(2)}, u32[]{:S(2)}) collective-permute-start(s16[16,5248]{1,0:T(8,128)(2,1)S(1)} %get-tuple-element.26), channel_id=1, source_target_pairs={{0,3},{1,2},{2,1},{3,0},{4,7},{5,6},{6,5},{7,4},{8,11},{9,10},{10,... | collective-permute-start | bytes 503816 | tf_op jit(solution)/shard_map/ppermute | solution.py:551
  18.3 7.1 %pairs.2 = (bf16[20,512,256]{2,1,0:T(8,128)(2,1)S(1)}, f32[5,1,1280]{2,1,0:T(1,128)S(1)}, f32[48,128]{1,0:T(8,128)S(1)}, f32[32,128]{1,0:T(8,128)S(1)}) custom-call(f32[24,16]{1,0:T(8,128)S(1)} %collective-permute-done.before_ref, f32[24,16]{1,0:T(8,128)S(1)} %pack.1.own_ref, f32[24,16]{1,0:T(8,128)S(1)} %collective-permute-done.1.after_ref, ...), custom_call_target="tpu_custom_call" | custom-call | flops 2621440000 | bytes 5242880 | tf_op jit(solution)/shard_map/pairs/pallas_call | solution.py:350
  25.4 0.0 collective-permute-done.3.refs_2_
  25.4 0.4 rhs.1.own_ref
  25.8 2.2 %collective-permute-start.6 = (f32[16,1024]{1,0:T(8,128)S(1)}, f32[16,1024]{1,0:T(8,128)S(1)}, u32[]{:S(2)}, u32[]{:S(2)}) collective-permute-start(f32[16,1024]{1,0:T(8,128)S(1)} %rhs.1.own_ref), channel_id=1, source_target_pairs={{1,0},{2,1},{3,2},{4,3},{5,4},{6,5},{7,6},{8,7},{9,8},{10,9},{11,1... | collective-permute-start | bytes 196616 | tf_op jit(solution)/shard_map/ppermute | solution.py:564
  28.0 0.0 collective-permute-start.5
  28.0 3.8 %pairs.3.rest_ref = bf16[12,512,256]{2,1,0:T(8,128)(2,1)S(1)} custom-call(f32[48,128]{1,0:T(8,128)S(1)} %get-tuple-element.31.geo, f32[32,128]{1,0:T(8,128)S(1)} %get-tuple-element.33.mask, f32[8,640]{1,0:T(8,128)S(1)} %copy-done.4, bf16[640,256]{1,0:T(8,128)(2,1)S(1)} %copy-done.3), custom_call_target="tpu_custom_call" | custom-call | flops 1572864000 | bytes 3145728 | tf_op jit(solution)/shard_map/pairs/pallas_call | solution.py:350
  31.8 3.6 %collective-permute-done.5.before_ref = f32[16,1024]{1,0:T(8,128)S(1)} collective-permute-done((f32[16,1024]{1,0:T(8,128)S(1)}, f32[16,1024]{1,0:T(8,128)S(1)}, u32[]{:S(2)}, u32[]{:S(2)}) %collective-permute-start.5) | collective-permute-done | bytes 65568 | tf_op jit(solution)/shard_map/ppermute | solution.py:564
  35.4 2.1 %sweeps.1.pay_ref = f32[16,1408]{1,0:T(8,128)S(1)} custom-call(f32[16,1024]{1,0:T(8,128)S(1)} %collective-permute-done.5.before_ref, f32[16,1024]{1,0:T(8,128)S(1)} %rhs.1.own_ref, f32[16,1024]{1,0:T(8,128)S(1)} %collective-permute-done.6.after_ref, bf16[20,512,256]{2,1,0:T(8,128)(2,1)S(1)} %get-tuple-element.30.t_ref, ...), custom_call_target="tpu_custom_call" | custom-call | flops 805306368 | bytes 8388608 | tf_op jit(solution)/shard_map/sweeps/pallas_call | solution.py:469
  37.5 0.0 collective-permute-start.9
  37.5 0.1 collective-permute-start.8
  37.6 3.4 %collective-permute-start.7 = (f32[16,1408]{1,0:T(8,128)S(1)}, f32[16,1408]{1,0:T(8,128)S(1)}, u32[]{:S(2)}, u32[]{:S(2)}) collective-permute-start(f32[16,1408]{1,0:T(8,128)S(1)} %sweeps.1.pay_ref), channel_id=1, source_target_pairs={{0,3},{1,2},{2,1},{3,0},{4,7},{5,6},{6,5},{7,4},{8,11},{9,10},{10,... | collective-permute-start | bytes 270344 | tf_op jit(solution)/shard_map/ppermute | solution.py:551
  41.0 1.1 %fock.4.rest_0_ = f32[16,256]{1,0:T(8,128)S(1)} custom-call(f32[16,1408]{1,0:T(8,128)S(1)} %sweeps.1.pay_ref, bf16[256,1280]{1,0:T(8,128)(2,1)S(1)} %copy-done, bf16[256,20480]{1,0:T(8,128)(2,1)S(1)} %get-tuple-element.34.tile_ref), custom_call_target="tpu_custom_call" | custom-call | flops 41943040 | bytes 2621440 | tf_op jit(solution)/shard_map/fock/pallas_call | solution.py:535
  42.1 1.1 %fock.5.rest_0_ = f32[16,256]{1,0:T(8,128)S(1)} custom-call(f32[16,1408]{1,0:T(8,128)S(1)} %collective-permute-done.9.pay_ref, bf16[256,1280]{1,0:T(8,128)(2,1)S(1)} %copy-done, bf16[256,20480]{1,0:T(8,128)(2,1)S(1)} %get-tuple-element.34.tile_ref, f32[16,256]{1,0:T(8,128)S(1)} %fock.4.rest_0_), custom_call_target="tpu_custom_call" | custom-call | flops 41943040 | bytes 2621440 | tf_op jit(solution)/shard_map/fock/pallas_call | solution.py:535
  43.2 1.1 %fock.6.rest_0_ = f32[16,256]{1,0:T(8,128)S(1)} custom-call(f32[16,1408]{1,0:T(8,128)S(1)} %collective-permute-done.8.pay_ref, bf16[256,1280]{1,0:T(8,128)(2,1)S(1)} %copy-done, bf16[256,20480]{1,0:T(8,128)(2,1)S(1)} %get-tuple-element.34.tile_ref, f32[16,256]{1,0:T(8,128)S(1)} %fock.5.rest_0_), custom_call_target="tpu_custom_call" | custom-call | flops 41943040 | bytes 2621440 | tf_op jit(solution)/shard_map/fock/pallas_call | solution.py:535
  44.3 1.1 %fock.7 = f32[16,256]{1,0:T(8,128)S(1)} custom-call(f32[16,1408]{1,0:T(8,128)S(1)} %collective-permute-done.7.pay_ref, bf16[256,1280]{1,0:T(8,128)(2,1)S(1)} %copy-done, bf16[256,20480]{1,0:T(8,128)(2,1)S(1)} %get-tuple-element.34.tile_ref, f32[16,256]{1,0:T(8,128)S(1)} %fock.6.rest_0_), custom_call_target="tpu_custom_call" | custom-call | flops 41943040 | bytes 2621440 | tf_op jit(solution)/shard_map/fock/pallas_call | solution.py:535
  45.4 1.2 %collective-permute-done.10 = f32[16,256]{1,0:T(8,128)S(1)} collective-permute-done((f32[16,256]{1,0:T(8,128)S(1)}, f32[16,256]{1,0:T(8,128)S(1)}, u32[]{:S(2)}, u32[]{:S(2)}) %collective-permute-start.10) | collective-permute-done | bytes 16416 | tf_op jit(solution)/shard_map/ppermute | solution.py:551
  46.6 0.1 collective-permute-start.12
  46.7 1.9 %collective-permute-start.11 = (f32[16,256]{1,0:T(8,128)S(1)}, f32[16,256]{1,0:T(8,128)S(1)}, u32[]{:S(2)}, u32[]{:S(2)}) collective-permute-start(f32[16,256]{1,0:T(8,128)S(1)} %add.12), channel_id=1, source_target_pairs={{0,8},{4,12},{8,16},{12,20},{16,24},{20,28},{24,0},{28,4},{1,9},{5... | collective-permute-start | bytes 49160 | tf_op jit(solution)/shard_map/ppermute | solution.py:556
  48.7 0.7 %moments.1 = f32[16,16,49]{2,1,0:T(8,128)} custom-call(f32[16,1408]{1,0:T(8,128)S(1)} %sweeps.1.pay_ref), custom_call_target="tpu_custom_call" | custom-call | bytes 200000 | tf_op jit(solution)/shard_map/moments/pallas_call | solution.py:494
  49.4 1.0 %collective-permute-done.13 = f32[16,256]{1,0:T(8,128)S(1)} collective-permute-done((f32[16,256]{1,0:T(8,128)S(1)}, f32[16,256]{1,0:T(8,128)S(1)}, u32[]{:S(2)}, u32[]{:S(2)}) %collective-permute-start.13) | collective-permute-done | bytes 16416 | tf_op jit(solution)/shard_map/ppermute | solution.py:556
  50.4 1.0 %collective-permute-done.12 = f32[16,256]{1,0:T(8,128)S(1)} collective-permute-done((f32[16,256]{1,0:T(8,128)S(1)}, f32[16,256]{1,0:T(8,128)S(1)}, u32[]{:S(2)}, u32[]{:S(2)}) %collective-permute-start.12) | collective-permute-done | bytes 16416 | tf_op jit(solution)/shard_map/ppermute | solution.py:556
  51.3 1.6 %collective-permute-done.11 = f32[16,256]{1,0:T(8,128)S(1)} collective-permute-done((f32[16,256]{1,0:T(8,128)S(1)}, f32[16,256]{1,0:T(8,128)S(1)}, u32[]{:S(2)}, u32[]{:S(2)}) %collective-permute-start.11) | collective-permute-done | bytes 16416 | tf_op jit(solution)/shard_map/ppermute | solution.py:556
  52.9 0.6 %add_add_fusion = f32[16,256]{1,0:T(8,128)} fusion(f32[16,256]{1,0:T(8,128)S(1)} %collective-permute-done.13, f32[16,256]{1,0:T(8,128)S(1)} %collective-permute-done.12, f32[16,256]{1,0:T(8,128)S(1)} %add.12, f32[16,256]{1,0:T(8,128)S(1)} %collective-permute-done.11), kind=kLoop, calls=%fused_computation | loop fusion | flops 12288 | bytes 81920 | tf_op jit(solution)/shard_map/add | solution.py:607
  (19 shorter events, 0.0 us)
Async XLA Ops:
  0.6 17.6 %copy-start.3 = (bf16[640,256]{1,0:T(8,128)(2,1)S(1)}, bf16[640,256]{1,0:T(8,128)(2,1)}, u32[]{:S(2)}) copy-start(bf16[640,256]{1,0:T(8,128)(2,1)} %constant.14.clone.w_ref) | copy-start | bytes 983044
  0.6 17.6 %copy-start.4 = (f32[8,640]{1,0:T(8,128)S(1)}, f32[8,640]{1,0:T(8,128)}, u32[]{:S(2)}) copy-start(f32[8,640]{1,0:T(8,128)} %constant.13.clone.dir_ref) | copy-start | bytes 61444
  0.7 24.7 %copy-start.1 = (bf16[640,256]{1,0:T(8,128)(2,1)S(1)}, bf16[640,256]{1,0:T(8,128)(2,1)}, u32[]{:S(2)}) copy-start(bf16[640,256]{1,0:T(8,128)(2,1)} %constant.10.clone.refs_5_) | copy-start | bytes 983044
  1.5 10.8 %collective-permute-start.1 = (f32[24,16]{1,0:T(8,128)S(1)}, f32[24,16]{1,0:T(8,128)S(1)}, u32[]{:S(2)}, u32[]{:S(2)}) collective-permute-start(f32[24,16]{1,0:T(8,128)S(1)} %pack.1.own_ref), channel_id=1, source_target_pairs={{1,0},{2,1},{3,2},{4,3},{5,4},{6,5},{7,6},{8,7},{9,8},{10,9},{11,1... | collective-permute-start | bytes 4616 | tf_op jit(solution)/shard_map/ppermute | solution.py:564
  7.9 6.8 %collective-permute-start = (f32[24,16]{1,0:T(8,128)S(1)}, f32[24,16]{1,0:T(8,128)S(1)}, u32[]{:S(2)}, u32[]{:S(2)}) collective-permute-start(f32[24,16]{1,0:T(8,128)S(1)} %pack.1.own_ref), channel_id=1, source_target_pairs={{0,1},{1,2},{2,3},{3,4},{4,5},{5,6},{6,7},{7,8},{8,9},{9,10},{10,1... | collective-permute-start | bytes 4616 | tf_op jit(solution)/shard_map/ppermute | solution.py:564
  12.3 23.1 %copy-start.2 = (f32[8,128]{1,0:T(8,128)S(1)}, f32[8,128]{1,0:T(8,128)}, u32[]{:S(2)}) copy-start(f32[8,128]{1,0:T(8,128)} %constant.12.clone.sc_ref) | copy-start | bytes 12292
  14.8 26.2 %copy-start = (bf16[256,1280]{1,0:T(8,128)(2,1)S(1)}, bf16[256,1280]{1,0:T(8,128)(2,1)}, u32[]{:S(2)}) copy-start(bf16[256,1280]{1,0:T(8,128)(2,1)} %constant.11.clone.y_ref) | copy-start | bytes 1966084
  14.8 10.6 %collective-permute-start.2 = (s16[16,5248]{1,0:T(8,128)(2,1)S(1)}, s16[16,5248]{1,0:T(8,128)(2,1)S(1)}, u32[]{:S(2)}, u32[]{:S(2)}) collective-permute-start(s16[16,5248]{1,0:T(8,128)(2,1)S(1)} %get-tuple-element.24), channel_id=1, source_target_pairs={{0,1},{1,0},{2,3},{3,2},{4,5},{5,4},{6,7},{7,6},{8,9},{9,8},{10,11... | collective-permute-start | bytes 503816 | tf_op jit(solution)/shard_map/ppermute | solution.py:551
  14.8 10.6 %collective-permute-start.3 = (s16[16,5248]{1,0:T(8,128)(2,1)S(1)}, s16[16,5248]{1,0:T(8,128)(2,1)S(1)}, u32[]{:S(2)}, u32[]{:S(2)}) collective-permute-start(s16[16,5248]{1,0:T(8,128)(2,1)S(1)} %get-tuple-element.25), channel_id=1, source_target_pairs={{0,2},{1,3},{2,0},{3,1},{4,6},{5,7},{6,4},{7,5},{8,10},{9,11},{10,... | collective-permute-start | bytes 503816 | tf_op jit(solution)/shard_map/ppermute | solution.py:551
  14.8 10.6 %collective-permute-start.4 = (s16[16,5248]{1,0:T(8,128)(2,1)S(1)}, s16[16,5248]{1,0:T(8,128)(2,1)S(1)}, u32[]{:S(2)}, u32[]{:S(2)}) collective-permute-start(s16[16,5248]{1,0:T(8,128)(2,1)S(1)} %get-tuple-element.26), channel_id=1, source_target_pairs={{0,3},{1,2},{2,1},{3,0},{4,7},{5,6},{6,5},{7,4},{8,11},{9,10},{10,... | collective-permute-start | bytes 503816 | tf_op jit(solution)/shard_map/ppermute | solution.py:551
  25.8 6.1 %collective-permute-start.6 = (f32[16,1024]{1,0:T(8,128)S(1)}, f32[16,1024]{1,0:T(8,128)S(1)}, u32[]{:S(2)}, u32[]{:S(2)}) collective-permute-start(f32[16,1024]{1,0:T(8,128)S(1)} %rhs.1.own_ref), channel_id=1, source_target_pairs={{1,0},{2,1},{3,2},{4,3},{5,4},{6,5},{7,6},{8,7},{9,8},{10,9},{11,1... | collective-permute-start | bytes 196616 | tf_op jit(solution)/shard_map/ppermute | solution.py:564
  28.0 7.4 %collective-permute-start.5 = (f32[16,1024]{1,0:T(8,128)S(1)}, f32[16,1024]{1,0:T(8,128)S(1)}, u32[]{:S(2)}, u32[]{:S(2)}) collective-permute-start(f32[16,1024]{1,0:T(8,128)S(1)} %rhs.1.own_ref), channel_id=1, source_target_pairs={{0,1},{1,2},{2,3},{3,4},{4,5},{5,6},{6,7},{7,8},{8,9},{9,10},{10,1... | collective-permute-start | bytes 196616 | tf_op jit(solution)/shard_map/ppermute | solution.py:564
  37.5 4.6 %collective-permute-start.9 = (f32[16,1408]{1,0:T(8,128)S(1)}, f32[16,1408]{1,0:T(8,128)S(1)}, u32[]{:S(2)}, u32[]{:S(2)}) collective-permute-start(f32[16,1408]{1,0:T(8,128)S(1)} %sweeps.1.pay_ref), channel_id=1, source_target_pairs={{0,1},{1,0},{2,3},{3,2},{4,5},{5,4},{6,7},{7,6},{8,9},{9,8},{10,11... | collective-permute-start | bytes 270344 | tf_op jit(solution)/shard_map/ppermute | solution.py:551
  37.5 5.7 %collective-permute-start.8 = (f32[16,1408]{1,0:T(8,128)S(1)}, f32[16,1408]{1,0:T(8,128)S(1)}, u32[]{:S(2)}, u32[]{:S(2)}) collective-permute-start(f32[16,1408]{1,0:T(8,128)S(1)} %sweeps.1.pay_ref), channel_id=1, source_target_pairs={{0,2},{1,3},{2,0},{3,1},{4,6},{5,7},{6,4},{7,5},{8,10},{9,11},{10,... | collective-permute-start | bytes 270344 | tf_op jit(solution)/shard_map/ppermute | solution.py:551
  37.6 6.7 %collective-permute-start.7 = (f32[16,1408]{1,0:T(8,128)S(1)}, f32[16,1408]{1,0:T(8,128)S(1)}, u32[]{:S(2)}, u32[]{:S(2)}) collective-permute-start(f32[16,1408]{1,0:T(8,128)S(1)} %sweeps.1.pay_ref), channel_id=1, source_target_pairs={{0,3},{1,2},{2,1},{3,0},{4,7},{5,6},{6,5},{7,4},{8,11},{9,10},{10,... | collective-permute-start | bytes 270344 | tf_op jit(solution)/shard_map/ppermute | solution.py:551
  45.4 1.2 %collective-permute-start.10 = (f32[16,256]{1,0:T(8,128)S(1)}, f32[16,256]{1,0:T(8,128)S(1)}, u32[]{:S(2)}, u32[]{:S(2)}) collective-permute-start(f32[16,256]{1,0:T(8,128)S(1)} %fock.7), channel_id=1, source_target_pairs={{0,4},{4,0},{8,12},{12,8},{16,20},{20,16},{24,28},{28,24},{1,5},{5... | collective-permute-start | bytes 49160 | tf_op jit(solution)/shard_map/ppermute | solution.py:551
  46.6 3.8 %collective-permute-start.13 = (f32[16,256]{1,0:T(8,128)S(1)}, f32[16,256]{1,0:T(8,128)S(1)}, u32[]{:S(2)}, u32[]{:S(2)}) collective-permute-start(f32[16,256]{1,0:T(8,128)S(1)} %add.12), channel_id=1, source_target_pairs={{0,24},{4,28},{8,0},{12,4},{16,8},{20,12},{24,16},{28,20},{1,25},{... | collective-permute-start | bytes 49160 | tf_op jit(solution)/shard_map/ppermute | solution.py:556
  46.6 4.7 %collective-permute-start.12 = (f32[16,256]{1,0:T(8,128)S(1)}, f32[16,256]{1,0:T(8,128)S(1)}, u32[]{:S(2)}, u32[]{:S(2)}) collective-permute-start(f32[16,256]{1,0:T(8,128)S(1)} %add.12), channel_id=1, source_target_pairs={{0,16},{4,20},{8,24},{12,28},{16,0},{20,4},{24,8},{28,12},{1,17},{... | collective-permute-start | bytes 49160 | tf_op jit(solution)/shard_map/ppermute | solution.py:556
  46.7 6.2 %collective-permute-start.11 = (f32[16,256]{1,0:T(8,128)S(1)}, f32[16,256]{1,0:T(8,128)S(1)}, u32[]{:S(2)}, u32[]{:S(2)}) collective-permute-start(f32[16,256]{1,0:T(8,128)S(1)} %add.12), channel_id=1, source_target_pairs={{0,8},{4,12},{8,16},{12,20},{16,24},{20,28},{24,0},{28,4},{1,9},{5... | collective-permute-start | bytes 49160 | tf_op jit(solution)/shard_map/ppermute | solution.py:556

commit v10 on v9

--- a/solution.py
+++ b/solution.py
@@ -130,8 +130,22 @@
     return ref[:, ls].astype(jnp.int32).astype(F32) * jnp.exp2(power)
 
 
+def pack(c, r, n, k, out_ref):
+    out_ref[...] = jnp.zeros_like(out_ref)
+    out_ref[0:3, :] = c[...]
+    out_ref[3:4, :] = r[...]
+    out_ref[4:5, :] = k[...].astype(F32)
+    out_ref[8:, :] = n[...].astype(F32)
+
+
 def phi_kernel(width, far_coef_ref, far_ref, *rest):
-    outs, (tile_ref, full, coef_ref, sem, coef_sem) = rest[:-5], rest[-5:]
+    geometry, outs = rest[:4], rest[4:-11]
+    tile_ref, pack_ref, full, coef_ref, sem, coef_sem, *held = rest[-11:]
+    small = [
+        pltpu.make_async_copy(a, b, held[4].at[i]) for i, (a, b) in enumerate(zip(geometry, held))
+    ]
+    for copy in small:
+        copy.start()
     first = pltpu.make_async_copy(far_coef_ref, coef_ref, coef_sem)
     first.start()
     per = width // PIECE
@@ -141,6 +155,9 @@
         at = chunk_piece(k, width, p)
         copies.append(pltpu.make_async_copy(far_ref.at[:, at], tile_ref.at[:, at], sem.at[i]))
         copies[-1].start()
+    for copy in small:
+        copy.wait()
+    pack(*held[:4], pack_ref)
     first.wait()
     for (k, p), copy in zip(todo, copies):
         copy.wait()
@@ -154,22 +171,28 @@
             outs[k][:, width:] = tail
 
 
-def phi_call(coefs, tiles, width):
+def phi_call(coefs, tiles, geometry, width):
     aux, points = tiles.shape
     count = points // width
+    spheres = geometry[0].shape[1]
     return pl.pallas_call(
         functools.partial(phi_kernel, width),
-        in_specs=[pl.BlockSpec(memory_space=pltpu.HBM)] * 2,
-        out_specs=[VMEM] * (count + 1),
+        in_specs=[pl.BlockSpec(memory_space=pltpu.HBM)] * 6,
+        out_specs=[VMEM] * (count + 2),
         out_shape=[jax.ShapeDtypeStruct((NDENS, width), F32)]
         + [jax.ShapeDtypeStruct((NDENS, width + 128), jnp.int16)] * (count - 1)
-        + [jax.ShapeDtypeStruct(tiles.shape, tiles.dtype)],
+        + [
+            jax.ShapeDtypeStruct(tiles.shape, tiles.dtype),
+            jax.ShapeDtypeStruct((8 + spheres, spheres), F32),
+        ],
         scratch_shapes=[
             pltpu.VMEM((NDENS, width), F32),
             pltpu.VMEM(coefs.shape, coefs.dtype),
             pltpu.SemaphoreType.DMA((points // PIECE,)),
             pltpu.SemaphoreType.DMA,
-        ],
+        ]
+        + [pltpu.VMEM(a.shape, a.dtype) for a in geometry]
+        + [pltpu.SemaphoreType.DMA((4,))],
         compiler_params=PARAMS,
         cost_estimate=pl.CostEstimate(
             flops=2 * NDENS * aux * points,
@@ -177,39 +200,7 @@
             transcendentals=0,
         ),
         name="phi",
-    )(*(pltpu.with_memory_space_constraint(a, pltpu.HBM) for a in (coefs, tiles)))
-
-
-def pack_kernel(centre_ref, radius_ref, nbr_ref, cnt_ref, out_ref, c, r, n, k, sem):
-    copies = [
-        pltpu.make_async_copy(a, b, sem.at[i])
-        for i, (a, b) in enumerate(zip((centre_ref, radius_ref, nbr_ref, cnt_ref), (c, r, n, k)))
-    ]
-    for copy in copies:
-        copy.start()
-    for copy in copies:
-        copy.wait()
-    spheres, slots = n.shape
-    out_ref[...] = jnp.zeros_like(out_ref)
-    out_ref[0:3, :] = c[...]
-    out_ref[3:4, :] = r[...]
-    out_ref[4:5, :] = k[...].astype(F32)
-    out_ref[8:, :] = n[...].astype(F32)
-
-
-def pack_call(centres, radii, neighbours, counts):
-    spheres, slots = neighbours.shape
-    args = (centres, radii.reshape(1, spheres), neighbours, counts.reshape(1, spheres))
-    return pl.pallas_call(
-        pack_kernel,
-        in_specs=[pl.BlockSpec(memory_space=pltpu.HBM)] * 4,
-        out_specs=VMEM,
-        out_shape=jax.ShapeDtypeStruct((8 + spheres, spheres), F32),
-        scratch_shapes=[pltpu.VMEM(a.shape, a.dtype) for a in args]
-        + [pltpu.SemaphoreType.DMA((4,))],
-        compiler_params=PARAMS,
-        name="pack",
-    )(*(pltpu.with_memory_space_constraint(a, pltpu.HBM) for a in args))
+    )(*(pltpu.with_memory_space_constraint(a, pltpu.HBM) for a in (coefs, tiles, *geometry)))
 
 
 def pair_build(e, geo, mask, dir_ref, bh):
@@ -574,10 +565,9 @@
     scales = jnp.asarray(lane_scales())
 
     width = spheres * NG
-    own = pack_call(centres, radii, neighbours, counts)
+    geometry = (centres, radii.reshape(1, spheres), neighbours, counts.reshape(1, spheres))
+    *phis, near_tiles, own = phi_call(coefs, tiles, geometry, width)
     before, after = from_beside(own)
-    *phis, near_tiles = phi_call(coefs, tiles, width)
-    phis, before, after = lax.optimization_barrier((phis, before, after))
     got = [trade(phis[k], "fit", k) for k in range(1, fits)]
     below_own, last_own = REACH // QUAD, (REACH + spheres) // QUAD
     soon = [*range(below_own - SOONER, last_own)]

time: 53.7 us -> 54.8 us (1.020)
  Pallas kernels: 23.7 us -> 24.8 us
    pallas_call x1, Pallas kernels: 4.39 us -> 6.38 us  [phi_call(): pl.pallas_call(functools.partial(phi_kernel, width), in_specs=[pl.BlockSp...]
    pallas_call x1 -> x0, Pallas kernels: 0.83 us -> none  [pack_call(): pl.pallas_call(pack_kernel, in_specs=[pl.BlockSpec(memory_space=pltpu.HBM...]
  transfers between devices with their start and end apart: 14 -> 14, of which waited for: 6 -> 6; matrix products, arithmetic and copies ran while one was open for 0% -> 0% of each run, Pallas kernels for 36% -> 27%
where the time goes in v10:
time: 54.8 us; the launch traced here: 54.6 us
  Pallas kernels  24.8 us (45%)
  starting transfers between devices  17.5 us (32%)
  waiting for transfers between devices  10.9 us (20%)
  between operations  0.76 us (1%)
  other arithmetic  0.62 us (1%)
    pallas_call x2, Pallas kernels, pair_call(): pl.pallas_call(functools.partial(kernel, quads), in_specs=[VMEM] * (len(a...  10.9 us
    ppermute x4, starting transfers between devices, from_beside(): return (lax.ppermute(x, axes, up), lax.ppermute(x, axes, down))  8.52 us
    ppermute x7, starting transfers between devices, trade(): return lax.ppermute(x, axis, [(i, i ^ k) for i in range(count)])  6.98 us
    pallas_call x1, Pallas kernels, phi_call(): pl.pallas_call(functools.partial(phi_kernel, width), in_specs=[pl.BlockSp...  6.38 us
    ppermute x4, waiting for transfers between devices, from_beside(): return (lax.ppermute(x, axes, up), lax.ppermute(x, axes, down))  6.15 us
    pallas_call x4, Pallas kernels, fock_call(): pl.pallas_call(functools.partial(fock_kernel, k), in_specs=[VMEM] * (3 +...  4.4 us
    ppermute x3, waiting for transfers between devices, shift(): return lax.ppermute(x, axis, [(i, (i + k) % count) for i in range(count)])  3.51 us
    pallas_call x1, Pallas kernels, sweep_call(): pl.pallas_call(sweep_kernel, in_specs=[VMEM] * 7, out_specs=VMEM, out_sha...  2.08 us
  transfers between devices with their start and end apart: 14, of which 6 were waited for; matrix products, arithmetic and copies ran while one was open for 0% of the time, Pallas kernels for 27%

profile of v10, /device:TPU:0, one launch (start us, length us, event | category | flops | bytes accessed | tf_op | source)
XLA Modules:
  0.0 54.6 jit_solution(16993606727155497990)
XLA Ops:
  0.6 0.0 copy-start.3
  0.6 0.0 copy-start.4
  0.7 0.0 copy-start.1
  0.7 6.4 %phi.1 = (f32[16,5120]{1,0:T(8,128)S(1)}, s16[16,5248]{1,0:T(8,128)(2,1)S(1)}, s16[16,5248]{1,0:T(8,128)(2,1)S(1)}, s16[16,5248]{1,0:T(8,128)(2,1)S(1)}, bf16[25...) custom-call(bf16[16,256]{1,0:T(8,128)(2,1)} %far_coef_ref.1, bf16[256,20480]{1,0:T(8,128)(2,1)} %far_ref.1, ...), custom_call_target="tpu_custom_call" | custom-call | flops 167772160 | bytes 11796480 | tf_op jit(solution)/shard_map/phi/pallas_call | solution.py:178
  7.1 0.0 copy-start.2
  7.1 6.4 %collective-permute-start.4 = (f32[24,16]{1,0:T(8,128)S(1)}, f32[24,16]{1,0:T(8,128)S(1)}, u32[]{:S(2)}, u32[]{:S(2)}) collective-permute-start(f32[24,16]{1,0:T(8,128)S(1)} %get-tuple-element.18.own_ref), channel_id=1, source_target_pairs={{1,0},{2,1},{3,2},{4,3},{5,4},{6,5},{7,6},{8,7},{9,8},{10,9},{11,1... | collective-permute-start | bytes 4616 | tf_op jit(solution)/shard_map/ppermute | solution.py:555
  13.5 0.7 %collective-permute-start.1 = (s16[16,5248]{1,0:T(8,128)(2,1)S(1)}, s16[16,5248]{1,0:T(8,128)(2,1)S(1)}, u32[]{:S(2)}, u32[]{:S(2)}) collective-permute-start(s16[16,5248]{1,0:T(8,128)(2,1)S(1)} %get-tuple-element.16), channel_id=1, source_target_pairs={{0,2},{1,3},{2,0},{3,1},{4,6},{5,7},{6,4},{7,5},{8,10},{9,11},{10,... | collective-permute-start | bytes 503816 | tf_op jit(solution)/shard_map/ppermute | solution.py:542
  14.2 2.8 %collective-permute-start.2 = (s16[16,5248]{1,0:T(8,128)(2,1)S(1)}, s16[16,5248]{1,0:T(8,128)(2,1)S(1)}, u32[]{:S(2)}, u32[]{:S(2)}) collective-permute-start(s16[16,5248]{1,0:T(8,128)(2,1)S(1)} %get-tuple-element.17), channel_id=1, source_target_pairs={{0,3},{1,2},{2,1},{3,0},{4,7},{5,6},{6,5},{7,4},{8,11},{9,10},{10,... | collective-permute-start | bytes 503816 | tf_op jit(solution)/shard_map/ppermute | solution.py:542
  17.0 3.4 %collective-permute-done.3.before_ref = f32[24,16]{1,0:T(8,128)S(1)} collective-permute-done((f32[24,16]{1,0:T(8,128)S(1)}, f32[24,16]{1,0:T(8,128)S(1)}, u32[]{:S(2)}, u32[]{:S(2)}) %collective-permute-start.3) | collective-permute-done | bytes 1568 | tf_op jit(solution)/shard_map/ppermute | solution.py:555
  20.4 7.1 %pairs.2 = (bf16[20,512,256]{2,1,0:T(8,128)(2,1)S(1)}, f32[5,1,1280]{2,1,0:T(1,128)S(1)}, f32[48,128]{1,0:T(8,128)S(1)}, f32[32,128]{1,0:T(8,128)S(1)}) custom-call(f32[24,16]{1,0:T(8,128)S(1)} %collective-permute-done.3.before_ref, f32[24,16]{1,0:T(8,128)S(1)} %get-tuple-element.18.own_ref, f32[24,16]{1,0:T(8,128)S(1)} %collective-permute-done.4.after_ref, ...), custom_call_target="tpu_custom_call" | custom-call | flops 2621440000 | bytes 5242880 | tf_op jit(solution)/shard_map/pairs/pallas_call | solution.py:341
  27.5 0.0 collective-permute-done.1.refs_2_
  27.5 0.4 rhs.1.own_ref
  27.9 1.2 %collective-permute-start.6 = (f32[16,1024]{1,0:T(8,128)S(1)}, f32[16,1024]{1,0:T(8,128)S(1)}, u32[]{:S(2)}, u32[]{:S(2)}) collective-permute-start(f32[16,1024]{1,0:T(8,128)S(1)} %rhs.1.own_ref), channel_id=1, source_target_pairs={{1,0},{2,1},{3,2},{4,3},{5,4},{6,5},{7,6},{8,7},{9,8},{10,9},{11,1... | collective-permute-start | bytes 196616 | tf_op jit(solution)/shard_map/ppermute | solution.py:555
  29.1 0.9 %collective-permute-start.5 = (f32[16,1024]{1,0:T(8,128)S(1)}, f32[16,1024]{1,0:T(8,128)S(1)}, u32[]{:S(2)}, u32[]{:S(2)}) collective-permute-start(f32[16,1024]{1,0:T(8,128)S(1)} %rhs.1.own_ref), channel_id=1, source_target_pairs={{0,1},{1,2},{2,3},{3,4},{4,5},{5,6},{6,7},{7,8},{8,9},{9,10},{10,1... | collective-permute-start | bytes 196616 | tf_op jit(solution)/shard_map/ppermute | solution.py:555
  30.0 3.8 %pairs.3.rest_ref = bf16[12,512,256]{2,1,0:T(8,128)(2,1)S(1)} custom-call(f32[48,128]{1,0:T(8,128)S(1)} %get-tuple-element.21.geo, f32[32,128]{1,0:T(8,128)S(1)} %get-tuple-element.23.mask, f32[8,640]{1,0:T(8,128)S(1)} %copy-done.4, bf16[640,256]{1,0:T(8,128)(2,1)S(1)} %copy-done.3), custom_call_target="tpu_custom_call" | custom-call | flops 1572864000 | bytes 3145728 | tf_op jit(solution)/shard_map/pairs/pallas_call | solution.py:341
  33.8 2.8 %collective-permute-done.5.before_ref = f32[16,1024]{1,0:T(8,128)S(1)} collective-permute-done((f32[16,1024]{1,0:T(8,128)S(1)}, f32[16,1024]{1,0:T(8,128)S(1)}, u32[]{:S(2)}, u32[]{:S(2)}) %collective-permute-start.5) | collective-permute-done | bytes 65568 | tf_op jit(solution)/shard_map/ppermute | solution.py:555
  36.5 2.1 %sweeps.1.pay_ref = f32[16,1408]{1,0:T(8,128)S(1)} custom-call(f32[16,1024]{1,0:T(8,128)S(1)} %collective-permute-done.5.before_ref, f32[16,1024]{1,0:T(8,128)S(1)} %rhs.1.own_ref, f32[16,1024]{1,0:T(8,128)S(1)} %collective-permute-done.6.after_ref, bf16[20,512,256]{2,1,0:T(8,128)(2,1)S(1)} %get-tuple-element.20.t_ref, ...), custom_call_target="tpu_custom_call" | custom-call | flops 805306368 | bytes 8388608 | tf_op jit(solution)/shard_map/sweeps/pallas_call | solution.py:460
  38.6 0.0 collective-permute-start.9
  38.6 0.1 collective-permute-start.8
  38.7 3.4 %collective-permute-start.7 = (f32[16,1408]{1,0:T(8,128)S(1)}, f32[16,1408]{1,0:T(8,128)S(1)}, u32[]{:S(2)}, u32[]{:S(2)}) collective-permute-start(f32[16,1408]{1,0:T(8,128)S(1)} %sweeps.1.pay_ref), channel_id=1, source_target_pairs={{0,3},{1,2},{2,1},{3,0},{4,7},{5,6},{6,5},{7,4},{8,11},{9,10},{10,... | collective-permute-start | bytes 270344 | tf_op jit(solution)/shard_map/ppermute | solution.py:542
  42.1 1.1 %fock.4.rest_0_ = f32[16,256]{1,0:T(8,128)S(1)} custom-call(f32[16,1408]{1,0:T(8,128)S(1)} %sweeps.1.pay_ref, bf16[256,1280]{1,0:T(8,128)(2,1)S(1)} %copy-done, bf16[256,20480]{1,0:T(8,128)(2,1)S(1)} %get-tuple-element.24.tile_ref), custom_call_target="tpu_custom_call" | custom-call | flops 41943040 | bytes 2621440 | tf_op jit(solution)/shard_map/fock/pallas_call | solution.py:526
  43.2 1.1 %fock.5.rest_0_ = f32[16,256]{1,0:T(8,128)S(1)} custom-call(f32[16,1408]{1,0:T(8,128)S(1)} %collective-permute-done.9.pay_ref, bf16[256,1280]{1,0:T(8,128)(2,1)S(1)} %copy-done, bf16[256,20480]{1,0:T(8,128)(2,1)S(1)} %get-tuple-element.24.tile_ref, f32[16,256]{1,0:T(8,128)S(1)} %fock.4.rest_0_), custom_call_target="tpu_custom_call" | custom-call | flops 41943040 | bytes 2621440 | tf_op jit(solution)/shard_map/fock/pallas_call | solution.py:526
  44.3 1.1 %fock.6.rest_0_ = f32[16,256]{1,0:T(8,128)S(1)} custom-call(f32[16,1408]{1,0:T(8,128)S(1)} %collective-permute-done.8.pay_ref, bf16[256,1280]{1,0:T(8,128)(2,1)S(1)} %copy-done, bf16[256,20480]{1,0:T(8,128)(2,1)S(1)} %get-tuple-element.24.tile_ref, f32[16,256]{1,0:T(8,128)S(1)} %fock.5.rest_0_), custom_call_target="tpu_custom_call" | custom-call | flops 41943040 | bytes 2621440 | tf_op jit(solution)/shard_map/fock/pallas_call | solution.py:526
  45.4 1.1 %fock.7 = f32[16,256]{1,0:T(8,128)S(1)} custom-call(f32[16,1408]{1,0:T(8,128)S(1)} %collective-permute-done.7.pay_ref, bf16[256,1280]{1,0:T(8,128)(2,1)S(1)} %copy-done, bf16[256,20480]{1,0:T(8,128)(2,1)S(1)} %get-tuple-element.24.tile_ref, f32[16,256]{1,0:T(8,128)S(1)} %fock.6.rest_0_), custom_call_target="tpu_custom_call" | custom-call | flops 41943040 | bytes 2621440 | tf_op jit(solution)/shard_map/fock/pallas_call | solution.py:526
  46.5 1.2 %collective-permute-done.10 = f32[16,256]{1,0:T(8,128)S(1)} collective-permute-done((f32[16,256]{1,0:T(8,128)S(1)}, f32[16,256]{1,0:T(8,128)S(1)}, u32[]{:S(2)}, u32[]{:S(2)}) %collective-permute-start.10) | collective-permute-done | bytes 16416 | tf_op jit(solution)/shard_map/ppermute | solution.py:542
  47.8 0.1 collective-permute-start.12
  47.8 1.9 %collective-permute-start.11 = (f32[16,256]{1,0:T(8,128)S(1)}, f32[16,256]{1,0:T(8,128)S(1)}, u32[]{:S(2)}, u32[]{:S(2)}) collective-permute-start(f32[16,256]{1,0:T(8,128)S(1)} %add.12), channel_id=1, source_target_pairs={{0,8},{4,12},{8,16},{12,20},{16,24},{20,28},{24,0},{28,4},{1,9},{5... | collective-permute-start | bytes 49160 | tf_op jit(solution)/shard_map/ppermute | solution.py:547
  49.8 0.7 %moments.1 = f32[16,16,49]{2,1,0:T(8,128)} custom-call(f32[16,1408]{1,0:T(8,128)S(1)} %sweeps.1.pay_ref), custom_call_target="tpu_custom_call" | custom-call | bytes 200000 | tf_op jit(solution)/shard_map/moments/pallas_call | solution.py:485
  50.5 1.0 %collective-permute-done.13 = f32[16,256]{1,0:T(8,128)S(1)} collective-permute-done((f32[16,256]{1,0:T(8,128)S(1)}, f32[16,256]{1,0:T(8,128)S(1)}, u32[]{:S(2)}, u32[]{:S(2)}) %collective-permute-start.13) | collective-permute-done | bytes 16416 | tf_op jit(solution)/shard_map/ppermute | solution.py:547
  51.5 1.0 %collective-permute-done.12 = f32[16,256]{1,0:T(8,128)S(1)} collective-permute-done((f32[16,256]{1,0:T(8,128)S(1)}, f32[16,256]{1,0:T(8,128)S(1)}, u32[]{:S(2)}, u32[]{:S(2)}) %collective-permute-start.12) | collective-permute-done | bytes 16416 | tf_op jit(solution)/shard_map/ppermute | solution.py:547
  52.5 1.6 %collective-permute-done.11 = f32[16,256]{1,0:T(8,128)S(1)} collective-permute-done((f32[16,256]{1,0:T(8,128)S(1)}, f32[16,256]{1,0:T(8,128)S(1)}, u32[]{:S(2)}, u32[]{:S(2)}) %collective-permute-start.11) | collective-permute-done | bytes 16416 | tf_op jit(solution)/shard_map/ppermute | solution.py:547
  54.0 0.6 %add_add_fusion = f32[16,256]{1,0:T(8,128)} fusion(f32[16,256]{1,0:T(8,128)S(1)} %collective-permute-done.13, f32[16,256]{1,0:T(8,128)S(1)} %collective-permute-done.12, f32[16,256]{1,0:T(8,128)S(1)} %add.12, f32[16,256]{1,0:T(8,128)S(1)} %collective-permute-done.11), kind=kLoop, calls=%fused_computation | loop fusion | flops 12288 | bytes 81920 | tf_op jit(solution)/shard_map/add | solution.py:597
  (18 shorter events, 0.0 us)
Async XLA Ops:
  0.6 19.7 %copy-start.3 = (bf16[640,256]{1,0:T(8,128)(2,1)S(1)}, bf16[640,256]{1,0:T(8,128)(2,1)}, u32[]{:S(2)}) copy-start(bf16[640,256]{1,0:T(8,128)(2,1)} %constant.14.clone.w_ref) | copy-start | bytes 983044
  0.6 19.7 %copy-start.4 = (f32[8,640]{1,0:T(8,128)S(1)}, f32[8,640]{1,0:T(8,128)}, u32[]{:S(2)}) copy-start(f32[8,640]{1,0:T(8,128)} %constant.13.clone.dir_ref) | copy-start | bytes 61444
  0.7 26.8 %copy-start.1 = (bf16[640,256]{1,0:T(8,128)(2,1)S(1)}, bf16[640,256]{1,0:T(8,128)(2,1)}, u32[]{:S(2)}) copy-start(bf16[640,256]{1,0:T(8,128)(2,1)} %constant.10.clone.refs_5_) | copy-start | bytes 983044
  7.1 29.5 %copy-start.2 = (f32[8,128]{1,0:T(8,128)S(1)}, f32[8,128]{1,0:T(8,128)}, u32[]{:S(2)}) copy-start(f32[8,128]{1,0:T(8,128)} %constant.12.clone.sc_ref) | copy-start | bytes 12292
  7.1 9.9 %collective-permute-start.4 = (f32[24,16]{1,0:T(8,128)S(1)}, f32[24,16]{1,0:T(8,128)S(1)}, u32[]{:S(2)}, u32[]{:S(2)}) collective-permute-start(f32[24,16]{1,0:T(8,128)S(1)} %get-tuple-element.18.own_ref), channel_id=1, source_target_pairs={{1,0},{2,1},{3,2},{4,3},{5,4},{6,5},{7,6},{8,7},{9,8},{10,9},{11,1... | collective-permute-start | bytes 4616 | tf_op jit(solution)/shard_map/ppermute | solution.py:555
  13.5 6.9 %collective-permute-start.3 = (f32[24,16]{1,0:T(8,128)S(1)}, f32[24,16]{1,0:T(8,128)S(1)}, u32[]{:S(2)}, u32[]{:S(2)}) collective-permute-start(f32[24,16]{1,0:T(8,128)S(1)} %get-tuple-element.18.own_ref), channel_id=1, source_target_pairs={{0,1},{1,2},{2,3},{3,4},{4,5},{5,6},{6,7},{7,8},{8,9},{9,10},{10,1... | collective-permute-start | bytes 4616 | tf_op jit(solution)/shard_map/ppermute | solution.py:555
  13.5 14.0 %collective-permute-start = (s16[16,5248]{1,0:T(8,128)(2,1)S(1)}, s16[16,5248]{1,0:T(8,128)(2,1)S(1)}, u32[]{:S(2)}, u32[]{:S(2)}) collective-permute-start(s16[16,5248]{1,0:T(8,128)(2,1)S(1)} %get-tuple-element.15), channel_id=1, source_target_pairs={{0,1},{1,0},{2,3},{3,2},{4,5},{5,4},{6,7},{7,6},{8,9},{9,8},{10,11... | collective-permute-start | bytes 503816 | tf_op jit(solution)/shard_map/ppermute | solution.py:542
  13.5 14.0 %collective-permute-start.1 = (s16[16,5248]{1,0:T(8,128)(2,1)S(1)}, s16[16,5248]{1,0:T(8,128)(2,1)S(1)}, u32[]{:S(2)}, u32[]{:S(2)}) collective-permute-start(s16[16,5248]{1,0:T(8,128)(2,1)S(1)} %get-tuple-element.16), channel_id=1, source_target_pairs={{0,2},{1,3},{2,0},{3,1},{4,6},{5,7},{6,4},{7,5},{8,10},{9,11},{10,... | collective-permute-start | bytes 503816 | tf_op jit(solution)/shard_map/ppermute | solution.py:542
  14.2 27.9 %copy-start = (bf16[256,1280]{1,0:T(8,128)(2,1)S(1)}, bf16[256,1280]{1,0:T(8,128)(2,1)}, u32[]{:S(2)}) copy-start(bf16[256,1280]{1,0:T(8,128)(2,1)} %constant.11.clone.y_ref) | copy-start | bytes 1966084
  14.2 13.3 %collective-permute-start.2 = (s16[16,5248]{1,0:T(8,128)(2,1)S(1)}, s16[16,5248]{1,0:T(8,128)(2,1)S(1)}, u32[]{:S(2)}, u32[]{:S(2)}) collective-permute-start(s16[16,5248]{1,0:T(8,128)(2,1)S(1)} %get-tuple-element.17), channel_id=1, source_target_pairs={{0,3},{1,2},{2,1},{3,0},{4,7},{5,6},{6,5},{7,4},{8,11},{9,10},{10,... | collective-permute-start | bytes 503816 | tf_op jit(solution)/shard_map/ppermute | solution.py:542
  27.9 5.9 %collective-permute-start.6 = (f32[16,1024]{1,0:T(8,128)S(1)}, f32[16,1024]{1,0:T(8,128)S(1)}, u32[]{:S(2)}, u32[]{:S(2)}) collective-permute-start(f32[16,1024]{1,0:T(8,128)S(1)} %rhs.1.own_ref), channel_id=1, source_target_pairs={{1,0},{2,1},{3,2},{4,3},{5,4},{6,5},{7,6},{8,7},{9,8},{10,9},{11,1... | collective-permute-start | bytes 196616 | tf_op jit(solution)/shard_map/ppermute | solution.py:555
  29.1 7.4 %collective-permute-start.5 = (f32[16,1024]{1,0:T(8,128)S(1)}, f32[16,1024]{1,0:T(8,128)S(1)}, u32[]{:S(2)}, u32[]{:S(2)}) collective-permute-start(f32[16,1024]{1,0:T(8,128)S(1)} %rhs.1.own_ref), channel_id=1, source_target_pairs={{0,1},{1,2},{2,3},{3,4},{4,5},{5,6},{6,7},{7,8},{8,9},{9,10},{10,1... | collective-permute-start | bytes 196616 | tf_op jit(solution)/shard_map/ppermute | solution.py:555
  38.6 4.6 %collective-permute-start.9 = (f32[16,1408]{1,0:T(8,128)S(1)}, f32[16,1408]{1,0:T(8,128)S(1)}, u32[]{:S(2)}, u32[]{:S(2)}) collective-permute-start(f32[16,1408]{1,0:T(8,128)S(1)} %sweeps.1.pay_ref), channel_id=1, source_target_pairs={{0,1},{1,0},{2,3},{3,2},{4,5},{5,4},{6,7},{7,6},{8,9},{9,8},{10,11... | collective-permute-start | bytes 270344 | tf_op jit(solution)/shard_map/ppermute | solution.py:542
  38.6 5.7 %collective-permute-start.8 = (f32[16,1408]{1,0:T(8,128)S(1)}, f32[16,1408]{1,0:T(8,128)S(1)}, u32[]{:S(2)}, u32[]{:S(2)}) collective-permute-start(f32[16,1408]{1,0:T(8,128)S(1)} %sweeps.1.pay_ref), channel_id=1, source_target_pairs={{0,2},{1,3},{2,0},{3,1},{4,6},{5,7},{6,4},{7,5},{8,10},{9,11},{10,... | collective-permute-start | bytes 270344 | tf_op jit(solution)/shard_map/ppermute | solution.py:542
  38.7 6.7 %collective-permute-start.7 = (f32[16,1408]{1,0:T(8,128)S(1)}, f32[16,1408]{1,0:T(8,128)S(1)}, u32[]{:S(2)}, u32[]{:S(2)}) collective-permute-start(f32[16,1408]{1,0:T(8,128)S(1)} %sweeps.1.pay_ref), channel_id=1, source_target_pairs={{0,3},{1,2},{2,1},{3,0},{4,7},{5,6},{6,5},{7,4},{8,11},{9,10},{10,... | collective-permute-start | bytes 270344 | tf_op jit(solution)/shard_map/ppermute | solution.py:542
  46.5 1.2 %collective-permute-start.10 = (f32[16,256]{1,0:T(8,128)S(1)}, f32[16,256]{1,0:T(8,128)S(1)}, u32[]{:S(2)}, u32[]{:S(2)}) collective-permute-start(f32[16,256]{1,0:T(8,128)S(1)} %fock.7), channel_id=1, source_target_pairs={{0,4},{4,0},{8,12},{12,8},{16,20},{20,16},{24,28},{28,24},{1,5},{5... | collective-permute-start | bytes 49160 | tf_op jit(solution)/shard_map/ppermute | solution.py:542
  47.8 3.8 %collective-permute-start.13 = (f32[16,256]{1,0:T(8,128)S(1)}, f32[16,256]{1,0:T(8,128)S(1)}, u32[]{:S(2)}, u32[]{:S(2)}) collective-permute-start(f32[16,256]{1,0:T(8,128)S(1)} %add.12), channel_id=1, source_target_pairs={{0,24},{4,28},{8,0},{12,4},{16,8},{20,12},{24,16},{28,20},{1,25},{... | collective-permute-start | bytes 49160 | tf_op jit(solution)/shard_map/ppermute | solution.py:547
  47.8 4.7 %collective-permute-start.12 = (f32[16,256]{1,0:T(8,128)S(1)}, f32[16,256]{1,0:T(8,128)S(1)}, u32[]{:S(2)}, u32[]{:S(2)}) collective-permute-start(f32[16,256]{1,0:T(8,128)S(1)} %add.12), channel_id=1, source_target_pairs={{0,16},{4,20},{8,24},{12,28},{16,0},{20,4},{24,8},{28,12},{1,17},{... | collective-permute-start | bytes 49160 | tf_op jit(solution)/shard_map/ppermute | solution.py:547
  47.8 6.2 %collective-permute-start.11 = (f32[16,256]{1,0:T(8,128)S(1)}, f32[16,256]{1,0:T(8,128)S(1)}, u32[]{:S(2)}, u32[]{:S(2)}) collective-permute-start(f32[16,256]{1,0:T(8,128)S(1)} %add.12), channel_id=1, source_target_pairs={{0,8},{4,12},{8,16},{12,20},{16,24},{20,28},{24,0},{28,4},{1,9},{5... | collective-permute-start | bytes 49160 | tf_op jit(solution)/shard_map/ppermute | solution.py:547
